TPU v7x, 512 devices: a whole 4x8x8 slice. The times are simulated.
512 devices in a mesh: row: 16 (over x, y_hi, core), col: 32 (over z, y_lo).
Axes of the slice: x: 4, y: 8 (y_hi: 2, y_lo: 4; y = y_hi * 4 + y_lo), z: 8, core: 2. Of those that a mesh axis runs over, the one named last changes fastest.
Arguments:
- observations: float32 [4096, 32768], P('row', 'col'), may hold values from -6 to 6
- omega: float32 [32, 3, 16, 128, 128], P('col'), as said below
- block_slots: int32 [32, 3, 16], P('col'), may hold values from -1 to 63, as said below
Outputs:
- new_omega: float32 [32, 3, 16, 128, 128], P('col', None, 'row')
Inputs may be any that keep to these rules, and one draw needn't show every extreme that they name: `block_slots`: active slots come first in each tile. The pattern is symmetric: slot j of [t, 2] and slot j of [t + 1, 0] (modulo 32) name mirrored blocks, a and b swapped; in [t, 1] the 8 diagonal blocks come first in order, then mirrored pairs side by side. Some tile has all 16 slots active. `omega`: the blocks of active slots form one symmetric matrix: the block of slot j of [t, 2] is the transpose of that of slot j of [t + 1, 0], mirrored pairs of [t, 1] are transposes of each other, and diagonal blocks are symmetric with diagonal entries of 0.8 or more. Empty slots hold arbitrary values.
All inputs are finite; a program needn't handle non-finite values.
Results may differ from a plain program's by a relative error of at most 0.0003.
Values sent between devices are 32-bit elements; how exact they have to be, the bound alone decides.
No kernel may reach another device: no remote copies, remote signals or barrier semaphores. Data moves between devices by JAX's collectives and lax.ppermute only.
A program may use at most 128 MiB of HBM per device.

v0:
```python
import jax
import jax.numpy as jnp
from jax import lax
from jax.sharding import PartitionSpec as P

TILE = 1024
BLK = 128


step_size = 0.5
penalty = 0.1
highest = lax.Precision.HIGHEST


def shifted(value, axis, steps):
    count = lax.axis_size(axis)
    pairs = [(source, (source + steps) % count) for source in range(count)]
    return lax.ppermute(value, axis, pairs)


def local_terms(nearby, omega_strip, slot_ids):
    tile_blocks = TILE // BLK
    active = slot_ids >= 0
    row_pick = jax.nn.one_hot(
        jnp.where(active, slot_ids // tile_blocks, -1), tile_blocks, dtype=jnp.float32
    )
    col_pick = jax.nn.one_hot(
        jnp.where(active, slot_ids % tile_blocks, -1), tile_blocks, dtype=jnp.float32
    )
    chosen = jnp.einsum("ejn,epnk->ejpk", row_pick, nearby, precision=highest)
    product = jnp.einsum("ejpk,ejkl->ejpl", chosen, omega_strip, precision=highest)
    residual = jnp.einsum("ejn,ejpl->pnl", col_pick, product, precision=highest)
    picked = jnp.einsum("ejn,pnl->ejpl", col_pick, residual, precision=highest)
    return jnp.einsum("ejpk,ejpl->ejkl", chosen, picked, precision=highest)


def mirror_inner(forward_centre, centre_ids):
    tile_blocks = TILE // BLK
    active = centre_ids >= 0
    flipped = jnp.where(
        active, centre_ids % tile_blocks * tile_blocks + centre_ids // tile_blocks, -2
    )
    match_table = (
        (centre_ids[..., None, :] == flipped[..., :, None]) & active[..., None, :]
    ).astype(jnp.float32)
    return jnp.einsum("...jk,...kab->...jba", match_table, forward_centre, precision=highest)


def proximal(omega_part, slot_part, smooth):
    tile_blocks = TILE // BLK
    active = slot_part >= 0
    centre_mask = (jnp.arange(3) == 1)[:, None]
    diagonal_block = active & centre_mask & (slot_part // tile_blocks == slot_part % tile_blocks)
    identity = jnp.eye(BLK, dtype=jnp.float32)
    own_diag = jnp.diagonal(omega_part, axis1=-2, axis2=-1)
    safe_diag = jnp.where(diagonal_block[..., None], own_diag, 1.0)
    inverse = jnp.where(diagonal_block[..., None], 1.0 / safe_diag, 0.0)
    gradient = smooth - inverse[..., None] * identity
    trial_step = omega_part - step_size * gradient
    shrunk = jnp.sign(trial_step) * jnp.maximum(jnp.abs(trial_step) - step_size * penalty, 0.0)
    keep_mask = diagonal_block[..., None, None] & (identity > 0.5)
    result = jnp.where(keep_mask, trial_step, shrunk)
    return jnp.where(active[..., None, None], result, 0.0)


def on_device(observations, omega, block_slots):
    tile_blocks = TILE // BLK
    omega_strip = omega[0]
    slot_ids = block_slots[0]
    from_below = shifted(observations, "col", 1)
    from_above = shifted(observations, "col", -1)
    nearby = jnp.stack([from_below, observations, from_above])
    nearby = nearby.reshape(3, observations.shape[0], tile_blocks, BLK)
    forward = local_terms(nearby, omega_strip, slot_ids)
    inner_half = 0.5 * (forward[1] + mirror_inner(forward[1], slot_ids[1]))
    left_part = shifted(forward[2], "col", 1)
    right_part = shifted(forward[0], "col", -1)
    halves = jnp.stack(
        [
            0.5 * (forward[0] + jnp.swapaxes(left_part, 1, 2)),
            inner_half,
            0.5 * (forward[2] + jnp.swapaxes(right_part, 1, 2)),
        ]
    )
    summed = lax.psum_scatter(halves, "row", scatter_dimension=1, tiled=True)
    sample_count = observations.shape[0] * lax.axis_size("row")
    smooth = summed / sample_count
    share_slots = summed.shape[1]
    first_slot = lax.axis_index("row") * share_slots
    omega_share = lax.dynamic_slice_in_dim(omega_strip, first_slot, share_slots, 1)
    slot_share = lax.dynamic_slice_in_dim(slot_ids, first_slot, share_slots, 1)
    return proximal(omega_share, slot_share, smooth)[None]


def solution(mesh):
    return jax.shard_map(
        on_device,
        mesh=mesh,
        in_specs=(P("row", "col"), P("col", None, None, None, None), P("col", None, None)),
        out_specs=P("col", None, "row", None, None),
        check_vma=False,
    )
```

profile of v0, /device:TPU:175, one launch (start us, length us, event | category | flops | bytes accessed | tf_op | source)
XLA Modules:
  0.0 397.5 jit_solution(16834701100449850159)
XLA Ops:
  6.5 0.0 all-reduce.3.cloned.1.call-start
  6.5 2.3 collective-permute-start
  8.8 3.0 collective-permute-start.1
  11.8 1.4 copy.39
  13.3 0.7 fusion.42
  14.0 18.7 %collective-permute-done = f32[256,1024]{1,0:T(8,128)S(1)} collective-permute-done((f32[256,1024]{1,0:T(8,128)}, f32[256,1024]{1,0:T(8,128)S(1)}, u32[]{:S(2)}, u32[]{:S(2)}) %collective-permute-start) | collective-permute-done | bytes 1048608 | tf_op jit(solution)/shard_map/ppermute | solution.py:18
  32.7 0.2 copy.38
  32.9 24.4 %collective-permute-done.1 = f32[256,1024]{1,0:T(8,128)S(1)} collective-permute-done((f32[256,1024]{1,0:T(8,128)}, f32[256,1024]{1,0:T(8,128)S(1)}, u32[]{:S(2)}, u32[]{:S(2)}) %collective-permute-start.1) | collective-permute-done | bytes 1048608 | tf_op jit(solution)/shard_map/ppermute | solution.py:18
  57.3 0.2 copy.40
  57.5 4.6 %fusion.4 = f32[3,16,256,128]{3,1,2,0:T(8,128)} fusion(f32[1,256,8,128]{3,2,1,0:T(8,128)S(1)} %bitcast.124, f32[1,256,8,128]{3,2,1,0:T(8,128)S(1)} %bitcast.122, f32[1,256,8,128]{3,2,1,0:T(8,128)S(1)} %bitcast.123, s32[3,16]{1,0:T(4,128)S(1)} %get-tuple-element.11), kind=kOutput, calls=%fused_computation.5 | convolution fusion | flops 152568192 | bytes 9437376 | tf_op jit(solution)/shard_map/ejn,epnk->ejpk/dot_general | solution.py:30
  62.0 0.0 copy-start.1
  62.0 6.8 %copy.22 = f32[3,16,256,128]{2,3,1,0:T(8,128)} copy(f32[3,16,256,128]{3,1,2,0:T(8,128)} %fusion.4) | data formatting | bytes 12582912 | tf_op jit(solution)/shard_map/ejn,epnk->ejpk/dot_general | solution.py:30
  68.8 0.0 copy-done.1
  68.8 13.2 %fusion.10 = f32[3,16,256,128]{3,2,1,0:T(8,128)S(1)} fusion(f32[3,16,256,128]{2,3,1,0:T(8,128)} %copy.22, f32[1,3,16,128,128]{4,3,2,1,0:T(8,128)S(1)} %copy-done.1), kind=kOutput, calls=%fused_computation.12 | convolution fusion | flops 2415919104 | bytes 15728640 | tf_op jit(solution)/shard_map/ejpk,ejkl->ejpl/dot_general | solution.py:31
  82.0 5.7 %fusion.12 = f32[256,8,128,1]{2,1,0,3:T(8,128)S(1)} fusion(f32[3,16,256,128]{3,2,1,0:T(8,128)S(1)} %fusion.10, s32[3,16]{1,0:T(4,128)S(1)} %get-tuple-element.10), kind=kOutput, calls=%fused_computation.14 | convolution fusion | flops 150995328 | bytes 7340224 | tf_op jit(solution)/shard_map/ejn,ejpl->pnl/dot_general | solution.py:32
  87.7 0.0 copy-start
  87.7 2.7 fusion.30
  90.4 0.1 copy-done
  90.5 7.9 %fusion = f32[3,16,128,128]{3,2,1,0:T(8,128)S(1)} fusion(f32[3,16,256,128]{2,3,1,0:T(8,128)S(1)} %copy-done, f32[3,16,256,128]{3,1,2,0:T(8,128)S(1)} %fusion.30), kind=kOutput, calls=%fused_computation.1 | convolution fusion | flops 2415919104 | bytes 15728640 | tf_op jit(solution)/shard_map/ejpk,ejpl->ejkl/dot_general | solution.py:34
  98.4 0.0 copy-start.2
  98.5 1.7 slice_bitcast_fusion
  100.2 2.8 collective-permute-start.3
  103.0 0.0 copy-done.2
  103.1 2.5 copy.37
  105.6 2.7 collective-permute-start.2
  108.3 3.4 fusion.19
  111.8 2.6 copy.26
  114.3 11.6 %collective-permute-done.3 = f32[16,128,128]{2,1,0:T(8,128)} collective-permute-done((f32[16,128,128]{2,1,0:T(8,128)}, f32[16,128,128]{2,1,0:T(8,128)}, u32[]{:S(2)}, u32[]{:S(2)}) %collective-permute-start.3) | collective-permute-done | bytes 1048608 | tf_op jit(solution)/shard_map/ppermute | solution.py:18
  125.9 2.6 bitcast_add_fusion
  128.5 2.5 copy.27
  131.1 1.3 multiply_bitcast_fusion
  132.4 17.1 %collective-permute-done.2 = f32[16,128,128]{1,2,0:T(8,128)} collective-permute-done((f32[16,128,128]{1,2,0:T(8,128)}, f32[16,128,128]{1,2,0:T(8,128)}, u32[]{:S(2)}, u32[]{:S(2)}) %collective-permute-start.2) | collective-permute-done | bytes 1048608 | tf_op jit(solution)/shard_map/ppermute | solution.py:18
  149.5 1.8 fusion.18
  151.3 1.9 pad_maximum_fusion
  153.3 0.0 all-reduce.3.cloned.1.call-update
  153.3 0.9 constant_dynamic-slice_fusion
  154.3 4.6 %copy.28 = f32[1,3,1,128,128]{1,4,3,2,0:T(8,128)} copy(f32[1,3,1,128,128]{4,3,2,1,0:T(8,128)S(1)} %constant_dynamic-slice_fusion) | data formatting | bytes 393216 | tf_op jit(solution)/shard_map/dynamic_slice | solution.py:90
  158.9 1.8 gather_fusion
  160.7 0.2 dynamic-slice_reduce_fusion
  161.0 0.1 copy.29
  161.0 1.3 dynamic-slice.2
  162.4 225.7 %all-reduce.3.cloned.1.call-done = f32[3,16,128,128]{3,2,1,0:T(8,128)} async-done(((f32[3,16,128,128]{3,2,1,0:T(8,128)}), f32[3,16,128,128]{3,2,1,0:T(8,128)}) %all-reduce.3.cloned.1.call-update) | async-done | bytes 3145744
  388.1 2.5 select_bitcast_fusion
  (7 shorter events, 0.1 us)
Async XLA Ops:
  6.5 381.5 %all-reduce.3.cloned.1.call-start = ((), (), s32[]{:S(2)}) async-start(), calls=%async_computation | async-start | bytes 6291456
  6.5 26.1 %collective-permute-start = (f32[256,1024]{1,0:T(8,128)}, f32[256,1024]{1,0:T(8,128)S(1)}, u32[]{:S(2)}, u32[]{:S(2)}) collective-permute-start(f32[256,1024]{1,0:T(8,128)} %param.3), channel_id=1, source_target_pairs={{0,1},{1,2},{2,3},{3,4},{4,5},{5,6},{6,7},{7,8},{8,9},{9,10},{10,1... | collective-permute-start | bytes 3145736 | tf_op jit(solution)/shard_map/ppermute | solution.py:18
  8.8 48.4 %collective-permute-start.1 = (f32[256,1024]{1,0:T(8,128)}, f32[256,1024]{1,0:T(8,128)S(1)}, u32[]{:S(2)}, u32[]{:S(2)}) collective-permute-start(f32[256,1024]{1,0:T(8,128)} %param.3), channel_id=1, source_target_pairs={{0,31},{1,0},{2,1},{3,2},{4,3},{5,4},{6,5},{7,6},{8,7},{9,8},{10,9... | collective-permute-start | bytes 3145736 | tf_op jit(solution)/shard_map/ppermute | solution.py:18
  62.0 6.8 %copy-start.1 = (f32[1,3,16,128,128]{4,3,2,1,0:T(8,128)S(1)}, f32[1,3,16,128,128]{4,3,2,1,0:T(8,128)}, u32[]{:S(2)}) copy-start(f32[1,3,16,128,128]{4,3,2,1,0:T(8,128)} %param.4) | copy-start | bytes 9437188
  87.7 2.8 copy-start
  98.4 4.6 %copy-start.2 = (s32[1,3,16]{2,0,1:T(1,128)S(1)}, s32[1,3,16]{2,0,1:T(1,128)}, u32[]{:S(2)}) copy-start(s32[1,3,16]{2,0,1:T(1,128)} %param.5) | copy-start | bytes 580
  100.2 25.7 %collective-permute-start.3 = (f32[16,128,128]{2,1,0:T(8,128)}, f32[16,128,128]{2,1,0:T(8,128)}, u32[]{:S(2)}, u32[]{:S(2)}) collective-permute-start(f32[16,128,128]{2,1,0:T(8,128)} %get-tuple-element.9), channel_id=1, source_target_pairs={{0,31},{1,0},{2,1},{3,2},{4,3},{5,4},{6,5},{7,6},{8,7},{9,8},{10,9... | collective-permute-start | bytes 3145736 | tf_op jit(solution)/shard_map/ppermute | solution.py:18
  105.6 43.9 %collective-permute-start.2 = (f32[16,128,128]{1,2,0:T(8,128)}, f32[16,128,128]{1,2,0:T(8,128)}, u32[]{:S(2)}, u32[]{:S(2)}) collective-permute-start(f32[16,128,128]{1,2,0:T(8,128)} %bitcast.121), channel_id=1, source_target_pairs={{0,1},{1,2},{2,3},{3,4},{4,5},{5,6},{6,7},{7,8},{8,9},{9,10},{10,1... | collective-permute-start | bytes 3145736 | tf_op jit(solution)/shard_map/ppermute | solution.py:18
Sparse Core Ops, SparseCore 0:
  153.4 234.6 all-reduce.2
where the time goes:
time: 398 us; the launch traced here: 397 us
  waiting for transfers between devices  297 us (75%)
  matrix products  37.5 us (9%)
  local copies, waits for them, and re-layouts  27.1 us (7%)
  between operations  13.5 us (3%)
  other arithmetic  11 us (3%)
  starting transfers between devices  10.8 us (3%)
    unnamed x2, waiting for transfers between devices  226 us
    ppermute x4, waiting for transfers between devices, shifted(): return lax.ppermute(value, axis, pairs)  71.8 us
    dot_general x1, matrix products, local_terms(): jnp.einsum('ejpk,ejkl->ejpl', chosen, omega_strip, precision=highest)  13.2 us
    ppermute x4, starting transfers between devices, shifted(): return lax.ppermute(value, axis, pairs)  10.8 us
  transfers between devices with their start and end apart: 5, of which 5 were waited for; matrix products, arithmetic and copies ran while one was open for 7% of the time, Pallas kernels for 0%

commit v1 on v0

v1 whole, which is shorter than its diff:
```python
import jax
import jax.numpy as jnp
from jax import lax
from jax.experimental import pallas as pl
from jax.experimental.pallas import tpu as pltpu
from jax.sharding import Mesh, PartitionSpec as P

TILE = 1024
BLK = 128
NB = TILE // BLK
KMAX = 16
ROWS = 256
SAMPLES = 4096
step_size = 0.5
penalty = 0.1
f32 = jnp.float32
bf16 = jnp.bfloat16
VMEM_LIMIT = 48 * 1024 * 1024


def split(value):
    high = value.astype(bf16)
    low = (value - high.astype(f32)).astype(bf16)
    return high, low


def split_tile(x_ref, natural_ref, turned_ref):
    for a in range(NB):
        block = x_ref[:, a * BLK : (a + 1) * BLK]
        high, low = split(block)
        natural_ref[a, :, :BLK] = high
        natural_ref[a, :, BLK:] = low
        high, low = split(block.T)
        turned_ref[a, :BLK, :] = high
        turned_ref[a, BLK:, :] = low


def add_products(slots_ref, omega_ref, natural_ref, residual_ref, offset):
    def body(j, carry):
        slot = slots_ref[0, offset, j]
        active = slot >= 0
        place = jnp.maximum(slot, 0)
        a = place // NB
        b = place % NB
        weight = jnp.where(active, omega_ref[0, 0, j], 0.0)
        high, low = split(weight)
        half = jnp.concatenate([high, low], axis=1)
        weights = jnp.concatenate([half, half], axis=0)
        out = jnp.dot(natural_ref[a], weights, preferred_element_type=f32)
        residual_ref[b] += out[:, :BLK] + out[:, BLK:]
        return carry

    lax.fori_loop(0, KMAX, body, 0, unroll=4)


def partial_kernel(offset, first, *refs):
    if first:
        slots_ref, x_ref, omega_ref, residual_ref, turned_ref, natural_ref = refs
        residual_ref[...] = jnp.zeros_like(residual_ref)
    else:
        slots_ref, x_ref, omega_ref, before_ref, residual_ref, turned_ref, natural_ref = refs
        residual_ref[...] = before_ref[...]
    split_tile(x_ref, natural_ref, turned_ref)
    add_products(slots_ref, omega_ref, natural_ref, residual_ref, offset)


def quadrant_sum(out):
    out = out[:BLK] + out[BLK:]
    return out[:, :BLK] + out[:, BLK:]


def forward_kernel(
    slots_ref, core_ref, x_ref, omega_ref, before_ref, below_ref, centre_ref,
    own_ref, send_ref, residual_ref, natural_ref, above_ref, pieces_ref,
):
    residual_ref[...] = before_ref[...]
    split_tile(x_ref, natural_ref, above_ref)
    add_products(slots_ref, omega_ref, natural_ref, residual_ref, 2)
    for b in range(NB):
        high, low = split(residual_ref[b])
        pieces_ref[b, :, :BLK] = high
        pieces_ref[b, :, BLK:] = low
    core = core_ref[0]
    turned = (below_ref, centre_ref, above_ref)

    def body(i, carry):
        for e in range(3):
            found = []
            for k in range(2):
                place = jnp.maximum(slots_ref[0, e, 2 * i + k], 0)
                a = place // NB
                b = place % NB
                out = jnp.dot(turned[e][a], pieces_ref[b], preferred_element_type=f32)
                found.append(quadrant_sum(out))
            even, odd = found
            if e == 1:
                even_turned, odd_turned = even.T, odd.T
                diagonal = i < NB // 2
                even, odd = (
                    even + jnp.where(diagonal, even_turned, odd_turned),
                    odd + jnp.where(diagonal, odd_turned, even_turned),
                )
            own_ref[i, e] = jnp.where(core == 0, even, odd)
            send_ref[i, e] = jnp.where(core == 0, odd, even)
        return carry

    lax.fori_loop(0, KMAX // 2, body, 0)


def proximal_kernel(
    place_ref, slots_ref, total_ref, left_ref, right_ref, omega_ref, out_ref
):
    j = place_ref[0]
    rows = lax.broadcasted_iota(jnp.int32, (BLK, BLK), 0)
    columns = lax.broadcasted_iota(jnp.int32, (BLK, BLK), 1)
    for e in range(3):
        slot = slots_ref[0, e, j]
        total = total_ref[e]
        if e == 0:
            total = total + left_ref[...].T
        if e == 2:
            total = total + right_ref[...].T
        gradient = total * (0.5 / SAMPLES)
        omega = omega_ref[0, e, 0]
        if e == 1:
            diagonal = (slot >= 0) & (slot // NB == slot % NB)
            on_diagonal = (rows == columns) & diagonal
            inverse = 1.0 / jnp.where(on_diagonal, omega, 1.0)
            gradient = gradient - jnp.where(on_diagonal, inverse, 0.0)
        trial = omega - step_size * gradient
        shrunk = jnp.maximum(jnp.abs(trial) - step_size * penalty, 0.0)
        result = jnp.where(trial < 0.0, -shrunk, shrunk)
        if e == 1:
            result = jnp.where(on_diagonal, trial, result)
        out_ref[0, e, 0] = jnp.where(slot >= 0, result, 0.0)


def params():
    return pltpu.CompilerParams(vmem_limit_bytes=VMEM_LIMIT)


SMEM = pl.BlockSpec(memory_space=pltpu.SMEM)
WHOLE = pl.BlockSpec(memory_space=pltpu.VMEM)
TURNED = (NB, 2 * BLK, ROWS)
NATURAL = (NB, ROWS, 2 * BLK)


def omega_spec(offset):
    return pl.BlockSpec((1, 1, KMAX, BLK, BLK), lambda i: (0, offset, 0, 0, 0))


def full_spec(shape):
    return pl.BlockSpec(shape, lambda i: (0,) * len(shape))


def partial(offset, slots, tile, omega, before=None):
    first = before is None
    in_specs = [SMEM, full_spec((ROWS, TILE)), omega_spec(offset)]
    inputs = [slots, tile, omega]
    if not first:
        in_specs.append(full_spec((NB, ROWS, BLK)))
        inputs.append(before)
    return pl.pallas_call(
        lambda *refs: partial_kernel(offset, first, *refs),
        name="partial_residual",
        grid=(1,),
        out_shape=(
            jax.ShapeDtypeStruct((NB, ROWS, BLK), f32),
            jax.ShapeDtypeStruct(TURNED, bf16),
        ),
        in_specs=in_specs,
        out_specs=(full_spec((NB, ROWS, BLK)), full_spec(TURNED)),
        scratch_shapes=[pltpu.VMEM(NATURAL, bf16)],
        compiler_params=params(),
        cost_estimate=pl.CostEstimate(
            flops=2 * KMAX * ROWS * 256 * 256, bytes_accessed=5 << 20, transcendentals=0
        ),
    )(*inputs)


def forward_blocks(slots, core, tile, omega, before, below, centre):
    shape = (KMAX // 2, 3, BLK, BLK)
    return pl.pallas_call(
        forward_kernel,
        name="forward_blocks",
        grid=(1,),
        out_shape=(jax.ShapeDtypeStruct(shape, f32),) * 2,
        in_specs=[
            SMEM,
            SMEM,
            full_spec((ROWS, TILE)),
            omega_spec(2),
            full_spec((NB, ROWS, BLK)),
            full_spec(TURNED),
            full_spec(TURNED),
        ],
        out_specs=(full_spec(shape),) * 2,
        scratch_shapes=[
            pltpu.VMEM((NB, ROWS, BLK), f32),
            pltpu.VMEM(NATURAL, bf16),
            pltpu.VMEM(TURNED, bf16),
            pltpu.VMEM(NATURAL, bf16),
        ],
        compiler_params=params(),
        cost_estimate=pl.CostEstimate(
            flops=8 * KMAX * ROWS * 256 * 256, bytes_accessed=8 << 20, transcendentals=0
        ),
    )(slots, core, tile, omega, before, below, centre)


def proximal(place, slots, total, left, right, omega):
    return pl.pallas_call(
        proximal_kernel,
        name="proximal",
        grid_spec=pltpu.PrefetchScalarGridSpec(
            num_scalar_prefetch=2,
            grid=(1,),
            in_specs=[
                pl.BlockSpec((3, BLK, BLK), lambda i, place, slots: (0, 0, 0)),
                pl.BlockSpec((BLK, BLK), lambda i, place, slots: (0, 0)),
                pl.BlockSpec((BLK, BLK), lambda i, place, slots: (0, 0)),
                pl.BlockSpec(
                    (1, 3, 1, BLK, BLK), lambda i, place, slots: (0, 0, place[0], 0, 0)
                ),
            ],
            out_specs=pl.BlockSpec(
                (1, 3, 1, BLK, BLK), lambda i, place, slots: (0, 0, 0, 0, 0)
            ),
        ),
        out_shape=jax.ShapeDtypeStruct((1, 3, 1, BLK, BLK), f32),
        compiler_params=params(),
        cost_estimate=pl.CostEstimate(
            flops=20 * 3 * BLK * BLK, bytes_accessed=1 << 19, transcendentals=0
        ),
    )(place, slots, total, left, right, omega)


def shifted(value, axis, steps):
    count = lax.axis_size(axis)
    pairs = [(source, (source + steps) % count) for source in range(count)]
    return lax.ppermute(value, axis, pairs)


def on_device(observations, omega, block_slots):
    core = lax.axis_index("core").astype(jnp.int32)
    place = lax.axis_index(("x", "y_hi", "core")).astype(jnp.int32)
    from_below = shifted(observations, "col", 1)
    from_above = shifted(observations, "col", -1)
    residual, centre = partial(1, block_slots, observations, omega)
    residual, below = partial(0, block_slots, from_below, omega, residual)
    own, send = forward_blocks(
        block_slots, core.reshape(1), from_above, omega, residual, below, centre
    )
    chip = own + shifted(send, "core", 1)
    gathered = lax.all_to_all(chip, ("x", "y_hi"), 0, 0)
    total = jnp.sum(gathered, axis=0)
    left = shifted(total[2], "col", 1)
    right = shifted(total[0], "col", -1)
    return proximal(place.reshape(1), block_slots, total, left, right, omega)


def solution(mesh):
    devices = mesh.devices.reshape(4, 2, 2, 32)
    fine = Mesh(devices, ("x", "y_hi", "core", "col"))
    rows = ("x", "y_hi", "core")
    return jax.shard_map(
        on_device,
        mesh=fine,
        in_specs=(P(rows, "col"), P("col", None, None, None, None), P("col", None, None)),
        out_specs=P("col", None, rows, None, None),
        check_vma=False,
    )
```

time: 398 us -> 137 us (0.34)
  the two profiles are of different devices: /device:TPU:175 before, /device:TPU:6 now
where the time goes in v1:
time: 137 us
  starting transfers between devices  42.3 us (31%)
  waiting for transfers between devices  40.7 us (30%)
  blocking collectives  34.7 us (25%)
  Pallas kernels  14.5 us (11%)
  local copies, waits for them, and re-layouts  2.55 us (2%)
  other arithmetic  1.71 us (1%)
    ppermute x5, starting transfers between devices, shifted(): return lax.ppermute(value, axis, pairs)  42.3 us
    ppermute x5, waiting for transfers between devices, shifted(): return lax.ppermute(value, axis, pairs)  40.7 us
    all_to_all x1, blocking collectives, on_device(): gathered = lax.all_to_all(chip, ('x', 'y_hi'), 0, 0)  34.7 us
    pallas_call x1, Pallas kernels, forward_blocks(): pl.pallas_call(forward_kernel, name='forward_blocks', grid=(1,), out_shap...  7.3 us
    pallas_call x2, Pallas kernels, partial(): pl.pallas_call(lambda *refs: partial_kernel(offset, first, *refs), name='...  5.83 us
  transfers between devices with their start and end apart: 5, of which 5 were waited for; matrix products, arithmetic and copies ran while one was open for 1% of the time, Pallas kernels for 4%

profile of v1, /device:TPU:6, one launch (start us, length us, event | category | flops | bytes accessed | tf_op | source)
XLA Modules:
  0.0 136.5 jit_solution(16512459151237014010)
XLA Ops:
  0.0 3.5 %collective-permute-start.1 = (f32[256,1024]{1,0:T(8,128)}, f32[256,1024]{1,0:T(8,128)S(1)}, u32[]{:S(2)}, u32[]{:S(2)}) collective-permute-start(f32[256,1024]{1,0:T(8,128)} %refs_1_.1), channel_id=1, source_target_pairs={{0,1},{1,2},{2,3},{3,4},{4,5},{5,6},{6,7},{7,8},{8,9},{9,10},{10,1... | collective-permute-start | bytes 3145736 | tf_op jit(solution)/shard_map/ppermute | solution.py:241
  3.5 12.4 %collective-permute-start = (f32[256,1024]{1,0:T(8,128)}, f32[256,1024]{1,0:T(8,128)S(1)}, u32[]{:S(2)}, u32[]{:S(2)}) collective-permute-start(f32[256,1024]{1,0:T(8,128)} %refs_1_.1), channel_id=1, source_target_pairs={{0,31},{1,0},{2,1},{3,2},{4,3},{5,4},{6,5},{7,6},{8,7},{9,8},{10,9... | collective-permute-start | bytes 3145736 | tf_op jit(solution)/shard_map/ppermute | solution.py:241
  15.9 0.7 copy.7.refs_0_.slots_ref
  16.6 0.0 copy-start.1
  16.6 1.2 copy-done.1
  17.8 2.9 %partial_residual.2 = (f32[8,256,128]{2,1,0:T(8,128)S(1)}, bf16[8,256,256]{2,1,0:T(8,128)(2,1)S(1)}) custom-call(s32[1,3,16]{2,1,0:T(4,128)S(1)} %copy.7.refs_0_.slots_ref, f32[256,1024]{1,0:T(8,128)S(1)} %copy-done.1, f32[1,3,16,128,128]{4,3,2,1,0:T(8,128)} %omega_ref.3), custom_call_target="tpu_custom_call" | custom-call | flops 536870912 | bytes 5242880 | tf_op jit(solution)/shard_map/partial_residual/pallas_call | solution.py:163
  20.8 17.4 %collective-permute-done.1.refs_1_ = f32[256,1024]{1,0:T(8,128)S(1)} collective-permute-done((f32[256,1024]{1,0:T(8,128)}, f32[256,1024]{1,0:T(8,128)S(1)}, u32[]{:S(2)}, u32[]{:S(2)}) %collective-permute-start.1) | collective-permute-done | bytes 1048608 | tf_op jit(solution)/shard_map/ppermute | solution.py:241
  38.2 2.9 %partial_residual.3 = (f32[8,256,128]{2,1,0:T(8,128)S(1)}, bf16[8,256,256]{2,1,0:T(8,128)(2,1)S(1)}) custom-call(s32[1,3,16]{2,1,0:T(4,128)S(1)} %copy.7.refs_0_.slots_ref, f32[256,1024]{1,0:T(8,128)S(1)} %collective-permute-done.1.refs_1_, f32[1,3,16,128,128]{4,3,2,1,0:T(8,128)} %omega_ref.3, f32[8,256,128]{2,1,0:T(8,128)S(1)} %get-tuple-element.11.refs_3_), custom_call_target="tpu_custom_call" | custom-call | flops 536870912 | bytes 5242880 | tf_op jit(solution)/shard_map/partial_residual/pallas_call | solution.py:163
  41.1 11.5 %collective-permute-done.x_ref = f32[256,1024]{1,0:T(8,128)S(1)} collective-permute-done((f32[256,1024]{1,0:T(8,128)}, f32[256,1024]{1,0:T(8,128)S(1)}, u32[]{:S(2)}, u32[]{:S(2)}) %collective-permute-start) | collective-permute-done | bytes 1048608 | tf_op jit(solution)/shard_map/ppermute | solution.py:241
  52.7 7.3 %forward_blocks.1 = (f32[8,3,128,128]{3,2,1,0:T(8,128)S(1)}, f32[8,3,128,128]{3,2,1,0:T(8,128)}) custom-call(s32[1,3,16]{2,1,0:T(4,128)S(1)} %copy.7.refs_0_.slots_ref, s32[1]{0:T(128)} %bitcast.1.core_ref, f32[256,1024]{1,0:T(8,128)S(1)} %collective-permute-done.x_ref, f32[1,3,16,128,128]{4,3,2,1,0:T(8,128)} %omega_ref.3, ...), custom_call_target="tpu_custom_call" | custom-call | flops 2147483648 | bytes 8388608 | tf_op jit(solution)/shard_map/forward_blocks/pallas_call | solution.py:183
  60.0 1.9 %collective-permute-start.2 = (f32[8,3,128,128]{3,2,1,0:T(8,128)}, f32[8,3,128,128]{3,2,1,0:T(8,128)S(1)}, u32[]{:S(2)}, u32[]{:S(2)}) collective-permute-start(f32[8,3,128,128]{3,2,1,0:T(8,128)} %get-tuple-element.16), channel_id=1, source_target_pairs={{0,32},{32,0},{1,33},{33,1},{2,34},{34,2},{3,35},{35,3},{4,36},{36... | collective-permute-start | bytes 4718600 | tf_op jit(solution)/shard_map/ppermute | solution.py:241
  61.9 3.6 %collective-permute-done.2 = f32[8,3,128,128]{3,2,1,0:T(8,128)S(1)} collective-permute-done((f32[8,3,128,128]{3,2,1,0:T(8,128)}, f32[8,3,128,128]{3,2,1,0:T(8,128)S(1)}, u32[]{:S(2)}, u32[]{:S(2)}) %collective-permute-start.2) | collective-permute-done | bytes 1572896 | tf_op jit(solution)/shard_map/ppermute | solution.py:241
  65.5 0.2 add.11
  65.7 0.0 copy-start
  65.7 34.7 %all_to_all.5 = f32[8,3,128,128]{3,2,1,0:T(8,128)} all-to-all(f32[8,3,128,128]{3,2,1,0:T(8,128)S(1)} %add.11), channel_id=1, replica_groups=mesh['x'=4,'y_hi'=2,'core'=2,'col'=32] {'x','y_hi'}, dimensions={0} | all-to-all | bytes 3145728 | tf_op jit(solution)/shard_map/all_to_all | solution.py:255
  100.4 1.5 %reduce_sum.9.total_ref = f32[3,128,128]{2,1,0:T(8,128)S(1)} reduce(f32[8,3,128,128]{3,2,1,0:T(8,128)} %all_to_all.5, f32[]{:T(128)} %constant.21.clone.1), dimensions={0}, to_apply=%region_0.0 | reduce | flops 344064 | bytes 1769476 | tf_op jit(solution)/shard_map/reduce_sum | solution.py:256
  101.9 0.6 slice_bitcast_fusion
  102.5 22.6 %collective-permute-start.4 = (f32[128,128]{1,0:T(8,128)}, f32[128,128]{1,0:T(8,128)S(1)}, u32[]{:S(2)}, u32[]{:S(2)}) collective-permute-start(f32[128,128]{1,0:T(8,128)} %get-tuple-element.17), channel_id=1, source_target_pairs={{0,31},{1,0},{2,1},{3,2},{4,3},{5,4},{6,5},{7,6},{8,7},{9,8},{10,9... | collective-permute-start | bytes 196616 | tf_op jit(solution)/shard_map/ppermute | solution.py:241
  125.1 1.9 %collective-permute-start.3 = (f32[128,128]{1,0:T(8,128)S(1)}, f32[128,128]{1,0:T(8,128)S(1)}, u32[]{:S(2)}, u32[]{:S(2)}) collective-permute-start(f32[128,128]{1,0:T(8,128)S(1)} %get-tuple-element.18), channel_id=1, source_target_pairs={{0,1},{1,2},{2,3},{3,4},{4,5},{5,6},{6,7},{7,8},{8,9},{9,10},{10,1... | collective-permute-start | bytes 196616 | tf_op jit(solution)/shard_map/ppermute | solution.py:241
  127.0 0.3 collective-permute-done.4.right_ref
  127.3 7.9 %collective-permute-done.3.left_ref = f32[128,128]{1,0:T(8,128)S(1)} collective-permute-done((f32[128,128]{1,0:T(8,128)S(1)}, f32[128,128]{1,0:T(8,128)S(1)}, u32[]{:S(2)}, u32[]{:S(2)}) %collective-permute-start.3) | collective-permute-done | bytes 65568 | tf_op jit(solution)/shard_map/ppermute | solution.py:241
  135.1 0.0 copy-done
  135.2 1.4 proximal.1
Async XLA Ops:
  0.0 38.2 %collective-permute-start.1 = (f32[256,1024]{1,0:T(8,128)}, f32[256,1024]{1,0:T(8,128)S(1)}, u32[]{:S(2)}, u32[]{:S(2)}) collective-permute-start(f32[256,1024]{1,0:T(8,128)} %refs_1_.1), channel_id=1, source_target_pairs={{0,1},{1,2},{2,3},{3,4},{4,5},{5,6},{6,7},{7,8},{8,9},{9,10},{10,1... | collective-permute-start | bytes 3145736 | tf_op jit(solution)/shard_map/ppermute | solution.py:241
  3.5 49.2 %collective-permute-start = (f32[256,1024]{1,0:T(8,128)}, f32[256,1024]{1,0:T(8,128)S(1)}, u32[]{:S(2)}, u32[]{:S(2)}) collective-permute-start(f32[256,1024]{1,0:T(8,128)} %refs_1_.1), channel_id=1, source_target_pairs={{0,31},{1,0},{2,1},{3,2},{4,3},{5,4},{6,5},{7,6},{8,7},{9,8},{10,9... | collective-permute-start | bytes 3145736 | tf_op jit(solution)/shard_map/ppermute | solution.py:241
  16.6 1.2 copy-start.1
  60.0 5.5 %collective-permute-start.2 = (f32[8,3,128,128]{3,2,1,0:T(8,128)}, f32[8,3,128,128]{3,2,1,0:T(8,128)S(1)}, u32[]{:S(2)}, u32[]{:S(2)}) collective-permute-start(f32[8,3,128,128]{3,2,1,0:T(8,128)} %get-tuple-element.16), channel_id=1, source_target_pairs={{0,32},{32,0},{1,33},{33,1},{2,34},{34,2},{3,35},{35,3},{4,36},{36... | collective-permute-start | bytes 4718600 | tf_op jit(solution)/shard_map/ppermute | solution.py:241
  65.7 69.5 %copy-start = (f32[1,3,16,128,128]{4,3,2,1,0:T(8,128)S(1)}, f32[1,3,16,128,128]{4,3,2,1,0:T(8,128)}, u32[]{:S(2)}) copy-start(f32[1,3,16,128,128]{4,3,2,1,0:T(8,128)} %omega_ref.3) | copy-start | bytes 9437188
  102.5 24.8 %collective-permute-start.4 = (f32[128,128]{1,0:T(8,128)}, f32[128,128]{1,0:T(8,128)S(1)}, u32[]{:S(2)}, u32[]{:S(2)}) collective-permute-start(f32[128,128]{1,0:T(8,128)} %get-tuple-element.17), channel_id=1, source_target_pairs={{0,31},{1,0},{2,1},{3,2},{4,3},{5,4},{6,5},{7,6},{8,7},{9,8},{10,9... | collective-permute-start | bytes 196616 | tf_op jit(solution)/shard_map/ppermute | solution.py:241
  125.1 10.1 %collective-permute-start.3 = (f32[128,128]{1,0:T(8,128)S(1)}, f32[128,128]{1,0:T(8,128)S(1)}, u32[]{:S(2)}, u32[]{:S(2)}) collective-permute-start(f32[128,128]{1,0:T(8,128)S(1)} %get-tuple-element.18), channel_id=1, source_target_pairs={{0,1},{1,2},{2,3},{3,4},{4,5},{5,6},{6,7},{7,8},{8,9},{9,10},{10,1... | collective-permute-start | bytes 196616 | tf_op jit(solution)/shard_map/ppermute | solution.py:241

commit v2 on v1

--- a/solution.py
+++ b/solution.py
@@ -15,7 +15,7 @@
 penalty = 0.1
 f32 = jnp.float32
 bf16 = jnp.bfloat16
-VMEM_LIMIT = 48 * 1024 * 1024
+VMEM_LIMIT = 24 * 1024 * 1024
 
 
 def split(value):
@@ -69,9 +69,39 @@
     return out[:, :BLK] + out[:, BLK:]
 
 
-def forward_kernel(
-    slots_ref, core_ref, x_ref, omega_ref, before_ref, below_ref, centre_ref,
-    own_ref, send_ref, residual_ref, natural_ref, above_ref, pieces_ref,
+def slot_block(slots_ref, e, j, turned, pieces_ref):
+    place = jnp.maximum(slots_ref[0, e, j], 0)
+    out = jnp.dot(
+        turned[e][place // NB], pieces_ref[place % NB], preferred_element_type=f32
+    )
+    return quadrant_sum(out)
+
+
+def group_products(slots_ref, where_ref, turned, pieces_ref, y_hi, keep_ref, pass_ref, send_ref):
+    x, core = where_ref[0], where_ref[2]
+    even_pair, odd_pair = x ^ 1, 3 - x
+    first = jnp.where(core == 0, even_pair, odd_pair)
+    second = jnp.where(core == 0, odd_pair, even_pair)
+    for r, x_of in enumerate((x, second, first, x ^ 2)):
+        i = 2 * x_of + y_hi
+        for e in range(3):
+            even = slot_block(slots_ref, e, 2 * i, turned, pieces_ref)
+            odd = slot_block(slots_ref, e, 2 * i + 1, turned, pieces_ref)
+            if e == 1:
+                even_turned, odd_turned = even.T, odd.T
+                diagonal = i < NB // 2
+                even, odd = (
+                    even + jnp.where(diagonal, even_turned, odd_turned),
+                    odd + jnp.where(diagonal, odd_turned, even_turned),
+                )
+            own_ref = keep_ref if r < 2 else pass_ref
+            own_ref[r % 2, e] = jnp.where(core == 0, even, odd)
+            send_ref[(0, 2, 1, 3)[r], e] = jnp.where(core == 0, odd, even)
+
+
+def far_kernel(
+    slots_ref, where_ref, x_ref, omega_ref, before_ref, below_ref, centre_ref,
+    keep_ref, pass_ref, send_ref, above_ref, pieces_ref, residual_ref, natural_ref,
 ):
     residual_ref[...] = before_ref[...]
     split_tile(x_ref, natural_ref, above_ref)
@@ -80,31 +110,20 @@
         high, low = split(residual_ref[b])
         pieces_ref[b, :, :BLK] = high
         pieces_ref[b, :, BLK:] = low
-    core = core_ref[0]
-    turned = (below_ref, centre_ref, above_ref)
-
-    def body(i, carry):
-        for e in range(3):
-            found = []
-            for k in range(2):
-                place = jnp.maximum(slots_ref[0, e, 2 * i + k], 0)
-                a = place // NB
-                b = place % NB
-                out = jnp.dot(turned[e][a], pieces_ref[b], preferred_element_type=f32)
-                found.append(quadrant_sum(out))
-            even, odd = found
-            if e == 1:
-                even_turned, odd_turned = even.T, odd.T
-                diagonal = i < NB // 2
-                even, odd = (
-                    even + jnp.where(diagonal, even_turned, odd_turned),
-                    odd + jnp.where(diagonal, odd_turned, even_turned),
-                )
-            own_ref[i, e] = jnp.where(core == 0, even, odd)
-            send_ref[i, e] = jnp.where(core == 0, odd, even)
-        return carry
-
-    lax.fori_loop(0, KMAX // 2, body, 0)
+    group_products(
+        slots_ref, where_ref, (below_ref, centre_ref, above_ref), pieces_ref,
+        1 - where_ref[1], keep_ref, pass_ref, send_ref,
+    )
+
+
+def near_kernel(
+    slots_ref, where_ref, below_ref, centre_ref, above_ref, pieces_ref,
+    keep_ref, pass_ref, send_ref,
+):
+    group_products(
+        slots_ref, where_ref, (below_ref, centre_ref, above_ref), pieces_ref,
+        where_ref[1], keep_ref, pass_ref, send_ref,
+    )
 
 
 def proximal_kernel(
@@ -178,13 +197,19 @@
     )(*inputs)
 
 
-def forward_blocks(slots, core, tile, omega, before, below, centre):
-    shape = (KMAX // 2, 3, BLK, BLK)
+HALF = (2, 3, BLK, BLK)
+WAY = (4, 3, BLK, BLK)
+GROUP_OUT = tuple(jax.ShapeDtypeStruct(shape, f32) for shape in (HALF, HALF, WAY))
+GROUP_SPECS = tuple(full_spec(shape) for shape in (HALF, HALF, WAY))
+
+
+def far_blocks(slots, where, tile, omega, before, below, centre):
     return pl.pallas_call(
-        forward_kernel,
-        name="forward_blocks",
+        far_kernel,
+        name="far_blocks",
         grid=(1,),
-        out_shape=(jax.ShapeDtypeStruct(shape, f32),) * 2,
+        out_shape=GROUP_OUT
+        + (jax.ShapeDtypeStruct(TURNED, bf16), jax.ShapeDtypeStruct(NATURAL, bf16)),
         in_specs=[
             SMEM,
             SMEM,
@@ -194,18 +219,30 @@
             full_spec(TURNED),
             full_spec(TURNED),
         ],
-        out_specs=(full_spec(shape),) * 2,
-        scratch_shapes=[
-            pltpu.VMEM((NB, ROWS, BLK), f32),
-            pltpu.VMEM(NATURAL, bf16),
-            pltpu.VMEM(TURNED, bf16),
-            pltpu.VMEM(NATURAL, bf16),
-        ],
+        out_specs=GROUP_SPECS + (full_spec(TURNED), full_spec(NATURAL)),
+        scratch_shapes=[pltpu.VMEM((NB, ROWS, BLK), f32), pltpu.VMEM(NATURAL, bf16)],
         compiler_params=params(),
         cost_estimate=pl.CostEstimate(
-            flops=8 * KMAX * ROWS * 256 * 256, bytes_accessed=8 << 20, transcendentals=0
-        ),
-    )(slots, core, tile, omega, before, below, centre)
+            flops=5 * KMAX * ROWS * 256 * 256, bytes_accessed=8 << 20, transcendentals=0
+        ),
+    )(slots, where, tile, omega, before, below, centre)
+
+
+def near_blocks(slots, where, below, centre, above, pieces):
+    return pl.pallas_call(
+        near_kernel,
+        name="near_blocks",
+        grid=(1,),
+        out_shape=GROUP_OUT,
+        in_specs=[SMEM, SMEM]
+        + [full_spec(TURNED)] * 3
+        + [full_spec(NATURAL)],
+        out_specs=GROUP_SPECS,
+        compiler_params=params(),
+        cost_estimate=pl.CostEstimate(
+            flops=3 * KMAX * ROWS * 256 * 256, bytes_accessed=8 << 20, transcendentals=0
+        ),
+    )(slots, where, below, centre, above, pieces)
 
 
 def proximal(place, slots, total, left, right, omega):
@@ -241,19 +278,39 @@
     return lax.ppermute(value, axis, pairs)
 
 
+def x_exchange(value, step):
+    pairs = []
+    for x in range(4):
+        for core in range(2):
+            partner = x ^ 1 if core == step else 3 - x
+            pairs.append((2 * x + core, 2 * partner + core))
+    return lax.ppermute(value, ("x", "core"), pairs)
+
+
 def on_device(observations, omega, block_slots):
-    core = lax.axis_index("core").astype(jnp.int32)
-    place = lax.axis_index(("x", "y_hi", "core")).astype(jnp.int32)
+    x, y_hi, core = (lax.axis_index(n).astype(jnp.int32) for n in ("x", "y_hi", "core"))
+    where = jnp.stack([x, y_hi, core])
+    place = 4 * x + 2 * y_hi + core
     from_below = shifted(observations, "col", 1)
     from_above = shifted(observations, "col", -1)
     residual, centre = partial(1, block_slots, observations, omega)
     residual, below = partial(0, block_slots, from_below, omega, residual)
-    own, send = forward_blocks(
-        block_slots, core.reshape(1), from_above, omega, residual, below, centre
-    )
-    chip = own + shifted(send, "core", 1)
-    gathered = lax.all_to_all(chip, ("x", "y_hi"), 0, 0)
-    total = jnp.sum(gathered, axis=0)
+    far_keep, far_pass, far_send, above, pieces = far_blocks(
+        block_slots, where, from_above, omega, residual, below, centre
+    )
+    far_got = shifted(far_send, "core", 1)
+    near_keep, near_pass, near_send = near_blocks(
+        block_slots, where, below, centre, above, pieces
+    )
+    near_got = shifted(near_send, "core", 1)
+    far_first = x_exchange(far_pass + far_got[2:], 0)
+    near_first = x_exchange(near_pass + near_got[2:], 0)
+    far_second = x_exchange(far_keep[1] + far_got[1] + far_first[1], 1)
+    far_sum = far_keep[0] + far_got[0] + far_first[0] + far_second
+    other = shifted(far_sum, "y_hi", 1)
+    near_second = x_exchange(near_keep[1] + near_got[1] + near_first[1], 1)
+    near_sum = near_keep[0] + near_got[0] + near_first[0] + near_second
+    total = near_sum + other
     left = shifted(total[2], "col", 1)
     right = shifted(total[0], "col", -1)
     return proximal(place.reshape(1), block_slots, total, left, right, omega)

time: 137 us -> 122 us (0.89)
  blocking collectives: 34.7 us -> 0 us
  starting transfers between devices: 42.3 us -> 55.3 us
  waiting for transfers between devices: 40.7 us -> 48.4 us
  Pallas kernels: 14.5 us -> 12.3 us
  local copies, waits for them, and re-layouts: 2.55 us -> 4.44 us
    all_to_all x1 -> x0, blocking collectives: 34.7 us -> none  [on_device(): gathered = lax.all_to_all(chip, ('x', 'y_hi'), 0, 0)]
    ppermute x0 -> x4, starting transfers between devices: none -> 11.1 us  [x_exchange(): return lax.ppermute(value, ('x', 'core'), pairs)]
    ppermute x0 -> x4, waiting for transfers between devices: none -> 7.18 us  [x_exchange(): return lax.ppermute(value, ('x', 'core'), pairs)]
    unnamed x5 -> x7, local copies, waits for them, and re-layouts: 1.91 us -> 3.8 us
    ppermute x5 -> x7, starting transfers between devices: 42.3 us -> 44.1 us  [shifted(): return lax.ppermute(value, axis, pairs)]
    pallas_call x1 -> x2, Pallas kernels: 7.3 us -> 5.73 us  [the longest x1 4.13 us: far_blocks(): pl.pallas_call(far_kernel, name='far_blocks', grid=(1,), out_shape=GROUP_...]
    reduce_sum x1 -> x0, other arithmetic: 1.51 us -> none  [on_device(): total = jnp.sum(gathered, axis=0)]
    ppermute x5 -> x7, waiting for transfers between devices: 40.7 us -> 41.2 us  [shifted(): return lax.ppermute(value, axis, pairs)]
  transfers between devices with their start and end apart: 5 -> 11, of which waited for: 5 -> 8; matrix products, arithmetic and copies ran while one was open for 1% -> 1% of each run, Pallas kernels for 4% -> 6%
where the time goes in v2:
time: 122 us; the launch traced here: 121 us
  starting transfers between devices  55.3 us (45%)
  waiting for transfers between devices  48.4 us (40%)
  Pallas kernels  12.3 us (10%)
  local copies, waits for them, and re-layouts  4.44 us (4%)
    ppermute x7, starting transfers between devices, shifted(): return lax.ppermute(value, axis, pairs)  44.1 us
    ppermute x7, waiting for transfers between devices, shifted(): return lax.ppermute(value, axis, pairs)  41.2 us
    ppermute x4, starting transfers between devices, x_exchange(): return lax.ppermute(value, ('x', 'core'), pairs)  11.1 us
    ppermute x4, waiting for transfers between devices, x_exchange(): return lax.ppermute(value, ('x', 'core'), pairs)  7.18 us
    pallas_call x2, Pallas kernels, partial(): pl.pallas_call(lambda *refs: partial_kernel(offset, first, *refs), name='...  5.17 us
    pallas_call x1, Pallas kernels, far_blocks(): pl.pallas_call(far_kernel, name='far_blocks', grid=(1,), out_shape=GROUP_...  4.13 us
    unnamed x7, local copies, waits for them, and re-layouts  3.8 us
  transfers between devices with their start and end apart: 11, of which 8 were waited for; matrix products, arithmetic and copies ran while one was open for 1% of the time, Pallas kernels for 6%

profile of v2, /device:TPU:6, one launch (start us, length us, event | category | flops | bytes accessed | tf_op | source)
XLA Modules:
  0.0 120.9 jit_solution(10898400284726168036)
XLA Ops:
  0.0 3.5 %collective-permute-start = (f32[256,1024]{1,0:T(8,128)}, f32[256,1024]{1,0:T(8,128)}, u32[]{:S(2)}, u32[]{:S(2)}) collective-permute-start(f32[256,1024]{1,0:T(8,128)} %refs_1_.1), channel_id=1, source_target_pairs={{0,1},{1,2},{2,3},{3,4},{4,5},{5,6},{6,7},{7,8},{8,9},{9,10},{10,1... | collective-permute-start | bytes 3145736 | tf_op jit(solution)/shard_map/ppermute | solution.py:278
  3.5 12.4 %collective-permute-start.1 = (f32[256,1024]{1,0:T(8,128)}, f32[256,1024]{1,0:T(8,128)}, u32[]{:S(2)}, u32[]{:S(2)}) collective-permute-start(f32[256,1024]{1,0:T(8,128)} %refs_1_.1), channel_id=1, source_target_pairs={{0,31},{1,0},{2,1},{3,2},{4,3},{5,4},{6,5},{7,6},{8,7},{9,8},{10,9... | collective-permute-start | bytes 3145736 | tf_op jit(solution)/shard_map/ppermute | solution.py:278
  15.9 0.7 copy.8.refs_0_.slots_ref
  16.6 0.0 copy-start
  16.6 1.9 %copy-done = f32[1,3,16,128,128]{4,3,2,1,0:T(8,128)S(1)} copy-done((f32[1,3,16,128,128]{4,3,2,1,0:T(8,128)S(1)}, f32[1,3,16,128,128]{4,3,2,1,0:T(8,128)}, u32[]{:S(2)}) %copy-start) | copy-done | bytes 3145752
  18.5 0.0 copy-start.2
  18.5 1.2 %copy-done.2 = f32[256,1024]{1,0:T(8,128)S(1)} copy-done((f32[256,1024]{1,0:T(8,128)S(1)}, f32[256,1024]{1,0:T(8,128)}, u32[]{:S(2)}) %copy-start.2) | copy-done | bytes 1048600
  19.7 0.0 copy-start.1
  19.7 2.3 %partial_residual.2 = (f32[8,256,128]{2,1,0:T(8,128)S(1)}, bf16[8,256,256]{2,1,0:T(8,128)(2,1)S(1)}) custom-call(s32[1,3,16]{2,1,0:T(4,128)S(1)} %copy.8.refs_0_.slots_ref, f32[256,1024]{1,0:T(8,128)S(1)} %copy-done.2, f32[1,3,16,128,128]{4,3,2,1,0:T(8,128)S(1)} %copy-done), custom_call_target="tpu_custom_call" | custom-call | flops 536870912 | bytes 5242880 | tf_op jit(solution)/shard_map/partial_residual/pallas_call | solution.py:182
  22.0 0.1 pad_add_fusion.where_ref
  22.1 16.2 %collective-permute-done.refs_1_ = f32[256,1024]{1,0:T(8,128)} collective-permute-done((f32[256,1024]{1,0:T(8,128)}, f32[256,1024]{1,0:T(8,128)}, u32[]{:S(2)}, u32[]{:S(2)}) %collective-permute-start) | collective-permute-done | bytes 1048608 | tf_op jit(solution)/shard_map/ppermute | solution.py:278
  38.3 0.0 copy-done.1
  38.3 2.9 %partial_residual.3 = (f32[8,256,128]{2,1,0:T(8,128)S(1)}, bf16[8,256,256]{2,1,0:T(8,128)(2,1)S(1)}) custom-call(s32[1,3,16]{2,1,0:T(4,128)S(1)} %copy.8.refs_0_.slots_ref, f32[256,1024]{1,0:T(8,128)} %collective-permute-done.refs_1_, f32[1,3,16,128,128]{4,3,2,1,0:T(8,128)S(1)} %copy-done.1, f32[8,256,128]{2,1,0:T(8,128)S(1)} %get-tuple-element.17.refs_3_), custom_call_target="tpu_custom_call" | custom-call | flops 536870912 | bytes 5242880 | tf_op jit(solution)/shard_map/partial_residual/pallas_call | solution.py:182
  41.2 11.5 %collective-permute-done.1.x_ref = f32[256,1024]{1,0:T(8,128)} collective-permute-done((f32[256,1024]{1,0:T(8,128)}, f32[256,1024]{1,0:T(8,128)}, u32[]{:S(2)}, u32[]{:S(2)}) %collective-permute-start.1) | collective-permute-done | bytes 1048608 | tf_op jit(solution)/shard_map/ppermute | solution.py:278
  52.8 4.1 %far_blocks.1 = (f32[2,3,128,128]{3,2,1,0:T(8,128)S(1)}, f32[2,3,128,128]{3,2,1,0:T(8,128)S(1)}, f32[4,3,128,128]{3,2,1,0:T(8,128)S(1)}, bf16[8,256,256]{2,1,0:T(8,128)(2,1)S(1)}, bf16[8,256,256]{2,1,0:T(8,128)(2,1)S(1)}) custom-call(s32[1,3,16]{2,1,0:T(4,128)S(1)} %copy.8.refs_0_.slots_ref, s32[3]{0:T(128)S(1)} %pad_add_fusion.where_ref, ...), custom_call_target="tpu_custom_call" | custom-call | flops 1342177280 | bytes 8388608 | tf_op jit(solution)/shard_map/far_blocks/pallas_call | solution.py:207
  56.9 1.9 %collective-permute-start.5 = (f32[4,3,128,128]{3,2,1,0:T(8,128)S(1)}, f32[4,3,128,128]{3,2,1,0:T(8,128)S(1)}, u32[]{:S(2)}, u32[]{:S(2)}) collective-permute-start(f32[4,3,128,128]{3,2,1,0:T(8,128)S(1)} %get-tuple-element.27), channel_id=1, source_target_pairs={{0,32},{32,0},{1,33},{33,1},{2,34},{34,2},{3,35},{35,3},{4,36},{36... | collective-permute-start | bytes 2359304 | tf_op jit(solution)/shard_map/ppermute | solution.py:278
  58.9 1.6 %near_blocks.1 = (f32[2,3,128,128]{3,2,1,0:T(8,128)S(1)}, f32[2,3,128,128]{3,2,1,0:T(8,128)S(1)}, f32[4,3,128,128]{3,2,1,0:T(8,128)S(1)}) custom-call(s32[1,3,16]{2,1,0:T(4,128)S(1)} %copy.8.refs_0_.slots_ref, s32[3]{0:T(128)S(1)} %pad_add_fusion.where_ref, bf16[8,256,256]{2,1,0:T(8,128)(2,1)S(1)} %get-tuple-element.18.below_ref, ...), custom_call_target="tpu_custom_call" | custom-call | flops 805306368 | bytes 8388608 | tf_op jit(solution)/shard_map/near_blocks/pallas_call | solution.py:232
  60.5 2.4 %collective-permute-start.2 = (f32[4,3,128,128]{3,2,1,0:T(8,128)S(1)}, f32[4,3,128,128]{3,2,1,0:T(8,128)S(1)}, u32[]{:S(2)}, u32[]{:S(2)}) collective-permute-start(f32[4,3,128,128]{3,2,1,0:T(8,128)S(1)} %get-tuple-element.24), channel_id=1, source_target_pairs={{0,32},{32,0},{1,33},{33,1},{2,34},{34,2},{3,35},{35,3},{4,36},{36... | collective-permute-start | bytes 2359304 | tf_op jit(solution)/shard_map/ppermute | solution.py:278
  62.9 0.0 collective-permute-done.5
  62.9 2.7 %collective-permute-start.6 = (f32[2,3,128,128]{3,2,1,0:T(8,128)S(1)}, f32[2,3,128,128]{3,2,1,0:T(8,128)S(1)}, u32[]{:S(2)}, u32[]{:S(2)}) collective-permute-start(f32[2,3,128,128]{3,2,1,0:T(8,128)S(1)} %slice_add_fusion), channel_id=1, source_target_pairs={{0,128},{32,416},{128,0},{160,288},{256,384},{288,160},{384,256},{... | collective-permute-start | bytes 1179656 | tf_op jit(solution)/shard_map/ppermute | solution.py:287
  65.7 0.0 collective-permute-done.2
  65.7 3.1 %collective-permute-start.3 = (f32[2,3,128,128]{3,2,1,0:T(8,128)S(1)}, f32[2,3,128,128]{3,2,1,0:T(8,128)S(1)}, u32[]{:S(2)}, u32[]{:S(2)}) collective-permute-start(f32[2,3,128,128]{3,2,1,0:T(8,128)S(1)} %slice_add_fusion.1), channel_id=1, source_target_pairs={{0,128},{32,416},{128,0},{160,288},{256,384},{288,160},{384,256},{... | collective-permute-start | bytes 1179656 | tf_op jit(solution)/shard_map/ppermute | solution.py:287
  68.8 3.7 %collective-permute-done.6 = f32[2,3,128,128]{3,2,1,0:T(8,128)S(1)} collective-permute-done((f32[2,3,128,128]{3,2,1,0:T(8,128)S(1)}, f32[2,3,128,128]{3,2,1,0:T(8,128)S(1)}, u32[]{:S(2)}, u32[]{:S(2)}) %collective-permute-start.6) | collective-permute-done | bytes 393248 | tf_op jit(solution)/shard_map/ppermute | solution.py:287
  72.6 2.4 %collective-permute-start.7 = (f32[3,128,128]{2,1,0:T(8,128)S(1)}, f32[3,128,128]{2,1,0:T(8,128)S(1)}, u32[]{:S(2)}, u32[]{:S(2)}) collective-permute-start(f32[3,128,128]{2,1,0:T(8,128)S(1)} %fusion), channel_id=1, source_target_pairs={{0,384},{32,160},{128,256},{160,32},{256,128},{288,416},{384,0},{4... | collective-permute-start | bytes 589832 | tf_op jit(solution)/shard_map/ppermute | solution.py:287
  75.0 1.8 %collective-permute-done.3 = f32[2,3,128,128]{3,2,1,0:T(8,128)S(1)} collective-permute-done((f32[2,3,128,128]{3,2,1,0:T(8,128)S(1)}, f32[2,3,128,128]{3,2,1,0:T(8,128)S(1)}, u32[]{:S(2)}, u32[]{:S(2)}) %collective-permute-start.3) | collective-permute-done | bytes 393248 | tf_op jit(solution)/shard_map/ppermute | solution.py:287
  76.8 2.9 %collective-permute-start.4 = (f32[3,128,128]{2,1,0:T(8,128)S(1)}, f32[3,128,128]{2,1,0:T(8,128)S(1)}, u32[]{:S(2)}, u32[]{:S(2)}) collective-permute-start(f32[3,128,128]{2,1,0:T(8,128)S(1)} %fusion.3), channel_id=1, source_target_pairs={{0,384},{32,160},{128,256},{160,32},{256,128},{288,416},{384,0},{4... | collective-permute-start | bytes 589832 | tf_op jit(solution)/shard_map/ppermute | solution.py:287
  79.8 1.7 %collective-permute-done.7 = f32[3,128,128]{2,1,0:T(8,128)S(1)} collective-permute-done((f32[3,128,128]{2,1,0:T(8,128)S(1)}, f32[3,128,128]{2,1,0:T(8,128)S(1)}, u32[]{:S(2)}, u32[]{:S(2)}) %collective-permute-start.7) | collective-permute-done | bytes 196640 | tf_op jit(solution)/shard_map/ppermute | solution.py:287
  81.4 0.1 fusion.2
  81.5 6.8 %collective-permute-start.8 = (f32[3,128,128]{2,1,0:T(8,128)S(1)}, f32[3,128,128]{2,1,0:T(8,128)S(1)}, u32[]{:S(2)}, u32[]{:S(2)}) collective-permute-start(f32[3,128,128]{2,1,0:T(8,128)S(1)} %fusion.2), channel_id=1, source_target_pairs={{0,64},{64,0},{1,65},{65,1},{2,66},{66,2},{3,67},{67,3},{4,68},{68... | collective-permute-start | bytes 589832 | tf_op jit(solution)/shard_map/ppermute | solution.py:278
  88.3 0.0 collective-permute-done.4
  88.3 5.3 %collective-permute-done.8 = f32[3,128,128]{2,1,0:T(8,128)S(1)} collective-permute-done((f32[3,128,128]{2,1,0:T(8,128)S(1)}, f32[3,128,128]{2,1,0:T(8,128)S(1)}, u32[]{:S(2)}, u32[]{:S(2)}) %collective-permute-start.8) | collective-permute-done | bytes 196640 | tf_op jit(solution)/shard_map/ppermute | solution.py:278
  93.7 0.6 slice_bitcast_fusion
  94.3 15.1 %collective-permute-start.10 = (f32[128,128]{1,0:T(8,128)}, f32[128,128]{1,0:T(8,128)S(1)}, u32[]{:S(2)}, u32[]{:S(2)}) collective-permute-start(f32[128,128]{1,0:T(8,128)} %get-tuple-element.29), channel_id=1, source_target_pairs={{0,31},{1,0},{2,1},{3,2},{4,3},{5,4},{6,5},{7,6},{8,7},{9,8},{10,9... | collective-permute-start | bytes 196616 | tf_op jit(solution)/shard_map/ppermute | solution.py:278
  109.5 1.9 %collective-permute-start.9 = (f32[128,128]{1,0:T(8,128)S(1)}, f32[128,128]{1,0:T(8,128)S(1)}, u32[]{:S(2)}, u32[]{:S(2)}) collective-permute-start(f32[128,128]{1,0:T(8,128)S(1)} %get-tuple-element.30), channel_id=1, source_target_pairs={{0,1},{1,2},{2,3},{3,4},{4,5},{5,6},{6,7},{7,8},{8,9},{9,10},{10,1... | collective-permute-start | bytes 196616 | tf_op jit(solution)/shard_map/ppermute | solution.py:278
  111.4 0.5 collective-permute-done.10.right_ref
  111.9 7.6 %collective-permute-done.9.left_ref = f32[128,128]{1,0:T(8,128)S(1)} collective-permute-done((f32[128,128]{1,0:T(8,128)S(1)}, f32[128,128]{1,0:T(8,128)S(1)}, u32[]{:S(2)}, u32[]{:S(2)}) %collective-permute-start.9) | collective-permute-done | bytes 65568 | tf_op jit(solution)/shard_map/ppermute | solution.py:278
  119.5 1.4 %proximal.1 = f32[1,3,1,128,128]{4,3,2,1,0:T(8,128)} custom-call(s32[1]{0:T(128)} %bitcast.place_ref, s32[1,3,16]{2,1,0:T(4,128)S(1)} %copy.8.refs_0_.slots_ref, f32[3,128,128]{2,1,0:T(8,128)S(1)} %fusion.6.total_ref, f32[128,128]{1,0:T(8,128)S(1)} %collective-permute-done.9.left_ref, f32[128,128]{1,0:T(8,128)S(1)} %collective-permute-done.10.right_ref, ...), custom_call_target="tpu_custom_call" | custom-call | flops 983040 | bytes 524288 | tf_op jit(solution)/shard_map/proximal/pallas_call | solution.py:249
  (5 shorter events, 0.2 us)
Async XLA Ops:
  0.0 38.3 %collective-permute-start = (f32[256,1024]{1,0:T(8,128)}, f32[256,1024]{1,0:T(8,128)}, u32[]{:S(2)}, u32[]{:S(2)}) collective-permute-start(f32[256,1024]{1,0:T(8,128)} %refs_1_.1), channel_id=1, source_target_pairs={{0,1},{1,2},{2,3},{3,4},{4,5},{5,6},{6,7},{7,8},{8,9},{9,10},{10,1... | collective-permute-start | bytes 3145736 | tf_op jit(solution)/shard_map/ppermute | solution.py:278
  3.5 49.3 %collective-permute-start.1 = (f32[256,1024]{1,0:T(8,128)}, f32[256,1024]{1,0:T(8,128)}, u32[]{:S(2)}, u32[]{:S(2)}) collective-permute-start(f32[256,1024]{1,0:T(8,128)} %refs_1_.1), channel_id=1, source_target_pairs={{0,31},{1,0},{2,1},{3,2},{4,3},{5,4},{6,5},{7,6},{8,7},{9,8},{10,9... | collective-permute-start | bytes 3145736 | tf_op jit(solution)/shard_map/ppermute | solution.py:278
  16.6 1.9 %copy-start = (f32[1,3,16,128,128]{4,3,2,1,0:T(8,128)S(1)}, f32[1,3,16,128,128]{4,3,2,1,0:T(8,128)}, u32[]{:S(2)}) copy-start(f32[1,3,16,128,128]{4,3,2,1,0:T(8,128)} %omega_ref.3) | copy-start | bytes 9437188
  18.5 1.2 %copy-start.2 = (f32[256,1024]{1,0:T(8,128)S(1)}, f32[256,1024]{1,0:T(8,128)}, u32[]{:S(2)}) copy-start(f32[256,1024]{1,0:T(8,128)} %refs_1_.1) | copy-start | bytes 3145732
  19.7 18.6 %copy-start.1 = (f32[1,3,16,128,128]{4,3,2,1,0:T(8,128)S(1)}, f32[1,3,16,128,128]{4,3,2,1,0:T(8,128)}, u32[]{:S(2)}) copy-start(f32[1,3,16,128,128]{4,3,2,1,0:T(8,128)} %omega_ref.3) | copy-start | bytes 9437188
  56.9 5.9 %collective-permute-start.5 = (f32[4,3,128,128]{3,2,1,0:T(8,128)S(1)}, f32[4,3,128,128]{3,2,1,0:T(8,128)S(1)}, u32[]{:S(2)}, u32[]{:S(2)}) collective-permute-start(f32[4,3,128,128]{3,2,1,0:T(8,128)S(1)} %get-tuple-element.27), channel_id=1, source_target_pairs={{0,32},{32,0},{1,33},{33,1},{2,34},{34,2},{3,35},{35,3},{4,36},{36... | collective-permute-start | bytes 2359304 | tf_op jit(solution)/shard_map/ppermute | solution.py:278
  60.5 5.2 %collective-permute-start.2 = (f32[4,3,128,128]{3,2,1,0:T(8,128)S(1)}, f32[4,3,128,128]{3,2,1,0:T(8,128)S(1)}, u32[]{:S(2)}, u32[]{:S(2)}) collective-permute-start(f32[4,3,128,128]{3,2,1,0:T(8,128)S(1)} %get-tuple-element.24), channel_id=1, source_target_pairs={{0,32},{32,0},{1,33},{33,1},{2,34},{34,2},{3,35},{35,3},{4,36},{36... | collective-permute-start | bytes 2359304 | tf_op jit(solution)/shard_map/ppermute | solution.py:278
  62.9 9.7 %collective-permute-start.6 = (f32[2,3,128,128]{3,2,1,0:T(8,128)S(1)}, f32[2,3,128,128]{3,2,1,0:T(8,128)S(1)}, u32[]{:S(2)}, u32[]{:S(2)}) collective-permute-start(f32[2,3,128,128]{3,2,1,0:T(8,128)S(1)} %slice_add_fusion), channel_id=1, source_target_pairs={{0,128},{32,416},{128,0},{160,288},{256,384},{288,160},{384,256},{... | collective-permute-start | bytes 1179656 | tf_op jit(solution)/shard_map/ppermute | solution.py:287
  65.7 11.1 %collective-permute-start.3 = (f32[2,3,128,128]{3,2,1,0:T(8,128)S(1)}, f32[2,3,128,128]{3,2,1,0:T(8,128)S(1)}, u32[]{:S(2)}, u32[]{:S(2)}) collective-permute-start(f32[2,3,128,128]{3,2,1,0:T(8,128)S(1)} %slice_add_fusion.1), channel_id=1, source_target_pairs={{0,128},{32,416},{128,0},{160,288},{256,384},{288,160},{384,256},{... | collective-permute-start | bytes 1179656 | tf_op jit(solution)/shard_map/ppermute | solution.py:287
  72.6 8.8 %collective-permute-start.7 = (f32[3,128,128]{2,1,0:T(8,128)S(1)}, f32[3,128,128]{2,1,0:T(8,128)S(1)}, u32[]{:S(2)}, u32[]{:S(2)}) collective-permute-start(f32[3,128,128]{2,1,0:T(8,128)S(1)} %fusion), channel_id=1, source_target_pairs={{0,384},{32,160},{128,256},{160,32},{256,128},{288,416},{384,0},{4... | collective-permute-start | bytes 589832 | tf_op jit(solution)/shard_map/ppermute | solution.py:287
  76.8 11.5 %collective-permute-start.4 = (f32[3,128,128]{2,1,0:T(8,128)S(1)}, f32[3,128,128]{2,1,0:T(8,128)S(1)}, u32[]{:S(2)}, u32[]{:S(2)}) collective-permute-start(f32[3,128,128]{2,1,0:T(8,128)S(1)} %fusion.3), channel_id=1, source_target_pairs={{0,384},{32,160},{128,256},{160,32},{256,128},{288,416},{384,0},{4... | collective-permute-start | bytes 589832 | tf_op jit(solution)/shard_map/ppermute | solution.py:287
  81.5 12.2 %collective-permute-start.8 = (f32[3,128,128]{2,1,0:T(8,128)S(1)}, f32[3,128,128]{2,1,0:T(8,128)S(1)}, u32[]{:S(2)}, u32[]{:S(2)}) collective-permute-start(f32[3,128,128]{2,1,0:T(8,128)S(1)} %fusion.2), channel_id=1, source_target_pairs={{0,64},{64,0},{1,65},{65,1},{2,66},{66,2},{3,67},{67,3},{4,68},{68... | collective-permute-start | bytes 589832 | tf_op jit(solution)/shard_map/ppermute | solution.py:278
  94.3 17.6 %collective-permute-start.10 = (f32[128,128]{1,0:T(8,128)}, f32[128,128]{1,0:T(8,128)S(1)}, u32[]{:S(2)}, u32[]{:S(2)}) collective-permute-start(f32[128,128]{1,0:T(8,128)} %get-tuple-element.29), channel_id=1, source_target_pairs={{0,31},{1,0},{2,1},{3,2},{4,3},{5,4},{6,5},{7,6},{8,7},{9,8},{10,9... | collective-permute-start | bytes 196616 | tf_op jit(solution)/shard_map/ppermute | solution.py:278
  109.5 10.1 %collective-permute-start.9 = (f32[128,128]{1,0:T(8,128)S(1)}, f32[128,128]{1,0:T(8,128)S(1)}, u32[]{:S(2)}, u32[]{:S(2)}) collective-permute-start(f32[128,128]{1,0:T(8,128)S(1)} %get-tuple-element.30), channel_id=1, source_target_pairs={{0,1},{1,2},{2,3},{3,4},{4,5},{5,6},{6,7},{7,8},{8,9},{9,10},{10,1... | collective-permute-start | bytes 196616 | tf_op jit(solution)/shard_map/ppermute | solution.py:278

commit v3 on v2

--- a/solution.py
+++ b/solution.py
@@ -287,6 +287,10 @@
     return lax.ppermute(value, ("x", "core"), pairs)
 
 
+def after(value, earlier):
+    return lax.optimization_barrier((value, earlier))[0]
+
+
 def on_device(observations, omega, block_slots):
     x, y_hi, core = (lax.axis_index(n).astype(jnp.int32) for n in ("x", "y_hi", "core"))
     where = jnp.stack([x, y_hi, core])
@@ -299,16 +303,22 @@
         block_slots, where, from_above, omega, residual, below, centre
     )
     far_got = shifted(far_send, "core", 1)
+    far_out = far_pass + far_got[2:]
+    pieces = after(pieces, far_out)
+    far_first = x_exchange(far_out, 0)
     near_keep, near_pass, near_send = near_blocks(
         block_slots, where, below, centre, above, pieces
     )
     near_got = shifted(near_send, "core", 1)
-    far_first = x_exchange(far_pass + far_got[2:], 0)
-    near_first = x_exchange(near_pass + near_got[2:], 0)
-    far_second = x_exchange(far_keep[1] + far_got[1] + far_first[1], 1)
+    far_out = far_keep[1] + far_got[1] + far_first[1]
+    near_out = after(near_pass + near_got[2:], far_out)
+    far_second = x_exchange(far_out, 1)
+    near_first = x_exchange(near_out, 0)
     far_sum = far_keep[0] + far_got[0] + far_first[0] + far_second
+    near_out = near_keep[1] + near_got[1] + near_first[1]
+    near_out = after(near_out, far_sum)
     other = shifted(far_sum, "y_hi", 1)
-    near_second = x_exchange(near_keep[1] + near_got[1] + near_first[1], 1)
+    near_second = x_exchange(near_out, 1)
     near_sum = near_keep[0] + near_got[0] + near_first[0] + near_second
     total = near_sum + other
     left = shifted(total[2], "col", 1)

time: 122 us -> 124 us (1.016)
  waiting for transfers between devices: 48.4 us -> 55.9 us
  starting transfers between devices: 55.3 us -> 49.9 us
    ppermute x4, waiting for transfers between devices: 7.18 us -> 14.6 us  [x_exchange(): return lax.ppermute(value, ('x', 'core'), pairs)]
    ppermute x7, starting transfers between devices: 44.1 us -> 39.9 us  [shifted(): return lax.ppermute(value, axis, pairs)]
  transfers between devices with their start and end apart: 11 -> 11, of which waited for: 8 -> 9; matrix products, arithmetic and copies ran while one was open for 1% -> 1% of each run, Pallas kernels for 6% -> 4%
where the time goes in v3:
time: 124 us; the launch traced here: 123 us
  waiting for transfers between devices  55.9 us (45%)
  starting transfers between devices  49.9 us (40%)
  Pallas kernels  12.3 us (10%)
  local copies, waits for them, and re-layouts  4.44 us (4%)
    ppermute x7, waiting for transfers between devices, shifted(): return lax.ppermute(value, axis, pairs)  41.3 us
    ppermute x7, starting transfers between devices, shifted(): return lax.ppermute(value, axis, pairs)  39.9 us
    ppermute x4, waiting for transfers between devices, x_exchange(): return lax.ppermute(value, ('x', 'core'), pairs)  14.6 us
    ppermute x4, starting transfers between devices, x_exchange(): return lax.ppermute(value, ('x', 'core'), pairs)  9.99 us
    pallas_call x2, Pallas kernels, partial(): pl.pallas_call(lambda *refs: partial_kernel(offset, first, *refs), name='...  5.17 us
    pallas_call x1, Pallas kernels, far_blocks(): pl.pallas_call(far_kernel, name='far_blocks', grid=(1,), out_shape=GROUP_...  4.13 us
    unnamed x7, local copies, waits for them, and re-layouts  3.8 us
  transfers between devices with their start and end apart: 11, of which 9 were waited for; matrix products, arithmetic and copies ran while one was open for 1% of the time, Pallas kernels for 4%

profile of v3, /device:TPU:6, one launch (start us, length us, event | category | flops | bytes accessed | tf_op | source)
XLA Modules:
  0.0 123.0 jit_solution(3917073190790044211)
XLA Ops:
  0.0 3.5 %collective-permute-start = (f32[256,1024]{1,0:T(8,128)}, f32[256,1024]{1,0:T(8,128)}, u32[]{:S(2)}, u32[]{:S(2)}) collective-permute-start(f32[256,1024]{1,0:T(8,128)} %refs_1_.1), channel_id=1, source_target_pairs={{0,1},{1,2},{2,3},{3,4},{4,5},{5,6},{6,7},{7,8},{8,9},{9,10},{10,1... | collective-permute-start | bytes 3145736 | tf_op jit(solution)/shard_map/ppermute | solution.py:278
  3.5 12.4 %collective-permute-start.1 = (f32[256,1024]{1,0:T(8,128)}, f32[256,1024]{1,0:T(8,128)}, u32[]{:S(2)}, u32[]{:S(2)}) collective-permute-start(f32[256,1024]{1,0:T(8,128)} %refs_1_.1), channel_id=1, source_target_pairs={{0,31},{1,0},{2,1},{3,2},{4,3},{5,4},{6,5},{7,6},{8,7},{9,8},{10,9... | collective-permute-start | bytes 3145736 | tf_op jit(solution)/shard_map/ppermute | solution.py:278
  15.9 0.7 copy.8.refs_0_.slots_ref
  16.6 0.0 copy-start
  16.6 1.9 %copy-done = f32[1,3,16,128,128]{4,3,2,1,0:T(8,128)S(1)} copy-done((f32[1,3,16,128,128]{4,3,2,1,0:T(8,128)S(1)}, f32[1,3,16,128,128]{4,3,2,1,0:T(8,128)}, u32[]{:S(2)}) %copy-start) | copy-done | bytes 3145752
  18.5 0.0 copy-start.2
  18.5 1.2 copy-done.2
  19.7 0.0 copy-start.1
  19.7 2.3 %partial_residual.2 = (f32[8,256,128]{2,1,0:T(8,128)S(1)}, bf16[8,256,256]{2,1,0:T(8,128)(2,1)S(1)}) custom-call(s32[1,3,16]{2,1,0:T(4,128)S(1)} %copy.8.refs_0_.slots_ref, f32[256,1024]{1,0:T(8,128)S(1)} %copy-done.2, f32[1,3,16,128,128]{4,3,2,1,0:T(8,128)S(1)} %copy-done), custom_call_target="tpu_custom_call" | custom-call | flops 536870912 | bytes 5242880 | tf_op jit(solution)/shard_map/partial_residual/pallas_call | solution.py:182
  22.0 0.1 pad_add_fusion.where_ref
  22.1 16.2 %collective-permute-done.refs_1_ = f32[256,1024]{1,0:T(8,128)} collective-permute-done((f32[256,1024]{1,0:T(8,128)}, f32[256,1024]{1,0:T(8,128)}, u32[]{:S(2)}, u32[]{:S(2)}) %collective-permute-start) | collective-permute-done | bytes 1048608 | tf_op jit(solution)/shard_map/ppermute | solution.py:278
  38.3 0.0 copy-done.1
  38.3 2.9 %partial_residual.3 = (f32[8,256,128]{2,1,0:T(8,128)S(1)}, bf16[8,256,256]{2,1,0:T(8,128)(2,1)S(1)}) custom-call(s32[1,3,16]{2,1,0:T(4,128)S(1)} %copy.8.refs_0_.slots_ref, f32[256,1024]{1,0:T(8,128)} %collective-permute-done.refs_1_, f32[1,3,16,128,128]{4,3,2,1,0:T(8,128)S(1)} %copy-done.1, f32[8,256,128]{2,1,0:T(8,128)S(1)} %get-tuple-element.20.refs_3_), custom_call_target="tpu_custom_call" | custom-call | flops 536870912 | bytes 5242880 | tf_op jit(solution)/shard_map/partial_residual/pallas_call | solution.py:182
  41.2 11.5 %collective-permute-done.1.x_ref = f32[256,1024]{1,0:T(8,128)} collective-permute-done((f32[256,1024]{1,0:T(8,128)}, f32[256,1024]{1,0:T(8,128)}, u32[]{:S(2)}, u32[]{:S(2)}) %collective-permute-start.1) | collective-permute-done | bytes 1048608 | tf_op jit(solution)/shard_map/ppermute | solution.py:278
  52.8 4.1 %far_blocks.1 = (f32[2,3,128,128]{3,2,1,0:T(8,128)S(1)}, f32[2,3,128,128]{3,2,1,0:T(8,128)S(1)}, f32[4,3,128,128]{3,2,1,0:T(8,128)S(1)}, bf16[8,256,256]{2,1,0:T(8,128)(2,1)S(1)}, bf16[8,256,256]{2,1,0:T(8,128)(2,1)S(1)}) custom-call(s32[1,3,16]{2,1,0:T(4,128)S(1)} %copy.8.refs_0_.slots_ref, s32[3]{0:T(128)S(1)} %pad_add_fusion.where_ref, ...), custom_call_target="tpu_custom_call" | custom-call | flops 1342177280 | bytes 8388608 | tf_op jit(solution)/shard_map/far_blocks/pallas_call | solution.py:207
  56.9 1.9 %collective-permute-start.2 = (f32[4,3,128,128]{3,2,1,0:T(8,128)S(1)}, f32[4,3,128,128]{3,2,1,0:T(8,128)S(1)}, u32[]{:S(2)}, u32[]{:S(2)}) collective-permute-start(f32[4,3,128,128]{3,2,1,0:T(8,128)S(1)} %get-tuple-element.27), channel_id=1, source_target_pairs={{0,32},{32,0},{1,33},{33,1},{2,34},{34,2},{3,35},{35,3},{4,36},{36... | collective-permute-start | bytes 2359304 | tf_op jit(solution)/shard_map/ppermute | solution.py:278
  58.9 2.3 %collective-permute-done.2 = f32[4,3,128,128]{3,2,1,0:T(8,128)S(1)} collective-permute-done((f32[4,3,128,128]{3,2,1,0:T(8,128)S(1)}, f32[4,3,128,128]{3,2,1,0:T(8,128)S(1)}, u32[]{:S(2)}, u32[]{:S(2)}) %collective-permute-start.2) | collective-permute-done | bytes 786464 | tf_op jit(solution)/shard_map/ppermute | solution.py:278
  61.2 1.6 %near_blocks.1 = (f32[2,3,128,128]{3,2,1,0:T(8,128)S(1)}, f32[2,3,128,128]{3,2,1,0:T(8,128)S(1)}, f32[4,3,128,128]{3,2,1,0:T(8,128)S(1)}) custom-call(s32[1,3,16]{2,1,0:T(4,128)S(1)} %copy.8.refs_0_.slots_ref, s32[3]{0:T(128)S(1)} %pad_add_fusion.where_ref, bf16[8,256,256]{2,1,0:T(8,128)(2,1)S(1)} %get-tuple-element.21.below_ref, ...), custom_call_target="tpu_custom_call" | custom-call | flops 805306368 | bytes 8388608 | tf_op jit(solution)/shard_map/near_blocks/pallas_call | solution.py:232
  62.8 2.0 %collective-permute-start.3 = (f32[4,3,128,128]{3,2,1,0:T(8,128)S(1)}, f32[4,3,128,128]{3,2,1,0:T(8,128)S(1)}, u32[]{:S(2)}, u32[]{:S(2)}) collective-permute-start(f32[4,3,128,128]{3,2,1,0:T(8,128)S(1)} %get-tuple-element.30), channel_id=1, source_target_pairs={{0,32},{32,0},{1,33},{33,1},{2,34},{34,2},{3,35},{35,3},{4,36},{36... | collective-permute-start | bytes 2359304 | tf_op jit(solution)/shard_map/ppermute | solution.py:278
  64.8 2.7 %collective-permute-start.4 = (f32[2,3,128,128]{3,2,1,0:T(8,128)S(1)}, f32[2,3,128,128]{3,2,1,0:T(8,128)S(1)}, u32[]{:S(2)}, u32[]{:S(2)}) collective-permute-start(f32[2,3,128,128]{3,2,1,0:T(8,128)S(1)} %slice_add_fusion.1), channel_id=1, source_target_pairs={{0,128},{32,416},{128,0},{160,288},{256,384},{288,160},{384,256},{... | collective-permute-start | bytes 1179656 | tf_op jit(solution)/shard_map/ppermute | solution.py:287
  67.5 6.9 %collective-permute-done.4 = f32[2,3,128,128]{3,2,1,0:T(8,128)S(1)} collective-permute-done((f32[2,3,128,128]{3,2,1,0:T(8,128)S(1)}, f32[2,3,128,128]{3,2,1,0:T(8,128)S(1)}, u32[]{:S(2)}, u32[]{:S(2)}) %collective-permute-start.4) | collective-permute-done | bytes 393248 | tf_op jit(solution)/shard_map/ppermute | solution.py:287
  74.5 2.4 %collective-permute-start.6 = (f32[3,128,128]{2,1,0:T(8,128)S(1)}, f32[3,128,128]{2,1,0:T(8,128)S(1)}, u32[]{:S(2)}, u32[]{:S(2)}) collective-permute-start(f32[3,128,128]{2,1,0:T(8,128)S(1)} %fusion.6), channel_id=1, source_target_pairs={{0,384},{32,160},{128,256},{160,32},{256,128},{288,416},{384,0},{4... | collective-permute-start | bytes 589832 | tf_op jit(solution)/shard_map/ppermute | solution.py:287
  76.9 0.0 collective-permute-done.3
  77.0 2.8 %collective-permute-start.5 = (f32[2,3,128,128]{3,2,1,0:T(8,128)S(1)}, f32[2,3,128,128]{3,2,1,0:T(8,128)S(1)}, u32[]{:S(2)}, u32[]{:S(2)}) collective-permute-start(f32[2,3,128,128]{3,2,1,0:T(8,128)S(1)} %slice_add_fusion), channel_id=1, source_target_pairs={{0,128},{32,416},{128,0},{160,288},{256,384},{288,160},{384,256},{... | collective-permute-start | bytes 1179656 | tf_op jit(solution)/shard_map/ppermute | solution.py:287
  79.8 4.1 %collective-permute-done.6 = f32[3,128,128]{2,1,0:T(8,128)S(1)} collective-permute-done((f32[3,128,128]{2,1,0:T(8,128)S(1)}, f32[3,128,128]{2,1,0:T(8,128)S(1)}, u32[]{:S(2)}, u32[]{:S(2)}) %collective-permute-start.6) | collective-permute-done | bytes 196640 | tf_op jit(solution)/shard_map/ppermute | solution.py:287
  83.9 6.8 %collective-permute-start.8 = (f32[3,128,128]{2,1,0:T(8,128)S(1)}, f32[3,128,128]{2,1,0:T(8,128)S(1)}, u32[]{:S(2)}, u32[]{:S(2)}) collective-permute-start(f32[3,128,128]{2,1,0:T(8,128)S(1)} %fusion.1), channel_id=1, source_target_pairs={{0,64},{64,0},{1,65},{65,1},{2,66},{66,2},{3,67},{67,3},{4,68},{68... | collective-permute-start | bytes 589832 | tf_op jit(solution)/shard_map/ppermute | solution.py:278
  90.8 0.0 collective-permute-done.5
  90.8 2.1 %collective-permute-start.7 = (f32[3,128,128]{2,1,0:T(8,128)S(1)}, f32[3,128,128]{2,1,0:T(8,128)S(1)}, u32[]{:S(2)}, u32[]{:S(2)}) collective-permute-start(f32[3,128,128]{2,1,0:T(8,128)S(1)} %fusion.2), channel_id=1, source_target_pairs={{0,384},{32,160},{128,256},{160,32},{256,128},{288,416},{384,0},{4... | collective-permute-start | bytes 589832 | tf_op jit(solution)/shard_map/ppermute | solution.py:287
  92.9 3.1 %collective-permute-done.8 = f32[3,128,128]{2,1,0:T(8,128)S(1)} collective-permute-done((f32[3,128,128]{2,1,0:T(8,128)S(1)}, f32[3,128,128]{2,1,0:T(8,128)S(1)}, u32[]{:S(2)}, u32[]{:S(2)}) %collective-permute-start.8) | collective-permute-done | bytes 196640 | tf_op jit(solution)/shard_map/ppermute | solution.py:278
  96.0 3.5 %collective-permute-done.7 = f32[3,128,128]{2,1,0:T(8,128)S(1)} collective-permute-done((f32[3,128,128]{2,1,0:T(8,128)S(1)}, f32[3,128,128]{2,1,0:T(8,128)S(1)}, u32[]{:S(2)}, u32[]{:S(2)}) %collective-permute-start.7) | collective-permute-done | bytes 196640 | tf_op jit(solution)/shard_map/ppermute | solution.py:287
  99.6 0.1 fusion.5.total_ref
  99.6 0.6 slice_bitcast_fusion
  100.3 11.3 %collective-permute-start.10 = (f32[128,128]{1,0:T(8,128)}, f32[128,128]{1,0:T(8,128)S(1)}, u32[]{:S(2)}, u32[]{:S(2)}) collective-permute-start(f32[128,128]{1,0:T(8,128)} %get-tuple-element.35), channel_id=1, source_target_pairs={{0,31},{1,0},{2,1},{3,2},{4,3},{5,4},{6,5},{7,6},{8,7},{9,8},{10,9... | collective-permute-start | bytes 196616 | tf_op jit(solution)/shard_map/ppermute | solution.py:278
  111.6 1.9 %collective-permute-start.9 = (f32[128,128]{1,0:T(8,128)S(1)}, f32[128,128]{1,0:T(8,128)S(1)}, u32[]{:S(2)}, u32[]{:S(2)}) collective-permute-start(f32[128,128]{1,0:T(8,128)S(1)} %get-tuple-element.36), channel_id=1, source_target_pairs={{0,1},{1,2},{2,3},{3,4},{4,5},{5,6},{6,7},{7,8},{8,9},{9,10},{10,1... | collective-permute-start | bytes 196616 | tf_op jit(solution)/shard_map/ppermute | solution.py:278
  113.5 0.6 collective-permute-done.10.right_ref
  114.1 7.6 %collective-permute-done.9.left_ref = f32[128,128]{1,0:T(8,128)S(1)} collective-permute-done((f32[128,128]{1,0:T(8,128)S(1)}, f32[128,128]{1,0:T(8,128)S(1)}, u32[]{:S(2)}, u32[]{:S(2)}) %collective-permute-start.9) | collective-permute-done | bytes 65568 | tf_op jit(solution)/shard_map/ppermute | solution.py:278
  121.7 1.4 %proximal.1 = f32[1,3,1,128,128]{4,3,2,1,0:T(8,128)} custom-call(s32[1]{0:T(128)} %bitcast.place_ref, s32[1,3,16]{2,1,0:T(4,128)S(1)} %copy.8.refs_0_.slots_ref, f32[3,128,128]{2,1,0:T(8,128)S(1)} %fusion.5.total_ref, f32[128,128]{1,0:T(8,128)S(1)} %collective-permute-done.9.left_ref, f32[128,128]{1,0:T(8,128)S(1)} %collective-permute-done.10.right_ref, ...), custom_call_target="tpu_custom_call" | custom-call | flops 983040 | bytes 524288 | tf_op jit(solution)/shard_map/proximal/pallas_call | solution.py:249
  (5 shorter events, 0.2 us)
Async XLA Ops:
  0.0 38.3 %collective-permute-start = (f32[256,1024]{1,0:T(8,128)}, f32[256,1024]{1,0:T(8,128)}, u32[]{:S(2)}, u32[]{:S(2)}) collective-permute-start(f32[256,1024]{1,0:T(8,128)} %refs_1_.1), channel_id=1, source_target_pairs={{0,1},{1,2},{2,3},{3,4},{4,5},{5,6},{6,7},{7,8},{8,9},{9,10},{10,1... | collective-permute-start | bytes 3145736 | tf_op jit(solution)/shard_map/ppermute | solution.py:278
  3.5 49.3 %collective-permute-start.1 = (f32[256,1024]{1,0:T(8,128)}, f32[256,1024]{1,0:T(8,128)}, u32[]{:S(2)}, u32[]{:S(2)}) collective-permute-start(f32[256,1024]{1,0:T(8,128)} %refs_1_.1), channel_id=1, source_target_pairs={{0,31},{1,0},{2,1},{3,2},{4,3},{5,4},{6,5},{7,6},{8,7},{9,8},{10,9... | collective-permute-start | bytes 3145736 | tf_op jit(solution)/shard_map/ppermute | solution.py:278
  16.6 1.9 %copy-start = (f32[1,3,16,128,128]{4,3,2,1,0:T(8,128)S(1)}, f32[1,3,16,128,128]{4,3,2,1,0:T(8,128)}, u32[]{:S(2)}) copy-start(f32[1,3,16,128,128]{4,3,2,1,0:T(8,128)} %omega_ref.3) | copy-start | bytes 9437188
  18.5 1.2 copy-start.2
  19.7 18.6 %copy-start.1 = (f32[1,3,16,128,128]{4,3,2,1,0:T(8,128)S(1)}, f32[1,3,16,128,128]{4,3,2,1,0:T(8,128)}, u32[]{:S(2)}) copy-start(f32[1,3,16,128,128]{4,3,2,1,0:T(8,128)} %omega_ref.3) | copy-start | bytes 9437188
  56.9 4.2 %collective-permute-start.2 = (f32[4,3,128,128]{3,2,1,0:T(8,128)S(1)}, f32[4,3,128,128]{3,2,1,0:T(8,128)S(1)}, u32[]{:S(2)}, u32[]{:S(2)}) collective-permute-start(f32[4,3,128,128]{3,2,1,0:T(8,128)S(1)} %get-tuple-element.27), channel_id=1, source_target_pairs={{0,32},{32,0},{1,33},{33,1},{2,34},{34,2},{3,35},{35,3},{4,36},{36... | collective-permute-start | bytes 2359304 | tf_op jit(solution)/shard_map/ppermute | solution.py:278
  62.8 14.1 %collective-permute-start.3 = (f32[4,3,128,128]{3,2,1,0:T(8,128)S(1)}, f32[4,3,128,128]{3,2,1,0:T(8,128)S(1)}, u32[]{:S(2)}, u32[]{:S(2)}) collective-permute-start(f32[4,3,128,128]{3,2,1,0:T(8,128)S(1)} %get-tuple-element.30), channel_id=1, source_target_pairs={{0,32},{32,0},{1,33},{33,1},{2,34},{34,2},{3,35},{35,3},{4,36},{36... | collective-permute-start | bytes 2359304 | tf_op jit(solution)/shard_map/ppermute | solution.py:278
  64.8 9.7 %collective-permute-start.4 = (f32[2,3,128,128]{3,2,1,0:T(8,128)S(1)}, f32[2,3,128,128]{3,2,1,0:T(8,128)S(1)}, u32[]{:S(2)}, u32[]{:S(2)}) collective-permute-start(f32[2,3,128,128]{3,2,1,0:T(8,128)S(1)} %slice_add_fusion.1), channel_id=1, source_target_pairs={{0,128},{32,416},{128,0},{160,288},{256,384},{288,160},{384,256},{... | collective-permute-start | bytes 1179656 | tf_op jit(solution)/shard_map/ppermute | solution.py:287
  74.5 9.4 %collective-permute-start.6 = (f32[3,128,128]{2,1,0:T(8,128)S(1)}, f32[3,128,128]{2,1,0:T(8,128)S(1)}, u32[]{:S(2)}, u32[]{:S(2)}) collective-permute-start(f32[3,128,128]{2,1,0:T(8,128)S(1)} %fusion.6), channel_id=1, source_target_pairs={{0,384},{32,160},{128,256},{160,32},{256,128},{288,416},{384,0},{4... | collective-permute-start | bytes 589832 | tf_op jit(solution)/shard_map/ppermute | solution.py:287
  77.0 13.8 %collective-permute-start.5 = (f32[2,3,128,128]{3,2,1,0:T(8,128)S(1)}, f32[2,3,128,128]{3,2,1,0:T(8,128)S(1)}, u32[]{:S(2)}, u32[]{:S(2)}) collective-permute-start(f32[2,3,128,128]{3,2,1,0:T(8,128)S(1)} %slice_add_fusion), channel_id=1, source_target_pairs={{0,128},{32,416},{128,0},{160,288},{256,384},{288,160},{384,256},{... | collective-permute-start | bytes 1179656 | tf_op jit(solution)/shard_map/ppermute | solution.py:287
  83.9 12.1 %collective-permute-start.8 = (f32[3,128,128]{2,1,0:T(8,128)S(1)}, f32[3,128,128]{2,1,0:T(8,128)S(1)}, u32[]{:S(2)}, u32[]{:S(2)}) collective-permute-start(f32[3,128,128]{2,1,0:T(8,128)S(1)} %fusion.1), channel_id=1, source_target_pairs={{0,64},{64,0},{1,65},{65,1},{2,66},{66,2},{3,67},{67,3},{4,68},{68... | collective-permute-start | bytes 589832 | tf_op jit(solution)/shard_map/ppermute | solution.py:278
  90.8 8.8 %collective-permute-start.7 = (f32[3,128,128]{2,1,0:T(8,128)S(1)}, f32[3,128,128]{2,1,0:T(8,128)S(1)}, u32[]{:S(2)}, u32[]{:S(2)}) collective-permute-start(f32[3,128,128]{2,1,0:T(8,128)S(1)} %fusion.2), channel_id=1, source_target_pairs={{0,384},{32,160},{128,256},{160,32},{256,128},{288,416},{384,0},{4... | collective-permute-start | bytes 589832 | tf_op jit(solution)/shard_map/ppermute | solution.py:287
  100.3 13.8 %collective-permute-start.10 = (f32[128,128]{1,0:T(8,128)}, f32[128,128]{1,0:T(8,128)S(1)}, u32[]{:S(2)}, u32[]{:S(2)}) collective-permute-start(f32[128,128]{1,0:T(8,128)} %get-tuple-element.35), channel_id=1, source_target_pairs={{0,31},{1,0},{2,1},{3,2},{4,3},{5,4},{6,5},{7,6},{8,7},{9,8},{10,9... | collective-permute-start | bytes 196616 | tf_op jit(solution)/shard_map/ppermute | solution.py:278
  111.6 10.1 %collective-permute-start.9 = (f32[128,128]{1,0:T(8,128)S(1)}, f32[128,128]{1,0:T(8,128)S(1)}, u32[]{:S(2)}, u32[]{:S(2)}) collective-permute-start(f32[128,128]{1,0:T(8,128)S(1)} %get-tuple-element.36), channel_id=1, source_target_pairs={{0,1},{1,2},{2,3},{3,4},{4,5},{5,6},{6,7},{7,8},{8,9},{9,10},{10,1... | collective-permute-start | bytes 196616 | tf_op jit(solution)/shard_map/ppermute | solution.py:278

commit v4 on v1

v4 whole, which is shorter than its diff:
```python
import jax
import jax.numpy as jnp
from jax import lax
from jax.experimental import pallas as pl
from jax.experimental.pallas import tpu as pltpu
from jax.sharding import Mesh, PartitionSpec as P

TILE = 1024
BLK = 128
NB = TILE // BLK
KMAX = 16
ROWS = 256
SAMPLES = 4096
step_size = 0.5
penalty = 0.1
f32 = jnp.float32
bf16 = jnp.bfloat16
VMEM_LIMIT = 24 * 1024 * 1024


def split(value):
    high = value.astype(bf16)
    low = (value - high.astype(f32)).astype(bf16)
    return high, low


def split_tile(x_ref, natural_ref, turned_ref, start=0):
    rows = x_ref.shape[0]
    for a in range(NB):
        block = x_ref[:, a * BLK : (a + 1) * BLK]
        high, low = split(block)
        natural_ref[a, :, :BLK] = high
        natural_ref[a, :, BLK:] = low
        high, low = split(block.T)
        turned_ref[a, :BLK, start : start + rows] = high
        turned_ref[a, BLK:, start : start + rows] = low


def add_products(slots_ref, omega_ref, natural_ref, residual_ref, offset, start=0):
    rows = natural_ref.shape[1]

    def body(j, carry):
        slot = slots_ref[0, offset, j]
        active = slot >= 0
        place = jnp.maximum(slot, 0)
        a = place // NB
        b = place % NB
        weight = jnp.where(active, omega_ref[0, 0, j], 0.0)
        high, low = split(weight)
        half = jnp.concatenate([high, low], axis=1)
        weights = jnp.concatenate([half, half], axis=0)
        out = jnp.dot(natural_ref[a], weights, preferred_element_type=f32)
        residual_ref[b, start : start + rows] += out[:, :BLK] + out[:, BLK:]
        return carry

    lax.fori_loop(0, KMAX, body, 0, unroll=4)


def partial_kernel(offset, first, *refs):
    if first:
        slots_ref, x_ref, omega_ref, residual_ref, turned_ref, natural_ref = refs
        residual_ref[...] = jnp.zeros_like(residual_ref)
    else:
        slots_ref, x_ref, omega_ref, before_ref, residual_ref, turned_ref, natural_ref = refs
        residual_ref[...] = before_ref[...]
    split_tile(x_ref, natural_ref, turned_ref)
    add_products(slots_ref, omega_ref, natural_ref, residual_ref, offset)


def quadrant_sum(out):
    out = out[:BLK] + out[BLK:]
    return out[:, :BLK] + out[:, BLK:]


def slot_block(slots_ref, e, j, turned, pieces_ref):
    place = jnp.maximum(slots_ref[0, e, j], 0)
    out = jnp.dot(
        turned[e][place // NB], pieces_ref[place % NB], preferred_element_type=f32
    )
    return quadrant_sum(out)


def forward_kernel(
    slots_ref, where_ref, x_ref, omega_ref, before_ref, half_ref, below_ref, centre_ref,
    keep_ref, pass_ref, send_ref, residual_ref, natural_ref, above_ref, pieces_ref,
):
    residual_ref[...] = before_ref[...]
    done = half_ref.shape[2]
    above_ref[:, :, :done] = half_ref[...]
    split_tile(x_ref, natural_ref, above_ref, done)
    add_products(slots_ref, omega_ref, natural_ref, residual_ref, 2, done)
    for b in range(NB):
        high, low = split(residual_ref[b])
        pieces_ref[b, :, :BLK] = high
        pieces_ref[b, :, BLK:] = low
    turned = (below_ref, centre_ref, above_ref)
    x, own_y, core = where_ref[0], where_ref[1], where_ref[2]
    even_pair, odd_pair = x ^ 1, 3 - x
    first = jnp.where(core == 0, even_pair, odd_pair)
    second = jnp.where(core == 0, odd_pair, even_pair)
    for r, x_of in enumerate((x, second, first, x ^ 2)):
        for q in range(2):
            i = 2 * x_of + (own_y ^ q)
            for e in range(3):
                even = slot_block(slots_ref, e, 2 * i, turned, pieces_ref)
                odd = slot_block(slots_ref, e, 2 * i + 1, turned, pieces_ref)
                if e == 1:
                    even_turned, odd_turned = even.T, odd.T
                    diagonal = i < NB // 2
                    even, odd = (
                        even + jnp.where(diagonal, even_turned, odd_turned),
                        odd + jnp.where(diagonal, odd_turned, even_turned),
                    )
                own_ref = keep_ref if r < 2 else pass_ref
                own_ref[r % 2, q, e] = jnp.where(core == 0, even, odd)
                send_ref[(0, 2, 1, 3)[r], q, e] = jnp.where(core == 0, odd, even)


def proximal_kernel(
    place_ref, slots_ref, near_ref, other_ref, right_ref, left_ref, omega_ref, out_ref
):
    j = place_ref[0]
    rows = lax.broadcasted_iota(jnp.int32, (BLK, BLK), 0)
    columns = lax.broadcasted_iota(jnp.int32, (BLK, BLK), 1)
    for e in range(3):
        slot = slots_ref[0, e, j]
        total = near_ref[e] + other_ref[e]
        if e == 0:
            total = total + left_ref[...].T
        if e == 2:
            total = total + right_ref[...].T
        gradient = total * (0.5 / SAMPLES)
        omega = omega_ref[0, e, 0]
        if e == 1:
            diagonal = (slot >= 0) & (slot // NB == slot % NB)
            on_diagonal = (rows == columns) & diagonal
            inverse = 1.0 / jnp.where(on_diagonal, omega, 1.0)
            gradient = gradient - jnp.where(on_diagonal, inverse, 0.0)
        trial = omega - step_size * gradient
        shrunk = jnp.maximum(jnp.abs(trial) - step_size * penalty, 0.0)
        result = jnp.where(trial < 0.0, -shrunk, shrunk)
        if e == 1:
            result = jnp.where(on_diagonal, trial, result)
        out_ref[0, e, 0] = jnp.where(slot >= 0, result, 0.0)


def params():
    return pltpu.CompilerParams(vmem_limit_bytes=VMEM_LIMIT)


SMEM = pl.BlockSpec(memory_space=pltpu.SMEM)
WHOLE = pl.BlockSpec(memory_space=pltpu.VMEM)
TURNED = (NB, 2 * BLK, ROWS)
NATURAL = (NB, ROWS, 2 * BLK)


def omega_spec(offset):
    return pl.BlockSpec((1, 1, KMAX, BLK, BLK), lambda i: (0, offset, 0, 0, 0))


def full_spec(shape):
    return pl.BlockSpec(shape, lambda i: (0,) * len(shape))


def partial(offset, slots, tile, omega, before=None):
    first = before is None
    rows = tile.shape[0]
    turned = (NB, 2 * BLK, rows)
    in_specs = [SMEM, full_spec((rows, TILE)), omega_spec(offset)]
    inputs = [slots, tile, omega]
    if not first:
        in_specs.append(full_spec((NB, ROWS, BLK)))
        inputs.append(before)
    return pl.pallas_call(
        lambda *refs: partial_kernel(offset, first, *refs),
        name="partial_residual",
        grid=(1,),
        out_shape=(
            jax.ShapeDtypeStruct((NB, ROWS, BLK), f32),
            jax.ShapeDtypeStruct(turned, bf16),
        ),
        in_specs=in_specs,
        out_specs=(full_spec((NB, ROWS, BLK)), full_spec(turned)),
        scratch_shapes=[pltpu.VMEM((NB, rows, 2 * BLK), bf16)],
        compiler_params=params(),
        cost_estimate=pl.CostEstimate(
            flops=2 * KMAX * rows * 256 * 256, bytes_accessed=5 << 20, transcendentals=0
        ),
    )(*inputs)


HALF = (2, 2, 3, BLK, BLK)
WAY = (4, 2, 3, BLK, BLK)


def forward_blocks(slots, where, tile, omega, before, half, below, centre):
    rows = tile.shape[0]
    return pl.pallas_call(
        forward_kernel,
        name="forward_blocks",
        grid=(1,),
        out_shape=tuple(jax.ShapeDtypeStruct(shape, f32) for shape in (HALF, HALF, WAY)),
        in_specs=[
            SMEM,
            SMEM,
            full_spec((rows, TILE)),
            omega_spec(2),
            full_spec((NB, ROWS, BLK)),
            full_spec((NB, 2 * BLK, ROWS - rows)),
            full_spec(TURNED),
            full_spec(TURNED),
        ],
        out_specs=tuple(full_spec(shape) for shape in (HALF, HALF, WAY)),
        scratch_shapes=[
            pltpu.VMEM((NB, ROWS, BLK), f32),
            pltpu.VMEM((NB, rows, 2 * BLK), bf16),
            pltpu.VMEM(TURNED, bf16),
            pltpu.VMEM(NATURAL, bf16),
        ],
        compiler_params=params(),
        cost_estimate=pl.CostEstimate(
            flops=7 * KMAX * ROWS * 256 * 256, bytes_accessed=8 << 20, transcendentals=0
        ),
    )(slots, where, tile, omega, before, half, below, centre)


def proximal(place, slots, near, other, right, left, omega):
    return pl.pallas_call(
        proximal_kernel,
        name="proximal",
        grid_spec=pltpu.PrefetchScalarGridSpec(
            num_scalar_prefetch=2,
            grid=(1,),
            in_specs=[
                pl.BlockSpec((3, BLK, BLK), lambda i, place, slots: (0, 0, 0)),
                pl.BlockSpec((3, BLK, BLK), lambda i, place, slots: (0, 0, 0)),
                pl.BlockSpec((BLK, BLK), lambda i, place, slots: (0, 0)),
                pl.BlockSpec((BLK, BLK), lambda i, place, slots: (0, 0)),
                pl.BlockSpec(
                    (1, 3, 1, BLK, BLK), lambda i, place, slots: (0, 0, place[0], 0, 0)
                ),
            ],
            out_specs=pl.BlockSpec(
                (1, 3, 1, BLK, BLK), lambda i, place, slots: (0, 0, 0, 0, 0)
            ),
        ),
        out_shape=jax.ShapeDtypeStruct((1, 3, 1, BLK, BLK), f32),
        compiler_params=params(),
        cost_estimate=pl.CostEstimate(
            flops=20 * 3 * BLK * BLK, bytes_accessed=1 << 19, transcendentals=0
        ),
    )(place, slots, near, other, right, left, omega)


def shifted(value, axis, steps):
    count = lax.axis_size(axis)
    pairs = [(source, (source + steps) % count) for source in range(count)]
    return lax.ppermute(value, axis, pairs)


def x_exchange(value, step):
    pairs = []
    for x in range(4):
        for core in range(2):
            partner = x ^ 1 if core == step else 3 - x
            pairs.append((2 * x + core, 2 * partner + core))
    return lax.ppermute(value, ("x", "core"), pairs)


def on_device(observations, omega, block_slots):
    x, y_hi, core = (lax.axis_index(n).astype(jnp.int32) for n in ("x", "y_hi", "core"))
    where = jnp.stack([x, y_hi, core])
    place = 4 * x + 2 * y_hi + core
    cut = ROWS // 2
    from_below = shifted(observations, "col", 1)
    above_early = shifted(observations[:cut], "col", -1)
    above_late = shifted(observations[cut:], "col", -1)
    residual, centre = partial(1, block_slots, observations, omega)
    residual, below = partial(0, block_slots, from_below, omega, residual)
    residual, half = partial(2, block_slots, above_early, omega, residual)
    keep, out, send = forward_blocks(
        block_slots, where, above_late, omega, residual, half, below, centre
    )
    got = shifted(send, "core", 1)
    first = x_exchange(out + got[2:], 0)
    second = x_exchange(keep[1] + got[1] + first[1], 1)
    kept = keep[0] + got[0] + first[0]
    other = shifted(kept[1] + second[1], "y_hi", 1)
    near = kept[0] + second[0]
    right = shifted(near[0] + other[0], "col", -1)
    left = shifted(near[2] + other[2], "col", 1)
    return proximal(place.reshape(1), block_slots, near, other, right, left, omega)


def solution(mesh):
    devices = mesh.devices.reshape(4, 2, 2, 32)
    fine = Mesh(devices, ("x", "y_hi", "core", "col"))
    rows = ("x", "y_hi", "core")
    return jax.shard_map(
        on_device,
        mesh=fine,
        in_specs=(P(rows, "col"), P("col", None, None, None, None), P("col", None, None)),
        out_specs=P("col", None, rows, None, None),
        check_vma=False,
    )
```

time: 137 us -> 125 us (0.912); the launches traced: 137 us -> 123 us
  blocking collectives: 34.7 us -> 0 us
  waiting for transfers between devices: 40.7 us -> 52.8 us
  starting transfers between devices: 42.3 us -> 49.1 us
  local copies, waits for them, and re-layouts: 2.55 us -> 5.46 us
    all_to_all x1 -> x0, blocking collectives: 34.7 us -> none  [on_device(): gathered = lax.all_to_all(chip, ('x', 'y_hi'), 0, 0)]
    ppermute x0 -> x2, waiting for transfers between devices: none -> 19.6 us  [x_exchange(): return lax.ppermute(value, ('x', 'core'), pairs)]
    ppermute x5 -> x7, waiting for transfers between devices: 40.7 us -> 33.1 us  [shifted(): return lax.ppermute(value, axis, pairs)]
    ppermute x0 -> x2, starting transfers between devices: none -> 5.12 us  [x_exchange(): return lax.ppermute(value, ('x', 'core'), pairs)]
    pallas_call x1, Pallas kernels: 7.3 us -> 4.41 us  [forward_blocks(): pl.pallas_call(forward_kernel, name='forward_blocks', grid=(1,), out_shap...]
    slice x0 -> x1, local copies, waits for them, and re-layouts: none -> 2.34 us  [on_device(): above_early = shifted(observations[:cut], 'col', -1)]
    ppermute x5 -> x7, starting transfers between devices: 42.3 us -> 44 us  [shifted(): return lax.ppermute(value, axis, pairs)]
    pallas_call x2 -> x3, Pallas kernels: 5.83 us -> 7.44 us  [partial(): pl.pallas_call(lambda *refs: partial_kernel(offset, first, *refs), name='...]
  transfers between devices with their start and end apart: 5 -> 9, of which waited for: 5 -> 9; matrix products, arithmetic and copies ran while one was open for 1% -> 2% of each run, Pallas kernels for 4% -> 6%
where the time goes in v4:
time: 125 us; the launch traced here: 123 us
  waiting for transfers between devices  52.8 us (42%)
  starting transfers between devices  49.1 us (39%)
  Pallas kernels  14.1 us (11%)
  local copies, waits for them, and re-layouts  5.46 us (4%)
    ppermute x7, starting transfers between devices, shifted(): return lax.ppermute(value, axis, pairs)  44 us
    ppermute x7, waiting for transfers between devices, shifted(): return lax.ppermute(value, axis, pairs)  33.1 us
    ppermute x2, waiting for transfers between devices, x_exchange(): return lax.ppermute(value, ('x', 'core'), pairs)  19.6 us
    pallas_call x3, Pallas kernels, partial(): pl.pallas_call(lambda *refs: partial_kernel(offset, first, *refs), name='...  7.44 us
    ppermute x2, starting transfers between devices, x_exchange(): return lax.ppermute(value, ('x', 'core'), pairs)  5.12 us
    pallas_call x1, Pallas kernels, forward_blocks(): pl.pallas_call(forward_kernel, name='forward_blocks', grid=(1,), out_shap...  4.41 us
    unnamed x9, local copies, waits for them, and re-layouts  3.12 us
  transfers between devices with their start and end apart: 9, of which 9 were waited for; matrix products, arithmetic and copies ran while one was open for 2% of the time, Pallas kernels for 6%

profile of v4, /device:TPU:6, one launch (start us, length us, event | category | flops | bytes accessed | tf_op | source)
XLA Modules:
  0.0 122.6 jit_solution(6019141740367336572)
XLA Ops:
  0.0 0.0 copy-start.3
  0.0 3.6 %collective-permute-start.2 = (f32[256,1024]{1,0:T(8,128)}, f32[256,1024]{1,0:T(8,128)}, u32[]{:S(2)}, u32[]{:S(2)}) collective-permute-start(f32[256,1024]{1,0:T(8,128)} %refs_1_.1), channel_id=1, source_target_pairs={{0,1},{1,2},{2,3},{3,4},{4,5},{5,6},{6,7},{7,8},{8,9},{9,10},{10,1... | collective-permute-start | bytes 3145736 | tf_op jit(solution)/shard_map/ppermute | solution.py:258
  3.6 2.3 %fusion.4 = (f32[128,1024]{1,0:T(8,128)}, f32[128,1024]{1,0:T(8,128)}) fusion(f32[256,1024]{1,0:T(8,128)} %refs_1_.1), kind=kLoop, calls=%fused_computation.18 | loop fusion | bytes 2097152 | tf_op jit(solution)/shard_map/slice | solution.py:276
  6.0 12.4 %collective-permute-start.1 = (f32[128,1024]{1,0:T(8,128)}, f32[128,1024]{1,0:T(8,128)}, u32[]{:S(2)}, u32[]{:S(2)}) collective-permute-start(f32[128,1024]{1,0:T(8,128)} %get-tuple-element.25), channel_id=1, source_target_pairs={{0,31},{1,0},{2,1},{3,2},{4,3},{5,4},{6,5},{7,6},{8,7},{9,8},{10,9... | collective-permute-start | bytes 1572872 | tf_op jit(solution)/shard_map/ppermute | solution.py:258
  18.4 3.9 %collective-permute-start = (f32[128,1024]{1,0:T(8,128)}, f32[128,1024]{1,0:T(8,128)}, u32[]{:S(2)}, u32[]{:S(2)}) collective-permute-start(f32[128,1024]{1,0:T(8,128)} %get-tuple-element.26), channel_id=1, source_target_pairs={{0,31},{1,0},{2,1},{3,2},{4,3},{5,4},{6,5},{7,6},{8,7},{9,8},{10,9... | collective-permute-start | bytes 1572872 | tf_op jit(solution)/shard_map/ppermute | solution.py:258
  22.3 0.0 copy-done.3
  22.3 0.0 copy-start
  22.4 1.9 %copy-done = f32[1,3,16,128,128]{4,3,2,1,0:T(8,128)S(1)} copy-done((f32[1,3,16,128,128]{4,3,2,1,0:T(8,128)S(1)}, f32[1,3,16,128,128]{4,3,2,1,0:T(8,128)}, u32[]{:S(2)}) %copy-start) | copy-done | bytes 3145752
  24.2 0.0 copy-start.2
  24.2 1.2 copy-done.2
  25.5 0.0 copy-start.1
  25.5 2.3 %partial_residual.3 = (f32[8,256,128]{2,1,0:T(8,128)S(1)}, bf16[8,256,256]{2,1,0:T(8,128)(2,1)S(1)}) custom-call(s32[1,3,16]{2,1,0:T(4,128)S(1)} %copy.8.refs_0_.slots_ref, f32[256,1024]{1,0:T(8,128)S(1)} %copy-done.2, f32[1,3,16,128,128]{4,3,2,1,0:T(8,128)S(1)} %copy-done), custom_call_target="tpu_custom_call" | custom-call | flops 536870912 | bytes 5242880 | tf_op jit(solution)/shard_map/partial_residual/pallas_call | solution.py:174
  27.7 0.1 pad_add_fusion.where_ref
  27.8 10.6 %collective-permute-done.2.refs_1_ = f32[256,1024]{1,0:T(8,128)} collective-permute-done((f32[256,1024]{1,0:T(8,128)}, f32[256,1024]{1,0:T(8,128)}, u32[]{:S(2)}, u32[]{:S(2)}) %collective-permute-start.2) | collective-permute-done | bytes 1048608 | tf_op jit(solution)/shard_map/ppermute | solution.py:258
  38.5 0.0 copy-done.1
  38.5 2.9 %partial_residual.4 = (f32[8,256,128]{2,1,0:T(8,128)S(1)}, bf16[8,256,256]{2,1,0:T(8,128)(2,1)S(1)}) custom-call(s32[1,3,16]{2,1,0:T(4,128)S(1)} %copy.8.refs_0_.slots_ref, f32[256,1024]{1,0:T(8,128)} %collective-permute-done.2.refs_1_, f32[1,3,16,128,128]{4,3,2,1,0:T(8,128)S(1)} %copy-done.1, f32[8,256,128]{2,1,0:T(8,128)S(1)} %get-tuple-element.14.refs_3_), custom_call_target="tpu_custom_call" | custom-call | flops 536870912 | bytes 5242880 | tf_op jit(solution)/shard_map/partial_residual/pallas_call | solution.py:174
  41.4 0.8 collective-permute-done.1.refs_1_
  42.2 2.3 %partial_residual.5 = (f32[8,256,128]{2,1,0:T(8,128)S(1)}, bf16[8,256,128]{2,1,0:T(8,128)(2,1)S(1)}) custom-call(s32[1,3,16]{2,1,0:T(4,128)S(1)} %copy.8.refs_0_.slots_ref, f32[128,1024]{1,0:T(8,128)} %collective-permute-done.1.refs_1_, f32[1,3,16,128,128]{4,3,2,1,0:T(8,128)S(1)} %copy-done.1, f32[8,256,128]{2,1,0:T(8,128)S(1)} %get-tuple-element.15.refs_3_), custom_call_target="tpu_custom_call" | custom-call | flops 268435456 | bytes 5242880 | tf_op jit(solution)/shard_map/partial_residual/pallas_call | solution.py:174
  44.5 8.9 %collective-permute-done.x_ref = f32[128,1024]{1,0:T(8,128)} collective-permute-done((f32[128,1024]{1,0:T(8,128)}, f32[128,1024]{1,0:T(8,128)}, u32[]{:S(2)}, u32[]{:S(2)}) %collective-permute-start) | collective-permute-done | bytes 524320 | tf_op jit(solution)/shard_map/ppermute | solution.py:258
  53.3 4.4 %forward_blocks.1 = (f32[2,2,3,128,128]{4,3,2,1,0:T(8,128)S(1)}, f32[2,2,3,128,128]{4,3,2,1,0:T(8,128)S(1)}, f32[4,2,3,128,128]{4,3,2,1,0:T(8,128)S(1)}) custom-call(s32[1,3,16]{2,1,0:T(4,128)S(1)} %copy.8.refs_0_.slots_ref, s32[3]{0:T(128)S(1)} %pad_add_fusion.where_ref, f32[128,1024]{1,0:T(8,128)} %collective-permute-done.x_ref, ...), custom_call_target="tpu_custom_call" | custom-call | flops 1879048192 | bytes 8388608 | tf_op jit(solution)/shard_map/forward_blocks/pallas_call | solution.py:198
  57.7 1.9 %collective-permute-start.3 = (f32[4,2,3,128,128]{4,3,2,1,0:T(8,128)S(1)}, f32[4,2,3,128,128]{4,3,2,1,0:T(8,128)S(1)}, u32[]{:S(2)}, u32[]{:S(2)}) collective-permute-start(f32[4,2,3,128,128]{4,3,2,1,0:T(8,128)S(1)} %get-tuple-element.21), channel_id=1, source_target_pairs={{0,32},{32,0},{1,33},{33,1},{2,34},{34,2},{3,35},{35,3},{4,36},{36... | collective-permute-start | bytes 4718600 | tf_op jit(solution)/shard_map/ppermute | solution.py:258
  59.7 3.4 %collective-permute-done.3 = f32[4,2,3,128,128]{4,3,2,1,0:T(8,128)S(1)} collective-permute-done((f32[4,2,3,128,128]{4,3,2,1,0:T(8,128)S(1)}, f32[4,2,3,128,128]{4,3,2,1,0:T(8,128)S(1)}, u32[]{:S(2)}, u32[]{:S(2)}) %collective-permute-start.3) | collective-permute-done | bytes 1572896 | tf_op jit(solution)/shard_map/ppermute | solution.py:258
  63.0 0.1 slice_add_fusion
  63.1 2.7 %collective-permute-start.4 = (f32[2,2,3,128,128]{4,3,2,1,0:T(8,128)S(1)}, f32[2,2,3,128,128]{4,3,2,1,0:T(8,128)S(1)}, u32[]{:S(2)}, u32[]{:S(2)}) collective-permute-start(f32[2,2,3,128,128]{4,3,2,1,0:T(8,128)S(1)} %slice_add_fusion), channel_id=1, source_target_pairs={{0,128},{32,416},{128,0},{160,288},{256,384},{288,160},{384,256},{... | collective-permute-start | bytes 2359304 | tf_op jit(solution)/shard_map/ppermute | solution.py:267
  65.9 11.1 %collective-permute-done.4 = f32[2,2,3,128,128]{4,3,2,1,0:T(8,128)S(1)} collective-permute-done((f32[2,2,3,128,128]{4,3,2,1,0:T(8,128)S(1)}, f32[2,2,3,128,128]{4,3,2,1,0:T(8,128)S(1)}, u32[]{:S(2)}, u32[]{:S(2)}) %collective-permute-start.4) | collective-permute-done | bytes 786464 | tf_op jit(solution)/shard_map/ppermute | solution.py:267
  77.0 0.1 slice_add_fusion.3
  77.2 2.4 %collective-permute-start.5 = (f32[2,3,128,128]{3,2,1,0:T(8,128)S(1)}, f32[2,3,128,128]{3,2,1,0:T(8,128)S(1)}, u32[]{:S(2)}, u32[]{:S(2)}) collective-permute-start(f32[2,3,128,128]{3,2,1,0:T(8,128)S(1)} %get-tuple-element.24), channel_id=1, source_target_pairs={{0,384},{32,160},{128,256},{160,32},{256,128},{288,416},{384,0},{4... | collective-permute-start | bytes 1179656 | tf_op jit(solution)/shard_map/ppermute | solution.py:267
  79.6 8.5 %collective-permute-done.5 = f32[2,3,128,128]{3,2,1,0:T(8,128)S(1)} collective-permute-done((f32[2,3,128,128]{3,2,1,0:T(8,128)S(1)}, f32[2,3,128,128]{3,2,1,0:T(8,128)S(1)}, u32[]{:S(2)}, u32[]{:S(2)}) %collective-permute-start.5) | collective-permute-done | bytes 393248 | tf_op jit(solution)/shard_map/ppermute | solution.py:267
  88.1 0.1 fusion.1
  88.1 7.7 %collective-permute-start.6 = (f32[3,128,128]{2,1,0:T(8,128)S(1)}, f32[3,128,128]{2,1,0:T(8,128)S(1)}, u32[]{:S(2)}, u32[]{:S(2)}) collective-permute-start(f32[3,128,128]{2,1,0:T(8,128)S(1)} %get-tuple-element.27), channel_id=1, source_target_pairs={{0,64},{64,0},{1,65},{65,1},{2,66},{66,2},{3,67},{67,3},{4,68},{68... | collective-permute-start | bytes 589832 | tf_op jit(solution)/shard_map/ppermute | solution.py:258
  95.9 7.3 %collective-permute-done.6.other_ref = f32[3,128,128]{2,1,0:T(8,128)S(1)} collective-permute-done((f32[3,128,128]{2,1,0:T(8,128)S(1)}, f32[3,128,128]{2,1,0:T(8,128)S(1)}, u32[]{:S(2)}, u32[]{:S(2)}) %collective-permute-start.6) | collective-permute-done | bytes 196640 | tf_op jit(solution)/shard_map/ppermute | solution.py:258
  103.1 0.6 fusion.2
  103.8 2.0 %collective-permute-start.8 = (f32[128,128]{1,0:T(8,128)}, f32[128,128]{1,0:T(8,128)}, u32[]{:S(2)}, u32[]{:S(2)}) collective-permute-start(f32[128,128]{1,0:T(8,128)} %get-tuple-element.29), channel_id=1, source_target_pairs={{0,1},{1,2},{2,3},{3,4},{4,5},{5,6},{6,7},{7,8},{8,9},{9,10},{10,1... | collective-permute-start | bytes 196616 | tf_op jit(solution)/shard_map/ppermute | solution.py:258
  105.7 12.4 %collective-permute-start.7 = (f32[128,128]{1,0:T(8,128)}, f32[128,128]{1,0:T(8,128)}, u32[]{:S(2)}, u32[]{:S(2)}) collective-permute-start(f32[128,128]{1,0:T(8,128)} %get-tuple-element.30), channel_id=1, source_target_pairs={{0,31},{1,0},{2,1},{3,2},{4,3},{5,4},{6,5},{7,6},{8,7},{9,8},{10,9... | collective-permute-start | bytes 196616 | tf_op jit(solution)/shard_map/ppermute | solution.py:258
  118.2 0.7 collective-permute-done.8.left_ref
  118.8 1.5 %collective-permute-done.7.right_ref = f32[128,128]{1,0:T(8,128)} collective-permute-done((f32[128,128]{1,0:T(8,128)}, f32[128,128]{1,0:T(8,128)}, u32[]{:S(2)}, u32[]{:S(2)}) %collective-permute-start.7) | collective-permute-done | bytes 65568 | tf_op jit(solution)/shard_map/ppermute | solution.py:258
  120.4 2.2 %proximal.1 = f32[1,3,1,128,128]{4,3,2,1,0:T(8,128)} custom-call(s32[1]{0:T(128)} %bitcast.place_ref, s32[1,3,16]{2,1,0:T(4,128)S(1)} %copy.8.refs_0_.slots_ref, f32[3,128,128]{2,1,0:T(8,128)S(1)} %bitcast.29, f32[3,128,128]{2,1,0:T(8,128)S(1)} %collective-permute-done.6.other_ref, f32[128,128]{1,0:T(8,128)} %collective-permute-done.7.right_ref, ...), custom_call_target="tpu_custom_call" | custom-call | flops 983040 | bytes 524288 | tf_op jit(solution)/shard_map/proximal/pallas_call | solution.py:228
  (1 shorter events, 0.0 us)
Async XLA Ops:
  0.0 22.3 %copy-start.3 = (s32[1,3,16]{2,0,1:T(1,128)S(1)}, s32[1,3,16]{2,0,1:T(1,128)}, u32[]{:S(2)}) copy-start(s32[1,3,16]{2,0,1:T(1,128)} %param.5) | copy-start | bytes 580
  0.0 38.5 %collective-permute-start.2 = (f32[256,1024]{1,0:T(8,128)}, f32[256,1024]{1,0:T(8,128)}, u32[]{:S(2)}, u32[]{:S(2)}) collective-permute-start(f32[256,1024]{1,0:T(8,128)} %refs_1_.1), channel_id=1, source_target_pairs={{0,1},{1,2},{2,3},{3,4},{4,5},{5,6},{6,7},{7,8},{8,9},{9,10},{10,1... | collective-permute-start | bytes 3145736 | tf_op jit(solution)/shard_map/ppermute | solution.py:258
  6.0 36.2 %collective-permute-start.1 = (f32[128,1024]{1,0:T(8,128)}, f32[128,1024]{1,0:T(8,128)}, u32[]{:S(2)}, u32[]{:S(2)}) collective-permute-start(f32[128,1024]{1,0:T(8,128)} %get-tuple-element.25), channel_id=1, source_target_pairs={{0,31},{1,0},{2,1},{3,2},{4,3},{5,4},{6,5},{7,6},{8,7},{9,8},{10,9... | collective-permute-start | bytes 1572872 | tf_op jit(solution)/shard_map/ppermute | solution.py:258
  18.4 34.9 %collective-permute-start = (f32[128,1024]{1,0:T(8,128)}, f32[128,1024]{1,0:T(8,128)}, u32[]{:S(2)}, u32[]{:S(2)}) collective-permute-start(f32[128,1024]{1,0:T(8,128)} %get-tuple-element.26), channel_id=1, source_target_pairs={{0,31},{1,0},{2,1},{3,2},{4,3},{5,4},{6,5},{7,6},{8,7},{9,8},{10,9... | collective-permute-start | bytes 1572872 | tf_op jit(solution)/shard_map/ppermute | solution.py:258
  22.3 1.9 %copy-start = (f32[1,3,16,128,128]{4,3,2,1,0:T(8,128)S(1)}, f32[1,3,16,128,128]{4,3,2,1,0:T(8,128)}, u32[]{:S(2)}) copy-start(f32[1,3,16,128,128]{4,3,2,1,0:T(8,128)} %omega_ref.3) | copy-start | bytes 9437188
  24.2 1.2 copy-start.2
  25.5 13.0 %copy-start.1 = (f32[1,3,16,128,128]{4,3,2,1,0:T(8,128)S(1)}, f32[1,3,16,128,128]{4,3,2,1,0:T(8,128)}, u32[]{:S(2)}) copy-start(f32[1,3,16,128,128]{4,3,2,1,0:T(8,128)} %omega_ref.3) | copy-start | bytes 9437188
  57.7 5.3 %collective-permute-start.3 = (f32[4,2,3,128,128]{4,3,2,1,0:T(8,128)S(1)}, f32[4,2,3,128,128]{4,3,2,1,0:T(8,128)S(1)}, u32[]{:S(2)}, u32[]{:S(2)}) collective-permute-start(f32[4,2,3,128,128]{4,3,2,1,0:T(8,128)S(1)} %get-tuple-element.21), channel_id=1, source_target_pairs={{0,32},{32,0},{1,33},{33,1},{2,34},{34,2},{3,35},{35,3},{4,36},{36... | collective-permute-start | bytes 4718600 | tf_op jit(solution)/shard_map/ppermute | solution.py:258
  63.1 13.9 %collective-permute-start.4 = (f32[2,2,3,128,128]{4,3,2,1,0:T(8,128)S(1)}, f32[2,2,3,128,128]{4,3,2,1,0:T(8,128)S(1)}, u32[]{:S(2)}, u32[]{:S(2)}) collective-permute-start(f32[2,2,3,128,128]{4,3,2,1,0:T(8,128)S(1)} %slice_add_fusion), channel_id=1, source_target_pairs={{0,128},{32,416},{128,0},{160,288},{256,384},{288,160},{384,256},{... | collective-permute-start | bytes 2359304 | tf_op jit(solution)/shard_map/ppermute | solution.py:267
  77.2 10.9 %collective-permute-start.5 = (f32[2,3,128,128]{3,2,1,0:T(8,128)S(1)}, f32[2,3,128,128]{3,2,1,0:T(8,128)S(1)}, u32[]{:S(2)}, u32[]{:S(2)}) collective-permute-start(f32[2,3,128,128]{3,2,1,0:T(8,128)S(1)} %get-tuple-element.24), channel_id=1, source_target_pairs={{0,384},{32,160},{128,256},{160,32},{256,128},{288,416},{384,0},{4... | collective-permute-start | bytes 1179656 | tf_op jit(solution)/shard_map/ppermute | solution.py:267
  88.1 15.0 %collective-permute-start.6 = (f32[3,128,128]{2,1,0:T(8,128)S(1)}, f32[3,128,128]{2,1,0:T(8,128)S(1)}, u32[]{:S(2)}, u32[]{:S(2)}) collective-permute-start(f32[3,128,128]{2,1,0:T(8,128)S(1)} %get-tuple-element.27), channel_id=1, source_target_pairs={{0,64},{64,0},{1,65},{65,1},{2,66},{66,2},{3,67},{67,3},{4,68},{68... | collective-permute-start | bytes 589832 | tf_op jit(solution)/shard_map/ppermute | solution.py:258
  103.8 15.1 %collective-permute-start.8 = (f32[128,128]{1,0:T(8,128)}, f32[128,128]{1,0:T(8,128)}, u32[]{:S(2)}, u32[]{:S(2)}) collective-permute-start(f32[128,128]{1,0:T(8,128)} %get-tuple-element.29), channel_id=1, source_target_pairs={{0,1},{1,2},{2,3},{3,4},{4,5},{5,6},{6,7},{7,8},{8,9},{9,10},{10,1... | collective-permute-start | bytes 196616 | tf_op jit(solution)/shard_map/ppermute | solution.py:258
  105.7 14.6 %collective-permute-start.7 = (f32[128,128]{1,0:T(8,128)}, f32[128,128]{1,0:T(8,128)}, u32[]{:S(2)}, u32[]{:S(2)}) collective-permute-start(f32[128,128]{1,0:T(8,128)} %get-tuple-element.30), channel_id=1, source_target_pairs={{0,31},{1,0},{2,1},{3,2},{4,3},{5,4},{6,5},{7,6},{8,7},{9,8},{10,9... | collective-permute-start | bytes 196616 | tf_op jit(solution)/shard_map/ppermute | solution.py:258

commit v5 on v4

--- a/solution.py
+++ b/solution.py
@@ -117,7 +117,8 @@
 
 
 def proximal_kernel(
-    place_ref, slots_ref, near_ref, other_ref, right_ref, left_ref, omega_ref, out_ref
+    place_ref, slots_ref, near_ref, right_ref, left_ref, far_right_ref, far_left_ref,
+    other_ref, omega_ref, out_ref,
 ):
     j = place_ref[0]
     rows = lax.broadcasted_iota(jnp.int32, (BLK, BLK), 0)
@@ -126,9 +127,9 @@
         slot = slots_ref[0, e, j]
         total = near_ref[e] + other_ref[e]
         if e == 0:
-            total = total + left_ref[...].T
+            total = total + (left_ref[...] + far_left_ref[...]).T
         if e == 2:
-            total = total + right_ref[...].T
+            total = total + (right_ref[...] + far_right_ref[...]).T
         gradient = total * (0.5 / SAMPLES)
         omega = omega_ref[0, e, 0]
         if e == 1:
@@ -224,22 +225,17 @@
     )(slots, where, tile, omega, before, half, below, centre)
 
 
-def proximal(place, slots, near, other, right, left, omega):
+def proximal(place, slots, near, sums, omega):
+    block = pl.BlockSpec((BLK, BLK), lambda i, place, slots: (0, 0))
+    triple = pl.BlockSpec((3, BLK, BLK), lambda i, place, slots: (0, 0, 0))
+    own = pl.BlockSpec((1, 3, 1, BLK, BLK), lambda i, place, slots: (0, 0, place[0], 0, 0))
     return pl.pallas_call(
         proximal_kernel,
         name="proximal",
         grid_spec=pltpu.PrefetchScalarGridSpec(
             num_scalar_prefetch=2,
             grid=(1,),
-            in_specs=[
-                pl.BlockSpec((3, BLK, BLK), lambda i, place, slots: (0, 0, 0)),
-                pl.BlockSpec((3, BLK, BLK), lambda i, place, slots: (0, 0, 0)),
-                pl.BlockSpec((BLK, BLK), lambda i, place, slots: (0, 0)),
-                pl.BlockSpec((BLK, BLK), lambda i, place, slots: (0, 0)),
-                pl.BlockSpec(
-                    (1, 3, 1, BLK, BLK), lambda i, place, slots: (0, 0, place[0], 0, 0)
-                ),
-            ],
+            in_specs=[triple] + [block] * 4 + [triple, own],
             out_specs=pl.BlockSpec(
                 (1, 3, 1, BLK, BLK), lambda i, place, slots: (0, 0, 0, 0, 0)
             ),
@@ -249,7 +245,7 @@
         cost_estimate=pl.CostEstimate(
             flops=20 * 3 * BLK * BLK, bytes_accessed=1 << 19, transcendentals=0
         ),
-    )(place, slots, near, other, right, left, omega)
+    )(place, slots, near, *sums, omega)
 
 
 def shifted(value, axis, steps):
@@ -265,6 +261,16 @@
             partner = x ^ 1 if core == step else 3 - x
             pairs.append((2 * x + core, 2 * partner + core))
     return lax.ppermute(value, ("x", "core"), pairs)
+
+
+def across(value, steps):
+    count = lax.axis_size("col")
+    pairs = [
+        (y * count + t, (1 - y) * count + (t + steps) % count)
+        for y in range(2)
+        for t in range(count)
+    ]
+    return lax.ppermute(value, ("y_hi", "col"), pairs)
 
 
 def on_device(observations, omega, block_slots):
@@ -285,11 +291,16 @@
     first = x_exchange(out + got[2:], 0)
     second = x_exchange(keep[1] + got[1] + first[1], 1)
     kept = keep[0] + got[0] + first[0]
-    other = shifted(kept[1] + second[1], "y_hi", 1)
     near = kept[0] + second[0]
-    right = shifted(near[0] + other[0], "col", -1)
-    left = shifted(near[2] + other[2], "col", 1)
-    return proximal(place.reshape(1), block_slots, near, other, right, left, omega)
+    far = kept[1] + second[1]
+    sums = (
+        shifted(kept[0, 0] + second[0, 0], "col", -1),
+        shifted(kept[0, 2] + second[0, 2], "col", 1),
+        across(kept[1, 0] + second[1, 0], -1),
+        across(kept[1, 2] + second[1, 2], 1),
+        shifted(far, "y_hi", 1),
+    )
+    return proximal(place.reshape(1), block_slots, near, sums, omega)
 
 
 def solution(mesh):

time: 125 us -> 127 us (1.016); the launches traced: 123 us -> 126 us
  starting transfers between devices: 49.1 us -> 58.8 us
  waiting for transfers between devices: 52.8 us -> 45.5 us
    ppermute x0 -> x2, starting transfers between devices: none -> 14.4 us  [across(): return lax.ppermute(value, ('y_hi', 'col'), pairs)]
    ppermute x7, waiting for transfers between devices: 33.1 us -> 25.9 us  [shifted(): return lax.ppermute(value, axis, pairs)]
    ppermute x7, starting transfers between devices: 44 us -> 39.3 us  [shifted(): return lax.ppermute(value, axis, pairs)]
  transfers between devices with their start and end apart: 9 -> 11, of which waited for: 9 -> 8; matrix products, arithmetic and copies ran while one was open for 2% -> 2% of each run, Pallas kernels for 6% -> 6%
where the time goes in v5:
time: 127 us; the launch traced here: 126 us
  starting transfers between devices  58.8 us (46%)
  waiting for transfers between devices  45.5 us (36%)
  Pallas kernels  14.2 us (11%)
  local copies, waits for them, and re-layouts  5.42 us (4%)
  other arithmetic  1.8 us (1%)
    ppermute x7, starting transfers between devices, shifted(): return lax.ppermute(value, axis, pairs)  39.3 us
    ppermute x7, waiting for transfers between devices, shifted(): return lax.ppermute(value, axis, pairs)  25.9 us
    ppermute x2, waiting for transfers between devices, x_exchange(): return lax.ppermute(value, ('x', 'core'), pairs)  19.6 us
    ppermute x2, starting transfers between devices, across(): return lax.ppermute(value, ('y_hi', 'col'), pairs)  14.4 us
    pallas_call x3, Pallas kernels, partial(): pl.pallas_call(lambda *refs: partial_kernel(offset, first, *refs), name='...  7.44 us
    ppermute x2, starting transfers between devices, x_exchange(): return lax.ppermute(value, ('x', 'core'), pairs)  5.11 us
    pallas_call x1, Pallas kernels, forward_blocks(): pl.pallas_call(forward_kernel, name='forward_blocks', grid=(1,), out_shap...  4.41 us
    unnamed x9, local copies, waits for them, and re-layouts  3.12 us
  transfers between devices with their start and end apart: 11, of which 8 were waited for; matrix products, arithmetic and copies ran while one was open for 2% of the time, Pallas kernels for 6%

profile of v5, /device:TPU:6, one launch (start us, length us, event | category | flops | bytes accessed | tf_op | source)
XLA Modules:
  0.0 125.9 jit_solution(177666368717862350)
XLA Ops:
  0.0 0.0 copy-start.3
  0.0 3.6 %collective-permute-start.2 = (f32[256,1024]{1,0:T(8,128)}, f32[256,1024]{1,0:T(8,128)}, u32[]{:S(2)}, u32[]{:S(2)}) collective-permute-start(f32[256,1024]{1,0:T(8,128)} %refs_1_.1), channel_id=1, source_target_pairs={{0,1},{1,2},{2,3},{3,4},{4,5},{5,6},{6,7},{7,8},{8,9},{9,10},{10,1... | collective-permute-start | bytes 3145736 | tf_op jit(solution)/shard_map/ppermute | solution.py:254
  3.6 2.3 %fusion.7 = (f32[128,1024]{1,0:T(8,128)}, f32[128,1024]{1,0:T(8,128)}) fusion(f32[256,1024]{1,0:T(8,128)} %refs_1_.1), kind=kLoop, calls=%fused_computation.21 | loop fusion | bytes 2097152 | tf_op jit(solution)/shard_map/slice | solution.py:282
  5.9 12.4 %collective-permute-start.1 = (f32[128,1024]{1,0:T(8,128)}, f32[128,1024]{1,0:T(8,128)}, u32[]{:S(2)}, u32[]{:S(2)}) collective-permute-start(f32[128,1024]{1,0:T(8,128)} %get-tuple-element.25), channel_id=1, source_target_pairs={{0,31},{1,0},{2,1},{3,2},{4,3},{5,4},{6,5},{7,6},{8,7},{9,8},{10,9... | collective-permute-start | bytes 1572872 | tf_op jit(solution)/shard_map/ppermute | solution.py:254
  18.3 3.9 %collective-permute-start = (f32[128,1024]{1,0:T(8,128)}, f32[128,1024]{1,0:T(8,128)}, u32[]{:S(2)}, u32[]{:S(2)}) collective-permute-start(f32[128,1024]{1,0:T(8,128)} %get-tuple-element.26), channel_id=1, source_target_pairs={{0,31},{1,0},{2,1},{3,2},{4,3},{5,4},{6,5},{7,6},{8,7},{9,8},{10,9... | collective-permute-start | bytes 1572872 | tf_op jit(solution)/shard_map/ppermute | solution.py:254
  22.3 0.0 copy-done.3
  22.3 0.0 copy-start
  22.3 1.9 %copy-done = f32[1,3,16,128,128]{4,3,2,1,0:T(8,128)S(1)} copy-done((f32[1,3,16,128,128]{4,3,2,1,0:T(8,128)S(1)}, f32[1,3,16,128,128]{4,3,2,1,0:T(8,128)}, u32[]{:S(2)}) %copy-start) | copy-done | bytes 3145752
  24.2 0.0 copy-start.2
  24.2 1.2 copy-done.2
  25.4 0.0 copy-start.1
  25.4 2.3 %partial_residual.3 = (f32[8,256,128]{2,1,0:T(8,128)S(1)}, bf16[8,256,256]{2,1,0:T(8,128)(2,1)S(1)}) custom-call(s32[1,3,16]{2,1,0:T(4,128)S(1)} %copy.8.refs_0_.slots_ref, f32[256,1024]{1,0:T(8,128)S(1)} %copy-done.2, f32[1,3,16,128,128]{4,3,2,1,0:T(8,128)S(1)} %copy-done), custom_call_target="tpu_custom_call" | custom-call | flops 536870912 | bytes 5242880 | tf_op jit(solution)/shard_map/partial_residual/pallas_call | solution.py:175
  27.7 0.1 pad_add_fusion.where_ref
  27.8 10.7 %collective-permute-done.2.refs_1_ = f32[256,1024]{1,0:T(8,128)} collective-permute-done((f32[256,1024]{1,0:T(8,128)}, f32[256,1024]{1,0:T(8,128)}, u32[]{:S(2)}, u32[]{:S(2)}) %collective-permute-start.2) | collective-permute-done | bytes 1048608 | tf_op jit(solution)/shard_map/ppermute | solution.py:254
  38.5 0.0 copy-done.1
  38.5 2.9 %partial_residual.4 = (f32[8,256,128]{2,1,0:T(8,128)S(1)}, bf16[8,256,256]{2,1,0:T(8,128)(2,1)S(1)}) custom-call(s32[1,3,16]{2,1,0:T(4,128)S(1)} %copy.8.refs_0_.slots_ref, f32[256,1024]{1,0:T(8,128)} %collective-permute-done.2.refs_1_, f32[1,3,16,128,128]{4,3,2,1,0:T(8,128)S(1)} %copy-done.1, f32[8,256,128]{2,1,0:T(8,128)S(1)} %get-tuple-element.14.refs_3_), custom_call_target="tpu_custom_call" | custom-call | flops 536870912 | bytes 5242880 | tf_op jit(solution)/shard_map/partial_residual/pallas_call | solution.py:175
  41.4 0.8 collective-permute-done.1.refs_1_
  42.2 2.3 %partial_residual.5 = (f32[8,256,128]{2,1,0:T(8,128)S(1)}, bf16[8,256,128]{2,1,0:T(8,128)(2,1)S(1)}) custom-call(s32[1,3,16]{2,1,0:T(4,128)S(1)} %copy.8.refs_0_.slots_ref, f32[128,1024]{1,0:T(8,128)} %collective-permute-done.1.refs_1_, f32[1,3,16,128,128]{4,3,2,1,0:T(8,128)S(1)} %copy-done.1, f32[8,256,128]{2,1,0:T(8,128)S(1)} %get-tuple-element.15.refs_3_), custom_call_target="tpu_custom_call" | custom-call | flops 268435456 | bytes 5242880 | tf_op jit(solution)/shard_map/partial_residual/pallas_call | solution.py:175
  44.5 8.9 %collective-permute-done.x_ref = f32[128,1024]{1,0:T(8,128)} collective-permute-done((f32[128,1024]{1,0:T(8,128)}, f32[128,1024]{1,0:T(8,128)}, u32[]{:S(2)}, u32[]{:S(2)}) %collective-permute-start) | collective-permute-done | bytes 524320 | tf_op jit(solution)/shard_map/ppermute | solution.py:254
  53.3 4.4 %forward_blocks.1 = (f32[2,2,3,128,128]{4,3,2,1,0:T(8,128)S(1)}, f32[2,2,3,128,128]{4,3,2,1,0:T(8,128)S(1)}, f32[4,2,3,128,128]{4,3,2,1,0:T(8,128)S(1)}) custom-call(s32[1,3,16]{2,1,0:T(4,128)S(1)} %copy.8.refs_0_.slots_ref, s32[3]{0:T(128)S(1)} %pad_add_fusion.where_ref, f32[128,1024]{1,0:T(8,128)} %collective-permute-done.x_ref, ...), custom_call_target="tpu_custom_call" | custom-call | flops 1879048192 | bytes 8388608 | tf_op jit(solution)/shard_map/forward_blocks/pallas_call | solution.py:199
  57.7 1.9 %collective-permute-start.3 = (f32[4,2,3,128,128]{4,3,2,1,0:T(8,128)S(1)}, f32[4,2,3,128,128]{4,3,2,1,0:T(8,128)S(1)}, u32[]{:S(2)}, u32[]{:S(2)}) collective-permute-start(f32[4,2,3,128,128]{4,3,2,1,0:T(8,128)S(1)} %get-tuple-element.21), channel_id=1, source_target_pairs={{0,32},{32,0},{1,33},{33,1},{2,34},{34,2},{3,35},{35,3},{4,36},{36... | collective-permute-start | bytes 4718600 | tf_op jit(solution)/shard_map/ppermute | solution.py:254
  59.7 3.4 %collective-permute-done.3 = f32[4,2,3,128,128]{4,3,2,1,0:T(8,128)S(1)} collective-permute-done((f32[4,2,3,128,128]{4,3,2,1,0:T(8,128)S(1)}, f32[4,2,3,128,128]{4,3,2,1,0:T(8,128)S(1)}, u32[]{:S(2)}, u32[]{:S(2)}) %collective-permute-start.3) | collective-permute-done | bytes 1572896 | tf_op jit(solution)/shard_map/ppermute | solution.py:254
  63.0 0.1 slice_add_fusion
  63.1 2.7 %collective-permute-start.4 = (f32[2,2,3,128,128]{4,3,2,1,0:T(8,128)S(1)}, f32[2,2,3,128,128]{4,3,2,1,0:T(8,128)S(1)}, u32[]{:S(2)}, u32[]{:S(2)}) collective-permute-start(f32[2,2,3,128,128]{4,3,2,1,0:T(8,128)S(1)} %slice_add_fusion), channel_id=1, source_target_pairs={{0,128},{32,416},{128,0},{160,288},{256,384},{288,160},{384,256},{... | collective-permute-start | bytes 2359304 | tf_op jit(solution)/shard_map/ppermute | solution.py:263
  65.9 11.1 %collective-permute-done.4 = f32[2,2,3,128,128]{4,3,2,1,0:T(8,128)S(1)} collective-permute-done((f32[2,2,3,128,128]{4,3,2,1,0:T(8,128)S(1)}, f32[2,2,3,128,128]{4,3,2,1,0:T(8,128)S(1)}, u32[]{:S(2)}, u32[]{:S(2)}) %collective-permute-start.4) | collective-permute-done | bytes 786464 | tf_op jit(solution)/shard_map/ppermute | solution.py:263
  77.0 0.1 slice_add_fusion.3
  77.2 2.4 %collective-permute-start.5 = (f32[2,3,128,128]{3,2,1,0:T(8,128)S(1)}, f32[2,3,128,128]{3,2,1,0:T(8,128)S(1)}, u32[]{:S(2)}, u32[]{:S(2)}) collective-permute-start(f32[2,3,128,128]{3,2,1,0:T(8,128)S(1)} %get-tuple-element.24), channel_id=1, source_target_pairs={{0,384},{32,160},{128,256},{160,32},{256,128},{288,416},{384,0},{4... | collective-permute-start | bytes 1179656 | tf_op jit(solution)/shard_map/ppermute | solution.py:263
  79.6 8.5 %collective-permute-done.5 = f32[2,3,128,128]{3,2,1,0:T(8,128)S(1)} collective-permute-done((f32[2,3,128,128]{3,2,1,0:T(8,128)S(1)}, f32[2,3,128,128]{3,2,1,0:T(8,128)S(1)}, u32[]{:S(2)}, u32[]{:S(2)}) %collective-permute-start.5) | collective-permute-done | bytes 393248 | tf_op jit(solution)/shard_map/ppermute | solution.py:263
  88.1 0.7 fusion.1
  88.8 7.7 %collective-permute-start.10 = (f32[3,128,128]{2,1,0:T(8,128)}, f32[3,128,128]{2,1,0:T(8,128)S(1)}, u32[]{:S(2)}, u32[]{:S(2)}) collective-permute-start(f32[3,128,128]{2,1,0:T(8,128)} %get-tuple-element.27), channel_id=1, source_target_pairs={{0,64},{64,0},{1,65},{65,1},{2,66},{66,2},{3,67},{67,3},{4,68},{68... | collective-permute-start | bytes 589832 | tf_op jit(solution)/shard_map/ppermute | solution.py:254
  96.5 0.7 fusion.3
  97.3 1.9 %collective-permute-start.9 = (f32[128,128]{1,0:T(8,128)}, f32[128,128]{1,0:T(8,128)}, u32[]{:S(2)}, u32[]{:S(2)}) collective-permute-start(f32[128,128]{1,0:T(8,128)} %get-tuple-element.29), channel_id=1, source_target_pairs={{0,65},{1,66},{2,67},{3,68},{4,69},{5,70},{6,71},{7,72},{8,73},{9,... | collective-permute-start | bytes 196616 | tf_op jit(solution)/shard_map/ppermute | solution.py:273
  99.2 12.5 %collective-permute-start.8 = (f32[128,128]{1,0:T(8,128)}, f32[128,128]{1,0:T(8,128)}, u32[]{:S(2)}, u32[]{:S(2)}) collective-permute-start(f32[128,128]{1,0:T(8,128)} %get-tuple-element.30), channel_id=1, source_target_pairs={{0,95},{1,64},{2,65},{3,66},{4,67},{5,68},{6,69},{7,70},{8,71},{9,... | collective-permute-start | bytes 196616 | tf_op jit(solution)/shard_map/ppermute | solution.py:273
  111.6 1.9 %collective-permute-start.7 = (f32[128,128]{1,0:T(8,128)}, f32[128,128]{1,0:T(8,128)}, u32[]{:S(2)}, u32[]{:S(2)}) collective-permute-start(f32[128,128]{1,0:T(8,128)} %get-tuple-element.31), channel_id=1, source_target_pairs={{0,1},{1,2},{2,3},{3,4},{4,5},{5,6},{6,7},{7,8},{8,9},{9,10},{10,1... | collective-permute-start | bytes 196616 | tf_op jit(solution)/shard_map/ppermute | solution.py:254
  113.6 7.8 %collective-permute-start.6 = (f32[128,128]{1,0:T(8,128)}, f32[128,128]{1,0:T(8,128)}, u32[]{:S(2)}, u32[]{:S(2)}) collective-permute-start(f32[128,128]{1,0:T(8,128)} %get-tuple-element.32), channel_id=1, source_target_pairs={{0,31},{1,0},{2,1},{3,2},{4,3},{5,4},{6,5},{7,6},{8,7},{9,8},{10,9... | collective-permute-start | bytes 196616 | tf_op jit(solution)/shard_map/ppermute | solution.py:254
  121.4 0.0 collective-permute-done.9.far_left_ref
  121.4 0.0 collective-permute-done.8.far_right_ref
  121.4 0.6 collective-permute-done.7.left_ref
  122.1 1.5 %collective-permute-done.6.right_ref = f32[128,128]{1,0:T(8,128)} collective-permute-done((f32[128,128]{1,0:T(8,128)}, f32[128,128]{1,0:T(8,128)}, u32[]{:S(2)}, u32[]{:S(2)}) %collective-permute-start.6) | collective-permute-done | bytes 65568 | tf_op jit(solution)/shard_map/ppermute | solution.py:254
  123.6 0.0 collective-permute-done.10.other_ref
  123.6 2.3 %proximal.1 = f32[1,3,1,128,128]{4,3,2,1,0:T(8,128)} custom-call(s32[1]{0:T(128)} %bitcast.place_ref, s32[1,3,16]{2,1,0:T(4,128)S(1)} %copy.8.refs_0_.slots_ref, f32[3,128,128]{2,1,0:T(8,128)S(1)} %get-tuple-element.28.near_ref, f32[128,128]{1,0:T(8,128)} %collective-permute-done.6.right_ref, f32[128,128]{1,0:T(8,128)} %collective-permute-done.7.left_ref, ...), custom_call_target="tpu_custom_call" | custom-call | flops 983040 | bytes 524288 | tf_op jit(solution)/shard_map/proximal/pallas_call | solution.py:232
  (1 shorter events, 0.0 us)
Async XLA Ops:
  0.0 22.3 %copy-start.3 = (s32[1,3,16]{2,0,1:T(1,128)S(1)}, s32[1,3,16]{2,0,1:T(1,128)}, u32[]{:S(2)}) copy-start(s32[1,3,16]{2,0,1:T(1,128)} %param.5) | copy-start | bytes 580
  0.0 38.5 %collective-permute-start.2 = (f32[256,1024]{1,0:T(8,128)}, f32[256,1024]{1,0:T(8,128)}, u32[]{:S(2)}, u32[]{:S(2)}) collective-permute-start(f32[256,1024]{1,0:T(8,128)} %refs_1_.1), channel_id=1, source_target_pairs={{0,1},{1,2},{2,3},{3,4},{4,5},{5,6},{6,7},{7,8},{8,9},{9,10},{10,1... | collective-permute-start | bytes 3145736 | tf_op jit(solution)/shard_map/ppermute | solution.py:254
  5.9 36.2 %collective-permute-start.1 = (f32[128,1024]{1,0:T(8,128)}, f32[128,1024]{1,0:T(8,128)}, u32[]{:S(2)}, u32[]{:S(2)}) collective-permute-start(f32[128,1024]{1,0:T(8,128)} %get-tuple-element.25), channel_id=1, source_target_pairs={{0,31},{1,0},{2,1},{3,2},{4,3},{5,4},{6,5},{7,6},{8,7},{9,8},{10,9... | collective-permute-start | bytes 1572872 | tf_op jit(solution)/shard_map/ppermute | solution.py:254
  18.3 35.0 %collective-permute-start = (f32[128,1024]{1,0:T(8,128)}, f32[128,1024]{1,0:T(8,128)}, u32[]{:S(2)}, u32[]{:S(2)}) collective-permute-start(f32[128,1024]{1,0:T(8,128)} %get-tuple-element.26), channel_id=1, source_target_pairs={{0,31},{1,0},{2,1},{3,2},{4,3},{5,4},{6,5},{7,6},{8,7},{9,8},{10,9... | collective-permute-start | bytes 1572872 | tf_op jit(solution)/shard_map/ppermute | solution.py:254
  22.3 1.9 %copy-start = (f32[1,3,16,128,128]{4,3,2,1,0:T(8,128)S(1)}, f32[1,3,16,128,128]{4,3,2,1,0:T(8,128)}, u32[]{:S(2)}) copy-start(f32[1,3,16,128,128]{4,3,2,1,0:T(8,128)} %omega_ref.3) | copy-start | bytes 9437188
  24.2 1.2 copy-start.2
  25.4 13.0 %copy-start.1 = (f32[1,3,16,128,128]{4,3,2,1,0:T(8,128)S(1)}, f32[1,3,16,128,128]{4,3,2,1,0:T(8,128)}, u32[]{:S(2)}) copy-start(f32[1,3,16,128,128]{4,3,2,1,0:T(8,128)} %omega_ref.3) | copy-start | bytes 9437188
  57.7 5.3 %collective-permute-start.3 = (f32[4,2,3,128,128]{4,3,2,1,0:T(8,128)S(1)}, f32[4,2,3,128,128]{4,3,2,1,0:T(8,128)S(1)}, u32[]{:S(2)}, u32[]{:S(2)}) collective-permute-start(f32[4,2,3,128,128]{4,3,2,1,0:T(8,128)S(1)} %get-tuple-element.21), channel_id=1, source_target_pairs={{0,32},{32,0},{1,33},{33,1},{2,34},{34,2},{3,35},{35,3},{4,36},{36... | collective-permute-start | bytes 4718600 | tf_op jit(solution)/shard_map/ppermute | solution.py:254
  63.1 13.9 %collective-permute-start.4 = (f32[2,2,3,128,128]{4,3,2,1,0:T(8,128)S(1)}, f32[2,2,3,128,128]{4,3,2,1,0:T(8,128)S(1)}, u32[]{:S(2)}, u32[]{:S(2)}) collective-permute-start(f32[2,2,3,128,128]{4,3,2,1,0:T(8,128)S(1)} %slice_add_fusion), channel_id=1, source_target_pairs={{0,128},{32,416},{128,0},{160,288},{256,384},{288,160},{384,256},{... | collective-permute-start | bytes 2359304 | tf_op jit(solution)/shard_map/ppermute | solution.py:263
  77.2 10.9 %collective-permute-start.5 = (f32[2,3,128,128]{3,2,1,0:T(8,128)S(1)}, f32[2,3,128,128]{3,2,1,0:T(8,128)S(1)}, u32[]{:S(2)}, u32[]{:S(2)}) collective-permute-start(f32[2,3,128,128]{3,2,1,0:T(8,128)S(1)} %get-tuple-element.24), channel_id=1, source_target_pairs={{0,384},{32,160},{128,256},{160,32},{256,128},{288,416},{384,0},{4... | collective-permute-start | bytes 1179656 | tf_op jit(solution)/shard_map/ppermute | solution.py:263
  88.8 34.8 %collective-permute-start.10 = (f32[3,128,128]{2,1,0:T(8,128)}, f32[3,128,128]{2,1,0:T(8,128)S(1)}, u32[]{:S(2)}, u32[]{:S(2)}) collective-permute-start(f32[3,128,128]{2,1,0:T(8,128)} %get-tuple-element.27), channel_id=1, source_target_pairs={{0,64},{64,0},{1,65},{65,1},{2,66},{66,2},{3,67},{67,3},{4,68},{68... | collective-permute-start | bytes 589832 | tf_op jit(solution)/shard_map/ppermute | solution.py:254
  97.3 24.2 %collective-permute-start.9 = (f32[128,128]{1,0:T(8,128)}, f32[128,128]{1,0:T(8,128)}, u32[]{:S(2)}, u32[]{:S(2)}) collective-permute-start(f32[128,128]{1,0:T(8,128)} %get-tuple-element.29), channel_id=1, source_target_pairs={{0,65},{1,66},{2,67},{3,68},{4,69},{5,70},{6,71},{7,72},{8,73},{9,... | collective-permute-start | bytes 196616 | tf_op jit(solution)/shard_map/ppermute | solution.py:273
  99.2 22.3 %collective-permute-start.8 = (f32[128,128]{1,0:T(8,128)}, f32[128,128]{1,0:T(8,128)}, u32[]{:S(2)}, u32[]{:S(2)}) collective-permute-start(f32[128,128]{1,0:T(8,128)} %get-tuple-element.30), channel_id=1, source_target_pairs={{0,95},{1,64},{2,65},{3,66},{4,67},{5,68},{6,69},{7,70},{8,71},{9,... | collective-permute-start | bytes 196616 | tf_op jit(solution)/shard_map/ppermute | solution.py:273
  111.6 10.4 %collective-permute-start.7 = (f32[128,128]{1,0:T(8,128)}, f32[128,128]{1,0:T(8,128)}, u32[]{:S(2)}, u32[]{:S(2)}) collective-permute-start(f32[128,128]{1,0:T(8,128)} %get-tuple-element.31), channel_id=1, source_target_pairs={{0,1},{1,2},{2,3},{3,4},{4,5},{5,6},{6,7},{7,8},{8,9},{9,10},{10,1... | collective-permute-start | bytes 196616 | tf_op jit(solution)/shard_map/ppermute | solution.py:254
  113.6 10.0 %collective-permute-start.6 = (f32[128,128]{1,0:T(8,128)}, f32[128,128]{1,0:T(8,128)}, u32[]{:S(2)}, u32[]{:S(2)}) collective-permute-start(f32[128,128]{1,0:T(8,128)} %get-tuple-element.32), channel_id=1, source_target_pairs={{0,31},{1,0},{2,1},{3,2},{4,3},{5,4},{6,5},{7,6},{8,7},{9,8},{10,9... | collective-permute-start | bytes 196616 | tf_op jit(solution)/shard_map/ppermute | solution.py:254

commit v6 on v2

--- a/solution.py
+++ b/solution.py
@@ -15,7 +15,7 @@
 penalty = 0.1
 f32 = jnp.float32
 bf16 = jnp.bfloat16
-VMEM_LIMIT = 24 * 1024 * 1024
+VMEM_LIMIT = 16 * 1024 * 1024
 
 
 def split(value):
@@ -24,18 +24,21 @@
     return high, low
 
 
-def split_tile(x_ref, natural_ref, turned_ref):
+def split_tile(x_ref, natural_ref, turned_ref, start=0):
+    rows = x_ref.shape[0]
     for a in range(NB):
         block = x_ref[:, a * BLK : (a + 1) * BLK]
         high, low = split(block)
         natural_ref[a, :, :BLK] = high
         natural_ref[a, :, BLK:] = low
         high, low = split(block.T)
-        turned_ref[a, :BLK, :] = high
-        turned_ref[a, BLK:, :] = low
-
-
-def add_products(slots_ref, omega_ref, natural_ref, residual_ref, offset):
+        turned_ref[a, :BLK, start : start + rows] = high
+        turned_ref[a, BLK:, start : start + rows] = low
+
+
+def add_products(slots_ref, omega_ref, natural_ref, residual_ref, offset, start=0):
+    rows = natural_ref.shape[1]
+
     def body(j, carry):
         slot = slots_ref[0, offset, j]
         active = slot >= 0
@@ -47,7 +50,7 @@
         half = jnp.concatenate([high, low], axis=1)
         weights = jnp.concatenate([half, half], axis=0)
         out = jnp.dot(natural_ref[a], weights, preferred_element_type=f32)
-        residual_ref[b] += out[:, :BLK] + out[:, BLK:]
+        residual_ref[b, start : start + rows] += out[:, :BLK] + out[:, BLK:]
         return carry
 
     lax.fori_loop(0, KMAX, body, 0, unroll=4)
@@ -100,12 +103,14 @@
 
 
 def far_kernel(
-    slots_ref, where_ref, x_ref, omega_ref, before_ref, below_ref, centre_ref,
+    slots_ref, where_ref, x_ref, omega_ref, before_ref, half_ref, below_ref, centre_ref,
     keep_ref, pass_ref, send_ref, above_ref, pieces_ref, residual_ref, natural_ref,
 ):
     residual_ref[...] = before_ref[...]
-    split_tile(x_ref, natural_ref, above_ref)
-    add_products(slots_ref, omega_ref, natural_ref, residual_ref, 2)
+    done = half_ref.shape[2]
+    above_ref[:, :, :done] = half_ref[...]
+    split_tile(x_ref, natural_ref, above_ref, done)
+    add_products(slots_ref, omega_ref, natural_ref, residual_ref, 2, done)
     for b in range(NB):
         high, low = split(residual_ref[b])
         pieces_ref[b, :, :BLK] = high
@@ -127,18 +132,19 @@
 
 
 def proximal_kernel(
-    place_ref, slots_ref, total_ref, left_ref, right_ref, omega_ref, out_ref
+    where_ref, slots_ref, near_ref, other_ref, late_ref, early_ref, omega_ref, out_ref
 ):
-    j = place_ref[0]
+    j = where_ref[3]
+    odd_tile = where_ref[4] == 1
     rows = lax.broadcasted_iota(jnp.int32, (BLK, BLK), 0)
     columns = lax.broadcasted_iota(jnp.int32, (BLK, BLK), 1)
     for e in range(3):
         slot = slots_ref[0, e, j]
-        total = total_ref[e]
+        total = near_ref[e] + other_ref[e]
         if e == 0:
-            total = total + left_ref[...].T
+            total = total + jnp.where(odd_tile, early_ref[...], late_ref[...]).T
         if e == 2:
-            total = total + right_ref[...].T
+            total = total + jnp.where(odd_tile, late_ref[...], early_ref[...]).T
         gradient = total * (0.5 / SAMPLES)
         omega = omega_ref[0, e, 0]
         if e == 1:
@@ -174,7 +180,9 @@
 
 def partial(offset, slots, tile, omega, before=None):
     first = before is None
-    in_specs = [SMEM, full_spec((ROWS, TILE)), omega_spec(offset)]
+    rows = tile.shape[0]
+    turned = (NB, 2 * BLK, rows)
+    in_specs = [SMEM, full_spec((rows, TILE)), omega_spec(offset)]
     inputs = [slots, tile, omega]
     if not first:
         in_specs.append(full_spec((NB, ROWS, BLK)))
@@ -185,14 +193,14 @@
         grid=(1,),
         out_shape=(
             jax.ShapeDtypeStruct((NB, ROWS, BLK), f32),
-            jax.ShapeDtypeStruct(TURNED, bf16),
+            jax.ShapeDtypeStruct(turned, bf16),
         ),
         in_specs=in_specs,
-        out_specs=(full_spec((NB, ROWS, BLK)), full_spec(TURNED)),
-        scratch_shapes=[pltpu.VMEM(NATURAL, bf16)],
-        compiler_params=params(),
-        cost_estimate=pl.CostEstimate(
-            flops=2 * KMAX * ROWS * 256 * 256, bytes_accessed=5 << 20, transcendentals=0
+        out_specs=(full_spec((NB, ROWS, BLK)), full_spec(turned)),
+        scratch_shapes=[pltpu.VMEM((NB, rows, 2 * BLK), bf16)],
+        compiler_params=params(),
+        cost_estimate=pl.CostEstimate(
+            flops=2 * KMAX * rows * 256 * 256, bytes_accessed=5 << 20, transcendentals=0
         ),
     )(*inputs)
 
@@ -203,7 +211,8 @@
 GROUP_SPECS = tuple(full_spec(shape) for shape in (HALF, HALF, WAY))
 
 
-def far_blocks(slots, where, tile, omega, before, below, centre):
+def far_blocks(slots, where, tile, omega, before, half, below, centre):
+    rows = tile.shape[0]
     return pl.pallas_call(
         far_kernel,
         name="far_blocks",
@@ -213,19 +222,23 @@
         in_specs=[
             SMEM,
             SMEM,
-            full_spec((ROWS, TILE)),
+            full_spec((rows, TILE)),
             omega_spec(2),
             full_spec((NB, ROWS, BLK)),
+            full_spec((NB, 2 * BLK, ROWS - rows)),
             full_spec(TURNED),
             full_spec(TURNED),
         ],
         out_specs=GROUP_SPECS + (full_spec(TURNED), full_spec(NATURAL)),
-        scratch_shapes=[pltpu.VMEM((NB, ROWS, BLK), f32), pltpu.VMEM(NATURAL, bf16)],
+        scratch_shapes=[
+            pltpu.VMEM((NB, ROWS, BLK), f32),
+            pltpu.VMEM((NB, rows, 2 * BLK), bf16),
+        ],
         compiler_params=params(),
         cost_estimate=pl.CostEstimate(
             flops=5 * KMAX * ROWS * 256 * 256, bytes_accessed=8 << 20, transcendentals=0
         ),
-    )(slots, where, tile, omega, before, below, centre)
+    )(slots, where, tile, omega, before, half, below, centre)
 
 
 def near_blocks(slots, where, below, centre, above, pieces):
@@ -245,23 +258,43 @@
     )(slots, where, below, centre, above, pieces)
 
 
-def proximal(place, slots, total, left, right, omega):
+def edge_kernel(where_ref, near_ref, other_ref, late_ref, early_ref):
+    odd_tile = where_ref[4] == 1
+    downward = near_ref[0] + other_ref[0]
+    upward = near_ref[2] + other_ref[2]
+    late_ref[...] = jnp.where(odd_tile, upward, downward)
+    early_ref[...] = jnp.where(odd_tile, downward, upward)
+
+
+def edge_values(where, near, other):
+    block = jax.ShapeDtypeStruct((BLK, BLK), f32)
+    return pl.pallas_call(
+        edge_kernel,
+        name="edge_values",
+        grid=(1,),
+        out_shape=(block, block),
+        in_specs=[SMEM] + [full_spec((3, BLK, BLK))] * 2,
+        out_specs=(full_spec((BLK, BLK)),) * 2,
+        compiler_params=params(),
+        cost_estimate=pl.CostEstimate(
+            flops=4 * BLK * BLK, bytes_accessed=6 * 4 * BLK * BLK, transcendentals=0
+        ),
+    )(where, near, other)
+
+
+def proximal(where, slots, near, other, late, early, omega):
+    block = pl.BlockSpec((BLK, BLK), lambda i, where, slots: (0, 0))
+    triple = pl.BlockSpec((3, BLK, BLK), lambda i, where, slots: (0, 0, 0))
+    own = pl.BlockSpec((1, 3, 1, BLK, BLK), lambda i, where, slots: (0, 0, where[3], 0, 0))
     return pl.pallas_call(
         proximal_kernel,
         name="proximal",
         grid_spec=pltpu.PrefetchScalarGridSpec(
             num_scalar_prefetch=2,
             grid=(1,),
-            in_specs=[
-                pl.BlockSpec((3, BLK, BLK), lambda i, place, slots: (0, 0, 0)),
-                pl.BlockSpec((BLK, BLK), lambda i, place, slots: (0, 0)),
-                pl.BlockSpec((BLK, BLK), lambda i, place, slots: (0, 0)),
-                pl.BlockSpec(
-                    (1, 3, 1, BLK, BLK), lambda i, place, slots: (0, 0, place[0], 0, 0)
-                ),
-            ],
+            in_specs=[triple, triple, block, block, own],
             out_specs=pl.BlockSpec(
-                (1, 3, 1, BLK, BLK), lambda i, place, slots: (0, 0, 0, 0, 0)
+                (1, 3, 1, BLK, BLK), lambda i, where, slots: (0, 0, 0, 0, 0)
             ),
         ),
         out_shape=jax.ShapeDtypeStruct((1, 3, 1, BLK, BLK), f32),
@@ -269,7 +302,7 @@
         cost_estimate=pl.CostEstimate(
             flops=20 * 3 * BLK * BLK, bytes_accessed=1 << 19, transcendentals=0
         ),
-    )(place, slots, total, left, right, omega)
+    )(where, slots, near, other, late, early, omega)
 
 
 def shifted(value, axis, steps):
@@ -287,16 +320,27 @@
     return lax.ppermute(value, ("x", "core"), pairs)
 
 
+def edge_exchange(value, offset):
+    count = lax.axis_size("col")
+    pairs = []
+    for t in range(offset, count + offset, 2):
+        pairs += [(t % count, (t + 1) % count), ((t + 1) % count, t % count)]
+    return lax.ppermute(value, "col", pairs)
+
+
 def on_device(observations, omega, block_slots):
     x, y_hi, core = (lax.axis_index(n).astype(jnp.int32) for n in ("x", "y_hi", "core"))
-    where = jnp.stack([x, y_hi, core])
-    place = 4 * x + 2 * y_hi + core
+    odd_tile = lax.axis_index("col").astype(jnp.int32) & 1
+    where = jnp.stack([x, y_hi, core, 4 * x + 2 * y_hi + core, odd_tile])
     from_below = shifted(observations, "col", 1)
-    from_above = shifted(observations, "col", -1)
+    cut = ROWS // 2
+    above_early = shifted(observations[:cut], "col", -1)
+    above_late = shifted(observations[cut:], "col", -1)
     residual, centre = partial(1, block_slots, observations, omega)
     residual, below = partial(0, block_slots, from_below, omega, residual)
+    residual, half = partial(2, block_slots, above_early, omega, residual)
     far_keep, far_pass, far_send, above, pieces = far_blocks(
-        block_slots, where, from_above, omega, residual, below, centre
+        block_slots, where, above_late, omega, residual, half, below, centre
     )
     far_got = shifted(far_send, "core", 1)
     near_keep, near_pass, near_send = near_blocks(
@@ -310,10 +354,10 @@
     other = shifted(far_sum, "y_hi", 1)
     near_second = x_exchange(near_keep[1] + near_got[1] + near_first[1], 1)
     near_sum = near_keep[0] + near_got[0] + near_first[0] + near_second
-    total = near_sum + other
-    left = shifted(total[2], "col", 1)
-    right = shifted(total[0], "col", -1)
-    return proximal(place.reshape(1), block_slots, total, left, right, omega)
+    late_out, early_out = edge_values(where, near_sum, other)
+    late = edge_exchange(late_out, 1)
+    early = edge_exchange(early_out, 0)
+    return proximal(where, block_slots, near_sum, other, late, early, omega)
 
 
 def solution(mesh):

time: 122 us -> 116 us (0.951)
  waiting for transfers between devices: 48.4 us -> 38.8 us
  starting transfers between devices: 55.3 us -> 58.4 us
    ppermute x0 -> x2, starting transfers between devices: none -> 15.6 us  [edge_exchange(): return lax.ppermute(value, 'col', pairs)]
    ppermute x7 -> x6, waiting for transfers between devices: 41.2 us -> 27.4 us  [shifted(): return lax.ppermute(value, axis, pairs)]
    ppermute x7 -> x6, starting transfers between devices: 44.1 us -> 31.7 us  [shifted(): return lax.ppermute(value, axis, pairs)]
    ppermute x0 -> x2, waiting for transfers between devices: none -> 4.23 us  [edge_exchange(): return lax.ppermute(value, 'col', pairs)]
    slice x0 -> x1, local copies, waits for them, and re-layouts: none -> 1.27 us  [on_device(): above_early = shifted(observations[:cut], 'col', -1)]
    pallas_call x2 -> x3, Pallas kernels: 5.17 us -> 6.3 us  [partial(): pl.pallas_call(lambda *refs: partial_kernel(offset, first, *refs), name='...]
  transfers between devices with their start and end apart: 11 -> 12, of which waited for: 8 -> 9; matrix products, arithmetic and copies ran while one was open for 1% -> 2% of each run, Pallas kernels for 6% -> 7%
where the time goes in v6:
time: 116 us
  starting transfers between devices  58.4 us (50%)
  waiting for transfers between devices  38.8 us (33%)
  Pallas kernels  13 us (11%)
  local copies, waits for them, and re-layouts  5.16 us (4%)
    ppermute x6, starting transfers between devices, shifted(): return lax.ppermute(value, axis, pairs)  31.7 us
    ppermute x6, waiting for transfers between devices, shifted(): return lax.ppermute(value, axis, pairs)  27.4 us
    ppermute x2, starting transfers between devices, edge_exchange(): return lax.ppermute(value, 'col', pairs)  15.6 us
    ppermute x4, starting transfers between devices, x_exchange(): return lax.ppermute(value, ('x', 'core'), pairs)  11.1 us
    ppermute x4, waiting for transfers between devices, x_exchange(): return lax.ppermute(value, ('x', 'core'), pairs)  7.18 us
    pallas_call x3, Pallas kernels, partial(): pl.pallas_call(lambda *refs: partial_kernel(offset, first, *refs), name='...  6.3 us
    ppermute x2, waiting for transfers between devices, edge_exchange(): return lax.ppermute(value, 'col', pairs)  4.23 us
    unnamed x7, local copies, waits for them, and re-layouts  3.8 us
  transfers between devices with their start and end apart: 12, of which 9 were waited for; matrix products, arithmetic and copies ran while one was open for 2% of the time, Pallas kernels for 7%

profile of v6, /device:TPU:6, one launch (start us, length us, event | category | flops | bytes accessed | tf_op | source)
XLA Modules:
  0.0 115.8 jit_solution(358768699105987925)
XLA Ops:
  0.0 3.5 %collective-permute-start = (f32[256,1024]{1,0:T(8,128)}, f32[256,1024]{1,0:T(8,128)S(1)}, u32[]{:S(2)}, u32[]{:S(2)}) collective-permute-start(f32[256,1024]{1,0:T(8,128)} %refs_1_.1), channel_id=1, source_target_pairs={{0,1},{1,2},{2,3},{3,4},{4,5},{5,6},{6,7},{7,8},{8,9},{9,10},{10,1... | collective-permute-start | bytes 3145736 | tf_op jit(solution)/shard_map/ppermute | solution.py:311
  3.5 1.3 %fusion.6 = (f32[128,1024]{1,0:T(8,128)S(1)}, f32[128,1024]{1,0:T(8,128)S(1)}) fusion(f32[256,1024]{1,0:T(8,128)} %refs_1_.1), kind=kLoop, calls=%fused_computation.16 | loop fusion | bytes 2097152 | tf_op jit(solution)/shard_map/slice | solution.py:337
  4.8 12.4 %collective-permute-start.2 = (f32[128,1024]{1,0:T(8,128)S(1)}, f32[128,1024]{1,0:T(8,128)S(1)}, u32[]{:S(2)}, u32[]{:S(2)}) collective-permute-start(f32[128,1024]{1,0:T(8,128)S(1)} %get-tuple-element.37), channel_id=1, source_target_pairs={{0,31},{1,0},{2,1},{3,2},{4,3},{5,4},{6,5},{7,6},{8,7},{9,8},{10,9... | collective-permute-start | bytes 1572872 | tf_op jit(solution)/shard_map/ppermute | solution.py:311
  17.2 3.9 %collective-permute-start.1 = (f32[128,1024]{1,0:T(8,128)S(1)}, f32[128,1024]{1,0:T(8,128)S(1)}, u32[]{:S(2)}, u32[]{:S(2)}) collective-permute-start(f32[128,1024]{1,0:T(8,128)S(1)} %get-tuple-element.38), channel_id=1, source_target_pairs={{0,31},{1,0},{2,1},{3,2},{4,3},{5,4},{6,5},{7,6},{8,7},{9,8},{10,9... | collective-permute-start | bytes 1572872 | tf_op jit(solution)/shard_map/ppermute | solution.py:311
  21.1 0.7 copy.9.refs_0_.slots_ref
  21.8 0.1 stack.23.where_ref
  21.9 0.0 copy-start
  21.9 1.9 %copy-done = f32[1,3,16,128,128]{4,3,2,1,0:T(8,128)S(1)} copy-done((f32[1,3,16,128,128]{4,3,2,1,0:T(8,128)S(1)}, f32[1,3,16,128,128]{4,3,2,1,0:T(8,128)}, u32[]{:S(2)}) %copy-start) | copy-done | bytes 3145752
  23.8 0.0 copy-start.2
  23.8 1.2 %copy-done.2 = f32[256,1024]{1,0:T(8,128)S(1)} copy-done((f32[256,1024]{1,0:T(8,128)S(1)}, f32[256,1024]{1,0:T(8,128)}, u32[]{:S(2)}) %copy-start.2) | copy-done | bytes 1048600
  25.0 0.0 copy-start.1
  25.0 2.3 %partial_residual.3 = (f32[8,256,128]{2,1,0:T(8,128)S(1)}, bf16[8,256,256]{2,1,0:T(8,128)(2,1)S(1)}) custom-call(s32[1,3,16]{2,1,0:T(4,128)S(1)} %copy.9.refs_0_.slots_ref, f32[256,1024]{1,0:T(8,128)S(1)} %copy-done.2, f32[1,3,16,128,128]{4,3,2,1,0:T(8,128)S(1)} %copy-done), custom_call_target="tpu_custom_call" | custom-call | flops 536870912 | bytes 5242880 | tf_op jit(solution)/shard_map/partial_residual/pallas_call | solution.py:190
  27.3 10.9 %collective-permute-done.refs_1_ = f32[256,1024]{1,0:T(8,128)S(1)} collective-permute-done((f32[256,1024]{1,0:T(8,128)}, f32[256,1024]{1,0:T(8,128)S(1)}, u32[]{:S(2)}, u32[]{:S(2)}) %collective-permute-start) | collective-permute-done | bytes 1048608 | tf_op jit(solution)/shard_map/ppermute | solution.py:311
  38.2 0.0 copy-done.1
  38.2 2.2 %partial_residual.4 = (f32[8,256,128]{2,1,0:T(8,128)S(1)}, bf16[8,256,256]{2,1,0:T(8,128)(2,1)S(1)}) custom-call(s32[1,3,16]{2,1,0:T(4,128)S(1)} %copy.9.refs_0_.slots_ref, f32[256,1024]{1,0:T(8,128)S(1)} %collective-permute-done.refs_1_, f32[1,3,16,128,128]{4,3,2,1,0:T(8,128)S(1)} %copy-done.1, f32[8,256,128]{2,1,0:T(8,128)S(1)} %get-tuple-element.21.refs_3_), custom_call_target="tpu_custom_call" | custom-call | flops 536870912 | bytes 5242880 | tf_op jit(solution)/shard_map/partial_residual/pallas_call | solution.py:190
  40.5 1.5 %collective-permute-done.2.refs_1_ = f32[128,1024]{1,0:T(8,128)S(1)} collective-permute-done((f32[128,1024]{1,0:T(8,128)S(1)}, f32[128,1024]{1,0:T(8,128)S(1)}, u32[]{:S(2)}, u32[]{:S(2)}) %collective-permute-start.2) | collective-permute-done | bytes 524320 | tf_op jit(solution)/shard_map/ppermute | solution.py:311
  41.9 1.8 %partial_residual.5 = (f32[8,256,128]{2,1,0:T(8,128)S(1)}, bf16[8,256,128]{2,1,0:T(8,128)(2,1)S(1)}) custom-call(s32[1,3,16]{2,1,0:T(4,128)S(1)} %copy.9.refs_0_.slots_ref, f32[128,1024]{1,0:T(8,128)S(1)} %collective-permute-done.2.refs_1_, f32[1,3,16,128,128]{4,3,2,1,0:T(8,128)S(1)} %copy-done.1, f32[8,256,128]{2,1,0:T(8,128)S(1)} %get-tuple-element.24.refs_3_), custom_call_target="tpu_custom_call" | custom-call | flops 268435456 | bytes 5242880 | tf_op jit(solution)/shard_map/partial_residual/pallas_call | solution.py:190
  43.7 9.3 %collective-permute-done.1.x_ref = f32[128,1024]{1,0:T(8,128)S(1)} collective-permute-done((f32[128,1024]{1,0:T(8,128)S(1)}, f32[128,1024]{1,0:T(8,128)S(1)}, u32[]{:S(2)}, u32[]{:S(2)}) %collective-permute-start.1) | collective-permute-done | bytes 524320 | tf_op jit(solution)/shard_map/ppermute | solution.py:311
  53.1 3.1 %far_blocks.1 = (f32[2,3,128,128]{3,2,1,0:T(8,128)S(1)}, f32[2,3,128,128]{3,2,1,0:T(8,128)S(1)}, f32[4,3,128,128]{3,2,1,0:T(8,128)S(1)}, bf16[8,256,256]{2,1,0:T(8,128)(2,1)S(1)}, bf16[8,256,256]{2,1,0:T(8,128)(2,1)S(1)}) custom-call(s32[1,3,16]{2,1,0:T(4,128)S(1)} %copy.9.refs_0_.slots_ref, s32[5]{0:T(128)S(1)} %stack.23.where_ref, ...), custom_call_target="tpu_custom_call" | custom-call | flops 1342177280 | bytes 8388608 | tf_op jit(solution)/shard_map/far_blocks/pallas_call | solution.py:216
  56.2 1.9 %collective-permute-start.6 = (f32[4,3,128,128]{3,2,1,0:T(8,128)S(1)}, f32[4,3,128,128]{3,2,1,0:T(8,128)S(1)}, u32[]{:S(2)}, u32[]{:S(2)}) collective-permute-start(f32[4,3,128,128]{3,2,1,0:T(8,128)S(1)} %get-tuple-element.33), channel_id=1, source_target_pairs={{0,32},{32,0},{1,33},{33,1},{2,34},{34,2},{3,35},{35,3},{4,36},{36... | collective-permute-start | bytes 2359304 | tf_op jit(solution)/shard_map/ppermute | solution.py:311
  58.1 1.6 %near_blocks.1 = (f32[2,3,128,128]{3,2,1,0:T(8,128)S(1)}, f32[2,3,128,128]{3,2,1,0:T(8,128)S(1)}, f32[4,3,128,128]{3,2,1,0:T(8,128)S(1)}) custom-call(s32[1,3,16]{2,1,0:T(4,128)S(1)} %copy.9.refs_0_.slots_ref, s32[5]{0:T(128)S(1)} %stack.23.where_ref, bf16[8,256,256]{2,1,0:T(8,128)(2,1)S(1)} %get-tuple-element.22.below_ref, ...), custom_call_target="tpu_custom_call" | custom-call | flops 805306368 | bytes 8388608 | tf_op jit(solution)/shard_map/near_blocks/pallas_call | solution.py:245
  59.7 2.4 %collective-permute-start.3 = (f32[4,3,128,128]{3,2,1,0:T(8,128)S(1)}, f32[4,3,128,128]{3,2,1,0:T(8,128)S(1)}, u32[]{:S(2)}, u32[]{:S(2)}) collective-permute-start(f32[4,3,128,128]{3,2,1,0:T(8,128)S(1)} %get-tuple-element.30), channel_id=1, source_target_pairs={{0,32},{32,0},{1,33},{33,1},{2,34},{34,2},{3,35},{35,3},{4,36},{36... | collective-permute-start | bytes 2359304 | tf_op jit(solution)/shard_map/ppermute | solution.py:311
  62.1 0.0 collective-permute-done.6
  62.2 2.7 %collective-permute-start.7 = (f32[2,3,128,128]{3,2,1,0:T(8,128)S(1)}, f32[2,3,128,128]{3,2,1,0:T(8,128)S(1)}, u32[]{:S(2)}, u32[]{:S(2)}) collective-permute-start(f32[2,3,128,128]{3,2,1,0:T(8,128)S(1)} %slice_add_fusion), channel_id=1, source_target_pairs={{0,128},{32,416},{128,0},{160,288},{256,384},{288,160},{384,256},{... | collective-permute-start | bytes 1179656 | tf_op jit(solution)/shard_map/ppermute | solution.py:320
  65.0 0.0 collective-permute-done.3
  65.0 3.1 %collective-permute-start.4 = (f32[2,3,128,128]{3,2,1,0:T(8,128)S(1)}, f32[2,3,128,128]{3,2,1,0:T(8,128)S(1)}, u32[]{:S(2)}, u32[]{:S(2)}) collective-permute-start(f32[2,3,128,128]{3,2,1,0:T(8,128)S(1)} %slice_add_fusion.1), channel_id=1, source_target_pairs={{0,128},{32,416},{128,0},{160,288},{256,384},{288,160},{384,256},{... | collective-permute-start | bytes 1179656 | tf_op jit(solution)/shard_map/ppermute | solution.py:320
  68.1 3.7 %collective-permute-done.7 = f32[2,3,128,128]{3,2,1,0:T(8,128)S(1)} collective-permute-done((f32[2,3,128,128]{3,2,1,0:T(8,128)S(1)}, f32[2,3,128,128]{3,2,1,0:T(8,128)S(1)}, u32[]{:S(2)}, u32[]{:S(2)}) %collective-permute-start.7) | collective-permute-done | bytes 393248 | tf_op jit(solution)/shard_map/ppermute | solution.py:320
  71.9 2.4 %collective-permute-start.8 = (f32[3,128,128]{2,1,0:T(8,128)S(1)}, f32[3,128,128]{2,1,0:T(8,128)S(1)}, u32[]{:S(2)}, u32[]{:S(2)}) collective-permute-start(f32[3,128,128]{2,1,0:T(8,128)S(1)} %fusion), channel_id=1, source_target_pairs={{0,384},{32,160},{128,256},{160,32},{256,128},{288,416},{384,0},{4... | collective-permute-start | bytes 589832 | tf_op jit(solution)/shard_map/ppermute | solution.py:320
  74.3 1.8 %collective-permute-done.4 = f32[2,3,128,128]{3,2,1,0:T(8,128)S(1)} collective-permute-done((f32[2,3,128,128]{3,2,1,0:T(8,128)S(1)}, f32[2,3,128,128]{3,2,1,0:T(8,128)S(1)}, u32[]{:S(2)}, u32[]{:S(2)}) %collective-permute-start.4) | collective-permute-done | bytes 393248 | tf_op jit(solution)/shard_map/ppermute | solution.py:320
  76.1 2.9 %collective-permute-start.5 = (f32[3,128,128]{2,1,0:T(8,128)S(1)}, f32[3,128,128]{2,1,0:T(8,128)S(1)}, u32[]{:S(2)}, u32[]{:S(2)}) collective-permute-start(f32[3,128,128]{2,1,0:T(8,128)S(1)} %fusion.3), channel_id=1, source_target_pairs={{0,384},{32,160},{128,256},{160,32},{256,128},{288,416},{384,0},{4... | collective-permute-start | bytes 589832 | tf_op jit(solution)/shard_map/ppermute | solution.py:320
  79.0 1.7 %collective-permute-done.8 = f32[3,128,128]{2,1,0:T(8,128)S(1)} collective-permute-done((f32[3,128,128]{2,1,0:T(8,128)S(1)}, f32[3,128,128]{2,1,0:T(8,128)S(1)}, u32[]{:S(2)}, u32[]{:S(2)}) %collective-permute-start.8) | collective-permute-done | bytes 196640 | tf_op jit(solution)/shard_map/ppermute | solution.py:320
  80.7 7.5 %collective-permute-start.9 = (f32[3,128,128]{2,1,0:T(8,128)S(1)}, f32[3,128,128]{2,1,0:T(8,128)S(1)}, u32[]{:S(2)}, u32[]{:S(2)}) collective-permute-start(f32[3,128,128]{2,1,0:T(8,128)S(1)} %fusion.2), channel_id=1, source_target_pairs={{0,64},{64,0},{1,65},{65,1},{2,66},{66,2},{3,67},{67,3},{4,68},{68... | collective-permute-start | bytes 589832 | tf_op jit(solution)/shard_map/ppermute | solution.py:311
  88.2 0.0 collective-permute-done.5
  88.3 5.6 %collective-permute-done.9.other_ref = f32[3,128,128]{2,1,0:T(8,128)S(1)} collective-permute-done((f32[3,128,128]{2,1,0:T(8,128)S(1)}, f32[3,128,128]{2,1,0:T(8,128)S(1)}, u32[]{:S(2)}, u32[]{:S(2)}) %collective-permute-start.9) | collective-permute-done | bytes 196640 | tf_op jit(solution)/shard_map/ppermute | solution.py:311
  93.9 0.6 edge_values.1
  94.5 13.7 %collective-permute-start.10 = (f32[128,128]{1,0:T(8,128)S(1)}, f32[128,128]{1,0:T(8,128)S(1)}, u32[]{:S(2)}, u32[]{:S(2)}) collective-permute-start(f32[128,128]{1,0:T(8,128)S(1)} %get-tuple-element.35), channel_id=1, source_target_pairs={{1,2},{2,1},{3,4},{4,3},{5,6},{6,5},{7,8},{8,7},{9,10},{10,9},{11,... | collective-permute-start | bytes 196616 | tf_op jit(solution)/shard_map/ppermute | solution.py:328
  108.2 1.9 %collective-permute-start.11 = (f32[128,128]{1,0:T(8,128)S(1)}, f32[128,128]{1,0:T(8,128)S(1)}, u32[]{:S(2)}, u32[]{:S(2)}) collective-permute-start(f32[128,128]{1,0:T(8,128)S(1)} %get-tuple-element.36), channel_id=1, source_target_pairs={{0,1},{1,0},{2,3},{3,2},{4,5},{5,4},{6,7},{7,6},{8,9},{9,8},{10,11... | collective-permute-start | bytes 196616 | tf_op jit(solution)/shard_map/ppermute | solution.py:328
  110.1 0.7 collective-permute-done.10.late_ref
  110.9 3.5 %collective-permute-done.11.early_ref = f32[128,128]{1,0:T(8,128)S(1)} collective-permute-done((f32[128,128]{1,0:T(8,128)S(1)}, f32[128,128]{1,0:T(8,128)S(1)}, u32[]{:S(2)}, u32[]{:S(2)}) %collective-permute-start.11) | collective-permute-done | bytes 65568 | tf_op jit(solution)/shard_map/ppermute | solution.py:328
  114.4 1.4 %proximal.1 = f32[1,3,1,128,128]{4,3,2,1,0:T(8,128)} custom-call(s32[5]{0:T(128)S(1)} %stack.23.where_ref, s32[1,3,16]{2,1,0:T(4,128)S(1)} %copy.9.refs_0_.slots_ref, f32[3,128,128]{2,1,0:T(8,128)S(1)} %fusion.5.near_ref, f32[3,128,128]{2,1,0:T(8,128)S(1)} %collective-permute-done.9.other_ref, f32[128,128]{1,0:T(8,128)S(1)} %collective-permute-done.10.late_ref, ...), custom_call_target="tpu_custom_call" | custom-call | flops 983040 | bytes 524288 | tf_op jit(solution)/shard_map/proximal/pallas_call | solution.py:289
  (6 shorter events, 0.2 us)
Async XLA Ops:
  0.0 38.2 %collective-permute-start = (f32[256,1024]{1,0:T(8,128)}, f32[256,1024]{1,0:T(8,128)S(1)}, u32[]{:S(2)}, u32[]{:S(2)}) collective-permute-start(f32[256,1024]{1,0:T(8,128)} %refs_1_.1), channel_id=1, source_target_pairs={{0,1},{1,2},{2,3},{3,4},{4,5},{5,6},{6,7},{7,8},{8,9},{9,10},{10,1... | collective-permute-start | bytes 3145736 | tf_op jit(solution)/shard_map/ppermute | solution.py:311
  4.8 37.2 %collective-permute-start.2 = (f32[128,1024]{1,0:T(8,128)S(1)}, f32[128,1024]{1,0:T(8,128)S(1)}, u32[]{:S(2)}, u32[]{:S(2)}) collective-permute-start(f32[128,1024]{1,0:T(8,128)S(1)} %get-tuple-element.37), channel_id=1, source_target_pairs={{0,31},{1,0},{2,1},{3,2},{4,3},{5,4},{6,5},{7,6},{8,7},{9,8},{10,9... | collective-permute-start | bytes 1572872 | tf_op jit(solution)/shard_map/ppermute | solution.py:311
  17.2 35.9 %collective-permute-start.1 = (f32[128,1024]{1,0:T(8,128)S(1)}, f32[128,1024]{1,0:T(8,128)S(1)}, u32[]{:S(2)}, u32[]{:S(2)}) collective-permute-start(f32[128,1024]{1,0:T(8,128)S(1)} %get-tuple-element.38), channel_id=1, source_target_pairs={{0,31},{1,0},{2,1},{3,2},{4,3},{5,4},{6,5},{7,6},{8,7},{9,8},{10,9... | collective-permute-start | bytes 1572872 | tf_op jit(solution)/shard_map/ppermute | solution.py:311
  21.9 1.9 %copy-start = (f32[1,3,16,128,128]{4,3,2,1,0:T(8,128)S(1)}, f32[1,3,16,128,128]{4,3,2,1,0:T(8,128)}, u32[]{:S(2)}) copy-start(f32[1,3,16,128,128]{4,3,2,1,0:T(8,128)} %omega_ref.3) | copy-start | bytes 9437188
  23.8 1.2 %copy-start.2 = (f32[256,1024]{1,0:T(8,128)S(1)}, f32[256,1024]{1,0:T(8,128)}, u32[]{:S(2)}) copy-start(f32[256,1024]{1,0:T(8,128)} %refs_1_.1) | copy-start | bytes 3145732
  25.0 13.2 %copy-start.1 = (f32[1,3,16,128,128]{4,3,2,1,0:T(8,128)S(1)}, f32[1,3,16,128,128]{4,3,2,1,0:T(8,128)}, u32[]{:S(2)}) copy-start(f32[1,3,16,128,128]{4,3,2,1,0:T(8,128)} %omega_ref.3) | copy-start | bytes 9437188
  56.2 5.9 %collective-permute-start.6 = (f32[4,3,128,128]{3,2,1,0:T(8,128)S(1)}, f32[4,3,128,128]{3,2,1,0:T(8,128)S(1)}, u32[]{:S(2)}, u32[]{:S(2)}) collective-permute-start(f32[4,3,128,128]{3,2,1,0:T(8,128)S(1)} %get-tuple-element.33), channel_id=1, source_target_pairs={{0,32},{32,0},{1,33},{33,1},{2,34},{34,2},{3,35},{35,3},{4,36},{36... | collective-permute-start | bytes 2359304 | tf_op jit(solution)/shard_map/ppermute | solution.py:311
  59.7 5.2 %collective-permute-start.3 = (f32[4,3,128,128]{3,2,1,0:T(8,128)S(1)}, f32[4,3,128,128]{3,2,1,0:T(8,128)S(1)}, u32[]{:S(2)}, u32[]{:S(2)}) collective-permute-start(f32[4,3,128,128]{3,2,1,0:T(8,128)S(1)} %get-tuple-element.30), channel_id=1, source_target_pairs={{0,32},{32,0},{1,33},{33,1},{2,34},{34,2},{3,35},{35,3},{4,36},{36... | collective-permute-start | bytes 2359304 | tf_op jit(solution)/shard_map/ppermute | solution.py:311
  62.2 9.7 %collective-permute-start.7 = (f32[2,3,128,128]{3,2,1,0:T(8,128)S(1)}, f32[2,3,128,128]{3,2,1,0:T(8,128)S(1)}, u32[]{:S(2)}, u32[]{:S(2)}) collective-permute-start(f32[2,3,128,128]{3,2,1,0:T(8,128)S(1)} %slice_add_fusion), channel_id=1, source_target_pairs={{0,128},{32,416},{128,0},{160,288},{256,384},{288,160},{384,256},{... | collective-permute-start | bytes 1179656 | tf_op jit(solution)/shard_map/ppermute | solution.py:320
  65.0 11.1 %collective-permute-start.4 = (f32[2,3,128,128]{3,2,1,0:T(8,128)S(1)}, f32[2,3,128,128]{3,2,1,0:T(8,128)S(1)}, u32[]{:S(2)}, u32[]{:S(2)}) collective-permute-start(f32[2,3,128,128]{3,2,1,0:T(8,128)S(1)} %slice_add_fusion.1), channel_id=1, source_target_pairs={{0,128},{32,416},{128,0},{160,288},{256,384},{288,160},{384,256},{... | collective-permute-start | bytes 1179656 | tf_op jit(solution)/shard_map/ppermute | solution.py:320
  71.9 8.8 %collective-permute-start.8 = (f32[3,128,128]{2,1,0:T(8,128)S(1)}, f32[3,128,128]{2,1,0:T(8,128)S(1)}, u32[]{:S(2)}, u32[]{:S(2)}) collective-permute-start(f32[3,128,128]{2,1,0:T(8,128)S(1)} %fusion), channel_id=1, source_target_pairs={{0,384},{32,160},{128,256},{160,32},{256,128},{288,416},{384,0},{4... | collective-permute-start | bytes 589832 | tf_op jit(solution)/shard_map/ppermute | solution.py:320
  76.1 12.1 %collective-permute-start.5 = (f32[3,128,128]{2,1,0:T(8,128)S(1)}, f32[3,128,128]{2,1,0:T(8,128)S(1)}, u32[]{:S(2)}, u32[]{:S(2)}) collective-permute-start(f32[3,128,128]{2,1,0:T(8,128)S(1)} %fusion.3), channel_id=1, source_target_pairs={{0,384},{32,160},{128,256},{160,32},{256,128},{288,416},{384,0},{4... | collective-permute-start | bytes 589832 | tf_op jit(solution)/shard_map/ppermute | solution.py:320
  80.7 13.2 %collective-permute-start.9 = (f32[3,128,128]{2,1,0:T(8,128)S(1)}, f32[3,128,128]{2,1,0:T(8,128)S(1)}, u32[]{:S(2)}, u32[]{:S(2)}) collective-permute-start(f32[3,128,128]{2,1,0:T(8,128)S(1)} %fusion.2), channel_id=1, source_target_pairs={{0,64},{64,0},{1,65},{65,1},{2,66},{66,2},{3,67},{67,3},{4,68},{68... | collective-permute-start | bytes 589832 | tf_op jit(solution)/shard_map/ppermute | solution.py:311
  94.5 16.4 %collective-permute-start.10 = (f32[128,128]{1,0:T(8,128)S(1)}, f32[128,128]{1,0:T(8,128)S(1)}, u32[]{:S(2)}, u32[]{:S(2)}) collective-permute-start(f32[128,128]{1,0:T(8,128)S(1)} %get-tuple-element.35), channel_id=1, source_target_pairs={{1,2},{2,1},{3,4},{4,3},{5,6},{6,5},{7,8},{8,7},{9,10},{10,9},{11,... | collective-permute-start | bytes 196616 | tf_op jit(solution)/shard_map/ppermute | solution.py:328
  108.2 6.2 %collective-permute-start.11 = (f32[128,128]{1,0:T(8,128)S(1)}, f32[128,128]{1,0:T(8,128)S(1)}, u32[]{:S(2)}, u32[]{:S(2)}) collective-permute-start(f32[128,128]{1,0:T(8,128)S(1)} %get-tuple-element.36), channel_id=1, source_target_pairs={{0,1},{1,0},{2,3},{3,2},{4,5},{5,4},{6,7},{7,6},{8,9},{9,8},{10,11... | collective-permute-start | bytes 196616 | tf_op jit(solution)/shard_map/ppermute | solution.py:328

commit v7 on v6

--- a/solution.py
+++ b/solution.py
@@ -81,12 +81,9 @@
 
 
 def group_products(slots_ref, where_ref, turned, pieces_ref, y_hi, keep_ref, pass_ref, send_ref):
-    x, core = where_ref[0], where_ref[2]
-    even_pair, odd_pair = x ^ 1, 3 - x
-    first = jnp.where(core == 0, even_pair, odd_pair)
-    second = jnp.where(core == 0, odd_pair, even_pair)
-    for r, x_of in enumerate((x, second, first, x ^ 2)):
-        i = 2 * x_of + y_hi
+    core = where_ref[2]
+    for r in range(4):
+        i = 2 * ((where_ref[0] + r) & 3) + y_hi
         for e in range(3):
             even = slot_block(slots_ref, e, 2 * i, turned, pieces_ref)
             odd = slot_block(slots_ref, e, 2 * i + 1, turned, pieces_ref)
@@ -97,9 +94,9 @@
                     even + jnp.where(diagonal, even_turned, odd_turned),
                     odd + jnp.where(diagonal, odd_turned, even_turned),
                 )
-            own_ref = keep_ref if r < 2 else pass_ref
-            own_ref[r % 2, e] = jnp.where(core == 0, even, odd)
-            send_ref[(0, 2, 1, 3)[r], e] = jnp.where(core == 0, odd, even)
+            own_ref = pass_ref.at[r - 1] if r else keep_ref
+            own_ref[e] = jnp.where(core == 0, even, odd)
+            send_ref[r, e] = jnp.where(core == 0, odd, even)
 
 
 def far_kernel(
@@ -132,7 +129,7 @@
 
 
 def proximal_kernel(
-    where_ref, slots_ref, near_ref, other_ref, late_ref, early_ref, omega_ref, out_ref
+    where_ref, slots_ref, total_ref, early_ref, late_ref, omega_ref, out_ref
 ):
     j = where_ref[3]
     odd_tile = where_ref[4] == 1
@@ -140,7 +137,7 @@
     columns = lax.broadcasted_iota(jnp.int32, (BLK, BLK), 1)
     for e in range(3):
         slot = slots_ref[0, e, j]
-        total = near_ref[e] + other_ref[e]
+        total = total_ref[e]
         if e == 0:
             total = total + jnp.where(odd_tile, early_ref[...], late_ref[...]).T
         if e == 2:
@@ -205,10 +202,17 @@
     )(*inputs)
 
 
-HALF = (2, 3, BLK, BLK)
 WAY = (4, 3, BLK, BLK)
-GROUP_OUT = tuple(jax.ShapeDtypeStruct(shape, f32) for shape in (HALF, HALF, WAY))
-GROUP_SPECS = tuple(full_spec(shape) for shape in (HALF, HALF, WAY))
+OWN = (3, BLK, BLK)
+OTHERS = (3, 3, BLK, BLK)
+
+
+def f32_outs(*shapes):
+    return tuple(jax.ShapeDtypeStruct(shape, f32) for shape in shapes)
+
+
+def full_specs(*shapes):
+    return tuple(full_spec(shape) for shape in shapes)
 
 
 def far_blocks(slots, where, tile, omega, before, half, below, centre):
@@ -217,7 +221,7 @@
         far_kernel,
         name="far_blocks",
         grid=(1,),
-        out_shape=GROUP_OUT
+        out_shape=f32_outs(OWN, OTHERS, WAY)
         + (jax.ShapeDtypeStruct(TURNED, bf16), jax.ShapeDtypeStruct(NATURAL, bf16)),
         in_specs=[
             SMEM,
@@ -229,7 +233,7 @@
             full_spec(TURNED),
             full_spec(TURNED),
         ],
-        out_specs=GROUP_SPECS + (full_spec(TURNED), full_spec(NATURAL)),
+        out_specs=full_specs(OWN, OTHERS, WAY, TURNED, NATURAL),
         scratch_shapes=[
             pltpu.VMEM((NB, ROWS, BLK), f32),
             pltpu.VMEM((NB, rows, 2 * BLK), bf16),
@@ -246,11 +250,11 @@
         near_kernel,
         name="near_blocks",
         grid=(1,),
-        out_shape=GROUP_OUT,
+        out_shape=f32_outs(OWN, OTHERS, WAY),
         in_specs=[SMEM, SMEM]
         + [full_spec(TURNED)] * 3
         + [full_spec(NATURAL)],
-        out_specs=GROUP_SPECS,
+        out_specs=full_specs(OWN, OTHERS, WAY),
         compiler_params=params(),
         cost_estimate=pl.CostEstimate(
             flops=3 * KMAX * ROWS * 256 * 256, bytes_accessed=8 << 20, transcendentals=0
@@ -258,31 +262,30 @@
     )(slots, where, below, centre, above, pieces)
 
 
-def edge_kernel(where_ref, near_ref, other_ref, late_ref, early_ref):
+def edge_kernel(where_ref, total_ref, late_ref, early_ref):
     odd_tile = where_ref[4] == 1
-    downward = near_ref[0] + other_ref[0]
-    upward = near_ref[2] + other_ref[2]
+    downward, upward = total_ref[0], total_ref[2]
     late_ref[...] = jnp.where(odd_tile, upward, downward)
     early_ref[...] = jnp.where(odd_tile, downward, upward)
 
 
-def edge_values(where, near, other):
+def edge_values(where, total):
     block = jax.ShapeDtypeStruct((BLK, BLK), f32)
     return pl.pallas_call(
         edge_kernel,
         name="edge_values",
         grid=(1,),
         out_shape=(block, block),
-        in_specs=[SMEM] + [full_spec((3, BLK, BLK))] * 2,
+        in_specs=[SMEM] + [full_spec((3, BLK, BLK))],
         out_specs=(full_spec((BLK, BLK)),) * 2,
         compiler_params=params(),
         cost_estimate=pl.CostEstimate(
             flops=4 * BLK * BLK, bytes_accessed=6 * 4 * BLK * BLK, transcendentals=0
         ),
-    )(where, near, other)
-
-
-def proximal(where, slots, near, other, late, early, omega):
+    )(where, total)
+
+
+def proximal(where, slots, total, early, late, omega):
     block = pl.BlockSpec((BLK, BLK), lambda i, where, slots: (0, 0))
     triple = pl.BlockSpec((3, BLK, BLK), lambda i, where, slots: (0, 0, 0))
     own = pl.BlockSpec((1, 3, 1, BLK, BLK), lambda i, where, slots: (0, 0, where[3], 0, 0))
@@ -292,7 +295,7 @@
         grid_spec=pltpu.PrefetchScalarGridSpec(
             num_scalar_prefetch=2,
             grid=(1,),
-            in_specs=[triple, triple, block, block, own],
+            in_specs=[triple, block, block, own],
             out_specs=pl.BlockSpec(
                 (1, 3, 1, BLK, BLK), lambda i, where, slots: (0, 0, 0, 0, 0)
             ),
@@ -302,7 +305,7 @@
         cost_estimate=pl.CostEstimate(
             flops=20 * 3 * BLK * BLK, bytes_accessed=1 << 19, transcendentals=0
         ),
-    )(where, slots, near, other, late, early, omega)
+    )(where, slots, total, early, late, omega)
 
 
 def shifted(value, axis, steps):
@@ -311,13 +314,8 @@
     return lax.ppermute(value, axis, pairs)
 
 
-def x_exchange(value, step):
-    pairs = []
-    for x in range(4):
-        for core in range(2):
-            partner = x ^ 1 if core == step else 3 - x
-            pairs.append((2 * x + core, 2 * partner + core))
-    return lax.ppermute(value, ("x", "core"), pairs)
+def after(value, earlier):
+    return lax.optimization_barrier((value, earlier))[0]
 
 
 def edge_exchange(value, offset):
@@ -347,17 +345,20 @@
         block_slots, where, below, centre, above, pieces
     )
     near_got = shifted(near_send, "core", 1)
-    far_first = x_exchange(far_pass + far_got[2:], 0)
-    near_first = x_exchange(near_pass + near_got[2:], 0)
-    far_second = x_exchange(far_keep[1] + far_got[1] + far_first[1], 1)
-    far_sum = far_keep[0] + far_got[0] + far_first[0] + far_second
-    other = shifted(far_sum, "y_hi", 1)
-    near_second = x_exchange(near_keep[1] + near_got[1] + near_first[1], 1)
-    near_sum = near_keep[0] + near_got[0] + near_first[0] + near_second
-    late_out, early_out = edge_values(where, near_sum, other)
+    far_sum = far_keep + far_got[0]
+    for k in (2, 1, 3):
+        far_sum = far_sum + shifted(far_pass[k - 1] + far_got[k], "x", k)
+    near_got = after(near_got, far_sum)
+    near_out = [near_pass[k - 1] + near_got[k] for k in (1, 2, 3)]
+    other = shifted(after(far_sum, near_out), "y_hi", 1)
+    total = near_keep + near_got[0]
+    for k in (1, 3, 2):
+        total = total + shifted(near_out[k - 1], "x", k)
+    total = total + other
+    late_out, early_out = edge_values(where, total)
     late = edge_exchange(late_out, 1)
     early = edge_exchange(early_out, 0)
-    return proximal(where, block_slots, near_sum, other, late, early, omega)
+    return proximal(where, block_slots, total, early, late, omega)
 
 
 def solution(mesh):

time: 116 us -> 119 us (1.026)
  the two profiles are of different devices: /device:TPU:6 before, /device:TPU:32 now
where the time goes in v7:
time: 119 us; the launch traced here: 118 us
  starting transfers between devices  59 us (50%)
  waiting for transfers between devices  40.6 us (34%)
  Pallas kernels  12.9 us (11%)
  local copies, waits for them, and re-layouts  5.16 us (4%)
    ppermute x12, starting transfers between devices, shifted(): return lax.ppermute(value, axis, pairs)  42.2 us
    ppermute x12, waiting for transfers between devices, shifted(): return lax.ppermute(value, axis, pairs)  38.3 us
    ppermute x2, starting transfers between devices, edge_exchange(): return lax.ppermute(value, 'col', pairs)  16.8 us
    pallas_call x3, Pallas kernels, partial(): pl.pallas_call(lambda *refs: partial_kernel(offset, first, *refs), name='...  6.29 us
    unnamed x7, local copies, waits for them, and re-layouts  3.8 us
    pallas_call x1, Pallas kernels, far_blocks(): pl.pallas_call(far_kernel, name='far_blocks', grid=(1,), out_shape=f32_ou...  3.12 us
  transfers between devices with their start and end apart: 14, of which 8 were waited for; matrix products, arithmetic and copies ran while one was open for 2% of the time, Pallas kernels for 7%

profile of v7, /device:TPU:32, one launch (start us, length us, event | category | flops | bytes accessed | tf_op | source)
XLA Modules:
  0.0 118.3 jit_solution(45303195589994919)
XLA Ops:
  0.0 2.6 %collective-permute-start = (f32[256,1024]{1,0:T(8,128)}, f32[256,1024]{1,0:T(8,128)S(1)}, u32[]{:S(2)}, u32[]{:S(2)}) collective-permute-start(f32[256,1024]{1,0:T(8,128)} %refs_1_.1), channel_id=1, source_target_pairs={{0,1},{1,2},{2,3},{3,4},{4,5},{5,6},{6,7},{7,8},{8,9},{9,10},{10,1... | collective-permute-start | bytes 3145736 | tf_op jit(solution)/shard_map/ppermute | solution.py:314
  2.6 1.3 %fusion.11 = (f32[128,1024]{1,0:T(8,128)S(1)}, f32[128,1024]{1,0:T(8,128)S(1)}) fusion(f32[256,1024]{1,0:T(8,128)} %refs_1_.1), kind=kLoop, calls=%fused_computation.19 | loop fusion | bytes 2097152 | tf_op jit(solution)/shard_map/slice | solution.py:335
  3.9 10.6 %collective-permute-start.2 = (f32[128,1024]{1,0:T(8,128)S(1)}, f32[128,1024]{1,0:T(8,128)S(1)}, u32[]{:S(2)}, u32[]{:S(2)}) collective-permute-start(f32[128,1024]{1,0:T(8,128)S(1)} %get-tuple-element.47), channel_id=1, source_target_pairs={{0,31},{1,0},{2,1},{3,2},{4,3},{5,4},{6,5},{7,6},{8,7},{9,8},{10,9... | collective-permute-start | bytes 1572872 | tf_op jit(solution)/shard_map/ppermute | solution.py:314
  14.5 3.9 %collective-permute-start.1 = (f32[128,1024]{1,0:T(8,128)S(1)}, f32[128,1024]{1,0:T(8,128)S(1)}, u32[]{:S(2)}, u32[]{:S(2)}) collective-permute-start(f32[128,1024]{1,0:T(8,128)S(1)} %get-tuple-element.48), channel_id=1, source_target_pairs={{0,31},{1,0},{2,1},{3,2},{4,3},{5,4},{6,5},{7,6},{8,7},{9,8},{10,9... | collective-permute-start | bytes 1572872 | tf_op jit(solution)/shard_map/ppermute | solution.py:314
  18.4 0.7 copy.9.refs_0_.slots_ref
  19.1 0.1 stack.23.where_ref
  19.2 0.0 copy-start
  19.2 1.9 %copy-done = f32[1,3,16,128,128]{4,3,2,1,0:T(8,128)S(1)} copy-done((f32[1,3,16,128,128]{4,3,2,1,0:T(8,128)S(1)}, f32[1,3,16,128,128]{4,3,2,1,0:T(8,128)}, u32[]{:S(2)}) %copy-start) | copy-done | bytes 3145752
  21.1 0.0 copy-start.2
  21.1 1.2 %copy-done.2 = f32[256,1024]{1,0:T(8,128)S(1)} copy-done((f32[256,1024]{1,0:T(8,128)S(1)}, f32[256,1024]{1,0:T(8,128)}, u32[]{:S(2)}) %copy-start.2) | copy-done | bytes 1048600
  22.3 0.0 copy-start.1
  22.3 2.3 %partial_residual.3 = (f32[8,256,128]{2,1,0:T(8,128)S(1)}, bf16[8,256,256]{2,1,0:T(8,128)(2,1)S(1)}) custom-call(s32[1,3,16]{2,1,0:T(4,128)S(1)} %copy.9.refs_0_.slots_ref, f32[256,1024]{1,0:T(8,128)S(1)} %copy-done.2, f32[1,3,16,128,128]{4,3,2,1,0:T(8,128)S(1)} %copy-done), custom_call_target="tpu_custom_call" | custom-call | flops 536870912 | bytes 5242880 | tf_op jit(solution)/shard_map/partial_residual/pallas_call | solution.py:187
  24.6 10.9 %collective-permute-done.refs_1_ = f32[256,1024]{1,0:T(8,128)S(1)} collective-permute-done((f32[256,1024]{1,0:T(8,128)}, f32[256,1024]{1,0:T(8,128)S(1)}, u32[]{:S(2)}, u32[]{:S(2)}) %collective-permute-start) | collective-permute-done | bytes 1048608 | tf_op jit(solution)/shard_map/ppermute | solution.py:314
  35.5 0.0 copy-done.1
  35.5 2.2 %partial_residual.4 = (f32[8,256,128]{2,1,0:T(8,128)S(1)}, bf16[8,256,256]{2,1,0:T(8,128)(2,1)S(1)}) custom-call(s32[1,3,16]{2,1,0:T(4,128)S(1)} %copy.9.refs_0_.slots_ref, f32[256,1024]{1,0:T(8,128)S(1)} %collective-permute-done.refs_1_, f32[1,3,16,128,128]{4,3,2,1,0:T(8,128)S(1)} %copy-done.1, f32[8,256,128]{2,1,0:T(8,128)S(1)} %get-tuple-element.23.refs_3_), custom_call_target="tpu_custom_call" | custom-call | flops 536870912 | bytes 5242880 | tf_op jit(solution)/shard_map/partial_residual/pallas_call | solution.py:187
  37.8 4.3 %collective-permute-done.2.refs_1_ = f32[128,1024]{1,0:T(8,128)S(1)} collective-permute-done((f32[128,1024]{1,0:T(8,128)S(1)}, f32[128,1024]{1,0:T(8,128)S(1)}, u32[]{:S(2)}, u32[]{:S(2)}) %collective-permute-start.2) | collective-permute-done | bytes 524320 | tf_op jit(solution)/shard_map/ppermute | solution.py:314
  42.0 1.8 %partial_residual.5 = (f32[8,256,128]{2,1,0:T(8,128)S(1)}, bf16[8,256,128]{2,1,0:T(8,128)(2,1)S(1)}) custom-call(s32[1,3,16]{2,1,0:T(4,128)S(1)} %copy.9.refs_0_.slots_ref, f32[128,1024]{1,0:T(8,128)S(1)} %collective-permute-done.2.refs_1_, f32[1,3,16,128,128]{4,3,2,1,0:T(8,128)S(1)} %copy-done.1, f32[8,256,128]{2,1,0:T(8,128)S(1)} %get-tuple-element.26.refs_3_), custom_call_target="tpu_custom_call" | custom-call | flops 268435456 | bytes 5242880 | tf_op jit(solution)/shard_map/partial_residual/pallas_call | solution.py:187
  43.8 9.0 %collective-permute-done.1.x_ref = f32[128,1024]{1,0:T(8,128)S(1)} collective-permute-done((f32[128,1024]{1,0:T(8,128)S(1)}, f32[128,1024]{1,0:T(8,128)S(1)}, u32[]{:S(2)}, u32[]{:S(2)}) %collective-permute-start.1) | collective-permute-done | bytes 524320 | tf_op jit(solution)/shard_map/ppermute | solution.py:314
  52.8 3.1 %far_blocks.1 = (f32[3,128,128]{2,1,0:T(8,128)S(1)}, f32[3,3,128,128]{3,2,1,0:T(8,128)S(1)}, f32[4,3,128,128]{3,2,1,0:T(8,128)S(1)}, bf16[8,256,256]{2,1,0:T(8,128)(2,1)S(1)}, bf16[8,256,256]{2,1,0:T(8,128)(2,1)S(1)}) custom-call(s32[1,3,16]{2,1,0:T(4,128)S(1)} %copy.9.refs_0_.slots_ref, s32[5]{0:T(128)S(1)} %stack.23.where_ref, ...), custom_call_target="tpu_custom_call" | custom-call | flops 1342177280 | bytes 8388608 | tf_op jit(solution)/shard_map/far_blocks/pallas_call | solution.py:220
  56.0 1.9 %collective-permute-start.4 = (f32[4,3,128,128]{3,2,1,0:T(8,128)S(1)}, f32[4,3,128,128]{3,2,1,0:T(8,128)S(1)}, u32[]{:S(2)}, u32[]{:S(2)}) collective-permute-start(f32[4,3,128,128]{3,2,1,0:T(8,128)S(1)} %get-tuple-element.34), channel_id=1, source_target_pairs={{0,32},{32,0},{1,33},{33,1},{2,34},{34,2},{3,35},{35,3},{4,36},{36... | collective-permute-start | bytes 2359304 | tf_op jit(solution)/shard_map/ppermute | solution.py:314
  57.9 1.6 %near_blocks.1 = (f32[3,128,128]{2,1,0:T(8,128)S(1)}, f32[3,3,128,128]{3,2,1,0:T(8,128)S(1)}, f32[4,3,128,128]{3,2,1,0:T(8,128)S(1)}) custom-call(s32[1,3,16]{2,1,0:T(4,128)S(1)} %copy.9.refs_0_.slots_ref, s32[5]{0:T(128)S(1)} %stack.23.where_ref, bf16[8,256,256]{2,1,0:T(8,128)(2,1)S(1)} %get-tuple-element.24.below_ref, ...), custom_call_target="tpu_custom_call" | custom-call | flops 805306368 | bytes 8388608 | tf_op jit(solution)/shard_map/near_blocks/pallas_call | solution.py:249
  59.5 2.4 %collective-permute-start.3 = (f32[4,3,128,128]{3,2,1,0:T(8,128)S(1)}, f32[4,3,128,128]{3,2,1,0:T(8,128)S(1)}, u32[]{:S(2)}, u32[]{:S(2)}) collective-permute-start(f32[4,3,128,128]{3,2,1,0:T(8,128)S(1)} %get-tuple-element.32), channel_id=1, source_target_pairs={{0,32},{32,0},{1,33},{33,1},{2,34},{34,2},{3,35},{35,3},{4,36},{36... | collective-permute-start | bytes 2359304 | tf_op jit(solution)/shard_map/ppermute | solution.py:314
  61.9 0.0 collective-permute-done.4
  61.9 0.1 fusion.2
  62.0 4.9 %collective-permute-start.5 = (f32[3,128,128]{2,1,0:T(8,128)S(1)}, f32[3,128,128]{2,1,0:T(8,128)S(1)}, u32[]{:S(2)}, u32[]{:S(2)}) collective-permute-start(f32[3,128,128]{2,1,0:T(8,128)S(1)} %get-tuple-element.44), channel_id=1, source_target_pairs={{0,256},{128,384},{256,0},{384,128},{1,257},{129,385},{257,1},{385... | collective-permute-start | bytes 589832 | tf_op jit(solution)/shard_map/ppermute | solution.py:314
  66.9 3.1 %collective-permute-start.7 = (f32[3,128,128]{2,1,0:T(8,128)S(1)}, f32[3,128,128]{2,1,0:T(8,128)S(1)}, u32[]{:S(2)}, u32[]{:S(2)}) collective-permute-start(f32[3,128,128]{2,1,0:T(8,128)S(1)} %get-tuple-element.45), channel_id=1, source_target_pairs={{0,384},{128,0},{256,128},{384,256},{1,385},{129,1},{257,129},{385... | collective-permute-start | bytes 589832 | tf_op jit(solution)/shard_map/ppermute | solution.py:314
  70.0 2.8 %collective-permute-start.6 = (f32[3,128,128]{2,1,0:T(8,128)S(1)}, f32[3,128,128]{2,1,0:T(8,128)S(1)}, u32[]{:S(2)}, u32[]{:S(2)}) collective-permute-start(f32[3,128,128]{2,1,0:T(8,128)S(1)} %get-tuple-element.46), channel_id=1, source_target_pairs={{0,128},{128,256},{256,384},{384,0},{1,129},{129,257},{257,385},{3... | collective-permute-start | bytes 589832 | tf_op jit(solution)/shard_map/ppermute | solution.py:314
  72.8 0.0 collective-permute-done.5
  72.8 3.7 %collective-permute-done.7 = f32[3,128,128]{2,1,0:T(8,128)S(1)} collective-permute-done((f32[3,128,128]{2,1,0:T(8,128)S(1)}, f32[3,128,128]{2,1,0:T(8,128)S(1)}, u32[]{:S(2)}, u32[]{:S(2)}) %collective-permute-start.7) | collective-permute-done | bytes 196640 | tf_op jit(solution)/shard_map/ppermute | solution.py:314
  76.5 2.8 %collective-permute-done.6 = f32[3,128,128]{2,1,0:T(8,128)S(1)} collective-permute-done((f32[3,128,128]{2,1,0:T(8,128)S(1)}, f32[3,128,128]{2,1,0:T(8,128)S(1)}, u32[]{:S(2)}, u32[]{:S(2)}) %collective-permute-start.6) | collective-permute-done | bytes 196640 | tf_op jit(solution)/shard_map/ppermute | solution.py:314
  79.4 0.1 fusion.6
  79.4 0.0 collective-permute-done.3
  79.4 0.1 add_bitcast_fusion.1
  79.5 2.3 %collective-permute-start.11 = (f32[3,128,128]{2,1,0:T(8,128)S(1)}, f32[3,128,128]{2,1,0:T(8,128)S(1)}, u32[]{:S(2)}, u32[]{:S(2)}) collective-permute-start(f32[3,128,128]{2,1,0:T(8,128)S(1)} %fusion.6), channel_id=1, source_target_pairs={{0,64},{64,0},{1,65},{65,1},{2,66},{66,2},{3,67},{67,3},{4,68},{68... | collective-permute-start | bytes 589832 | tf_op jit(solution)/shard_map/ppermute | solution.py:314
  81.8 1.9 %collective-permute-start.9 = (f32[3,128,128]{2,1,0:T(8,128)S(1)}, f32[3,128,128]{2,1,0:T(8,128)S(1)}, u32[]{:S(2)}, u32[]{:S(2)}) collective-permute-start(f32[3,128,128]{2,1,0:T(8,128)S(1)} %get-tuple-element.41), channel_id=1, source_target_pairs={{0,384},{128,0},{256,128},{384,256},{1,385},{129,1},{257,129},{385... | collective-permute-start | bytes 589832 | tf_op jit(solution)/shard_map/ppermute | solution.py:314
  83.7 3.6 %collective-permute-start.10 = (f32[3,128,128]{2,1,0:T(8,128)S(1)}, f32[3,128,128]{2,1,0:T(8,128)S(1)}, u32[]{:S(2)}, u32[]{:S(2)}) collective-permute-start(f32[3,128,128]{2,1,0:T(8,128)S(1)} %get-tuple-element.42), channel_id=1, source_target_pairs={{0,256},{128,384},{256,0},{384,128},{1,257},{129,385},{257,1},{385... | collective-permute-start | bytes 589832 | tf_op jit(solution)/shard_map/ppermute | solution.py:314
  87.4 2.2 %collective-permute-start.8 = (f32[3,128,128]{2,1,0:T(8,128)S(1)}, f32[3,128,128]{2,1,0:T(8,128)S(1)}, u32[]{:S(2)}, u32[]{:S(2)}) collective-permute-start(f32[3,128,128]{2,1,0:T(8,128)S(1)} %get-tuple-element.43), channel_id=1, source_target_pairs={{0,128},{128,256},{256,384},{384,0},{1,129},{129,257},{257,385},{3... | collective-permute-start | bytes 589832 | tf_op jit(solution)/shard_map/ppermute | solution.py:314
  89.6 5.3 %collective-permute-done.11 = f32[3,128,128]{2,1,0:T(8,128)S(1)} collective-permute-done((f32[3,128,128]{2,1,0:T(8,128)S(1)}, f32[3,128,128]{2,1,0:T(8,128)S(1)}, u32[]{:S(2)}, u32[]{:S(2)}) %collective-permute-start.11) | collective-permute-done | bytes 196640 | tf_op jit(solution)/shard_map/ppermute | solution.py:314
  94.9 0.0 collective-permute-done.9
  94.9 0.0 collective-permute-done.10
  94.9 2.2 %collective-permute-done.8 = f32[3,128,128]{2,1,0:T(8,128)S(1)} collective-permute-done((f32[3,128,128]{2,1,0:T(8,128)S(1)}, f32[3,128,128]{2,1,0:T(8,128)S(1)}, u32[]{:S(2)}, u32[]{:S(2)}) %collective-permute-start.8) | collective-permute-done | bytes 196640 | tf_op jit(solution)/shard_map/ppermute | solution.py:314
  97.1 0.1 fusion.10.total_ref
  97.2 0.6 edge_values.1
  97.8 2.5 %collective-permute-start.12 = (f32[128,128]{1,0:T(8,128)S(1)}, f32[128,128]{1,0:T(8,128)S(1)}, u32[]{:S(2)}, u32[]{:S(2)}) collective-permute-start(f32[128,128]{1,0:T(8,128)S(1)} %get-tuple-element.39), channel_id=1, source_target_pairs={{0,1},{1,0},{2,3},{3,2},{4,5},{5,4},{6,7},{7,6},{8,9},{9,8},{10,11... | collective-permute-start | bytes 196616 | tf_op jit(solution)/shard_map/ppermute | solution.py:326
  100.3 14.3 %collective-permute-start.13 = (f32[128,128]{1,0:T(8,128)S(1)}, f32[128,128]{1,0:T(8,128)S(1)}, u32[]{:S(2)}, u32[]{:S(2)}) collective-permute-start(f32[128,128]{1,0:T(8,128)S(1)} %get-tuple-element.40), channel_id=1, source_target_pairs={{1,2},{2,1},{3,4},{4,3},{5,6},{6,5},{7,8},{8,7},{9,10},{10,9},{11,... | collective-permute-start | bytes 196616 | tf_op jit(solution)/shard_map/ppermute | solution.py:326
  114.6 0.0 collective-permute-done.12.early_ref
  114.6 2.3 %collective-permute-done.13.late_ref = f32[128,128]{1,0:T(8,128)S(1)} collective-permute-done((f32[128,128]{1,0:T(8,128)S(1)}, f32[128,128]{1,0:T(8,128)S(1)}, u32[]{:S(2)}, u32[]{:S(2)}) %collective-permute-start.13) | collective-permute-done | bytes 65568 | tf_op jit(solution)/shard_map/ppermute | solution.py:326
  116.9 1.4 %proximal.1 = f32[1,3,1,128,128]{4,3,2,1,0:T(8,128)} custom-call(s32[5]{0:T(128)S(1)} %stack.23.where_ref, s32[1,3,16]{2,1,0:T(4,128)S(1)} %copy.9.refs_0_.slots_ref, f32[3,128,128]{2,1,0:T(8,128)S(1)} %fusion.10.total_ref, f32[128,128]{1,0:T(8,128)S(1)} %collective-permute-done.12.early_ref, f32[128,128]{1,0:T(8,128)S(1)} %collective-permute-done.13.late_ref, ...), custom_call_target="tpu_custom_call" | custom-call | flops 983040 | bytes 524288 | tf_op jit(solution)/shard_map/proximal/pallas_call | solution.py:292
Async XLA Ops:
  0.0 35.5 %collective-permute-start = (f32[256,1024]{1,0:T(8,128)}, f32[256,1024]{1,0:T(8,128)S(1)}, u32[]{:S(2)}, u32[]{:S(2)}) collective-permute-start(f32[256,1024]{1,0:T(8,128)} %refs_1_.1), channel_id=1, source_target_pairs={{0,1},{1,2},{2,3},{3,4},{4,5},{5,6},{6,7},{7,8},{8,9},{9,10},{10,1... | collective-permute-start | bytes 3145736 | tf_op jit(solution)/shard_map/ppermute | solution.py:314
  3.9 38.2 %collective-permute-start.2 = (f32[128,1024]{1,0:T(8,128)S(1)}, f32[128,1024]{1,0:T(8,128)S(1)}, u32[]{:S(2)}, u32[]{:S(2)}) collective-permute-start(f32[128,1024]{1,0:T(8,128)S(1)} %get-tuple-element.47), channel_id=1, source_target_pairs={{0,31},{1,0},{2,1},{3,2},{4,3},{5,4},{6,5},{7,6},{8,7},{9,8},{10,9... | collective-permute-start | bytes 1572872 | tf_op jit(solution)/shard_map/ppermute | solution.py:314
  14.5 38.4 %collective-permute-start.1 = (f32[128,1024]{1,0:T(8,128)S(1)}, f32[128,1024]{1,0:T(8,128)S(1)}, u32[]{:S(2)}, u32[]{:S(2)}) collective-permute-start(f32[128,1024]{1,0:T(8,128)S(1)} %get-tuple-element.48), channel_id=1, source_target_pairs={{0,31},{1,0},{2,1},{3,2},{4,3},{5,4},{6,5},{7,6},{8,7},{9,8},{10,9... | collective-permute-start | bytes 1572872 | tf_op jit(solution)/shard_map/ppermute | solution.py:314
  19.2 1.9 %copy-start = (f32[1,3,16,128,128]{4,3,2,1,0:T(8,128)S(1)}, f32[1,3,16,128,128]{4,3,2,1,0:T(8,128)}, u32[]{:S(2)}) copy-start(f32[1,3,16,128,128]{4,3,2,1,0:T(8,128)} %omega_ref.3) | copy-start | bytes 9437188
  21.1 1.2 %copy-start.2 = (f32[256,1024]{1,0:T(8,128)S(1)}, f32[256,1024]{1,0:T(8,128)}, u32[]{:S(2)}) copy-start(f32[256,1024]{1,0:T(8,128)} %refs_1_.1) | copy-start | bytes 3145732
  22.3 13.2 %copy-start.1 = (f32[1,3,16,128,128]{4,3,2,1,0:T(8,128)S(1)}, f32[1,3,16,128,128]{4,3,2,1,0:T(8,128)}, u32[]{:S(2)}) copy-start(f32[1,3,16,128,128]{4,3,2,1,0:T(8,128)} %omega_ref.3) | copy-start | bytes 9437188
  56.0 5.9 %collective-permute-start.4 = (f32[4,3,128,128]{3,2,1,0:T(8,128)S(1)}, f32[4,3,128,128]{3,2,1,0:T(8,128)S(1)}, u32[]{:S(2)}, u32[]{:S(2)}) collective-permute-start(f32[4,3,128,128]{3,2,1,0:T(8,128)S(1)} %get-tuple-element.34), channel_id=1, source_target_pairs={{0,32},{32,0},{1,33},{33,1},{2,34},{34,2},{3,35},{35,3},{4,36},{36... | collective-permute-start | bytes 2359304 | tf_op jit(solution)/shard_map/ppermute | solution.py:314
  59.5 19.9 %collective-permute-start.3 = (f32[4,3,128,128]{3,2,1,0:T(8,128)S(1)}, f32[4,3,128,128]{3,2,1,0:T(8,128)S(1)}, u32[]{:S(2)}, u32[]{:S(2)}) collective-permute-start(f32[4,3,128,128]{3,2,1,0:T(8,128)S(1)} %get-tuple-element.32), channel_id=1, source_target_pairs={{0,32},{32,0},{1,33},{33,1},{2,34},{34,2},{3,35},{35,3},{4,36},{36... | collective-permute-start | bytes 2359304 | tf_op jit(solution)/shard_map/ppermute | solution.py:314
  62.0 10.8 %collective-permute-start.5 = (f32[3,128,128]{2,1,0:T(8,128)S(1)}, f32[3,128,128]{2,1,0:T(8,128)S(1)}, u32[]{:S(2)}, u32[]{:S(2)}) collective-permute-start(f32[3,128,128]{2,1,0:T(8,128)S(1)} %get-tuple-element.44), channel_id=1, source_target_pairs={{0,256},{128,384},{256,0},{384,128},{1,257},{129,385},{257,1},{385... | collective-permute-start | bytes 589832 | tf_op jit(solution)/shard_map/ppermute | solution.py:314
  66.9 9.6 %collective-permute-start.7 = (f32[3,128,128]{2,1,0:T(8,128)S(1)}, f32[3,128,128]{2,1,0:T(8,128)S(1)}, u32[]{:S(2)}, u32[]{:S(2)}) collective-permute-start(f32[3,128,128]{2,1,0:T(8,128)S(1)} %get-tuple-element.45), channel_id=1, source_target_pairs={{0,384},{128,0},{256,128},{384,256},{1,385},{129,1},{257,129},{385... | collective-permute-start | bytes 589832 | tf_op jit(solution)/shard_map/ppermute | solution.py:314
  70.0 9.4 %collective-permute-start.6 = (f32[3,128,128]{2,1,0:T(8,128)S(1)}, f32[3,128,128]{2,1,0:T(8,128)S(1)}, u32[]{:S(2)}, u32[]{:S(2)}) collective-permute-start(f32[3,128,128]{2,1,0:T(8,128)S(1)} %get-tuple-element.46), channel_id=1, source_target_pairs={{0,128},{128,256},{256,384},{384,0},{1,129},{129,257},{257,385},{3... | collective-permute-start | bytes 589832 | tf_op jit(solution)/shard_map/ppermute | solution.py:314
  79.5 15.4 %collective-permute-start.11 = (f32[3,128,128]{2,1,0:T(8,128)S(1)}, f32[3,128,128]{2,1,0:T(8,128)S(1)}, u32[]{:S(2)}, u32[]{:S(2)}) collective-permute-start(f32[3,128,128]{2,1,0:T(8,128)S(1)} %fusion.6), channel_id=1, source_target_pairs={{0,64},{64,0},{1,65},{65,1},{2,66},{66,2},{3,67},{67,3},{4,68},{68... | collective-permute-start | bytes 589832 | tf_op jit(solution)/shard_map/ppermute | solution.py:314
  81.8 13.1 %collective-permute-start.9 = (f32[3,128,128]{2,1,0:T(8,128)S(1)}, f32[3,128,128]{2,1,0:T(8,128)S(1)}, u32[]{:S(2)}, u32[]{:S(2)}) collective-permute-start(f32[3,128,128]{2,1,0:T(8,128)S(1)} %get-tuple-element.41), channel_id=1, source_target_pairs={{0,384},{128,0},{256,128},{384,256},{1,385},{129,1},{257,129},{385... | collective-permute-start | bytes 589832 | tf_op jit(solution)/shard_map/ppermute | solution.py:314
  83.7 11.2 %collective-permute-start.10 = (f32[3,128,128]{2,1,0:T(8,128)S(1)}, f32[3,128,128]{2,1,0:T(8,128)S(1)}, u32[]{:S(2)}, u32[]{:S(2)}) collective-permute-start(f32[3,128,128]{2,1,0:T(8,128)S(1)} %get-tuple-element.42), channel_id=1, source_target_pairs={{0,256},{128,384},{256,0},{384,128},{1,257},{129,385},{257,1},{385... | collective-permute-start | bytes 589832 | tf_op jit(solution)/shard_map/ppermute | solution.py:314
  87.4 9.7 %collective-permute-start.8 = (f32[3,128,128]{2,1,0:T(8,128)S(1)}, f32[3,128,128]{2,1,0:T(8,128)S(1)}, u32[]{:S(2)}, u32[]{:S(2)}) collective-permute-start(f32[3,128,128]{2,1,0:T(8,128)S(1)} %get-tuple-element.43), channel_id=1, source_target_pairs={{0,128},{128,256},{256,384},{384,0},{1,129},{129,257},{257,385},{3... | collective-permute-start | bytes 589832 | tf_op jit(solution)/shard_map/ppermute | solution.py:314
  97.8 16.8 %collective-permute-start.12 = (f32[128,128]{1,0:T(8,128)S(1)}, f32[128,128]{1,0:T(8,128)S(1)}, u32[]{:S(2)}, u32[]{:S(2)}) collective-permute-start(f32[128,128]{1,0:T(8,128)S(1)} %get-tuple-element.39), channel_id=1, source_target_pairs={{0,1},{1,0},{2,3},{3,2},{4,5},{5,4},{6,7},{7,6},{8,9},{9,8},{10,11... | collective-permute-start | bytes 196616 | tf_op jit(solution)/shard_map/ppermute | solution.py:326
  100.3 16.6 %collective-permute-start.13 = (f32[128,128]{1,0:T(8,128)S(1)}, f32[128,128]{1,0:T(8,128)S(1)}, u32[]{:S(2)}, u32[]{:S(2)}) collective-permute-start(f32[128,128]{1,0:T(8,128)S(1)} %get-tuple-element.40), channel_id=1, source_target_pairs={{1,2},{2,1},{3,4},{4,3},{5,6},{6,5},{7,8},{8,7},{9,10},{10,9},{11,... | collective-permute-start | bytes 196616 | tf_op jit(solution)/shard_map/ppermute | solution.py:326

commit v8 on v6

--- a/solution.py
+++ b/solution.py
@@ -132,19 +132,22 @@
 
 
 def proximal_kernel(
-    where_ref, slots_ref, near_ref, other_ref, late_ref, early_ref, omega_ref, out_ref
+    where_ref, slots_ref, near_ref, early_ref, far_early_ref, late_ref, far_late_ref,
+    other_ref, omega_ref, out_ref,
 ):
     j = where_ref[3]
     odd_tile = where_ref[4] == 1
     rows = lax.broadcasted_iota(jnp.int32, (BLK, BLK), 0)
     columns = lax.broadcasted_iota(jnp.int32, (BLK, BLK), 1)
+    early = early_ref[...] + far_early_ref[...]
+    late = late_ref[...] + far_late_ref[...]
     for e in range(3):
         slot = slots_ref[0, e, j]
         total = near_ref[e] + other_ref[e]
         if e == 0:
-            total = total + jnp.where(odd_tile, early_ref[...], late_ref[...]).T
+            total = total + jnp.where(odd_tile, early, late).T
         if e == 2:
-            total = total + jnp.where(odd_tile, late_ref[...], early_ref[...]).T
+            total = total + jnp.where(odd_tile, late, early).T
         gradient = total * (0.5 / SAMPLES)
         omega = omega_ref[0, e, 0]
         if e == 1:
@@ -258,31 +261,35 @@
     )(slots, where, below, centre, above, pieces)
 
 
-def edge_kernel(where_ref, near_ref, other_ref, late_ref, early_ref):
+def sum_kernel(where_ref, keep_ref, got_ref, first_ref, second_ref, sum_ref, early_ref, late_ref):
     odd_tile = where_ref[4] == 1
-    downward = near_ref[0] + other_ref[0]
-    upward = near_ref[2] + other_ref[2]
-    late_ref[...] = jnp.where(odd_tile, upward, downward)
-    early_ref[...] = jnp.where(odd_tile, downward, upward)
-
-
-def edge_values(where, near, other):
-    block = jax.ShapeDtypeStruct((BLK, BLK), f32)
-    return pl.pallas_call(
-        edge_kernel,
-        name="edge_values",
+    for e in range(3):
+        sum_ref[e] = keep_ref[0, e] + got_ref[0, e] + first_ref[0, e] + second_ref[e]
+    early_ref[...] = jnp.where(odd_tile, sum_ref[0], sum_ref[2])
+    late_ref[...] = jnp.where(odd_tile, sum_ref[2], sum_ref[0])
+
+
+def group_sum(where, keep, got, first, second):
+    return pl.pallas_call(
+        sum_kernel,
+        name="group_sum",
         grid=(1,),
-        out_shape=(block, block),
-        in_specs=[SMEM] + [full_spec((3, BLK, BLK))] * 2,
-        out_specs=(full_spec((BLK, BLK)),) * 2,
-        compiler_params=params(),
-        cost_estimate=pl.CostEstimate(
-            flops=4 * BLK * BLK, bytes_accessed=6 * 4 * BLK * BLK, transcendentals=0
-        ),
-    )(where, near, other)
-
-
-def proximal(where, slots, near, other, late, early, omega):
+        out_shape=tuple(
+            jax.ShapeDtypeStruct(shape, f32)
+            for shape in ((3, BLK, BLK), (BLK, BLK), (BLK, BLK))
+        ),
+        in_specs=[SMEM] + [full_spec(x.shape) for x in (keep, got, first, second)],
+        out_specs=tuple(
+            full_spec(shape) for shape in ((3, BLK, BLK), (BLK, BLK), (BLK, BLK))
+        ),
+        compiler_params=params(),
+        cost_estimate=pl.CostEstimate(
+            flops=9 * BLK * BLK, bytes_accessed=17 * 4 * BLK * BLK, transcendentals=0
+        ),
+    )(where, keep, got, first, second)
+
+
+def proximal(where, slots, sums, omega):
     block = pl.BlockSpec((BLK, BLK), lambda i, where, slots: (0, 0))
     triple = pl.BlockSpec((3, BLK, BLK), lambda i, where, slots: (0, 0, 0))
     own = pl.BlockSpec((1, 3, 1, BLK, BLK), lambda i, where, slots: (0, 0, where[3], 0, 0))
@@ -292,7 +299,7 @@
         grid_spec=pltpu.PrefetchScalarGridSpec(
             num_scalar_prefetch=2,
             grid=(1,),
-            in_specs=[triple, triple, block, block, own],
+            in_specs=[triple] + [block] * 4 + [triple, own],
             out_specs=pl.BlockSpec(
                 (1, 3, 1, BLK, BLK), lambda i, where, slots: (0, 0, 0, 0, 0)
             ),
@@ -302,7 +309,7 @@
         cost_estimate=pl.CostEstimate(
             flops=20 * 3 * BLK * BLK, bytes_accessed=1 << 19, transcendentals=0
         ),
-    )(where, slots, near, other, late, early, omega)
+    )(where, slots, *sums, omega)
 
 
 def shifted(value, axis, steps):
@@ -320,12 +327,19 @@
     return lax.ppermute(value, ("x", "core"), pairs)
 
 
-def edge_exchange(value, offset):
+def after(value, earlier):
+    return lax.optimization_barrier((value, earlier))[0]
+
+
+def edge_exchange(value, offset, flip=0):
     count = lax.axis_size("col")
     pairs = []
-    for t in range(offset, count + offset, 2):
-        pairs += [(t % count, (t + 1) % count), ((t + 1) % count, t % count)]
-    return lax.ppermute(value, "col", pairs)
+    for y in range(2):
+        for t in range(offset, count + offset, 2):
+            low, high = t % count, (t + 1) % count
+            pairs.append((y * count + low, (y ^ flip) * count + high))
+            pairs.append((y * count + high, (y ^ flip) * count + low))
+    return lax.ppermute(value, ("y_hi", "col"), pairs)
 
 
 def on_device(observations, omega, block_slots):
@@ -350,14 +364,22 @@
     far_first = x_exchange(far_pass + far_got[2:], 0)
     near_first = x_exchange(near_pass + near_got[2:], 0)
     far_second = x_exchange(far_keep[1] + far_got[1] + far_first[1], 1)
-    far_sum = far_keep[0] + far_got[0] + far_first[0] + far_second
-    other = shifted(far_sum, "y_hi", 1)
     near_second = x_exchange(near_keep[1] + near_got[1] + near_first[1], 1)
-    near_sum = near_keep[0] + near_got[0] + near_first[0] + near_second
-    late_out, early_out = edge_values(where, near_sum, other)
-    late = edge_exchange(late_out, 1)
-    early = edge_exchange(early_out, 0)
-    return proximal(where, block_slots, near_sum, other, late, early, omega)
+    far_sum, far_early, far_late = group_sum(
+        where, far_keep, far_got, far_first, far_second
+    )
+    near_sum, near_early, near_late = group_sum(
+        where, near_keep, near_got, near_first, near_second
+    )
+    sums = (
+        near_sum,
+        edge_exchange(near_early, 0),
+        edge_exchange(far_early, 0, 1),
+        edge_exchange(near_late, 1),
+        edge_exchange(far_late, 1, 1),
+        shifted(far_sum, "y_hi", 1),
+    )
+    return proximal(where, block_slots, sums, omega)
 
 
 def solution(mesh):

time: 116 us -> 119 us (1.026)
  the two profiles are of different devices: /device:TPU:6 before, /device:TPU:8 now
where the time goes in v8:
time: 119 us; the launch traced here: 118 us
  starting transfers between devices  65.7 us (55%)
  waiting for transfers between devices  33.3 us (28%)
  Pallas kernels  13.6 us (11%)
  local copies, waits for them, and re-layouts  5.16 us (4%)
    ppermute x6, starting transfers between devices, shifted(): return lax.ppermute(value, axis, pairs)  30.2 us
    ppermute x6, waiting for transfers between devices, shifted(): return lax.ppermute(value, axis, pairs)  22.3 us
    ppermute x4, starting transfers between devices, edge_exchange(): return lax.ppermute(value, ('y_hi', 'col'), pairs)  20.9 us
    ppermute x4, starting transfers between devices, x_exchange(): return lax.ppermute(value, ('x', 'core'), pairs)  14.7 us
    ppermute x4, waiting for transfers between devices, edge_exchange(): return lax.ppermute(value, ('y_hi', 'col'), pairs)  7.22 us
    pallas_call x3, Pallas kernels, partial(): pl.pallas_call(lambda *refs: partial_kernel(offset, first, *refs), name='...  6.29 us
    unnamed x7, local copies, waits for them, and re-layouts  3.8 us
    ppermute x4, waiting for transfers between devices, x_exchange(): return lax.ppermute(value, ('x', 'core'), pairs)  3.75 us
  transfers between devices with their start and end apart: 14, of which 6 were waited for; matrix products, arithmetic and copies ran while one was open for 2% of the time, Pallas kernels for 8%

profile of v8, /device:TPU:8, one launch (start us, length us, event | category | flops | bytes accessed | tf_op | source)
XLA Modules:
  0.0 118.2 jit_solution(7862295129084839469)
XLA Ops:
  0.0 3.5 %collective-permute-start = (f32[256,1024]{1,0:T(8,128)}, f32[256,1024]{1,0:T(8,128)S(1)}, u32[]{:S(2)}, u32[]{:S(2)}) collective-permute-start(f32[256,1024]{1,0:T(8,128)} %refs_1_.1), channel_id=1, source_target_pairs={{0,1},{1,2},{2,3},{3,4},{4,5},{5,6},{6,7},{7,8},{8,9},{9,10},{10,1... | collective-permute-start | bytes 3145736 | tf_op jit(solution)/shard_map/ppermute | solution.py:318
  3.5 1.3 %fusion.2 = (f32[128,1024]{1,0:T(8,128)S(1)}, f32[128,1024]{1,0:T(8,128)S(1)}) fusion(f32[256,1024]{1,0:T(8,128)} %refs_1_.1), kind=kLoop, calls=%fused_computation.8 | loop fusion | bytes 2097152 | tf_op jit(solution)/shard_map/slice | solution.py:351
  4.8 6.2 %collective-permute-start.2 = (f32[128,1024]{1,0:T(8,128)S(1)}, f32[128,1024]{1,0:T(8,128)S(1)}, u32[]{:S(2)}, u32[]{:S(2)}) collective-permute-start(f32[128,1024]{1,0:T(8,128)S(1)} %get-tuple-element.45), channel_id=1, source_target_pairs={{0,31},{1,0},{2,1},{3,2},{4,3},{5,4},{6,5},{7,6},{8,7},{9,8},{10,9... | collective-permute-start | bytes 1572872 | tf_op jit(solution)/shard_map/ppermute | solution.py:318
  10.9 8.6 %collective-permute-start.1 = (f32[128,1024]{1,0:T(8,128)S(1)}, f32[128,1024]{1,0:T(8,128)S(1)}, u32[]{:S(2)}, u32[]{:S(2)}) collective-permute-start(f32[128,1024]{1,0:T(8,128)S(1)} %get-tuple-element.46), channel_id=1, source_target_pairs={{0,31},{1,0},{2,1},{3,2},{4,3},{5,4},{6,5},{7,6},{8,7},{9,8},{10,9... | collective-permute-start | bytes 1572872 | tf_op jit(solution)/shard_map/ppermute | solution.py:318
  19.6 0.7 copy.9.refs_0_.slots_ref
  20.2 0.1 stack.23.where_ref
  20.3 0.0 copy-start
  20.3 1.9 %copy-done = f32[1,3,16,128,128]{4,3,2,1,0:T(8,128)S(1)} copy-done((f32[1,3,16,128,128]{4,3,2,1,0:T(8,128)S(1)}, f32[1,3,16,128,128]{4,3,2,1,0:T(8,128)}, u32[]{:S(2)}) %copy-start) | copy-done | bytes 3145752
  22.2 0.0 copy-start.2
  22.2 1.2 %copy-done.2 = f32[256,1024]{1,0:T(8,128)S(1)} copy-done((f32[256,1024]{1,0:T(8,128)S(1)}, f32[256,1024]{1,0:T(8,128)}, u32[]{:S(2)}) %copy-start.2) | copy-done | bytes 1048600
  23.4 0.0 copy-start.1
  23.5 2.3 %partial_residual.3 = (f32[8,256,128]{2,1,0:T(8,128)S(1)}, bf16[8,256,256]{2,1,0:T(8,128)(2,1)S(1)}) custom-call(s32[1,3,16]{2,1,0:T(4,128)S(1)} %copy.9.refs_0_.slots_ref, f32[256,1024]{1,0:T(8,128)S(1)} %copy-done.2, f32[1,3,16,128,128]{4,3,2,1,0:T(8,128)S(1)} %copy-done), custom_call_target="tpu_custom_call" | custom-call | flops 536870912 | bytes 5242880 | tf_op jit(solution)/shard_map/partial_residual/pallas_call | solution.py:193
  25.7 6.3 %collective-permute-done.refs_1_ = f32[256,1024]{1,0:T(8,128)S(1)} collective-permute-done((f32[256,1024]{1,0:T(8,128)}, f32[256,1024]{1,0:T(8,128)S(1)}, u32[]{:S(2)}, u32[]{:S(2)}) %collective-permute-start) | collective-permute-done | bytes 1048608 | tf_op jit(solution)/shard_map/ppermute | solution.py:318
  32.0 0.0 copy-done.1
  32.0 2.2 %partial_residual.4 = (f32[8,256,128]{2,1,0:T(8,128)S(1)}, bf16[8,256,256]{2,1,0:T(8,128)(2,1)S(1)}) custom-call(s32[1,3,16]{2,1,0:T(4,128)S(1)} %copy.9.refs_0_.slots_ref, f32[256,1024]{1,0:T(8,128)S(1)} %collective-permute-done.refs_1_, f32[1,3,16,128,128]{4,3,2,1,0:T(8,128)S(1)} %copy-done.1, f32[8,256,128]{2,1,0:T(8,128)S(1)} %get-tuple-element.25.refs_3_), custom_call_target="tpu_custom_call" | custom-call | flops 536870912 | bytes 5242880 | tf_op jit(solution)/shard_map/partial_residual/pallas_call | solution.py:193
  34.2 6.7 %collective-permute-done.2.refs_1_ = f32[128,1024]{1,0:T(8,128)S(1)} collective-permute-done((f32[128,1024]{1,0:T(8,128)S(1)}, f32[128,1024]{1,0:T(8,128)S(1)}, u32[]{:S(2)}, u32[]{:S(2)}) %collective-permute-start.2) | collective-permute-done | bytes 524320 | tf_op jit(solution)/shard_map/ppermute | solution.py:318
  40.9 1.8 %partial_residual.5 = (f32[8,256,128]{2,1,0:T(8,128)S(1)}, bf16[8,256,128]{2,1,0:T(8,128)(2,1)S(1)}) custom-call(s32[1,3,16]{2,1,0:T(4,128)S(1)} %copy.9.refs_0_.slots_ref, f32[128,1024]{1,0:T(8,128)S(1)} %collective-permute-done.2.refs_1_, f32[1,3,16,128,128]{4,3,2,1,0:T(8,128)S(1)} %copy-done.1, f32[8,256,128]{2,1,0:T(8,128)S(1)} %get-tuple-element.28.refs_3_), custom_call_target="tpu_custom_call" | custom-call | flops 268435456 | bytes 5242880 | tf_op jit(solution)/shard_map/partial_residual/pallas_call | solution.py:193
  42.7 9.3 %collective-permute-done.1.x_ref = f32[128,1024]{1,0:T(8,128)S(1)} collective-permute-done((f32[128,1024]{1,0:T(8,128)S(1)}, f32[128,1024]{1,0:T(8,128)S(1)}, u32[]{:S(2)}, u32[]{:S(2)}) %collective-permute-start.1) | collective-permute-done | bytes 524320 | tf_op jit(solution)/shard_map/ppermute | solution.py:318
  52.1 3.1 %far_blocks.1 = (f32[2,3,128,128]{3,2,1,0:T(8,128)S(1)}, f32[2,3,128,128]{3,2,1,0:T(8,128)S(1)}, f32[4,3,128,128]{3,2,1,0:T(8,128)S(1)}, bf16[8,256,256]{2,1,0:T(8,128)(2,1)S(1)}, bf16[8,256,256]{2,1,0:T(8,128)(2,1)S(1)}) custom-call(s32[1,3,16]{2,1,0:T(4,128)S(1)} %copy.9.refs_0_.slots_ref, s32[5]{0:T(128)S(1)} %stack.23.where_ref, ...), custom_call_target="tpu_custom_call" | custom-call | flops 1342177280 | bytes 8388608 | tf_op jit(solution)/shard_map/far_blocks/pallas_call | solution.py:219
  55.2 1.9 %collective-permute-start.7 = (f32[4,3,128,128]{3,2,1,0:T(8,128)S(1)}, f32[4,3,128,128]{3,2,1,0:T(8,128)S(1)}, u32[]{:S(2)}, u32[]{:S(2)}) collective-permute-start(f32[4,3,128,128]{3,2,1,0:T(8,128)S(1)} %get-tuple-element.39), channel_id=1, source_target_pairs={{0,32},{32,0},{1,33},{33,1},{2,34},{34,2},{3,35},{35,3},{4,36},{36... | collective-permute-start | bytes 2359304 | tf_op jit(solution)/shard_map/ppermute | solution.py:318
  57.1 1.6 %near_blocks.1 = (f32[2,3,128,128]{3,2,1,0:T(8,128)S(1)}, f32[2,3,128,128]{3,2,1,0:T(8,128)S(1)}, f32[4,3,128,128]{3,2,1,0:T(8,128)S(1)}) custom-call(s32[1,3,16]{2,1,0:T(4,128)S(1)} %copy.9.refs_0_.slots_ref, s32[5]{0:T(128)S(1)} %stack.23.where_ref, bf16[8,256,256]{2,1,0:T(8,128)(2,1)S(1)} %get-tuple-element.26.below_ref, ...), custom_call_target="tpu_custom_call" | custom-call | flops 805306368 | bytes 8388608 | tf_op jit(solution)/shard_map/near_blocks/pallas_call | solution.py:248
  58.7 2.4 %collective-permute-start.3 = (f32[4,3,128,128]{3,2,1,0:T(8,128)S(1)}, f32[4,3,128,128]{3,2,1,0:T(8,128)S(1)}, u32[]{:S(2)}, u32[]{:S(2)}) collective-permute-start(f32[4,3,128,128]{3,2,1,0:T(8,128)S(1)} %get-tuple-element.34), channel_id=1, source_target_pairs={{0,32},{32,0},{1,33},{33,1},{2,34},{34,2},{3,35},{35,3},{4,36},{36... | collective-permute-start | bytes 2359304 | tf_op jit(solution)/shard_map/ppermute | solution.py:318
  61.1 0.0 collective-permute-done.7.got_ref
  61.2 3.4 %collective-permute-start.8 = (f32[2,3,128,128]{3,2,1,0:T(8,128)S(1)}, f32[2,3,128,128]{3,2,1,0:T(8,128)S(1)}, u32[]{:S(2)}, u32[]{:S(2)}) collective-permute-start(f32[2,3,128,128]{3,2,1,0:T(8,128)S(1)} %slice_add_fusion), channel_id=1, source_target_pairs={{0,128},{32,416},{128,0},{160,288},{256,384},{288,160},{384,256},{... | collective-permute-start | bytes 1179656 | tf_op jit(solution)/shard_map/ppermute | solution.py:327
  64.6 0.0 collective-permute-done.3.got_ref
  64.6 0.1 slice_add_fusion.1
  64.7 2.4 %collective-permute-start.4 = (f32[2,3,128,128]{3,2,1,0:T(8,128)S(1)}, f32[2,3,128,128]{3,2,1,0:T(8,128)S(1)}, u32[]{:S(2)}, u32[]{:S(2)}) collective-permute-start(f32[2,3,128,128]{3,2,1,0:T(8,128)S(1)} %slice_add_fusion.1), channel_id=1, source_target_pairs={{0,128},{32,416},{128,0},{160,288},{256,384},{288,160},{384,256},{... | collective-permute-start | bytes 1179656 | tf_op jit(solution)/shard_map/ppermute | solution.py:327
  67.1 3.7 %collective-permute-done.8.first_ref = f32[2,3,128,128]{3,2,1,0:T(8,128)S(1)} collective-permute-done((f32[2,3,128,128]{3,2,1,0:T(8,128)S(1)}, f32[2,3,128,128]{3,2,1,0:T(8,128)S(1)}, u32[]{:S(2)}, u32[]{:S(2)}) %collective-permute-start.8) | collective-permute-done | bytes 393248 | tf_op jit(solution)/shard_map/ppermute | solution.py:327
  70.9 4.7 %collective-permute-start.9 = (f32[3,128,128]{2,1,0:T(8,128)S(1)}, f32[3,128,128]{2,1,0:T(8,128)S(1)}, u32[]{:S(2)}, u32[]{:S(2)}) collective-permute-start(f32[3,128,128]{2,1,0:T(8,128)S(1)} %fusion), channel_id=1, source_target_pairs={{0,384},{32,160},{128,256},{160,32},{256,128},{288,416},{384,0},{4... | collective-permute-start | bytes 589832 | tf_op jit(solution)/shard_map/ppermute | solution.py:327
  75.6 0.0 collective-permute-done.4.first_ref
  75.6 4.2 %collective-permute-start.5 = (f32[3,128,128]{2,1,0:T(8,128)S(1)}, f32[3,128,128]{2,1,0:T(8,128)S(1)}, u32[]{:S(2)}, u32[]{:S(2)}) collective-permute-start(f32[3,128,128]{2,1,0:T(8,128)S(1)} %fusion.1), channel_id=1, source_target_pairs={{0,384},{32,160},{128,256},{160,32},{256,128},{288,416},{384,0},{4... | collective-permute-start | bytes 589832 | tf_op jit(solution)/shard_map/ppermute | solution.py:327
  79.8 0.0 collective-permute-done.9.second_ref
  79.8 0.6 group_sum.3
  80.4 7.6 %collective-permute-start.13 = (f32[3,128,128]{2,1,0:T(8,128)S(1)}, f32[3,128,128]{2,1,0:T(8,128)S(1)}, u32[]{:S(2)}, u32[]{:S(2)}) collective-permute-start(f32[3,128,128]{2,1,0:T(8,128)S(1)} %get-tuple-element.44), channel_id=1, source_target_pairs={{0,64},{64,0},{1,65},{65,1},{2,66},{66,2},{3,67},{67,3},{4,68},{68... | collective-permute-start | bytes 589832 | tf_op jit(solution)/shard_map/ppermute | solution.py:318
  88.0 0.0 collective-permute-done.5.second_ref
  88.0 0.6 group_sum.2
  88.6 3.3 %collective-permute-start.6 = (f32[128,128]{1,0:T(8,128)S(1)}, f32[128,128]{1,0:T(8,128)S(1)}, u32[]{:S(2)}, u32[]{:S(2)}) collective-permute-start(f32[128,128]{1,0:T(8,128)S(1)} %get-tuple-element.37), channel_id=1, source_target_pairs={{0,1},{1,0},{2,3},{3,2},{4,5},{5,4},{6,7},{7,6},{8,9},{9,8},{10,11... | collective-permute-start | bytes 196616 | tf_op jit(solution)/shard_map/ppermute | solution.py:342
  91.9 1.9 %collective-permute-start.11 = (f32[128,128]{1,0:T(8,128)S(1)}, f32[128,128]{1,0:T(8,128)S(1)}, u32[]{:S(2)}, u32[]{:S(2)}) collective-permute-start(f32[128,128]{1,0:T(8,128)S(1)} %get-tuple-element.42), channel_id=1, source_target_pairs={{1,2},{2,1},{3,4},{4,3},{5,6},{6,5},{7,8},{8,7},{9,10},{10,9},{11,... | collective-permute-start | bytes 196616 | tf_op jit(solution)/shard_map/ppermute | solution.py:342
  93.8 13.8 %collective-permute-start.10 = (f32[128,128]{1,0:T(8,128)S(1)}, f32[128,128]{1,0:T(8,128)S(1)}, u32[]{:S(2)}, u32[]{:S(2)}) collective-permute-start(f32[128,128]{1,0:T(8,128)S(1)} %get-tuple-element.41), channel_id=1, source_target_pairs={{0,65},{1,64},{2,67},{3,66},{4,69},{5,68},{6,71},{7,70},{8,73},{9,... | collective-permute-start | bytes 196616 | tf_op jit(solution)/shard_map/ppermute | solution.py:342
  107.6 1.9 %collective-permute-start.12 = (f32[128,128]{1,0:T(8,128)S(1)}, f32[128,128]{1,0:T(8,128)S(1)}, u32[]{:S(2)}, u32[]{:S(2)}) collective-permute-start(f32[128,128]{1,0:T(8,128)S(1)} %get-tuple-element.43), channel_id=1, source_target_pairs={{1,66},{2,65},{3,68},{4,67},{5,70},{6,69},{7,72},{8,71},{9,74},{10... | collective-permute-start | bytes 196616 | tf_op jit(solution)/shard_map/ppermute | solution.py:342
  109.5 0.0 collective-permute-done.6.early_ref
  109.6 0.0 collective-permute-done.11.late_ref
  109.6 1.6 %collective-permute-done.10.far_early_ref = f32[128,128]{1,0:T(8,128)S(1)} collective-permute-done((f32[128,128]{1,0:T(8,128)S(1)}, f32[128,128]{1,0:T(8,128)S(1)}, u32[]{:S(2)}, u32[]{:S(2)}) %collective-permute-start.10) | collective-permute-done | bytes 65568 | tf_op jit(solution)/shard_map/ppermute | solution.py:342
  111.1 5.7 %collective-permute-done.12.far_late_ref = f32[128,128]{1,0:T(8,128)S(1)} collective-permute-done((f32[128,128]{1,0:T(8,128)S(1)}, f32[128,128]{1,0:T(8,128)S(1)}, u32[]{:S(2)}, u32[]{:S(2)}) %collective-permute-start.12) | collective-permute-done | bytes 65568 | tf_op jit(solution)/shard_map/ppermute | solution.py:342
  116.8 0.0 collective-permute-done.13.other_ref
  116.8 1.4 %proximal.1 = f32[1,3,1,128,128]{4,3,2,1,0:T(8,128)} custom-call(s32[5]{0:T(128)S(1)} %stack.23.where_ref, s32[1,3,16]{2,1,0:T(4,128)S(1)} %copy.9.refs_0_.slots_ref, f32[3,128,128]{2,1,0:T(8,128)S(1)} %get-tuple-element.36.near_ref, f32[128,128]{1,0:T(8,128)S(1)} %collective-permute-done.6.early_ref, f32[128,128]{1,0:T(8,128)S(1)} %collective-permute-done.10.far_early_ref, ...), custom_call_target="tpu_custom_call" | custom-call | flops 983040 | bytes 524288 | tf_op jit(solution)/shard_map/proximal/pallas_call | solution.py:296
  (3 shorter events, 0.1 us)
Async XLA Ops:
  0.0 32.0 %collective-permute-start = (f32[256,1024]{1,0:T(8,128)}, f32[256,1024]{1,0:T(8,128)S(1)}, u32[]{:S(2)}, u32[]{:S(2)}) collective-permute-start(f32[256,1024]{1,0:T(8,128)} %refs_1_.1), channel_id=1, source_target_pairs={{0,1},{1,2},{2,3},{3,4},{4,5},{5,6},{6,7},{7,8},{8,9},{9,10},{10,1... | collective-permute-start | bytes 3145736 | tf_op jit(solution)/shard_map/ppermute | solution.py:318
  4.8 36.2 %collective-permute-start.2 = (f32[128,1024]{1,0:T(8,128)S(1)}, f32[128,1024]{1,0:T(8,128)S(1)}, u32[]{:S(2)}, u32[]{:S(2)}) collective-permute-start(f32[128,1024]{1,0:T(8,128)S(1)} %get-tuple-element.45), channel_id=1, source_target_pairs={{0,31},{1,0},{2,1},{3,2},{4,3},{5,4},{6,5},{7,6},{8,7},{9,8},{10,9... | collective-permute-start | bytes 1572872 | tf_op jit(solution)/shard_map/ppermute | solution.py:318
  10.9 41.1 %collective-permute-start.1 = (f32[128,1024]{1,0:T(8,128)S(1)}, f32[128,1024]{1,0:T(8,128)S(1)}, u32[]{:S(2)}, u32[]{:S(2)}) collective-permute-start(f32[128,1024]{1,0:T(8,128)S(1)} %get-tuple-element.46), channel_id=1, source_target_pairs={{0,31},{1,0},{2,1},{3,2},{4,3},{5,4},{6,5},{7,6},{8,7},{9,8},{10,9... | collective-permute-start | bytes 1572872 | tf_op jit(solution)/shard_map/ppermute | solution.py:318
  20.3 1.9 %copy-start = (f32[1,3,16,128,128]{4,3,2,1,0:T(8,128)S(1)}, f32[1,3,16,128,128]{4,3,2,1,0:T(8,128)}, u32[]{:S(2)}) copy-start(f32[1,3,16,128,128]{4,3,2,1,0:T(8,128)} %omega_ref.3) | copy-start | bytes 9437188
  22.2 1.2 %copy-start.2 = (f32[256,1024]{1,0:T(8,128)S(1)}, f32[256,1024]{1,0:T(8,128)}, u32[]{:S(2)}) copy-start(f32[256,1024]{1,0:T(8,128)} %refs_1_.1) | copy-start | bytes 3145732
  23.4 8.6 %copy-start.1 = (f32[1,3,16,128,128]{4,3,2,1,0:T(8,128)S(1)}, f32[1,3,16,128,128]{4,3,2,1,0:T(8,128)}, u32[]{:S(2)}) copy-start(f32[1,3,16,128,128]{4,3,2,1,0:T(8,128)} %omega_ref.3) | copy-start | bytes 9437188
  55.2 5.9 %collective-permute-start.7 = (f32[4,3,128,128]{3,2,1,0:T(8,128)S(1)}, f32[4,3,128,128]{3,2,1,0:T(8,128)S(1)}, u32[]{:S(2)}, u32[]{:S(2)}) collective-permute-start(f32[4,3,128,128]{3,2,1,0:T(8,128)S(1)} %get-tuple-element.39), channel_id=1, source_target_pairs={{0,32},{32,0},{1,33},{33,1},{2,34},{34,2},{3,35},{35,3},{4,36},{36... | collective-permute-start | bytes 2359304 | tf_op jit(solution)/shard_map/ppermute | solution.py:318
  58.7 5.9 %collective-permute-start.3 = (f32[4,3,128,128]{3,2,1,0:T(8,128)S(1)}, f32[4,3,128,128]{3,2,1,0:T(8,128)S(1)}, u32[]{:S(2)}, u32[]{:S(2)}) collective-permute-start(f32[4,3,128,128]{3,2,1,0:T(8,128)S(1)} %get-tuple-element.34), channel_id=1, source_target_pairs={{0,32},{32,0},{1,33},{33,1},{2,34},{34,2},{3,35},{35,3},{4,36},{36... | collective-permute-start | bytes 2359304 | tf_op jit(solution)/shard_map/ppermute | solution.py:318
  61.2 9.7 %collective-permute-start.8 = (f32[2,3,128,128]{3,2,1,0:T(8,128)S(1)}, f32[2,3,128,128]{3,2,1,0:T(8,128)S(1)}, u32[]{:S(2)}, u32[]{:S(2)}) collective-permute-start(f32[2,3,128,128]{3,2,1,0:T(8,128)S(1)} %slice_add_fusion), channel_id=1, source_target_pairs={{0,128},{32,416},{128,0},{160,288},{256,384},{288,160},{384,256},{... | collective-permute-start | bytes 1179656 | tf_op jit(solution)/shard_map/ppermute | solution.py:327
  64.7 10.9 %collective-permute-start.4 = (f32[2,3,128,128]{3,2,1,0:T(8,128)S(1)}, f32[2,3,128,128]{3,2,1,0:T(8,128)S(1)}, u32[]{:S(2)}, u32[]{:S(2)}) collective-permute-start(f32[2,3,128,128]{3,2,1,0:T(8,128)S(1)} %slice_add_fusion.1), channel_id=1, source_target_pairs={{0,128},{32,416},{128,0},{160,288},{256,384},{288,160},{384,256},{... | collective-permute-start | bytes 1179656 | tf_op jit(solution)/shard_map/ppermute | solution.py:327
  70.9 8.9 %collective-permute-start.9 = (f32[3,128,128]{2,1,0:T(8,128)S(1)}, f32[3,128,128]{2,1,0:T(8,128)S(1)}, u32[]{:S(2)}, u32[]{:S(2)}) collective-permute-start(f32[3,128,128]{2,1,0:T(8,128)S(1)} %fusion), channel_id=1, source_target_pairs={{0,384},{32,160},{128,256},{160,32},{256,128},{288,416},{384,0},{4... | collective-permute-start | bytes 589832 | tf_op jit(solution)/shard_map/ppermute | solution.py:327
  75.6 12.4 %collective-permute-start.5 = (f32[3,128,128]{2,1,0:T(8,128)S(1)}, f32[3,128,128]{2,1,0:T(8,128)S(1)}, u32[]{:S(2)}, u32[]{:S(2)}) collective-permute-start(f32[3,128,128]{2,1,0:T(8,128)S(1)} %fusion.1), channel_id=1, source_target_pairs={{0,384},{32,160},{128,256},{160,32},{256,128},{288,416},{384,0},{4... | collective-permute-start | bytes 589832 | tf_op jit(solution)/shard_map/ppermute | solution.py:327
  80.4 36.4 %collective-permute-start.13 = (f32[3,128,128]{2,1,0:T(8,128)S(1)}, f32[3,128,128]{2,1,0:T(8,128)S(1)}, u32[]{:S(2)}, u32[]{:S(2)}) collective-permute-start(f32[3,128,128]{2,1,0:T(8,128)S(1)} %get-tuple-element.44), channel_id=1, source_target_pairs={{0,64},{64,0},{1,65},{65,1},{2,66},{66,2},{3,67},{67,3},{4,68},{68... | collective-permute-start | bytes 589832 | tf_op jit(solution)/shard_map/ppermute | solution.py:318
  88.6 20.9 %collective-permute-start.6 = (f32[128,128]{1,0:T(8,128)S(1)}, f32[128,128]{1,0:T(8,128)S(1)}, u32[]{:S(2)}, u32[]{:S(2)}) collective-permute-start(f32[128,128]{1,0:T(8,128)S(1)} %get-tuple-element.37), channel_id=1, source_target_pairs={{0,1},{1,0},{2,3},{3,2},{4,5},{5,4},{6,7},{7,6},{8,9},{9,8},{10,11... | collective-permute-start | bytes 196616 | tf_op jit(solution)/shard_map/ppermute | solution.py:342
  91.9 17.6 %collective-permute-start.11 = (f32[128,128]{1,0:T(8,128)S(1)}, f32[128,128]{1,0:T(8,128)S(1)}, u32[]{:S(2)}, u32[]{:S(2)}) collective-permute-start(f32[128,128]{1,0:T(8,128)S(1)} %get-tuple-element.42), channel_id=1, source_target_pairs={{1,2},{2,1},{3,4},{4,3},{5,6},{6,5},{7,8},{8,7},{9,10},{10,9},{11,... | collective-permute-start | bytes 196616 | tf_op jit(solution)/shard_map/ppermute | solution.py:342
  93.8 17.3 %collective-permute-start.10 = (f32[128,128]{1,0:T(8,128)S(1)}, f32[128,128]{1,0:T(8,128)S(1)}, u32[]{:S(2)}, u32[]{:S(2)}) collective-permute-start(f32[128,128]{1,0:T(8,128)S(1)} %get-tuple-element.41), channel_id=1, source_target_pairs={{0,65},{1,64},{2,67},{3,66},{4,69},{5,68},{6,71},{7,70},{8,73},{9,... | collective-permute-start | bytes 196616 | tf_op jit(solution)/shard_map/ppermute | solution.py:342
  107.6 9.2 %collective-permute-start.12 = (f32[128,128]{1,0:T(8,128)S(1)}, f32[128,128]{1,0:T(8,128)S(1)}, u32[]{:S(2)}, u32[]{:S(2)}) collective-permute-start(f32[128,128]{1,0:T(8,128)S(1)} %get-tuple-element.43), channel_id=1, source_target_pairs={{1,66},{2,65},{3,68},{4,67},{5,70},{6,69},{7,72},{8,71},{9,74},{10... | collective-permute-start | bytes 196616 | tf_op jit(solution)/shard_map/ppermute | solution.py:342

commit v9 on v6

--- a/solution.py
+++ b/solution.py
@@ -132,7 +132,7 @@
 
 
 def proximal_kernel(
-    where_ref, slots_ref, near_ref, other_ref, late_ref, early_ref, omega_ref, out_ref
+    where_ref, slots_ref, near_ref, other_ref, early_ref, late_ref, omega_ref, out_ref
 ):
     j = where_ref[3]
     odd_tile = where_ref[4] == 1
@@ -282,7 +282,7 @@
     )(where, near, other)
 
 
-def proximal(where, slots, near, other, late, early, omega):
+def proximal(where, slots, near, other, early, late, omega):
     block = pl.BlockSpec((BLK, BLK), lambda i, where, slots: (0, 0))
     triple = pl.BlockSpec((3, BLK, BLK), lambda i, where, slots: (0, 0, 0))
     own = pl.BlockSpec((1, 3, 1, BLK, BLK), lambda i, where, slots: (0, 0, where[3], 0, 0))
@@ -302,7 +302,7 @@
         cost_estimate=pl.CostEstimate(
             flops=20 * 3 * BLK * BLK, bytes_accessed=1 << 19, transcendentals=0
         ),
-    )(where, slots, near, other, late, early, omega)
+    )(where, slots, near, other, early, late, omega)
 
 
 def shifted(value, axis, steps):
@@ -357,7 +357,7 @@
     late_out, early_out = edge_values(where, near_sum, other)
     late = edge_exchange(late_out, 1)
     early = edge_exchange(early_out, 0)
-    return proximal(where, block_slots, near_sum, other, late, early, omega)
+    return proximal(where, block_slots, near_sum, other, early, late, omega)
 
 
 def solution(mesh):

time: 116 us -> 115 us (level)
    ppermute x2, waiting for transfers between devices: 4.23 us -> 2.28 us  [edge_exchange(): return lax.ppermute(value, 'col', pairs)]
    ppermute x6, waiting for transfers between devices: 27.4 us -> 28.6 us  [shifted(): return lax.ppermute(value, axis, pairs)]
  transfers between devices with their start and end apart: 12 -> 12, of which waited for: 9 -> 8; matrix products, arithmetic and copies ran while one was open for 2% -> 2% of each run, Pallas kernels for 7% -> 7%
where the time goes in v9:
time: 115 us; the launch traced here: 114 us
  starting transfers between devices  57.7 us (50%)
  waiting for transfers between devices  38.1 us (33%)
  Pallas kernels  12.9 us (11%)
  local copies, waits for them, and re-layouts  5.16 us (4%)
    ppermute x6, starting transfers between devices, shifted(): return lax.ppermute(value, axis, pairs)  31.7 us
    ppermute x6, waiting for transfers between devices, shifted(): return lax.ppermute(value, axis, pairs)  28.6 us
    ppermute x2, starting transfers between devices, edge_exchange(): return lax.ppermute(value, 'col', pairs)  14.9 us
    ppermute x4, starting transfers between devices, x_exchange(): return lax.ppermute(value, ('x', 'core'), pairs)  11.1 us
    ppermute x4, waiting for transfers between devices, x_exchange(): return lax.ppermute(value, ('x', 'core'), pairs)  7.2 us
    pallas_call x3, Pallas kernels, partial(): pl.pallas_call(lambda *refs: partial_kernel(offset, first, *refs), name='...  6.29 us
    unnamed x7, local copies, waits for them, and re-layouts  3.8 us
    pallas_call x1, Pallas kernels, far_blocks(): pl.pallas_call(far_kernel, name='far_blocks', grid=(1,), out_shape=GROUP_...  3.12 us
  transfers between devices with their start and end apart: 12, of which 8 were waited for; matrix products, arithmetic and copies ran while one was open for 2% of the time, Pallas kernels for 7%

profile of v9, /device:TPU:6, one launch (start us, length us, event | category | flops | bytes accessed | tf_op | source)
XLA Modules:
  0.0 114.3 jit_solution(17526968208954411665)
XLA Ops:
  0.0 3.5 %collective-permute-start = (f32[256,1024]{1,0:T(8,128)}, f32[256,1024]{1,0:T(8,128)S(1)}, u32[]{:S(2)}, u32[]{:S(2)}) collective-permute-start(f32[256,1024]{1,0:T(8,128)} %refs_1_.1), channel_id=1, source_target_pairs={{0,1},{1,2},{2,3},{3,4},{4,5},{5,6},{6,7},{7,8},{8,9},{9,10},{10,1... | collective-permute-start | bytes 3145736 | tf_op jit(solution)/shard_map/ppermute | solution.py:311
  3.5 1.3 %fusion.6 = (f32[128,1024]{1,0:T(8,128)S(1)}, f32[128,1024]{1,0:T(8,128)S(1)}) fusion(f32[256,1024]{1,0:T(8,128)} %refs_1_.1), kind=kLoop, calls=%fused_computation.16 | loop fusion | bytes 2097152 | tf_op jit(solution)/shard_map/slice | solution.py:337
  4.8 12.4 %collective-permute-start.2 = (f32[128,1024]{1,0:T(8,128)S(1)}, f32[128,1024]{1,0:T(8,128)S(1)}, u32[]{:S(2)}, u32[]{:S(2)}) collective-permute-start(f32[128,1024]{1,0:T(8,128)S(1)} %get-tuple-element.37), channel_id=1, source_target_pairs={{0,31},{1,0},{2,1},{3,2},{4,3},{5,4},{6,5},{7,6},{8,7},{9,8},{10,9... | collective-permute-start | bytes 1572872 | tf_op jit(solution)/shard_map/ppermute | solution.py:311
  17.2 3.9 %collective-permute-start.1 = (f32[128,1024]{1,0:T(8,128)S(1)}, f32[128,1024]{1,0:T(8,128)S(1)}, u32[]{:S(2)}, u32[]{:S(2)}) collective-permute-start(f32[128,1024]{1,0:T(8,128)S(1)} %get-tuple-element.38), channel_id=1, source_target_pairs={{0,31},{1,0},{2,1},{3,2},{4,3},{5,4},{6,5},{7,6},{8,7},{9,8},{10,9... | collective-permute-start | bytes 1572872 | tf_op jit(solution)/shard_map/ppermute | solution.py:311
  21.1 0.7 copy.9.refs_0_.slots_ref
  21.8 0.1 stack.23.where_ref
  21.9 0.0 copy-start
  21.9 1.9 %copy-done = f32[1,3,16,128,128]{4,3,2,1,0:T(8,128)S(1)} copy-done((f32[1,3,16,128,128]{4,3,2,1,0:T(8,128)S(1)}, f32[1,3,16,128,128]{4,3,2,1,0:T(8,128)}, u32[]{:S(2)}) %copy-start) | copy-done | bytes 3145752
  23.8 0.0 copy-start.2
  23.8 1.2 %copy-done.2 = f32[256,1024]{1,0:T(8,128)S(1)} copy-done((f32[256,1024]{1,0:T(8,128)S(1)}, f32[256,1024]{1,0:T(8,128)}, u32[]{:S(2)}) %copy-start.2) | copy-done | bytes 1048600
  25.0 0.0 copy-start.1
  25.0 2.3 %partial_residual.3 = (f32[8,256,128]{2,1,0:T(8,128)S(1)}, bf16[8,256,256]{2,1,0:T(8,128)(2,1)S(1)}) custom-call(s32[1,3,16]{2,1,0:T(4,128)S(1)} %copy.9.refs_0_.slots_ref, f32[256,1024]{1,0:T(8,128)S(1)} %copy-done.2, f32[1,3,16,128,128]{4,3,2,1,0:T(8,128)S(1)} %copy-done), custom_call_target="tpu_custom_call" | custom-call | flops 536870912 | bytes 5242880 | tf_op jit(solution)/shard_map/partial_residual/pallas_call | solution.py:190
  27.3 10.9 %collective-permute-done.refs_1_ = f32[256,1024]{1,0:T(8,128)S(1)} collective-permute-done((f32[256,1024]{1,0:T(8,128)}, f32[256,1024]{1,0:T(8,128)S(1)}, u32[]{:S(2)}, u32[]{:S(2)}) %collective-permute-start) | collective-permute-done | bytes 1048608 | tf_op jit(solution)/shard_map/ppermute | solution.py:311
  38.2 0.0 copy-done.1
  38.2 2.2 %partial_residual.4 = (f32[8,256,128]{2,1,0:T(8,128)S(1)}, bf16[8,256,256]{2,1,0:T(8,128)(2,1)S(1)}) custom-call(s32[1,3,16]{2,1,0:T(4,128)S(1)} %copy.9.refs_0_.slots_ref, f32[256,1024]{1,0:T(8,128)S(1)} %collective-permute-done.refs_1_, f32[1,3,16,128,128]{4,3,2,1,0:T(8,128)S(1)} %copy-done.1, f32[8,256,128]{2,1,0:T(8,128)S(1)} %get-tuple-element.21.refs_3_), custom_call_target="tpu_custom_call" | custom-call | flops 536870912 | bytes 5242880 | tf_op jit(solution)/shard_map/partial_residual/pallas_call | solution.py:190
  40.5 1.5 %collective-permute-done.2.refs_1_ = f32[128,1024]{1,0:T(8,128)S(1)} collective-permute-done((f32[128,1024]{1,0:T(8,128)S(1)}, f32[128,1024]{1,0:T(8,128)S(1)}, u32[]{:S(2)}, u32[]{:S(2)}) %collective-permute-start.2) | collective-permute-done | bytes 524320 | tf_op jit(solution)/shard_map/ppermute | solution.py:311
  41.9 1.8 %partial_residual.5 = (f32[8,256,128]{2,1,0:T(8,128)S(1)}, bf16[8,256,128]{2,1,0:T(8,128)(2,1)S(1)}) custom-call(s32[1,3,16]{2,1,0:T(4,128)S(1)} %copy.9.refs_0_.slots_ref, f32[128,1024]{1,0:T(8,128)S(1)} %collective-permute-done.2.refs_1_, f32[1,3,16,128,128]{4,3,2,1,0:T(8,128)S(1)} %copy-done.1, f32[8,256,128]{2,1,0:T(8,128)S(1)} %get-tuple-element.24.refs_3_), custom_call_target="tpu_custom_call" | custom-call | flops 268435456 | bytes 5242880 | tf_op jit(solution)/shard_map/partial_residual/pallas_call | solution.py:190
  43.7 9.3 %collective-permute-done.1.x_ref = f32[128,1024]{1,0:T(8,128)S(1)} collective-permute-done((f32[128,1024]{1,0:T(8,128)S(1)}, f32[128,1024]{1,0:T(8,128)S(1)}, u32[]{:S(2)}, u32[]{:S(2)}) %collective-permute-start.1) | collective-permute-done | bytes 524320 | tf_op jit(solution)/shard_map/ppermute | solution.py:311
  53.1 3.1 %far_blocks.1 = (f32[2,3,128,128]{3,2,1,0:T(8,128)S(1)}, f32[2,3,128,128]{3,2,1,0:T(8,128)S(1)}, f32[4,3,128,128]{3,2,1,0:T(8,128)S(1)}, bf16[8,256,256]{2,1,0:T(8,128)(2,1)S(1)}, bf16[8,256,256]{2,1,0:T(8,128)(2,1)S(1)}) custom-call(s32[1,3,16]{2,1,0:T(4,128)S(1)} %copy.9.refs_0_.slots_ref, s32[5]{0:T(128)S(1)} %stack.23.where_ref, ...), custom_call_target="tpu_custom_call" | custom-call | flops 1342177280 | bytes 8388608 | tf_op jit(solution)/shard_map/far_blocks/pallas_call | solution.py:216
  56.2 1.9 %collective-permute-start.6 = (f32[4,3,128,128]{3,2,1,0:T(8,128)S(1)}, f32[4,3,128,128]{3,2,1,0:T(8,128)S(1)}, u32[]{:S(2)}, u32[]{:S(2)}) collective-permute-start(f32[4,3,128,128]{3,2,1,0:T(8,128)S(1)} %get-tuple-element.33), channel_id=1, source_target_pairs={{0,32},{32,0},{1,33},{33,1},{2,34},{34,2},{3,35},{35,3},{4,36},{36... | collective-permute-start | bytes 2359304 | tf_op jit(solution)/shard_map/ppermute | solution.py:311
  58.1 1.6 %near_blocks.1 = (f32[2,3,128,128]{3,2,1,0:T(8,128)S(1)}, f32[2,3,128,128]{3,2,1,0:T(8,128)S(1)}, f32[4,3,128,128]{3,2,1,0:T(8,128)S(1)}) custom-call(s32[1,3,16]{2,1,0:T(4,128)S(1)} %copy.9.refs_0_.slots_ref, s32[5]{0:T(128)S(1)} %stack.23.where_ref, bf16[8,256,256]{2,1,0:T(8,128)(2,1)S(1)} %get-tuple-element.22.below_ref, ...), custom_call_target="tpu_custom_call" | custom-call | flops 805306368 | bytes 8388608 | tf_op jit(solution)/shard_map/near_blocks/pallas_call | solution.py:245
  59.7 2.4 %collective-permute-start.3 = (f32[4,3,128,128]{3,2,1,0:T(8,128)S(1)}, f32[4,3,128,128]{3,2,1,0:T(8,128)S(1)}, u32[]{:S(2)}, u32[]{:S(2)}) collective-permute-start(f32[4,3,128,128]{3,2,1,0:T(8,128)S(1)} %get-tuple-element.30), channel_id=1, source_target_pairs={{0,32},{32,0},{1,33},{33,1},{2,34},{34,2},{3,35},{35,3},{4,36},{36... | collective-permute-start | bytes 2359304 | tf_op jit(solution)/shard_map/ppermute | solution.py:311
  62.1 0.0 collective-permute-done.6
  62.2 2.7 %collective-permute-start.7 = (f32[2,3,128,128]{3,2,1,0:T(8,128)S(1)}, f32[2,3,128,128]{3,2,1,0:T(8,128)S(1)}, u32[]{:S(2)}, u32[]{:S(2)}) collective-permute-start(f32[2,3,128,128]{3,2,1,0:T(8,128)S(1)} %slice_add_fusion), channel_id=1, source_target_pairs={{0,128},{32,416},{128,0},{160,288},{256,384},{288,160},{384,256},{... | collective-permute-start | bytes 1179656 | tf_op jit(solution)/shard_map/ppermute | solution.py:320
  65.0 0.0 collective-permute-done.3
  65.0 3.1 %collective-permute-start.4 = (f32[2,3,128,128]{3,2,1,0:T(8,128)S(1)}, f32[2,3,128,128]{3,2,1,0:T(8,128)S(1)}, u32[]{:S(2)}, u32[]{:S(2)}) collective-permute-start(f32[2,3,128,128]{3,2,1,0:T(8,128)S(1)} %slice_add_fusion.1), channel_id=1, source_target_pairs={{0,128},{32,416},{128,0},{160,288},{256,384},{288,160},{384,256},{... | collective-permute-start | bytes 1179656 | tf_op jit(solution)/shard_map/ppermute | solution.py:320
  68.1 3.7 %collective-permute-done.7 = f32[2,3,128,128]{3,2,1,0:T(8,128)S(1)} collective-permute-done((f32[2,3,128,128]{3,2,1,0:T(8,128)S(1)}, f32[2,3,128,128]{3,2,1,0:T(8,128)S(1)}, u32[]{:S(2)}, u32[]{:S(2)}) %collective-permute-start.7) | collective-permute-done | bytes 393248 | tf_op jit(solution)/shard_map/ppermute | solution.py:320
  71.9 2.4 %collective-permute-start.8 = (f32[3,128,128]{2,1,0:T(8,128)S(1)}, f32[3,128,128]{2,1,0:T(8,128)S(1)}, u32[]{:S(2)}, u32[]{:S(2)}) collective-permute-start(f32[3,128,128]{2,1,0:T(8,128)S(1)} %fusion), channel_id=1, source_target_pairs={{0,384},{32,160},{128,256},{160,32},{256,128},{288,416},{384,0},{4... | collective-permute-start | bytes 589832 | tf_op jit(solution)/shard_map/ppermute | solution.py:320
  74.3 1.8 %collective-permute-done.4 = f32[2,3,128,128]{3,2,1,0:T(8,128)S(1)} collective-permute-done((f32[2,3,128,128]{3,2,1,0:T(8,128)S(1)}, f32[2,3,128,128]{3,2,1,0:T(8,128)S(1)}, u32[]{:S(2)}, u32[]{:S(2)}) %collective-permute-start.4) | collective-permute-done | bytes 393248 | tf_op jit(solution)/shard_map/ppermute | solution.py:320
  76.1 2.9 %collective-permute-start.5 = (f32[3,128,128]{2,1,0:T(8,128)S(1)}, f32[3,128,128]{2,1,0:T(8,128)S(1)}, u32[]{:S(2)}, u32[]{:S(2)}) collective-permute-start(f32[3,128,128]{2,1,0:T(8,128)S(1)} %fusion.3), channel_id=1, source_target_pairs={{0,384},{32,160},{128,256},{160,32},{256,128},{288,416},{384,0},{4... | collective-permute-start | bytes 589832 | tf_op jit(solution)/shard_map/ppermute | solution.py:320
  79.0 1.7 %collective-permute-done.8 = f32[3,128,128]{2,1,0:T(8,128)S(1)} collective-permute-done((f32[3,128,128]{2,1,0:T(8,128)S(1)}, f32[3,128,128]{2,1,0:T(8,128)S(1)}, u32[]{:S(2)}, u32[]{:S(2)}) %collective-permute-start.8) | collective-permute-done | bytes 196640 | tf_op jit(solution)/shard_map/ppermute | solution.py:320
  80.7 7.5 %collective-permute-start.9 = (f32[3,128,128]{2,1,0:T(8,128)S(1)}, f32[3,128,128]{2,1,0:T(8,128)S(1)}, u32[]{:S(2)}, u32[]{:S(2)}) collective-permute-start(f32[3,128,128]{2,1,0:T(8,128)S(1)} %fusion.2), channel_id=1, source_target_pairs={{0,64},{64,0},{1,65},{65,1},{2,66},{66,2},{3,67},{67,3},{4,68},{68... | collective-permute-start | bytes 589832 | tf_op jit(solution)/shard_map/ppermute | solution.py:311
  88.2 0.0 collective-permute-done.5
  88.3 6.9 %collective-permute-done.9.other_ref = f32[3,128,128]{2,1,0:T(8,128)S(1)} collective-permute-done((f32[3,128,128]{2,1,0:T(8,128)S(1)}, f32[3,128,128]{2,1,0:T(8,128)S(1)}, u32[]{:S(2)}, u32[]{:S(2)}) %collective-permute-start.9) | collective-permute-done | bytes 196640 | tf_op jit(solution)/shard_map/ppermute | solution.py:311
  95.2 0.6 edge_values.1
  95.7 2.6 %collective-permute-start.10 = (f32[128,128]{1,0:T(8,128)S(1)}, f32[128,128]{1,0:T(8,128)S(1)}, u32[]{:S(2)}, u32[]{:S(2)}) collective-permute-start(f32[128,128]{1,0:T(8,128)S(1)} %get-tuple-element.35), channel_id=1, source_target_pairs={{0,1},{1,0},{2,3},{3,2},{4,5},{5,4},{6,7},{7,6},{8,9},{9,8},{10,11... | collective-permute-start | bytes 196616 | tf_op jit(solution)/shard_map/ppermute | solution.py:328
  98.4 12.3 %collective-permute-start.11 = (f32[128,128]{1,0:T(8,128)S(1)}, f32[128,128]{1,0:T(8,128)S(1)}, u32[]{:S(2)}, u32[]{:S(2)}) collective-permute-start(f32[128,128]{1,0:T(8,128)S(1)} %get-tuple-element.36), channel_id=1, source_target_pairs={{1,2},{2,1},{3,4},{4,3},{5,6},{6,5},{7,8},{8,7},{9,10},{10,9},{11,... | collective-permute-start | bytes 196616 | tf_op jit(solution)/shard_map/ppermute | solution.py:328
  110.7 0.0 collective-permute-done.10.early_ref
  110.7 2.3 %collective-permute-done.11.late_ref = f32[128,128]{1,0:T(8,128)S(1)} collective-permute-done((f32[128,128]{1,0:T(8,128)S(1)}, f32[128,128]{1,0:T(8,128)S(1)}, u32[]{:S(2)}, u32[]{:S(2)}) %collective-permute-start.11) | collective-permute-done | bytes 65568 | tf_op jit(solution)/shard_map/ppermute | solution.py:328
  113.0 1.4 %proximal.1 = f32[1,3,1,128,128]{4,3,2,1,0:T(8,128)} custom-call(s32[5]{0:T(128)S(1)} %stack.23.where_ref, s32[1,3,16]{2,1,0:T(4,128)S(1)} %copy.9.refs_0_.slots_ref, f32[3,128,128]{2,1,0:T(8,128)S(1)} %fusion.5.near_ref, f32[3,128,128]{2,1,0:T(8,128)S(1)} %collective-permute-done.9.other_ref, f32[128,128]{1,0:T(8,128)S(1)} %collective-permute-done.10.early_ref, ...), custom_call_target="tpu_custom_call" | custom-call | flops 983040 | bytes 524288 | tf_op jit(solution)/shard_map/proximal/pallas_call | solution.py:289
  (6 shorter events, 0.2 us)
Async XLA Ops:
  0.0 38.2 %collective-permute-start = (f32[256,1024]{1,0:T(8,128)}, f32[256,1024]{1,0:T(8,128)S(1)}, u32[]{:S(2)}, u32[]{:S(2)}) collective-permute-start(f32[256,1024]{1,0:T(8,128)} %refs_1_.1), channel_id=1, source_target_pairs={{0,1},{1,2},{2,3},{3,4},{4,5},{5,6},{6,7},{7,8},{8,9},{9,10},{10,1... | collective-permute-start | bytes 3145736 | tf_op jit(solution)/shard_map/ppermute | solution.py:311
  4.8 37.2 %collective-permute-start.2 = (f32[128,1024]{1,0:T(8,128)S(1)}, f32[128,1024]{1,0:T(8,128)S(1)}, u32[]{:S(2)}, u32[]{:S(2)}) collective-permute-start(f32[128,1024]{1,0:T(8,128)S(1)} %get-tuple-element.37), channel_id=1, source_target_pairs={{0,31},{1,0},{2,1},{3,2},{4,3},{5,4},{6,5},{7,6},{8,7},{9,8},{10,9... | collective-permute-start | bytes 1572872 | tf_op jit(solution)/shard_map/ppermute | solution.py:311
  17.2 35.9 %collective-permute-start.1 = (f32[128,1024]{1,0:T(8,128)S(1)}, f32[128,1024]{1,0:T(8,128)S(1)}, u32[]{:S(2)}, u32[]{:S(2)}) collective-permute-start(f32[128,1024]{1,0:T(8,128)S(1)} %get-tuple-element.38), channel_id=1, source_target_pairs={{0,31},{1,0},{2,1},{3,2},{4,3},{5,4},{6,5},{7,6},{8,7},{9,8},{10,9... | collective-permute-start | bytes 1572872 | tf_op jit(solution)/shard_map/ppermute | solution.py:311
  21.9 1.9 %copy-start = (f32[1,3,16,128,128]{4,3,2,1,0:T(8,128)S(1)}, f32[1,3,16,128,128]{4,3,2,1,0:T(8,128)}, u32[]{:S(2)}) copy-start(f32[1,3,16,128,128]{4,3,2,1,0:T(8,128)} %omega_ref.3) | copy-start | bytes 9437188
  23.8 1.2 %copy-start.2 = (f32[256,1024]{1,0:T(8,128)S(1)}, f32[256,1024]{1,0:T(8,128)}, u32[]{:S(2)}) copy-start(f32[256,1024]{1,0:T(8,128)} %refs_1_.1) | copy-start | bytes 3145732
  25.0 13.2 %copy-start.1 = (f32[1,3,16,128,128]{4,3,2,1,0:T(8,128)S(1)}, f32[1,3,16,128,128]{4,3,2,1,0:T(8,128)}, u32[]{:S(2)}) copy-start(f32[1,3,16,128,128]{4,3,2,1,0:T(8,128)} %omega_ref.3) | copy-start | bytes 9437188
  56.2 6.0 %collective-permute-start.6 = (f32[4,3,128,128]{3,2,1,0:T(8,128)S(1)}, f32[4,3,128,128]{3,2,1,0:T(8,128)S(1)}, u32[]{:S(2)}, u32[]{:S(2)}) collective-permute-start(f32[4,3,128,128]{3,2,1,0:T(8,128)S(1)} %get-tuple-element.33), channel_id=1, source_target_pairs={{0,32},{32,0},{1,33},{33,1},{2,34},{34,2},{3,35},{35,3},{4,36},{36... | collective-permute-start | bytes 2359304 | tf_op jit(solution)/shard_map/ppermute | solution.py:311
  59.7 5.2 %collective-permute-start.3 = (f32[4,3,128,128]{3,2,1,0:T(8,128)S(1)}, f32[4,3,128,128]{3,2,1,0:T(8,128)S(1)}, u32[]{:S(2)}, u32[]{:S(2)}) collective-permute-start(f32[4,3,128,128]{3,2,1,0:T(8,128)S(1)} %get-tuple-element.30), channel_id=1, source_target_pairs={{0,32},{32,0},{1,33},{33,1},{2,34},{34,2},{3,35},{35,3},{4,36},{36... | collective-permute-start | bytes 2359304 | tf_op jit(solution)/shard_map/ppermute | solution.py:311
  62.2 9.7 %collective-permute-start.7 = (f32[2,3,128,128]{3,2,1,0:T(8,128)S(1)}, f32[2,3,128,128]{3,2,1,0:T(8,128)S(1)}, u32[]{:S(2)}, u32[]{:S(2)}) collective-permute-start(f32[2,3,128,128]{3,2,1,0:T(8,128)S(1)} %slice_add_fusion), channel_id=1, source_target_pairs={{0,128},{32,416},{128,0},{160,288},{256,384},{288,160},{384,256},{... | collective-permute-start | bytes 1179656 | tf_op jit(solution)/shard_map/ppermute | solution.py:320
  65.0 11.1 %collective-permute-start.4 = (f32[2,3,128,128]{3,2,1,0:T(8,128)S(1)}, f32[2,3,128,128]{3,2,1,0:T(8,128)S(1)}, u32[]{:S(2)}, u32[]{:S(2)}) collective-permute-start(f32[2,3,128,128]{3,2,1,0:T(8,128)S(1)} %slice_add_fusion.1), channel_id=1, source_target_pairs={{0,128},{32,416},{128,0},{160,288},{256,384},{288,160},{384,256},{... | collective-permute-start | bytes 1179656 | tf_op jit(solution)/shard_map/ppermute | solution.py:320
  71.9 8.8 %collective-permute-start.8 = (f32[3,128,128]{2,1,0:T(8,128)S(1)}, f32[3,128,128]{2,1,0:T(8,128)S(1)}, u32[]{:S(2)}, u32[]{:S(2)}) collective-permute-start(f32[3,128,128]{2,1,0:T(8,128)S(1)} %fusion), channel_id=1, source_target_pairs={{0,384},{32,160},{128,256},{160,32},{256,128},{288,416},{384,0},{4... | collective-permute-start | bytes 589832 | tf_op jit(solution)/shard_map/ppermute | solution.py:320
  76.1 12.1 %collective-permute-start.5 = (f32[3,128,128]{2,1,0:T(8,128)S(1)}, f32[3,128,128]{2,1,0:T(8,128)S(1)}, u32[]{:S(2)}, u32[]{:S(2)}) collective-permute-start(f32[3,128,128]{2,1,0:T(8,128)S(1)} %fusion.3), channel_id=1, source_target_pairs={{0,384},{32,160},{128,256},{160,32},{256,128},{288,416},{384,0},{4... | collective-permute-start | bytes 589832 | tf_op jit(solution)/shard_map/ppermute | solution.py:320
  80.7 14.4 %collective-permute-start.9 = (f32[3,128,128]{2,1,0:T(8,128)S(1)}, f32[3,128,128]{2,1,0:T(8,128)S(1)}, u32[]{:S(2)}, u32[]{:S(2)}) collective-permute-start(f32[3,128,128]{2,1,0:T(8,128)S(1)} %fusion.2), channel_id=1, source_target_pairs={{0,64},{64,0},{1,65},{65,1},{2,66},{66,2},{3,67},{67,3},{4,68},{68... | collective-permute-start | bytes 589832 | tf_op jit(solution)/shard_map/ppermute | solution.py:311
  95.7 14.9 %collective-permute-start.10 = (f32[128,128]{1,0:T(8,128)S(1)}, f32[128,128]{1,0:T(8,128)S(1)}, u32[]{:S(2)}, u32[]{:S(2)}) collective-permute-start(f32[128,128]{1,0:T(8,128)S(1)} %get-tuple-element.35), channel_id=1, source_target_pairs={{0,1},{1,0},{2,3},{3,2},{4,5},{5,4},{6,7},{7,6},{8,9},{9,8},{10,11... | collective-permute-start | bytes 196616 | tf_op jit(solution)/shard_map/ppermute | solution.py:328
  98.4 14.6 %collective-permute-start.11 = (f32[128,128]{1,0:T(8,128)S(1)}, f32[128,128]{1,0:T(8,128)S(1)}, u32[]{:S(2)}, u32[]{:S(2)}) collective-permute-start(f32[128,128]{1,0:T(8,128)S(1)} %get-tuple-element.36), channel_id=1, source_target_pairs={{1,2},{2,1},{3,4},{4,3},{5,6},{6,5},{7,8},{8,7},{9,10},{10,9},{11,... | collective-permute-start | bytes 196616 | tf_op jit(solution)/shard_map/ppermute | solution.py:328

commit v10 on v9

--- a/solution.py
+++ b/solution.py
@@ -132,19 +132,21 @@
 
 
 def proximal_kernel(
-    where_ref, slots_ref, near_ref, other_ref, early_ref, late_ref, omega_ref, out_ref
+    where_ref, slots_ref, near_ref, other_ref, early_ref, late_ref, last_ref, omega_ref, out_ref
 ):
     j = where_ref[3]
     odd_tile = where_ref[4] == 1
     rows = lax.broadcasted_iota(jnp.int32, (BLK, BLK), 0)
     columns = lax.broadcasted_iota(jnp.int32, (BLK, BLK), 1)
+    early = early_ref[...] + last_ref[...]
+    late = late_ref[...]
     for e in range(3):
         slot = slots_ref[0, e, j]
         total = near_ref[e] + other_ref[e]
         if e == 0:
-            total = total + jnp.where(odd_tile, early_ref[...], late_ref[...]).T
+            total = total + jnp.where(odd_tile, early, late).T
         if e == 2:
-            total = total + jnp.where(odd_tile, late_ref[...], early_ref[...]).T
+            total = total + jnp.where(odd_tile, late, early).T
         gradient = total * (0.5 / SAMPLES)
         omega = omega_ref[0, e, 0]
         if e == 1:
@@ -258,12 +260,14 @@
     )(slots, where, below, centre, above, pieces)
 
 
-def edge_kernel(where_ref, near_ref, other_ref, late_ref, early_ref):
+def edge_kernel(where_ref, near_ref, other_ref, early_ref, late_ref, last_ref):
     odd_tile = where_ref[4] == 1
     downward = near_ref[0] + other_ref[0]
     upward = near_ref[2] + other_ref[2]
     late_ref[...] = jnp.where(odd_tile, upward, downward)
-    early_ref[...] = jnp.where(odd_tile, downward, upward)
+    short = jnp.where(odd_tile, downward, upward)
+    early_ref[...] = short
+    last_ref[...] = short
 
 
 def edge_values(where, near, other):
@@ -272,9 +276,9 @@
         edge_kernel,
         name="edge_values",
         grid=(1,),
-        out_shape=(block, block),
+        out_shape=(block,) * 3,
         in_specs=[SMEM] + [full_spec((3, BLK, BLK))] * 2,
-        out_specs=(full_spec((BLK, BLK)),) * 2,
+        out_specs=(full_spec((BLK, BLK)),) * 3,
         compiler_params=params(),
         cost_estimate=pl.CostEstimate(
             flops=4 * BLK * BLK, bytes_accessed=6 * 4 * BLK * BLK, transcendentals=0
@@ -282,7 +286,7 @@
     )(where, near, other)
 
 
-def proximal(where, slots, near, other, early, late, omega):
+def proximal(where, slots, near, other, early, late, last, omega):
     block = pl.BlockSpec((BLK, BLK), lambda i, where, slots: (0, 0))
     triple = pl.BlockSpec((3, BLK, BLK), lambda i, where, slots: (0, 0, 0))
     own = pl.BlockSpec((1, 3, 1, BLK, BLK), lambda i, where, slots: (0, 0, where[3], 0, 0))
@@ -292,7 +296,7 @@
         grid_spec=pltpu.PrefetchScalarGridSpec(
             num_scalar_prefetch=2,
             grid=(1,),
-            in_specs=[triple, triple, block, block, own],
+            in_specs=[triple, triple, block, block, block, own],
             out_specs=pl.BlockSpec(
                 (1, 3, 1, BLK, BLK), lambda i, where, slots: (0, 0, 0, 0, 0)
             ),
@@ -302,7 +306,7 @@
         cost_estimate=pl.CostEstimate(
             flops=20 * 3 * BLK * BLK, bytes_accessed=1 << 19, transcendentals=0
         ),
-    )(where, slots, near, other, early, late, omega)
+    )(where, slots, near, other, early, late, last, omega)
 
 
 def shifted(value, axis, steps):
@@ -320,11 +324,11 @@
     return lax.ppermute(value, ("x", "core"), pairs)
 
 
-def edge_exchange(value, offset):
+def edge_exchange(value, offset, step):
     count = lax.axis_size("col")
     pairs = []
-    for t in range(offset, count + offset, 2):
-        pairs += [(t % count, (t + 1) % count), ((t + 1) % count, t % count)]
+    for t in range(offset, count, step):
+        pairs += [(t, (t + 1) % count), ((t + 1) % count, t)]
     return lax.ppermute(value, "col", pairs)
 
 
@@ -354,10 +358,11 @@
     other = shifted(far_sum, "y_hi", 1)
     near_second = x_exchange(near_keep[1] + near_got[1] + near_first[1], 1)
     near_sum = near_keep[0] + near_got[0] + near_first[0] + near_second
-    late_out, early_out = edge_values(where, near_sum, other)
-    late = edge_exchange(late_out, 1)
-    early = edge_exchange(early_out, 0)
-    return proximal(where, block_slots, near_sum, other, early, late, omega)
+    early_out, late_out, last_out = edge_values(where, near_sum, other)
+    early = edge_exchange(early_out, 0, 4)
+    late = edge_exchange(late_out, 1, 2)
+    last = edge_exchange(last_out, 2, 4)
+    return proximal(where, block_slots, near_sum, other, early, late, last, omega)
 
 
 def solution(mesh):

time: 115 us -> 114 us (level)
  waiting for transfers between devices: 38.1 us -> 36.1 us
    ppermute x6, waiting for transfers between devices: 28.6 us -> 27.1 us  [shifted(): return lax.ppermute(value, axis, pairs)]
    ppermute x2 -> x3, starting transfers between devices: 14.9 us -> 15.7 us  [edge_exchange(): return lax.ppermute(value, 'col', pairs)]
  transfers between devices with their start and end apart: 12 -> 13, of which waited for: 8 -> 8; matrix products, arithmetic and copies ran while one was open for 2% -> 2% of each run, Pallas kernels for 7% -> 7%
where the time goes in v10:
time: 114 us; the launch traced here: 113 us
  starting transfers between devices  58.5 us (51%)
  waiting for transfers between devices  36.1 us (32%)
  Pallas kernels  13 us (11%)
  local copies, waits for them, and re-layouts  5.16 us (5%)
    ppermute x6, starting transfers between devices, shifted(): return lax.ppermute(value, axis, pairs)  31.7 us
    ppermute x6, waiting for transfers between devices, shifted(): return lax.ppermute(value, axis, pairs)  27.1 us
    ppermute x3, starting transfers between devices, edge_exchange(): return lax.ppermute(value, 'col', pairs)  15.7 us
    ppermute x4, starting transfers between devices, x_exchange(): return lax.ppermute(value, ('x', 'core'), pairs)  11.1 us
    ppermute x4, waiting for transfers between devices, x_exchange(): return lax.ppermute(value, ('x', 'core'), pairs)  7.18 us
    pallas_call x3, Pallas kernels, partial(): pl.pallas_call(lambda *refs: partial_kernel(offset, first, *refs), name='...  6.3 us
    unnamed x7, local copies, waits for them, and re-layouts  3.8 us
    pallas_call x1, Pallas kernels, far_blocks(): pl.pallas_call(far_kernel, name='far_blocks', grid=(1,), out_shape=GROUP_...  3.12 us
  transfers between devices with their start and end apart: 13, of which 8 were waited for; matrix products, arithmetic and copies ran while one was open for 2% of the time, Pallas kernels for 7%

profile of v10, /device:TPU:6, one launch (start us, length us, event | category | flops | bytes accessed | tf_op | source)
XLA Modules:
  0.0 113.2 jit_solution(8332388412350202005)
XLA Ops:
  0.0 3.5 %collective-permute-start = (f32[256,1024]{1,0:T(8,128)}, f32[256,1024]{1,0:T(8,128)S(1)}, u32[]{:S(2)}, u32[]{:S(2)}) collective-permute-start(f32[256,1024]{1,0:T(8,128)} %refs_1_.1), channel_id=1, source_target_pairs={{0,1},{1,2},{2,3},{3,4},{4,5},{5,6},{6,7},{7,8},{8,9},{9,10},{10,1... | collective-permute-start | bytes 3145736 | tf_op jit(solution)/shard_map/ppermute | solution.py:315
  3.5 1.3 %fusion.6 = (f32[128,1024]{1,0:T(8,128)S(1)}, f32[128,1024]{1,0:T(8,128)S(1)}) fusion(f32[256,1024]{1,0:T(8,128)} %refs_1_.1), kind=kLoop, calls=%fused_computation.16 | loop fusion | bytes 2097152 | tf_op jit(solution)/shard_map/slice | solution.py:341
  4.8 12.4 %collective-permute-start.2 = (f32[128,1024]{1,0:T(8,128)S(1)}, f32[128,1024]{1,0:T(8,128)S(1)}, u32[]{:S(2)}, u32[]{:S(2)}) collective-permute-start(f32[128,1024]{1,0:T(8,128)S(1)} %get-tuple-element.39), channel_id=1, source_target_pairs={{0,31},{1,0},{2,1},{3,2},{4,3},{5,4},{6,5},{7,6},{8,7},{9,8},{10,9... | collective-permute-start | bytes 1572872 | tf_op jit(solution)/shard_map/ppermute | solution.py:315
  17.2 3.9 %collective-permute-start.1 = (f32[128,1024]{1,0:T(8,128)S(1)}, f32[128,1024]{1,0:T(8,128)S(1)}, u32[]{:S(2)}, u32[]{:S(2)}) collective-permute-start(f32[128,1024]{1,0:T(8,128)S(1)} %get-tuple-element.40), channel_id=1, source_target_pairs={{0,31},{1,0},{2,1},{3,2},{4,3},{5,4},{6,5},{7,6},{8,7},{9,8},{10,9... | collective-permute-start | bytes 1572872 | tf_op jit(solution)/shard_map/ppermute | solution.py:315
  21.1 0.7 copy.9.refs_0_.slots_ref
  21.8 0.1 stack.23.where_ref
  21.9 0.0 copy-start
  21.9 1.9 %copy-done = f32[1,3,16,128,128]{4,3,2,1,0:T(8,128)S(1)} copy-done((f32[1,3,16,128,128]{4,3,2,1,0:T(8,128)S(1)}, f32[1,3,16,128,128]{4,3,2,1,0:T(8,128)}, u32[]{:S(2)}) %copy-start) | copy-done | bytes 3145752
  23.8 0.0 copy-start.2
  23.8 1.2 %copy-done.2 = f32[256,1024]{1,0:T(8,128)S(1)} copy-done((f32[256,1024]{1,0:T(8,128)S(1)}, f32[256,1024]{1,0:T(8,128)}, u32[]{:S(2)}) %copy-start.2) | copy-done | bytes 1048600
  25.0 0.0 copy-start.1
  25.0 2.3 %partial_residual.3 = (f32[8,256,128]{2,1,0:T(8,128)S(1)}, bf16[8,256,256]{2,1,0:T(8,128)(2,1)S(1)}) custom-call(s32[1,3,16]{2,1,0:T(4,128)S(1)} %copy.9.refs_0_.slots_ref, f32[256,1024]{1,0:T(8,128)S(1)} %copy-done.2, f32[1,3,16,128,128]{4,3,2,1,0:T(8,128)S(1)} %copy-done), custom_call_target="tpu_custom_call" | custom-call | flops 536870912 | bytes 5242880 | tf_op jit(solution)/shard_map/partial_residual/pallas_call | solution.py:192
  27.3 10.9 %collective-permute-done.refs_1_ = f32[256,1024]{1,0:T(8,128)S(1)} collective-permute-done((f32[256,1024]{1,0:T(8,128)}, f32[256,1024]{1,0:T(8,128)S(1)}, u32[]{:S(2)}, u32[]{:S(2)}) %collective-permute-start) | collective-permute-done | bytes 1048608 | tf_op jit(solution)/shard_map/ppermute | solution.py:315
  38.2 0.0 copy-done.1
  38.2 2.2 %partial_residual.4 = (f32[8,256,128]{2,1,0:T(8,128)S(1)}, bf16[8,256,256]{2,1,0:T(8,128)(2,1)S(1)}) custom-call(s32[1,3,16]{2,1,0:T(4,128)S(1)} %copy.9.refs_0_.slots_ref, f32[256,1024]{1,0:T(8,128)S(1)} %collective-permute-done.refs_1_, f32[1,3,16,128,128]{4,3,2,1,0:T(8,128)S(1)} %copy-done.1, f32[8,256,128]{2,1,0:T(8,128)S(1)} %get-tuple-element.22.refs_3_), custom_call_target="tpu_custom_call" | custom-call | flops 536870912 | bytes 5242880 | tf_op jit(solution)/shard_map/partial_residual/pallas_call | solution.py:192
  40.5 1.5 %collective-permute-done.2.refs_1_ = f32[128,1024]{1,0:T(8,128)S(1)} collective-permute-done((f32[128,1024]{1,0:T(8,128)S(1)}, f32[128,1024]{1,0:T(8,128)S(1)}, u32[]{:S(2)}, u32[]{:S(2)}) %collective-permute-start.2) | collective-permute-done | bytes 524320 | tf_op jit(solution)/shard_map/ppermute | solution.py:315
  41.9 1.8 %partial_residual.5 = (f32[8,256,128]{2,1,0:T(8,128)S(1)}, bf16[8,256,128]{2,1,0:T(8,128)(2,1)S(1)}) custom-call(s32[1,3,16]{2,1,0:T(4,128)S(1)} %copy.9.refs_0_.slots_ref, f32[128,1024]{1,0:T(8,128)S(1)} %collective-permute-done.2.refs_1_, f32[1,3,16,128,128]{4,3,2,1,0:T(8,128)S(1)} %copy-done.1, f32[8,256,128]{2,1,0:T(8,128)S(1)} %get-tuple-element.25.refs_3_), custom_call_target="tpu_custom_call" | custom-call | flops 268435456 | bytes 5242880 | tf_op jit(solution)/shard_map/partial_residual/pallas_call | solution.py:192
  43.7 9.3 %collective-permute-done.1.x_ref = f32[128,1024]{1,0:T(8,128)S(1)} collective-permute-done((f32[128,1024]{1,0:T(8,128)S(1)}, f32[128,1024]{1,0:T(8,128)S(1)}, u32[]{:S(2)}, u32[]{:S(2)}) %collective-permute-start.1) | collective-permute-done | bytes 524320 | tf_op jit(solution)/shard_map/ppermute | solution.py:315
  53.1 3.1 %far_blocks.1 = (f32[2,3,128,128]{3,2,1,0:T(8,128)S(1)}, f32[2,3,128,128]{3,2,1,0:T(8,128)S(1)}, f32[4,3,128,128]{3,2,1,0:T(8,128)S(1)}, bf16[8,256,256]{2,1,0:T(8,128)(2,1)S(1)}, bf16[8,256,256]{2,1,0:T(8,128)(2,1)S(1)}) custom-call(s32[1,3,16]{2,1,0:T(4,128)S(1)} %copy.9.refs_0_.slots_ref, s32[5]{0:T(128)S(1)} %stack.23.where_ref, ...), custom_call_target="tpu_custom_call" | custom-call | flops 1342177280 | bytes 8388608 | tf_op jit(solution)/shard_map/far_blocks/pallas_call | solution.py:218
  56.2 1.9 %collective-permute-start.6 = (f32[4,3,128,128]{3,2,1,0:T(8,128)S(1)}, f32[4,3,128,128]{3,2,1,0:T(8,128)S(1)}, u32[]{:S(2)}, u32[]{:S(2)}) collective-permute-start(f32[4,3,128,128]{3,2,1,0:T(8,128)S(1)} %get-tuple-element.34), channel_id=1, source_target_pairs={{0,32},{32,0},{1,33},{33,1},{2,34},{34,2},{3,35},{35,3},{4,36},{36... | collective-permute-start | bytes 2359304 | tf_op jit(solution)/shard_map/ppermute | solution.py:315
  58.1 1.6 %near_blocks.1 = (f32[2,3,128,128]{3,2,1,0:T(8,128)S(1)}, f32[2,3,128,128]{3,2,1,0:T(8,128)S(1)}, f32[4,3,128,128]{3,2,1,0:T(8,128)S(1)}) custom-call(s32[1,3,16]{2,1,0:T(4,128)S(1)} %copy.9.refs_0_.slots_ref, s32[5]{0:T(128)S(1)} %stack.23.where_ref, bf16[8,256,256]{2,1,0:T(8,128)(2,1)S(1)} %get-tuple-element.23.below_ref, ...), custom_call_target="tpu_custom_call" | custom-call | flops 805306368 | bytes 8388608 | tf_op jit(solution)/shard_map/near_blocks/pallas_call | solution.py:247
  59.7 2.4 %collective-permute-start.3 = (f32[4,3,128,128]{3,2,1,0:T(8,128)S(1)}, f32[4,3,128,128]{3,2,1,0:T(8,128)S(1)}, u32[]{:S(2)}, u32[]{:S(2)}) collective-permute-start(f32[4,3,128,128]{3,2,1,0:T(8,128)S(1)} %get-tuple-element.31), channel_id=1, source_target_pairs={{0,32},{32,0},{1,33},{33,1},{2,34},{34,2},{3,35},{35,3},{4,36},{36... | collective-permute-start | bytes 2359304 | tf_op jit(solution)/shard_map/ppermute | solution.py:315
  62.1 0.0 collective-permute-done.6
  62.2 2.7 %collective-permute-start.7 = (f32[2,3,128,128]{3,2,1,0:T(8,128)S(1)}, f32[2,3,128,128]{3,2,1,0:T(8,128)S(1)}, u32[]{:S(2)}, u32[]{:S(2)}) collective-permute-start(f32[2,3,128,128]{3,2,1,0:T(8,128)S(1)} %slice_add_fusion), channel_id=1, source_target_pairs={{0,128},{32,416},{128,0},{160,288},{256,384},{288,160},{384,256},{... | collective-permute-start | bytes 1179656 | tf_op jit(solution)/shard_map/ppermute | solution.py:324
  65.0 0.0 collective-permute-done.3
  65.0 3.1 %collective-permute-start.4 = (f32[2,3,128,128]{3,2,1,0:T(8,128)S(1)}, f32[2,3,128,128]{3,2,1,0:T(8,128)S(1)}, u32[]{:S(2)}, u32[]{:S(2)}) collective-permute-start(f32[2,3,128,128]{3,2,1,0:T(8,128)S(1)} %slice_add_fusion.1), channel_id=1, source_target_pairs={{0,128},{32,416},{128,0},{160,288},{256,384},{288,160},{384,256},{... | collective-permute-start | bytes 1179656 | tf_op jit(solution)/shard_map/ppermute | solution.py:324
  68.1 3.7 %collective-permute-done.7 = f32[2,3,128,128]{3,2,1,0:T(8,128)S(1)} collective-permute-done((f32[2,3,128,128]{3,2,1,0:T(8,128)S(1)}, f32[2,3,128,128]{3,2,1,0:T(8,128)S(1)}, u32[]{:S(2)}, u32[]{:S(2)}) %collective-permute-start.7) | collective-permute-done | bytes 393248 | tf_op jit(solution)/shard_map/ppermute | solution.py:324
  71.9 2.4 %collective-permute-start.8 = (f32[3,128,128]{2,1,0:T(8,128)S(1)}, f32[3,128,128]{2,1,0:T(8,128)S(1)}, u32[]{:S(2)}, u32[]{:S(2)}) collective-permute-start(f32[3,128,128]{2,1,0:T(8,128)S(1)} %fusion), channel_id=1, source_target_pairs={{0,384},{32,160},{128,256},{160,32},{256,128},{288,416},{384,0},{4... | collective-permute-start | bytes 589832 | tf_op jit(solution)/shard_map/ppermute | solution.py:324
  74.3 1.8 %collective-permute-done.4 = f32[2,3,128,128]{3,2,1,0:T(8,128)S(1)} collective-permute-done((f32[2,3,128,128]{3,2,1,0:T(8,128)S(1)}, f32[2,3,128,128]{3,2,1,0:T(8,128)S(1)}, u32[]{:S(2)}, u32[]{:S(2)}) %collective-permute-start.4) | collective-permute-done | bytes 393248 | tf_op jit(solution)/shard_map/ppermute | solution.py:324
  76.1 2.9 %collective-permute-start.5 = (f32[3,128,128]{2,1,0:T(8,128)S(1)}, f32[3,128,128]{2,1,0:T(8,128)S(1)}, u32[]{:S(2)}, u32[]{:S(2)}) collective-permute-start(f32[3,128,128]{2,1,0:T(8,128)S(1)} %fusion.3), channel_id=1, source_target_pairs={{0,384},{32,160},{128,256},{160,32},{256,128},{288,416},{384,0},{4... | collective-permute-start | bytes 589832 | tf_op jit(solution)/shard_map/ppermute | solution.py:324
  79.0 1.7 %collective-permute-done.8 = f32[3,128,128]{2,1,0:T(8,128)S(1)} collective-permute-done((f32[3,128,128]{2,1,0:T(8,128)S(1)}, f32[3,128,128]{2,1,0:T(8,128)S(1)}, u32[]{:S(2)}, u32[]{:S(2)}) %collective-permute-start.8) | collective-permute-done | bytes 196640 | tf_op jit(solution)/shard_map/ppermute | solution.py:324
  80.7 7.5 %collective-permute-start.9 = (f32[3,128,128]{2,1,0:T(8,128)S(1)}, f32[3,128,128]{2,1,0:T(8,128)S(1)}, u32[]{:S(2)}, u32[]{:S(2)}) collective-permute-start(f32[3,128,128]{2,1,0:T(8,128)S(1)} %fusion.2), channel_id=1, source_target_pairs={{0,64},{64,0},{1,65},{65,1},{2,66},{66,2},{3,67},{67,3},{4,68},{68... | collective-permute-start | bytes 589832 | tf_op jit(solution)/shard_map/ppermute | solution.py:315
  88.2 0.0 collective-permute-done.5
  88.3 5.3 %collective-permute-done.9.other_ref = f32[3,128,128]{2,1,0:T(8,128)S(1)} collective-permute-done((f32[3,128,128]{2,1,0:T(8,128)S(1)}, f32[3,128,128]{2,1,0:T(8,128)S(1)}, u32[]{:S(2)}, u32[]{:S(2)}) %collective-permute-start.9) | collective-permute-done | bytes 196640 | tf_op jit(solution)/shard_map/ppermute | solution.py:315
  93.6 0.6 edge_values.1
  94.2 3.9 %collective-permute-start.10 = (f32[128,128]{1,0:T(8,128)S(1)}, f32[128,128]{1,0:T(8,128)S(1)}, u32[]{:S(2)}, u32[]{:S(2)}) collective-permute-start(f32[128,128]{1,0:T(8,128)S(1)} %get-tuple-element.36), channel_id=1, source_target_pairs={{0,1},{1,0},{4,5},{5,4},{8,9},{9,8},{12,13},{13,12},{16,17},{17,16... | collective-permute-start | bytes 196616 | tf_op jit(solution)/shard_map/ppermute | solution.py:332
  98.1 11.2 %collective-permute-start.11 = (f32[128,128]{1,0:T(8,128)S(1)}, f32[128,128]{1,0:T(8,128)S(1)}, u32[]{:S(2)}, u32[]{:S(2)}) collective-permute-start(f32[128,128]{1,0:T(8,128)S(1)} %get-tuple-element.37), channel_id=1, source_target_pairs={{1,2},{2,1},{3,4},{4,3},{5,6},{6,5},{7,8},{8,7},{9,10},{10,9},{11,... | collective-permute-start | bytes 196616 | tf_op jit(solution)/shard_map/ppermute | solution.py:332
  109.3 0.7 collective-permute-start.12
  109.9 0.0 collective-permute-done.10.early_ref
  110.0 1.9 %collective-permute-done.11.late_ref = f32[128,128]{1,0:T(8,128)S(1)} collective-permute-done((f32[128,128]{1,0:T(8,128)S(1)}, f32[128,128]{1,0:T(8,128)S(1)}, u32[]{:S(2)}, u32[]{:S(2)}) %collective-permute-start.11) | collective-permute-done | bytes 65568 | tf_op jit(solution)/shard_map/ppermute | solution.py:332
  111.8 0.0 collective-permute-done.12.last_ref
  111.8 1.4 %proximal.1 = f32[1,3,1,128,128]{4,3,2,1,0:T(8,128)} custom-call(s32[5]{0:T(128)S(1)} %stack.23.where_ref, s32[1,3,16]{2,1,0:T(4,128)S(1)} %copy.9.refs_0_.slots_ref, f32[3,128,128]{2,1,0:T(8,128)S(1)} %fusion.5.near_ref, f32[3,128,128]{2,1,0:T(8,128)S(1)} %collective-permute-done.9.other_ref, f32[128,128]{1,0:T(8,128)S(1)} %collective-permute-done.10.early_ref, ...), custom_call_target="tpu_custom_call" | custom-call | flops 983040 | bytes 524288 | tf_op jit(solution)/shard_map/proximal/pallas_call | solution.py:293
  (6 shorter events, 0.2 us)
Async XLA Ops:
  0.0 38.2 %collective-permute-start = (f32[256,1024]{1,0:T(8,128)}, f32[256,1024]{1,0:T(8,128)S(1)}, u32[]{:S(2)}, u32[]{:S(2)}) collective-permute-start(f32[256,1024]{1,0:T(8,128)} %refs_1_.1), channel_id=1, source_target_pairs={{0,1},{1,2},{2,3},{3,4},{4,5},{5,6},{6,7},{7,8},{8,9},{9,10},{10,1... | collective-permute-start | bytes 3145736 | tf_op jit(solution)/shard_map/ppermute | solution.py:315
  4.8 37.2 %collective-permute-start.2 = (f32[128,1024]{1,0:T(8,128)S(1)}, f32[128,1024]{1,0:T(8,128)S(1)}, u32[]{:S(2)}, u32[]{:S(2)}) collective-permute-start(f32[128,1024]{1,0:T(8,128)S(1)} %get-tuple-element.39), channel_id=1, source_target_pairs={{0,31},{1,0},{2,1},{3,2},{4,3},{5,4},{6,5},{7,6},{8,7},{9,8},{10,9... | collective-permute-start | bytes 1572872 | tf_op jit(solution)/shard_map/ppermute | solution.py:315
  17.2 35.9 %collective-permute-start.1 = (f32[128,1024]{1,0:T(8,128)S(1)}, f32[128,1024]{1,0:T(8,128)S(1)}, u32[]{:S(2)}, u32[]{:S(2)}) collective-permute-start(f32[128,1024]{1,0:T(8,128)S(1)} %get-tuple-element.40), channel_id=1, source_target_pairs={{0,31},{1,0},{2,1},{3,2},{4,3},{5,4},{6,5},{7,6},{8,7},{9,8},{10,9... | collective-permute-start | bytes 1572872 | tf_op jit(solution)/shard_map/ppermute | solution.py:315
  21.9 1.9 %copy-start = (f32[1,3,16,128,128]{4,3,2,1,0:T(8,128)S(1)}, f32[1,3,16,128,128]{4,3,2,1,0:T(8,128)}, u32[]{:S(2)}) copy-start(f32[1,3,16,128,128]{4,3,2,1,0:T(8,128)} %omega_ref.3) | copy-start | bytes 9437188
  23.8 1.2 %copy-start.2 = (f32[256,1024]{1,0:T(8,128)S(1)}, f32[256,1024]{1,0:T(8,128)}, u32[]{:S(2)}) copy-start(f32[256,1024]{1,0:T(8,128)} %refs_1_.1) | copy-start | bytes 3145732
  25.0 13.2 %copy-start.1 = (f32[1,3,16,128,128]{4,3,2,1,0:T(8,128)S(1)}, f32[1,3,16,128,128]{4,3,2,1,0:T(8,128)}, u32[]{:S(2)}) copy-start(f32[1,3,16,128,128]{4,3,2,1,0:T(8,128)} %omega_ref.3) | copy-start | bytes 9437188
  56.2 5.9 %collective-permute-start.6 = (f32[4,3,128,128]{3,2,1,0:T(8,128)S(1)}, f32[4,3,128,128]{3,2,1,0:T(8,128)S(1)}, u32[]{:S(2)}, u32[]{:S(2)}) collective-permute-start(f32[4,3,128,128]{3,2,1,0:T(8,128)S(1)} %get-tuple-element.34), channel_id=1, source_target_pairs={{0,32},{32,0},{1,33},{33,1},{2,34},{34,2},{3,35},{35,3},{4,36},{36... | collective-permute-start | bytes 2359304 | tf_op jit(solution)/shard_map/ppermute | solution.py:315
  59.7 5.2 %collective-permute-start.3 = (f32[4,3,128,128]{3,2,1,0:T(8,128)S(1)}, f32[4,3,128,128]{3,2,1,0:T(8,128)S(1)}, u32[]{:S(2)}, u32[]{:S(2)}) collective-permute-start(f32[4,3,128,128]{3,2,1,0:T(8,128)S(1)} %get-tuple-element.31), channel_id=1, source_target_pairs={{0,32},{32,0},{1,33},{33,1},{2,34},{34,2},{3,35},{35,3},{4,36},{36... | collective-permute-start | bytes 2359304 | tf_op jit(solution)/shard_map/ppermute | solution.py:315
  62.2 9.7 %collective-permute-start.7 = (f32[2,3,128,128]{3,2,1,0:T(8,128)S(1)}, f32[2,3,128,128]{3,2,1,0:T(8,128)S(1)}, u32[]{:S(2)}, u32[]{:S(2)}) collective-permute-start(f32[2,3,128,128]{3,2,1,0:T(8,128)S(1)} %slice_add_fusion), channel_id=1, source_target_pairs={{0,128},{32,416},{128,0},{160,288},{256,384},{288,160},{384,256},{... | collective-permute-start | bytes 1179656 | tf_op jit(solution)/shard_map/ppermute | solution.py:324
  65.0 11.1 %collective-permute-start.4 = (f32[2,3,128,128]{3,2,1,0:T(8,128)S(1)}, f32[2,3,128,128]{3,2,1,0:T(8,128)S(1)}, u32[]{:S(2)}, u32[]{:S(2)}) collective-permute-start(f32[2,3,128,128]{3,2,1,0:T(8,128)S(1)} %slice_add_fusion.1), channel_id=1, source_target_pairs={{0,128},{32,416},{128,0},{160,288},{256,384},{288,160},{384,256},{... | collective-permute-start | bytes 1179656 | tf_op jit(solution)/shard_map/ppermute | solution.py:324
  71.9 8.8 %collective-permute-start.8 = (f32[3,128,128]{2,1,0:T(8,128)S(1)}, f32[3,128,128]{2,1,0:T(8,128)S(1)}, u32[]{:S(2)}, u32[]{:S(2)}) collective-permute-start(f32[3,128,128]{2,1,0:T(8,128)S(1)} %fusion), channel_id=1, source_target_pairs={{0,384},{32,160},{128,256},{160,32},{256,128},{288,416},{384,0},{4... | collective-permute-start | bytes 589832 | tf_op jit(solution)/shard_map/ppermute | solution.py:324
  76.1 12.1 %collective-permute-start.5 = (f32[3,128,128]{2,1,0:T(8,128)S(1)}, f32[3,128,128]{2,1,0:T(8,128)S(1)}, u32[]{:S(2)}, u32[]{:S(2)}) collective-permute-start(f32[3,128,128]{2,1,0:T(8,128)S(1)} %fusion.3), channel_id=1, source_target_pairs={{0,384},{32,160},{128,256},{160,32},{256,128},{288,416},{384,0},{4... | collective-permute-start | bytes 589832 | tf_op jit(solution)/shard_map/ppermute | solution.py:324
  80.7 12.9 %collective-permute-start.9 = (f32[3,128,128]{2,1,0:T(8,128)S(1)}, f32[3,128,128]{2,1,0:T(8,128)S(1)}, u32[]{:S(2)}, u32[]{:S(2)}) collective-permute-start(f32[3,128,128]{2,1,0:T(8,128)S(1)} %fusion.2), channel_id=1, source_target_pairs={{0,64},{64,0},{1,65},{65,1},{2,66},{66,2},{3,67},{67,3},{4,68},{68... | collective-permute-start | bytes 589832 | tf_op jit(solution)/shard_map/ppermute | solution.py:315
  94.2 15.7 %collective-permute-start.10 = (f32[128,128]{1,0:T(8,128)S(1)}, f32[128,128]{1,0:T(8,128)S(1)}, u32[]{:S(2)}, u32[]{:S(2)}) collective-permute-start(f32[128,128]{1,0:T(8,128)S(1)} %get-tuple-element.36), channel_id=1, source_target_pairs={{0,1},{1,0},{4,5},{5,4},{8,9},{9,8},{12,13},{13,12},{16,17},{17,16... | collective-permute-start | bytes 196616 | tf_op jit(solution)/shard_map/ppermute | solution.py:332
  98.1 13.7 %collective-permute-start.11 = (f32[128,128]{1,0:T(8,128)S(1)}, f32[128,128]{1,0:T(8,128)S(1)}, u32[]{:S(2)}, u32[]{:S(2)}) collective-permute-start(f32[128,128]{1,0:T(8,128)S(1)} %get-tuple-element.37), channel_id=1, source_target_pairs={{1,2},{2,1},{3,4},{4,3},{5,6},{6,5},{7,8},{8,7},{9,10},{10,9},{11,... | collective-permute-start | bytes 196616 | tf_op jit(solution)/shard_map/ppermute | solution.py:332
  109.3 2.6 %collective-permute-start.12 = (f32[128,128]{1,0:T(8,128)S(1)}, f32[128,128]{1,0:T(8,128)S(1)}, u32[]{:S(2)}, u32[]{:S(2)}) collective-permute-start(f32[128,128]{1,0:T(8,128)S(1)} %get-tuple-element.38), channel_id=1, source_target_pairs={{2,3},{3,2},{6,7},{7,6},{10,11},{11,10},{14,15},{15,14},{18,19},{1... | collective-permute-start | bytes 196616 | tf_op jit(solution)/shard_map/ppermute | solution.py:332

commit v11 on v10

--- a/solution.py
+++ b/solution.py
@@ -15,6 +15,7 @@
 penalty = 0.1
 f32 = jnp.float32
 bf16 = jnp.bfloat16
+PLACE = (0, 2, 1)
 VMEM_LIMIT = 16 * 1024 * 1024
 
 
@@ -98,8 +99,8 @@
                     odd + jnp.where(diagonal, odd_turned, even_turned),
                 )
             own_ref = keep_ref if r < 2 else pass_ref
-            own_ref[r % 2, e] = jnp.where(core == 0, even, odd)
-            send_ref[(0, 2, 1, 3)[r], e] = jnp.where(core == 0, odd, even)
+            own_ref[r % 2, PLACE[e]] = jnp.where(core == 0, even, odd)
+            send_ref[(0, 2, 1, 3)[r], PLACE[e]] = jnp.where(core == 0, odd, even)
 
 
 def far_kernel(
@@ -132,7 +133,8 @@
 
 
 def proximal_kernel(
-    where_ref, slots_ref, near_ref, other_ref, early_ref, late_ref, last_ref, omega_ref, out_ref
+    where_ref, slots_ref, near_ref, outer_ref, centre_ref, early_ref, late_ref, last_ref,
+    omega_ref, out_ref,
 ):
     j = where_ref[3]
     odd_tile = where_ref[4] == 1
@@ -142,7 +144,7 @@
     late = late_ref[...]
     for e in range(3):
         slot = slots_ref[0, e, j]
-        total = near_ref[e] + other_ref[e]
+        total = near_ref[PLACE[e]] + (centre_ref[...] if e == 1 else outer_ref[PLACE[e]])
         if e == 0:
             total = total + jnp.where(odd_tile, early, late).T
         if e == 2:
@@ -260,35 +262,36 @@
     )(slots, where, below, centre, above, pieces)
 
 
-def edge_kernel(where_ref, near_ref, other_ref, early_ref, late_ref, last_ref):
+def edge_kernel(where_ref, near_ref, outer_ref, early_ref, late_ref, last_ref):
     odd_tile = where_ref[4] == 1
-    downward = near_ref[0] + other_ref[0]
-    upward = near_ref[2] + other_ref[2]
+    downward = near_ref[0] + outer_ref[0]
+    upward = near_ref[1] + outer_ref[1]
     late_ref[...] = jnp.where(odd_tile, upward, downward)
     short = jnp.where(odd_tile, downward, upward)
     early_ref[...] = short
     last_ref[...] = short
 
 
-def edge_values(where, near, other):
+def edge_values(where, near, outer):
     block = jax.ShapeDtypeStruct((BLK, BLK), f32)
     return pl.pallas_call(
         edge_kernel,
         name="edge_values",
         grid=(1,),
         out_shape=(block,) * 3,
-        in_specs=[SMEM] + [full_spec((3, BLK, BLK))] * 2,
+        in_specs=[SMEM, full_spec((3, BLK, BLK)), full_spec((2, BLK, BLK))],
         out_specs=(full_spec((BLK, BLK)),) * 3,
         compiler_params=params(),
         cost_estimate=pl.CostEstimate(
             flops=4 * BLK * BLK, bytes_accessed=6 * 4 * BLK * BLK, transcendentals=0
         ),
-    )(where, near, other)
-
-
-def proximal(where, slots, near, other, early, late, last, omega):
+    )(where, near, outer)
+
+
+def proximal(where, slots, near, outer, centre, early, late, last, omega):
     block = pl.BlockSpec((BLK, BLK), lambda i, where, slots: (0, 0))
     triple = pl.BlockSpec((3, BLK, BLK), lambda i, where, slots: (0, 0, 0))
+    pair = pl.BlockSpec((2, BLK, BLK), lambda i, where, slots: (0, 0, 0))
     own = pl.BlockSpec((1, 3, 1, BLK, BLK), lambda i, where, slots: (0, 0, where[3], 0, 0))
     return pl.pallas_call(
         proximal_kernel,
@@ -296,7 +299,7 @@
         grid_spec=pltpu.PrefetchScalarGridSpec(
             num_scalar_prefetch=2,
             grid=(1,),
-            in_specs=[triple, triple, block, block, block, own],
+            in_specs=[triple, pair] + [block] * 4 + [own],
             out_specs=pl.BlockSpec(
                 (1, 3, 1, BLK, BLK), lambda i, where, slots: (0, 0, 0, 0, 0)
             ),
@@ -306,7 +309,7 @@
         cost_estimate=pl.CostEstimate(
             flops=20 * 3 * BLK * BLK, bytes_accessed=1 << 19, transcendentals=0
         ),
-    )(where, slots, near, other, early, late, last, omega)
+    )(where, slots, near, outer, centre, early, late, last, omega)
 
 
 def shifted(value, axis, steps):
@@ -322,6 +325,10 @@
             partner = x ^ 1 if core == step else 3 - x
             pairs.append((2 * x + core, 2 * partner + core))
     return lax.ppermute(value, ("x", "core"), pairs)
+
+
+def after(value, earlier):
+    return lax.optimization_barrier((value, earlier))[0]
 
 
 def edge_exchange(value, offset, step):
@@ -354,15 +361,18 @@
     far_first = x_exchange(far_pass + far_got[2:], 0)
     near_first = x_exchange(near_pass + near_got[2:], 0)
     far_second = x_exchange(far_keep[1] + far_got[1] + far_first[1], 1)
-    far_sum = far_keep[0] + far_got[0] + far_first[0] + far_second
-    other = shifted(far_sum, "y_hi", 1)
+    parts = (far_keep[0], far_got[0], far_first[0], far_second)
+    outer_out = sum(x[:2] for x in parts)
+    outer = shifted(outer_out, "y_hi", 1)
+    centre_out = sum(after(x[2], outer_out) for x in parts)
+    centre_sum = shifted(centre_out, "y_hi", 1)
     near_second = x_exchange(near_keep[1] + near_got[1] + near_first[1], 1)
     near_sum = near_keep[0] + near_got[0] + near_first[0] + near_second
-    early_out, late_out, last_out = edge_values(where, near_sum, other)
+    early_out, late_out, last_out = edge_values(where, near_sum, outer)
     early = edge_exchange(early_out, 0, 4)
     late = edge_exchange(late_out, 1, 2)
     last = edge_exchange(last_out, 2, 4)
-    return proximal(where, block_slots, near_sum, other, early, late, last, omega)
+    return proximal(where, block_slots, near_sum, outer, centre_sum, early, late, last, omega)
 
 
 def solution(mesh):

time: 114 us -> 117 us (1.026)
  waiting for transfers between devices: 36.1 us -> 38 us
    ppermute x4, waiting for transfers between devices: 7.18 us -> 11.4 us  [x_exchange(): return lax.ppermute(value, ('x', 'core'), pairs)]
    ppermute x6 -> x7, starting transfers between devices: 31.7 us -> 33.9 us  [shifted(): return lax.ppermute(value, axis, pairs)]
    ppermute x6 -> x7, waiting for transfers between devices: 27.1 us -> 25 us  [shifted(): return lax.ppermute(value, axis, pairs)]
    ppermute x3, starting transfers between devices: 15.7 us -> 14.5 us  [edge_exchange(): return lax.ppermute(value, 'col', pairs)]
  transfers between devices with their start and end apart: 13 -> 14, of which waited for: 8 -> 8; matrix products, arithmetic and copies ran while one was open for 2% -> 2% of each run, Pallas kernels for 7% -> 6%
where the time goes in v11:
time: 117 us; the launch traced here: 116 us
  starting transfers between devices  59.6 us (51%)
  waiting for transfers between devices  38 us (32%)
  Pallas kernels  12.9 us (11%)
  local copies, waits for them, and re-layouts  5.18 us (4%)
    ppermute x7, starting transfers between devices, shifted(): return lax.ppermute(value, axis, pairs)  33.9 us
    ppermute x7, waiting for transfers between devices, shifted(): return lax.ppermute(value, axis, pairs)  25 us
    ppermute x3, starting transfers between devices, edge_exchange(): return lax.ppermute(value, 'col', pairs)  14.5 us
    ppermute x4, waiting for transfers between devices, x_exchange(): return lax.ppermute(value, ('x', 'core'), pairs)  11.4 us
    ppermute x4, starting transfers between devices, x_exchange(): return lax.ppermute(value, ('x', 'core'), pairs)  11.1 us
    pallas_call x3, Pallas kernels, partial(): pl.pallas_call(lambda *refs: partial_kernel(offset, first, *refs), name='...  6.29 us
    unnamed x7, local copies, waits for them, and re-layouts  3.8 us
    pallas_call x1, Pallas kernels, far_blocks(): pl.pallas_call(far_kernel, name='far_blocks', grid=(1,), out_shape=GROUP_...  3.12 us
  transfers between devices with their start and end apart: 14, of which 8 were waited for; matrix products, arithmetic and copies ran while one was open for 2% of the time, Pallas kernels for 6%

profile of v11, /device:TPU:6, one launch (start us, length us, event | category | flops | bytes accessed | tf_op | source)
XLA Modules:
  0.0 116.2 jit_solution(14415344877530422651)
XLA Ops:
  0.0 3.5 %collective-permute-start = (f32[256,1024]{1,0:T(8,128)}, f32[256,1024]{1,0:T(8,128)S(1)}, u32[]{:S(2)}, u32[]{:S(2)}) collective-permute-start(f32[256,1024]{1,0:T(8,128)} %refs_1_.1), channel_id=1, source_target_pairs={{0,1},{1,2},{2,3},{3,4},{4,5},{5,6},{6,7},{7,8},{8,9},{9,10},{10,1... | collective-permute-start | bytes 3145736 | tf_op jit(solution)/shard_map/ppermute | solution.py:318
  3.5 1.3 %fusion.5 = (f32[128,1024]{1,0:T(8,128)S(1)}, f32[128,1024]{1,0:T(8,128)S(1)}) fusion(f32[256,1024]{1,0:T(8,128)} %refs_1_.1), kind=kLoop, calls=%fused_computation.21 | loop fusion | bytes 2097152 | tf_op jit(solution)/shard_map/slice | solution.py:348
  4.8 12.4 %collective-permute-start.2 = (f32[128,1024]{1,0:T(8,128)S(1)}, f32[128,1024]{1,0:T(8,128)S(1)}, u32[]{:S(2)}, u32[]{:S(2)}) collective-permute-start(f32[128,1024]{1,0:T(8,128)S(1)} %get-tuple-element.47), channel_id=1, source_target_pairs={{0,31},{1,0},{2,1},{3,2},{4,3},{5,4},{6,5},{7,6},{8,7},{9,8},{10,9... | collective-permute-start | bytes 1572872 | tf_op jit(solution)/shard_map/ppermute | solution.py:318
  17.2 3.9 %collective-permute-start.1 = (f32[128,1024]{1,0:T(8,128)S(1)}, f32[128,1024]{1,0:T(8,128)S(1)}, u32[]{:S(2)}, u32[]{:S(2)}) collective-permute-start(f32[128,1024]{1,0:T(8,128)S(1)} %get-tuple-element.48), channel_id=1, source_target_pairs={{0,31},{1,0},{2,1},{3,2},{4,3},{5,4},{6,5},{7,6},{8,7},{9,8},{10,9... | collective-permute-start | bytes 1572872 | tf_op jit(solution)/shard_map/ppermute | solution.py:318
  21.1 0.7 copy.9.refs_0_.slots_ref
  21.8 0.1 stack.23.where_ref
  21.9 0.0 copy-start
  21.9 1.9 %copy-done = f32[1,3,16,128,128]{4,3,2,1,0:T(8,128)S(1)} copy-done((f32[1,3,16,128,128]{4,3,2,1,0:T(8,128)S(1)}, f32[1,3,16,128,128]{4,3,2,1,0:T(8,128)}, u32[]{:S(2)}) %copy-start) | copy-done | bytes 3145752
  23.8 0.0 copy-start.2
  23.8 1.2 %copy-done.2 = f32[256,1024]{1,0:T(8,128)S(1)} copy-done((f32[256,1024]{1,0:T(8,128)S(1)}, f32[256,1024]{1,0:T(8,128)}, u32[]{:S(2)}) %copy-start.2) | copy-done | bytes 1048600
  25.0 0.0 copy-start.1
  25.0 2.3 %partial_residual.3 = (f32[8,256,128]{2,1,0:T(8,128)S(1)}, bf16[8,256,256]{2,1,0:T(8,128)(2,1)S(1)}) custom-call(s32[1,3,16]{2,1,0:T(4,128)S(1)} %copy.9.refs_0_.slots_ref, f32[256,1024]{1,0:T(8,128)S(1)} %copy-done.2, f32[1,3,16,128,128]{4,3,2,1,0:T(8,128)S(1)} %copy-done), custom_call_target="tpu_custom_call" | custom-call | flops 536870912 | bytes 5242880 | tf_op jit(solution)/shard_map/partial_residual/pallas_call | solution.py:194
  27.3 10.9 %collective-permute-done.refs_1_ = f32[256,1024]{1,0:T(8,128)S(1)} collective-permute-done((f32[256,1024]{1,0:T(8,128)}, f32[256,1024]{1,0:T(8,128)S(1)}, u32[]{:S(2)}, u32[]{:S(2)}) %collective-permute-start) | collective-permute-done | bytes 1048608 | tf_op jit(solution)/shard_map/ppermute | solution.py:318
  38.2 0.0 copy-done.1
  38.2 2.2 %partial_residual.4 = (f32[8,256,128]{2,1,0:T(8,128)S(1)}, bf16[8,256,256]{2,1,0:T(8,128)(2,1)S(1)}) custom-call(s32[1,3,16]{2,1,0:T(4,128)S(1)} %copy.9.refs_0_.slots_ref, f32[256,1024]{1,0:T(8,128)S(1)} %collective-permute-done.refs_1_, f32[1,3,16,128,128]{4,3,2,1,0:T(8,128)S(1)} %copy-done.1, f32[8,256,128]{2,1,0:T(8,128)S(1)} %get-tuple-element.26.refs_3_), custom_call_target="tpu_custom_call" | custom-call | flops 536870912 | bytes 5242880 | tf_op jit(solution)/shard_map/partial_residual/pallas_call | solution.py:194
  40.5 1.5 %collective-permute-done.2.refs_1_ = f32[128,1024]{1,0:T(8,128)S(1)} collective-permute-done((f32[128,1024]{1,0:T(8,128)S(1)}, f32[128,1024]{1,0:T(8,128)S(1)}, u32[]{:S(2)}, u32[]{:S(2)}) %collective-permute-start.2) | collective-permute-done | bytes 524320 | tf_op jit(solution)/shard_map/ppermute | solution.py:318
  41.9 1.8 %partial_residual.5 = (f32[8,256,128]{2,1,0:T(8,128)S(1)}, bf16[8,256,128]{2,1,0:T(8,128)(2,1)S(1)}) custom-call(s32[1,3,16]{2,1,0:T(4,128)S(1)} %copy.9.refs_0_.slots_ref, f32[128,1024]{1,0:T(8,128)S(1)} %collective-permute-done.2.refs_1_, f32[1,3,16,128,128]{4,3,2,1,0:T(8,128)S(1)} %copy-done.1, f32[8,256,128]{2,1,0:T(8,128)S(1)} %get-tuple-element.29.refs_3_), custom_call_target="tpu_custom_call" | custom-call | flops 268435456 | bytes 5242880 | tf_op jit(solution)/shard_map/partial_residual/pallas_call | solution.py:194
  43.7 9.3 %collective-permute-done.1.x_ref = f32[128,1024]{1,0:T(8,128)S(1)} collective-permute-done((f32[128,1024]{1,0:T(8,128)S(1)}, f32[128,1024]{1,0:T(8,128)S(1)}, u32[]{:S(2)}, u32[]{:S(2)}) %collective-permute-start.1) | collective-permute-done | bytes 524320 | tf_op jit(solution)/shard_map/ppermute | solution.py:318
  53.1 3.1 %far_blocks.1 = (f32[2,3,128,128]{3,2,1,0:T(8,128)S(1)}, f32[2,3,128,128]{3,2,1,0:T(8,128)S(1)}, f32[4,3,128,128]{3,2,1,0:T(8,128)S(1)}, bf16[8,256,256]{2,1,0:T(8,128)(2,1)S(1)}, bf16[8,256,256]{2,1,0:T(8,128)(2,1)S(1)}) custom-call(s32[1,3,16]{2,1,0:T(4,128)S(1)} %copy.9.refs_0_.slots_ref, s32[5]{0:T(128)S(1)} %stack.23.where_ref, ...), custom_call_target="tpu_custom_call" | custom-call | flops 1342177280 | bytes 8388608 | tf_op jit(solution)/shard_map/far_blocks/pallas_call | solution.py:220
  56.2 1.6 %near_blocks.1 = (f32[2,3,128,128]{3,2,1,0:T(8,128)S(1)}, f32[2,3,128,128]{3,2,1,0:T(8,128)S(1)}, f32[4,3,128,128]{3,2,1,0:T(8,128)S(1)}) custom-call(s32[1,3,16]{2,1,0:T(4,128)S(1)} %copy.9.refs_0_.slots_ref, s32[5]{0:T(128)S(1)} %stack.23.where_ref, bf16[8,256,256]{2,1,0:T(8,128)(2,1)S(1)} %get-tuple-element.27.below_ref, ...), custom_call_target="tpu_custom_call" | custom-call | flops 805306368 | bytes 8388608 | tf_op jit(solution)/shard_map/near_blocks/pallas_call | solution.py:249
  57.8 1.9 %collective-permute-start.3 = (f32[4,3,128,128]{3,2,1,0:T(8,128)S(1)}, f32[4,3,128,128]{3,2,1,0:T(8,128)S(1)}, u32[]{:S(2)}, u32[]{:S(2)}) collective-permute-start(f32[4,3,128,128]{3,2,1,0:T(8,128)S(1)} %get-tuple-element.35), channel_id=1, source_target_pairs={{0,32},{32,0},{1,33},{33,1},{2,34},{34,2},{3,35},{35,3},{4,36},{36... | collective-permute-start | bytes 2359304 | tf_op jit(solution)/shard_map/ppermute | solution.py:318
  59.7 2.4 %collective-permute-start.6 = (f32[4,3,128,128]{3,2,1,0:T(8,128)S(1)}, f32[4,3,128,128]{3,2,1,0:T(8,128)S(1)}, u32[]{:S(2)}, u32[]{:S(2)}) collective-permute-start(f32[4,3,128,128]{3,2,1,0:T(8,128)S(1)} %get-tuple-element.38), channel_id=1, source_target_pairs={{0,32},{32,0},{1,33},{33,1},{2,34},{34,2},{3,35},{35,3},{4,36},{36... | collective-permute-start | bytes 2359304 | tf_op jit(solution)/shard_map/ppermute | solution.py:318
  62.2 0.0 collective-permute-done.3
  62.2 2.7 %collective-permute-start.4 = (f32[2,3,128,128]{3,2,1,0:T(8,128)S(1)}, f32[2,3,128,128]{3,2,1,0:T(8,128)S(1)}, u32[]{:S(2)}, u32[]{:S(2)}) collective-permute-start(f32[2,3,128,128]{3,2,1,0:T(8,128)S(1)} %slice_add_fusion.1), channel_id=1, source_target_pairs={{0,128},{32,416},{128,0},{160,288},{256,384},{288,160},{384,256},{... | collective-permute-start | bytes 1179656 | tf_op jit(solution)/shard_map/ppermute | solution.py:327
  65.0 0.0 collective-permute-done.6
  65.0 3.1 %collective-permute-start.7 = (f32[2,3,128,128]{3,2,1,0:T(8,128)S(1)}, f32[2,3,128,128]{3,2,1,0:T(8,128)S(1)}, u32[]{:S(2)}, u32[]{:S(2)}) collective-permute-start(f32[2,3,128,128]{3,2,1,0:T(8,128)S(1)} %slice_add_fusion), channel_id=1, source_target_pairs={{0,128},{32,416},{128,0},{160,288},{256,384},{288,160},{384,256},{... | collective-permute-start | bytes 1179656 | tf_op jit(solution)/shard_map/ppermute | solution.py:327
  68.1 3.7 %collective-permute-done.4 = f32[2,3,128,128]{3,2,1,0:T(8,128)S(1)} collective-permute-done((f32[2,3,128,128]{3,2,1,0:T(8,128)S(1)}, f32[2,3,128,128]{3,2,1,0:T(8,128)S(1)}, u32[]{:S(2)}, u32[]{:S(2)}) %collective-permute-start.4) | collective-permute-done | bytes 393248 | tf_op jit(solution)/shard_map/ppermute | solution.py:327
  71.9 2.4 %collective-permute-start.5 = (f32[3,128,128]{2,1,0:T(8,128)S(1)}, f32[3,128,128]{2,1,0:T(8,128)S(1)}, u32[]{:S(2)}, u32[]{:S(2)}) collective-permute-start(f32[3,128,128]{2,1,0:T(8,128)S(1)} %fusion.1), channel_id=1, source_target_pairs={{0,384},{32,160},{128,256},{160,32},{256,128},{288,416},{384,0},{4... | collective-permute-start | bytes 589832 | tf_op jit(solution)/shard_map/ppermute | solution.py:327
  74.3 1.8 %collective-permute-done.7 = f32[2,3,128,128]{3,2,1,0:T(8,128)S(1)} collective-permute-done((f32[2,3,128,128]{3,2,1,0:T(8,128)S(1)}, f32[2,3,128,128]{3,2,1,0:T(8,128)S(1)}, u32[]{:S(2)}, u32[]{:S(2)}) %collective-permute-start.7) | collective-permute-done | bytes 393248 | tf_op jit(solution)/shard_map/ppermute | solution.py:327
  76.1 2.9 %collective-permute-start.8 = (f32[3,128,128]{2,1,0:T(8,128)S(1)}, f32[3,128,128]{2,1,0:T(8,128)S(1)}, u32[]{:S(2)}, u32[]{:S(2)}) collective-permute-start(f32[3,128,128]{2,1,0:T(8,128)S(1)} %fusion), channel_id=1, source_target_pairs={{0,384},{32,160},{128,256},{160,32},{256,128},{288,416},{384,0},{4... | collective-permute-start | bytes 589832 | tf_op jit(solution)/shard_map/ppermute | solution.py:327
  79.1 5.9 %collective-permute-done.8 = f32[3,128,128]{2,1,0:T(8,128)S(1)} collective-permute-done((f32[3,128,128]{2,1,0:T(8,128)S(1)}, f32[3,128,128]{2,1,0:T(8,128)S(1)}, u32[]{:S(2)}, u32[]{:S(2)}) %collective-permute-start.8) | collective-permute-done | bytes 196640 | tf_op jit(solution)/shard_map/ppermute | solution.py:327
  84.9 7.5 %collective-permute-start.9 = (f32[2,128,128]{2,1,0:T(8,128)S(1)}, f32[2,128,128]{2,1,0:T(8,128)S(1)}, u32[]{:S(2)}, u32[]{:S(2)}) collective-permute-start(f32[2,128,128]{2,1,0:T(8,128)S(1)} %slice_add_fusion.8), channel_id=1, source_target_pairs={{0,64},{64,0},{1,65},{65,1},{2,66},{66,2},{3,67},{67,3},{4,68},{68... | collective-permute-start | bytes 393224 | tf_op jit(solution)/shard_map/ppermute | solution.py:318
  92.5 2.2 %collective-permute-start.10 = (f32[128,128]{1,0:T(8,128)S(1)}, f32[128,128]{1,0:T(8,128)S(1)}, u32[]{:S(2)}, u32[]{:S(2)}) collective-permute-start(f32[128,128]{1,0:T(8,128)S(1)} %add_add_fusion), channel_id=1, source_target_pairs={{0,64},{64,0},{1,65},{65,1},{2,66},{66,2},{3,67},{67,3},{4,68},{68... | collective-permute-start | bytes 196616 | tf_op jit(solution)/shard_map/ppermute | solution.py:318
  94.7 0.0 collective-permute-done.5
  94.8 3.3 %collective-permute-done.9.outer_ref = f32[2,128,128]{2,1,0:T(8,128)S(1)} collective-permute-done((f32[2,128,128]{2,1,0:T(8,128)S(1)}, f32[2,128,128]{2,1,0:T(8,128)S(1)}, u32[]{:S(2)}, u32[]{:S(2)}) %collective-permute-start.9) | collective-permute-done | bytes 131104 | tf_op jit(solution)/shard_map/ppermute | solution.py:318
  98.1 0.6 edge_values.1
  98.6 1.9 %collective-permute-start.11 = (f32[128,128]{1,0:T(8,128)S(1)}, f32[128,128]{1,0:T(8,128)S(1)}, u32[]{:S(2)}, u32[]{:S(2)}) collective-permute-start(f32[128,128]{1,0:T(8,128)S(1)} %get-tuple-element.44), channel_id=1, source_target_pairs={{0,1},{1,0},{4,5},{5,4},{8,9},{9,8},{12,13},{13,12},{16,17},{17,16... | collective-permute-start | bytes 196616 | tf_op jit(solution)/shard_map/ppermute | solution.py:339
  100.6 11.9 %collective-permute-start.12 = (f32[128,128]{1,0:T(8,128)S(1)}, f32[128,128]{1,0:T(8,128)S(1)}, u32[]{:S(2)}, u32[]{:S(2)}) collective-permute-start(f32[128,128]{1,0:T(8,128)S(1)} %get-tuple-element.45), channel_id=1, source_target_pairs={{1,2},{2,1},{3,4},{4,3},{5,6},{6,5},{7,8},{8,7},{9,10},{10,9},{11,... | collective-permute-start | bytes 196616 | tf_op jit(solution)/shard_map/ppermute | solution.py:339
  112.5 0.7 collective-permute-start.13
  113.2 0.0 collective-permute-done.10.centre_ref
  113.2 0.0 collective-permute-done.11.early_ref
  113.2 1.6 %collective-permute-done.12.late_ref = f32[128,128]{1,0:T(8,128)S(1)} collective-permute-done((f32[128,128]{1,0:T(8,128)S(1)}, f32[128,128]{1,0:T(8,128)S(1)}, u32[]{:S(2)}, u32[]{:S(2)}) %collective-permute-start.12) | collective-permute-done | bytes 65568 | tf_op jit(solution)/shard_map/ppermute | solution.py:339
  114.8 0.0 collective-permute-done.13.last_ref
  114.8 1.4 %proximal.1 = f32[1,3,1,128,128]{4,3,2,1,0:T(8,128)} custom-call(s32[5]{0:T(128)S(1)} %stack.23.where_ref, s32[1,3,16]{2,1,0:T(4,128)S(1)} %copy.9.refs_0_.slots_ref, f32[3,128,128]{2,1,0:T(8,128)S(1)} %fusion.3.near_ref, f32[2,128,128]{2,1,0:T(8,128)S(1)} %collective-permute-done.9.outer_ref, f32[128,128]{1,0:T(8,128)S(1)} %collective-permute-done.10.centre_ref, ...), custom_call_target="tpu_custom_call" | custom-call | flops 983040 | bytes 524288 | tf_op jit(solution)/shard_map/proximal/pallas_call | solution.py:296
  (11 shorter events, 0.3 us)
Async XLA Ops:
  0.0 38.2 %collective-permute-start = (f32[256,1024]{1,0:T(8,128)}, f32[256,1024]{1,0:T(8,128)S(1)}, u32[]{:S(2)}, u32[]{:S(2)}) collective-permute-start(f32[256,1024]{1,0:T(8,128)} %refs_1_.1), channel_id=1, source_target_pairs={{0,1},{1,2},{2,3},{3,4},{4,5},{5,6},{6,7},{7,8},{8,9},{9,10},{10,1... | collective-permute-start | bytes 3145736 | tf_op jit(solution)/shard_map/ppermute | solution.py:318
  4.8 37.2 %collective-permute-start.2 = (f32[128,1024]{1,0:T(8,128)S(1)}, f32[128,1024]{1,0:T(8,128)S(1)}, u32[]{:S(2)}, u32[]{:S(2)}) collective-permute-start(f32[128,1024]{1,0:T(8,128)S(1)} %get-tuple-element.47), channel_id=1, source_target_pairs={{0,31},{1,0},{2,1},{3,2},{4,3},{5,4},{6,5},{7,6},{8,7},{9,8},{10,9... | collective-permute-start | bytes 1572872 | tf_op jit(solution)/shard_map/ppermute | solution.py:318
  17.2 35.9 %collective-permute-start.1 = (f32[128,1024]{1,0:T(8,128)S(1)}, f32[128,1024]{1,0:T(8,128)S(1)}, u32[]{:S(2)}, u32[]{:S(2)}) collective-permute-start(f32[128,1024]{1,0:T(8,128)S(1)} %get-tuple-element.48), channel_id=1, source_target_pairs={{0,31},{1,0},{2,1},{3,2},{4,3},{5,4},{6,5},{7,6},{8,7},{9,8},{10,9... | collective-permute-start | bytes 1572872 | tf_op jit(solution)/shard_map/ppermute | solution.py:318
  21.9 1.9 %copy-start = (f32[1,3,16,128,128]{4,3,2,1,0:T(8,128)S(1)}, f32[1,3,16,128,128]{4,3,2,1,0:T(8,128)}, u32[]{:S(2)}) copy-start(f32[1,3,16,128,128]{4,3,2,1,0:T(8,128)} %omega_ref.3) | copy-start | bytes 9437188
  23.8 1.2 %copy-start.2 = (f32[256,1024]{1,0:T(8,128)S(1)}, f32[256,1024]{1,0:T(8,128)}, u32[]{:S(2)}) copy-start(f32[256,1024]{1,0:T(8,128)} %refs_1_.1) | copy-start | bytes 3145732
  25.0 13.2 %copy-start.1 = (f32[1,3,16,128,128]{4,3,2,1,0:T(8,128)S(1)}, f32[1,3,16,128,128]{4,3,2,1,0:T(8,128)}, u32[]{:S(2)}) copy-start(f32[1,3,16,128,128]{4,3,2,1,0:T(8,128)} %omega_ref.3) | copy-start | bytes 9437188
  57.8 4.4 %collective-permute-start.3 = (f32[4,3,128,128]{3,2,1,0:T(8,128)S(1)}, f32[4,3,128,128]{3,2,1,0:T(8,128)S(1)}, u32[]{:S(2)}, u32[]{:S(2)}) collective-permute-start(f32[4,3,128,128]{3,2,1,0:T(8,128)S(1)} %get-tuple-element.35), channel_id=1, source_target_pairs={{0,32},{32,0},{1,33},{33,1},{2,34},{34,2},{3,35},{35,3},{4,36},{36... | collective-permute-start | bytes 2359304 | tf_op jit(solution)/shard_map/ppermute | solution.py:318
  59.7 5.2 %collective-permute-start.6 = (f32[4,3,128,128]{3,2,1,0:T(8,128)S(1)}, f32[4,3,128,128]{3,2,1,0:T(8,128)S(1)}, u32[]{:S(2)}, u32[]{:S(2)}) collective-permute-start(f32[4,3,128,128]{3,2,1,0:T(8,128)S(1)} %get-tuple-element.38), channel_id=1, source_target_pairs={{0,32},{32,0},{1,33},{33,1},{2,34},{34,2},{3,35},{35,3},{4,36},{36... | collective-permute-start | bytes 2359304 | tf_op jit(solution)/shard_map/ppermute | solution.py:318
  62.2 9.7 %collective-permute-start.4 = (f32[2,3,128,128]{3,2,1,0:T(8,128)S(1)}, f32[2,3,128,128]{3,2,1,0:T(8,128)S(1)}, u32[]{:S(2)}, u32[]{:S(2)}) collective-permute-start(f32[2,3,128,128]{3,2,1,0:T(8,128)S(1)} %slice_add_fusion.1), channel_id=1, source_target_pairs={{0,128},{32,416},{128,0},{160,288},{256,384},{288,160},{384,256},{... | collective-permute-start | bytes 1179656 | tf_op jit(solution)/shard_map/ppermute | solution.py:327
  65.0 11.1 %collective-permute-start.7 = (f32[2,3,128,128]{3,2,1,0:T(8,128)S(1)}, f32[2,3,128,128]{3,2,1,0:T(8,128)S(1)}, u32[]{:S(2)}, u32[]{:S(2)}) collective-permute-start(f32[2,3,128,128]{3,2,1,0:T(8,128)S(1)} %slice_add_fusion), channel_id=1, source_target_pairs={{0,128},{32,416},{128,0},{160,288},{256,384},{288,160},{384,256},{... | collective-permute-start | bytes 1179656 | tf_op jit(solution)/shard_map/ppermute | solution.py:327
  71.9 22.8 %collective-permute-start.5 = (f32[3,128,128]{2,1,0:T(8,128)S(1)}, f32[3,128,128]{2,1,0:T(8,128)S(1)}, u32[]{:S(2)}, u32[]{:S(2)}) collective-permute-start(f32[3,128,128]{2,1,0:T(8,128)S(1)} %fusion.1), channel_id=1, source_target_pairs={{0,384},{32,160},{128,256},{160,32},{256,128},{288,416},{384,0},{4... | collective-permute-start | bytes 589832 | tf_op jit(solution)/shard_map/ppermute | solution.py:327
  76.1 8.8 %collective-permute-start.8 = (f32[3,128,128]{2,1,0:T(8,128)S(1)}, f32[3,128,128]{2,1,0:T(8,128)S(1)}, u32[]{:S(2)}, u32[]{:S(2)}) collective-permute-start(f32[3,128,128]{2,1,0:T(8,128)S(1)} %fusion), channel_id=1, source_target_pairs={{0,384},{32,160},{128,256},{160,32},{256,128},{288,416},{384,0},{4... | collective-permute-start | bytes 589832 | tf_op jit(solution)/shard_map/ppermute | solution.py:327
  84.9 13.1 %collective-permute-start.9 = (f32[2,128,128]{2,1,0:T(8,128)S(1)}, f32[2,128,128]{2,1,0:T(8,128)S(1)}, u32[]{:S(2)}, u32[]{:S(2)}) collective-permute-start(f32[2,128,128]{2,1,0:T(8,128)S(1)} %slice_add_fusion.8), channel_id=1, source_target_pairs={{0,64},{64,0},{1,65},{65,1},{2,66},{66,2},{3,67},{67,3},{4,68},{68... | collective-permute-start | bytes 393224 | tf_op jit(solution)/shard_map/ppermute | solution.py:318
  92.5 20.7 %collective-permute-start.10 = (f32[128,128]{1,0:T(8,128)S(1)}, f32[128,128]{1,0:T(8,128)S(1)}, u32[]{:S(2)}, u32[]{:S(2)}) collective-permute-start(f32[128,128]{1,0:T(8,128)S(1)} %add_add_fusion), channel_id=1, source_target_pairs={{0,64},{64,0},{1,65},{65,1},{2,66},{66,2},{3,67},{67,3},{4,68},{68... | collective-permute-start | bytes 196616 | tf_op jit(solution)/shard_map/ppermute | solution.py:318
  98.6 14.6 %collective-permute-start.11 = (f32[128,128]{1,0:T(8,128)S(1)}, f32[128,128]{1,0:T(8,128)S(1)}, u32[]{:S(2)}, u32[]{:S(2)}) collective-permute-start(f32[128,128]{1,0:T(8,128)S(1)} %get-tuple-element.44), channel_id=1, source_target_pairs={{0,1},{1,0},{4,5},{5,4},{8,9},{9,8},{12,13},{13,12},{16,17},{17,16... | collective-permute-start | bytes 196616 | tf_op jit(solution)/shard_map/ppermute | solution.py:339
  100.6 14.3 %collective-permute-start.12 = (f32[128,128]{1,0:T(8,128)S(1)}, f32[128,128]{1,0:T(8,128)S(1)}, u32[]{:S(2)}, u32[]{:S(2)}) collective-permute-start(f32[128,128]{1,0:T(8,128)S(1)} %get-tuple-element.45), channel_id=1, source_target_pairs={{1,2},{2,1},{3,4},{4,3},{5,6},{6,5},{7,8},{8,7},{9,10},{10,9},{11,... | collective-permute-start | bytes 196616 | tf_op jit(solution)/shard_map/ppermute | solution.py:339
  112.5 2.3 %collective-permute-start.13 = (f32[128,128]{1,0:T(8,128)S(1)}, f32[128,128]{1,0:T(8,128)S(1)}, u32[]{:S(2)}, u32[]{:S(2)}) collective-permute-start(f32[128,128]{1,0:T(8,128)S(1)} %get-tuple-element.46), channel_id=1, source_target_pairs={{2,3},{3,2},{6,7},{7,6},{10,11},{11,10},{14,15},{15,14},{18,19},{1... | collective-permute-start | bytes 196616 | tf_op jit(solution)/shard_map/ppermute | solution.py:339

commit v12 on v11

--- a/solution.py
+++ b/solution.py
@@ -262,8 +262,13 @@
     )(slots, where, below, centre, above, pieces)
 
 
-def edge_kernel(where_ref, near_ref, outer_ref, early_ref, late_ref, last_ref):
+def edge_kernel(
+    where_ref, outer_ref, keep_ref, got_ref, first_ref, second_ref,
+    near_ref, early_ref, late_ref, last_ref,
+):
     odd_tile = where_ref[4] == 1
+    for e in range(3):
+        near_ref[e] = keep_ref[0, e] + got_ref[0, e] + first_ref[0, e] + second_ref[e]
     downward = near_ref[0] + outer_ref[0]
     upward = near_ref[1] + outer_ref[1]
     late_ref[...] = jnp.where(odd_tile, upward, downward)
@@ -272,20 +277,20 @@
     last_ref[...] = short
 
 
-def edge_values(where, near, outer):
-    block = jax.ShapeDtypeStruct((BLK, BLK), f32)
+def edge_values(where, *parts):
+    shapes = ((3, BLK, BLK),) + ((BLK, BLK),) * 3
     return pl.pallas_call(
         edge_kernel,
         name="edge_values",
         grid=(1,),
-        out_shape=(block,) * 3,
-        in_specs=[SMEM, full_spec((3, BLK, BLK)), full_spec((2, BLK, BLK))],
-        out_specs=(full_spec((BLK, BLK)),) * 3,
-        compiler_params=params(),
-        cost_estimate=pl.CostEstimate(
-            flops=4 * BLK * BLK, bytes_accessed=6 * 4 * BLK * BLK, transcendentals=0
-        ),
-    )(where, near, outer)
+        out_shape=tuple(jax.ShapeDtypeStruct(shape, f32) for shape in shapes),
+        in_specs=[SMEM] + [full_spec(part.shape) for part in parts],
+        out_specs=tuple(full_spec(shape) for shape in shapes),
+        compiler_params=params(),
+        cost_estimate=pl.CostEstimate(
+            flops=16 * BLK * BLK, bytes_accessed=20 * 4 * BLK * BLK, transcendentals=0
+        ),
+    )(where, *parts)
 
 
 def proximal(where, slots, near, outer, centre, early, late, last, omega):
@@ -364,11 +369,12 @@
     parts = (far_keep[0], far_got[0], far_first[0], far_second)
     outer_out = sum(x[:2] for x in parts)
     outer = shifted(outer_out, "y_hi", 1)
-    centre_out = sum(after(x[2], outer_out) for x in parts)
+    centre_out = sum(x[2] for x in parts[:3]) + after(far_second, outer_out)[2]
     centre_sum = shifted(centre_out, "y_hi", 1)
     near_second = x_exchange(near_keep[1] + near_got[1] + near_first[1], 1)
-    near_sum = near_keep[0] + near_got[0] + near_first[0] + near_second
-    early_out, late_out, last_out = edge_values(where, near_sum, outer)
+    near_sum, early_out, late_out, last_out = edge_values(
+        where, outer, near_keep, near_got, near_first, near_second
+    )
     early = edge_exchange(early_out, 0, 4)
     late = edge_exchange(late_out, 1, 2)
     last = edge_exchange(last_out, 2, 4)

time: 117 us -> 113 us (0.966)
  waiting for transfers between devices: 38 us -> 33.5 us
    ppermute x4, waiting for transfers between devices: 11.4 us -> 7.17 us  [x_exchange(): return lax.ppermute(value, ('x', 'core'), pairs)]
  transfers between devices with their start and end apart: 14 -> 14, of which waited for: 8 -> 8; matrix products, arithmetic and copies ran while one was open for 2% -> 2% of each run, Pallas kernels for 6% -> 8%
where the time goes in v12:
time: 113 us; the launch traced here: 112 us
  starting transfers between devices  59.9 us (53%)
  waiting for transfers between devices  33.5 us (30%)
  Pallas kernels  13 us (12%)
  local copies, waits for them, and re-layouts  5.16 us (5%)
    ppermute x7, starting transfers between devices, shifted(): return lax.ppermute(value, axis, pairs)  33.9 us
    ppermute x7, waiting for transfers between devices, shifted(): return lax.ppermute(value, axis, pairs)  24.7 us
    ppermute x3, starting transfers between devices, edge_exchange(): return lax.ppermute(value, 'col', pairs)  14.9 us
    ppermute x4, starting transfers between devices, x_exchange(): return lax.ppermute(value, ('x', 'core'), pairs)  11.1 us
    ppermute x4, waiting for transfers between devices, x_exchange(): return lax.ppermute(value, ('x', 'core'), pairs)  7.17 us
    pallas_call x3, Pallas kernels, partial(): pl.pallas_call(lambda *refs: partial_kernel(offset, first, *refs), name='...  6.29 us
    unnamed x7, local copies, waits for them, and re-layouts  3.8 us
    pallas_call x1, Pallas kernels, far_blocks(): pl.pallas_call(far_kernel, name='far_blocks', grid=(1,), out_shape=GROUP_...  3.12 us
  transfers between devices with their start and end apart: 14, of which 8 were waited for; matrix products, arithmetic and copies ran while one was open for 2% of the time, Pallas kernels for 8%

profile of v12, /device:TPU:6, one launch (start us, length us, event | category | flops | bytes accessed | tf_op | source)
XLA Modules:
  0.0 112.1 jit_solution(7063716175371498766)
XLA Ops:
  0.0 3.5 %collective-permute-start.2 = (f32[256,1024]{1,0:T(8,128)}, f32[256,1024]{1,0:T(8,128)S(1)}, u32[]{:S(2)}, u32[]{:S(2)}) collective-permute-start(f32[256,1024]{1,0:T(8,128)} %refs_1_.1), channel_id=1, source_target_pairs={{0,1},{1,2},{2,3},{3,4},{4,5},{5,6},{6,7},{7,8},{8,9},{9,10},{10,1... | collective-permute-start | bytes 3145736 | tf_op jit(solution)/shard_map/ppermute | solution.py:323
  3.5 1.3 %fusion.5 = (f32[128,1024]{1,0:T(8,128)S(1)}, f32[128,1024]{1,0:T(8,128)S(1)}) fusion(f32[256,1024]{1,0:T(8,128)} %refs_1_.1), kind=kLoop, calls=%fused_computation.16 | loop fusion | bytes 2097152 | tf_op jit(solution)/shard_map/slice | solution.py:353
  4.8 12.4 %collective-permute-start.1 = (f32[128,1024]{1,0:T(8,128)S(1)}, f32[128,1024]{1,0:T(8,128)S(1)}, u32[]{:S(2)}, u32[]{:S(2)}) collective-permute-start(f32[128,1024]{1,0:T(8,128)S(1)} %get-tuple-element.43), channel_id=1, source_target_pairs={{0,31},{1,0},{2,1},{3,2},{4,3},{5,4},{6,5},{7,6},{8,7},{9,8},{10,9... | collective-permute-start | bytes 1572872 | tf_op jit(solution)/shard_map/ppermute | solution.py:323
  17.2 3.9 %collective-permute-start = (f32[128,1024]{1,0:T(8,128)S(1)}, f32[128,1024]{1,0:T(8,128)S(1)}, u32[]{:S(2)}, u32[]{:S(2)}) collective-permute-start(f32[128,1024]{1,0:T(8,128)S(1)} %get-tuple-element.44), channel_id=1, source_target_pairs={{0,31},{1,0},{2,1},{3,2},{4,3},{5,4},{6,5},{7,6},{8,7},{9,8},{10,9... | collective-permute-start | bytes 1572872 | tf_op jit(solution)/shard_map/ppermute | solution.py:323
  21.1 0.7 copy.9.refs_0_.slots_ref
  21.8 0.1 stack.23.where_ref
  21.9 0.0 copy-start
  21.9 1.9 %copy-done = f32[1,3,16,128,128]{4,3,2,1,0:T(8,128)S(1)} copy-done((f32[1,3,16,128,128]{4,3,2,1,0:T(8,128)S(1)}, f32[1,3,16,128,128]{4,3,2,1,0:T(8,128)}, u32[]{:S(2)}) %copy-start) | copy-done | bytes 3145752
  23.8 0.0 copy-start.2
  23.8 1.2 %copy-done.2 = f32[256,1024]{1,0:T(8,128)S(1)} copy-done((f32[256,1024]{1,0:T(8,128)S(1)}, f32[256,1024]{1,0:T(8,128)}, u32[]{:S(2)}) %copy-start.2) | copy-done | bytes 1048600
  25.0 0.0 copy-start.1
  25.0 2.3 %partial_residual.3 = (f32[8,256,128]{2,1,0:T(8,128)S(1)}, bf16[8,256,256]{2,1,0:T(8,128)(2,1)S(1)}) custom-call(s32[1,3,16]{2,1,0:T(4,128)S(1)} %copy.9.refs_0_.slots_ref, f32[256,1024]{1,0:T(8,128)S(1)} %copy-done.2, f32[1,3,16,128,128]{4,3,2,1,0:T(8,128)S(1)} %copy-done), custom_call_target="tpu_custom_call" | custom-call | flops 536870912 | bytes 5242880 | tf_op jit(solution)/shard_map/partial_residual/pallas_call | solution.py:194
  27.3 10.9 %collective-permute-done.2.refs_1_ = f32[256,1024]{1,0:T(8,128)S(1)} collective-permute-done((f32[256,1024]{1,0:T(8,128)}, f32[256,1024]{1,0:T(8,128)S(1)}, u32[]{:S(2)}, u32[]{:S(2)}) %collective-permute-start.2) | collective-permute-done | bytes 1048608 | tf_op jit(solution)/shard_map/ppermute | solution.py:323
  38.2 0.0 copy-done.1
  38.2 2.2 %partial_residual.4 = (f32[8,256,128]{2,1,0:T(8,128)S(1)}, bf16[8,256,256]{2,1,0:T(8,128)(2,1)S(1)}) custom-call(s32[1,3,16]{2,1,0:T(4,128)S(1)} %copy.9.refs_0_.slots_ref, f32[256,1024]{1,0:T(8,128)S(1)} %collective-permute-done.2.refs_1_, f32[1,3,16,128,128]{4,3,2,1,0:T(8,128)S(1)} %copy-done.1, f32[8,256,128]{2,1,0:T(8,128)S(1)} %get-tuple-element.24.refs_3_), custom_call_target="tpu_custom_call" | custom-call | flops 536870912 | bytes 5242880 | tf_op jit(solution)/shard_map/partial_residual/pallas_call | solution.py:194
  40.5 1.5 %collective-permute-done.1.refs_1_ = f32[128,1024]{1,0:T(8,128)S(1)} collective-permute-done((f32[128,1024]{1,0:T(8,128)S(1)}, f32[128,1024]{1,0:T(8,128)S(1)}, u32[]{:S(2)}, u32[]{:S(2)}) %collective-permute-start.1) | collective-permute-done | bytes 524320 | tf_op jit(solution)/shard_map/ppermute | solution.py:323
  41.9 1.8 %partial_residual.5 = (f32[8,256,128]{2,1,0:T(8,128)S(1)}, bf16[8,256,128]{2,1,0:T(8,128)(2,1)S(1)}) custom-call(s32[1,3,16]{2,1,0:T(4,128)S(1)} %copy.9.refs_0_.slots_ref, f32[128,1024]{1,0:T(8,128)S(1)} %collective-permute-done.1.refs_1_, f32[1,3,16,128,128]{4,3,2,1,0:T(8,128)S(1)} %copy-done.1, f32[8,256,128]{2,1,0:T(8,128)S(1)} %get-tuple-element.25.refs_3_), custom_call_target="tpu_custom_call" | custom-call | flops 268435456 | bytes 5242880 | tf_op jit(solution)/shard_map/partial_residual/pallas_call | solution.py:194
  43.7 9.3 %collective-permute-done.x_ref = f32[128,1024]{1,0:T(8,128)S(1)} collective-permute-done((f32[128,1024]{1,0:T(8,128)S(1)}, f32[128,1024]{1,0:T(8,128)S(1)}, u32[]{:S(2)}, u32[]{:S(2)}) %collective-permute-start) | collective-permute-done | bytes 524320 | tf_op jit(solution)/shard_map/ppermute | solution.py:323
  53.1 3.1 %far_blocks.1 = (f32[2,3,128,128]{3,2,1,0:T(8,128)S(1)}, f32[2,3,128,128]{3,2,1,0:T(8,128)S(1)}, f32[4,3,128,128]{3,2,1,0:T(8,128)S(1)}, bf16[8,256,256]{2,1,0:T(8,128)(2,1)S(1)}, bf16[8,256,256]{2,1,0:T(8,128)(2,1)S(1)}) custom-call(s32[1,3,16]{2,1,0:T(4,128)S(1)} %copy.9.refs_0_.slots_ref, s32[5]{0:T(128)S(1)} %stack.23.where_ref, ...), custom_call_target="tpu_custom_call" | custom-call | flops 1342177280 | bytes 8388608 | tf_op jit(solution)/shard_map/far_blocks/pallas_call | solution.py:220
  56.2 1.9 %collective-permute-start.3 = (f32[4,3,128,128]{3,2,1,0:T(8,128)S(1)}, f32[4,3,128,128]{3,2,1,0:T(8,128)S(1)}, u32[]{:S(2)}, u32[]{:S(2)}) collective-permute-start(f32[4,3,128,128]{3,2,1,0:T(8,128)S(1)} %get-tuple-element.31), channel_id=1, source_target_pairs={{0,32},{32,0},{1,33},{33,1},{2,34},{34,2},{3,35},{35,3},{4,36},{36... | collective-permute-start | bytes 2359304 | tf_op jit(solution)/shard_map/ppermute | solution.py:323
  58.1 1.6 %near_blocks.1 = (f32[2,3,128,128]{3,2,1,0:T(8,128)S(1)}, f32[2,3,128,128]{3,2,1,0:T(8,128)S(1)}, f32[4,3,128,128]{3,2,1,0:T(8,128)S(1)}) custom-call(s32[1,3,16]{2,1,0:T(4,128)S(1)} %copy.9.refs_0_.slots_ref, s32[5]{0:T(128)S(1)} %stack.23.where_ref, bf16[8,256,256]{2,1,0:T(8,128)(2,1)S(1)} %get-tuple-element.28.below_ref, ...), custom_call_target="tpu_custom_call" | custom-call | flops 805306368 | bytes 8388608 | tf_op jit(solution)/shard_map/near_blocks/pallas_call | solution.py:249
  59.7 2.4 %collective-permute-start.7 = (f32[4,3,128,128]{3,2,1,0:T(8,128)S(1)}, f32[4,3,128,128]{3,2,1,0:T(8,128)S(1)}, u32[]{:S(2)}, u32[]{:S(2)}) collective-permute-start(f32[4,3,128,128]{3,2,1,0:T(8,128)S(1)} %get-tuple-element.36), channel_id=1, source_target_pairs={{0,32},{32,0},{1,33},{33,1},{2,34},{34,2},{3,35},{35,3},{4,36},{36... | collective-permute-start | bytes 2359304 | tf_op jit(solution)/shard_map/ppermute | solution.py:323
  62.1 0.0 collective-permute-done.3
  62.2 2.7 %collective-permute-start.4 = (f32[2,3,128,128]{3,2,1,0:T(8,128)S(1)}, f32[2,3,128,128]{3,2,1,0:T(8,128)S(1)}, u32[]{:S(2)}, u32[]{:S(2)}) collective-permute-start(f32[2,3,128,128]{3,2,1,0:T(8,128)S(1)} %slice_add_fusion.1), channel_id=1, source_target_pairs={{0,128},{32,416},{128,0},{160,288},{256,384},{288,160},{384,256},{... | collective-permute-start | bytes 1179656 | tf_op jit(solution)/shard_map/ppermute | solution.py:332
  65.0 0.0 collective-permute-done.7.got_ref
  65.0 0.1 slice_add_fusion
  65.0 3.1 %collective-permute-start.8 = (f32[2,3,128,128]{3,2,1,0:T(8,128)S(1)}, f32[2,3,128,128]{3,2,1,0:T(8,128)S(1)}, u32[]{:S(2)}, u32[]{:S(2)}) collective-permute-start(f32[2,3,128,128]{3,2,1,0:T(8,128)S(1)} %slice_add_fusion), channel_id=1, source_target_pairs={{0,128},{32,416},{128,0},{160,288},{256,384},{288,160},{384,256},{... | collective-permute-start | bytes 1179656 | tf_op jit(solution)/shard_map/ppermute | solution.py:332
  68.1 3.7 %collective-permute-done.4 = f32[2,3,128,128]{3,2,1,0:T(8,128)S(1)} collective-permute-done((f32[2,3,128,128]{3,2,1,0:T(8,128)S(1)}, f32[2,3,128,128]{3,2,1,0:T(8,128)S(1)}, u32[]{:S(2)}, u32[]{:S(2)}) %collective-permute-start.4) | collective-permute-done | bytes 393248 | tf_op jit(solution)/shard_map/ppermute | solution.py:332
  71.9 2.4 %collective-permute-start.5 = (f32[3,128,128]{2,1,0:T(8,128)S(1)}, f32[3,128,128]{2,1,0:T(8,128)S(1)}, u32[]{:S(2)}, u32[]{:S(2)}) collective-permute-start(f32[3,128,128]{2,1,0:T(8,128)S(1)} %fusion.1), channel_id=1, source_target_pairs={{0,384},{32,160},{128,256},{160,32},{256,128},{288,416},{384,0},{4... | collective-permute-start | bytes 589832 | tf_op jit(solution)/shard_map/ppermute | solution.py:332
  74.3 1.8 %collective-permute-done.8.first_ref = f32[2,3,128,128]{3,2,1,0:T(8,128)S(1)} collective-permute-done((f32[2,3,128,128]{3,2,1,0:T(8,128)S(1)}, f32[2,3,128,128]{3,2,1,0:T(8,128)S(1)}, u32[]{:S(2)}, u32[]{:S(2)}) %collective-permute-start.8) | collective-permute-done | bytes 393248 | tf_op jit(solution)/shard_map/ppermute | solution.py:332
  76.1 2.9 %collective-permute-start.9 = (f32[3,128,128]{2,1,0:T(8,128)S(1)}, f32[3,128,128]{2,1,0:T(8,128)S(1)}, u32[]{:S(2)}, u32[]{:S(2)}) collective-permute-start(f32[3,128,128]{2,1,0:T(8,128)S(1)} %fusion), channel_id=1, source_target_pairs={{0,384},{32,160},{128,256},{160,32},{256,128},{288,416},{384,0},{4... | collective-permute-start | bytes 589832 | tf_op jit(solution)/shard_map/ppermute | solution.py:332
  79.0 1.7 %collective-permute-done.5 = f32[3,128,128]{2,1,0:T(8,128)S(1)} collective-permute-done((f32[3,128,128]{2,1,0:T(8,128)S(1)}, f32[3,128,128]{2,1,0:T(8,128)S(1)}, u32[]{:S(2)}, u32[]{:S(2)}) %collective-permute-start.5) | collective-permute-done | bytes 196640 | tf_op jit(solution)/shard_map/ppermute | solution.py:332
  80.7 7.5 %collective-permute-start.6 = (f32[2,128,128]{2,1,0:T(8,128)S(1)}, f32[2,128,128]{2,1,0:T(8,128)S(1)}, u32[]{:S(2)}, u32[]{:S(2)}) collective-permute-start(f32[2,128,128]{2,1,0:T(8,128)S(1)} %slice_add_fusion.6), channel_id=1, source_target_pairs={{0,64},{64,0},{1,65},{65,1},{2,66},{66,2},{3,67},{67,3},{4,68},{68... | collective-permute-start | bytes 393224 | tf_op jit(solution)/shard_map/ppermute | solution.py:323
  88.3 2.2 %collective-permute-start.10 = (f32[128,128]{1,0:T(8,128)S(1)}, f32[128,128]{1,0:T(8,128)S(1)}, u32[]{:S(2)}, u32[]{:S(2)}) collective-permute-start(f32[128,128]{1,0:T(8,128)S(1)} %fusion.4), channel_id=1, source_target_pairs={{0,64},{64,0},{1,65},{65,1},{2,66},{66,2},{3,67},{67,3},{4,68},{68... | collective-permute-start | bytes 196616 | tf_op jit(solution)/shard_map/ppermute | solution.py:323
  90.5 0.0 collective-permute-done.9.second_ref
  90.5 2.9 %collective-permute-done.6.outer_ref = f32[2,128,128]{2,1,0:T(8,128)S(1)} collective-permute-done((f32[2,128,128]{2,1,0:T(8,128)S(1)}, f32[2,128,128]{2,1,0:T(8,128)S(1)}, u32[]{:S(2)}, u32[]{:S(2)}) %collective-permute-start.6) | collective-permute-done | bytes 131104 | tf_op jit(solution)/shard_map/ppermute | solution.py:323
  93.5 0.6 edge_values.1
  94.1 2.2 %collective-permute-start.11 = (f32[128,128]{1,0:T(8,128)S(1)}, f32[128,128]{1,0:T(8,128)S(1)}, u32[]{:S(2)}, u32[]{:S(2)}) collective-permute-start(f32[128,128]{1,0:T(8,128)S(1)} %get-tuple-element.40), channel_id=1, source_target_pairs={{0,1},{1,0},{4,5},{5,4},{8,9},{9,8},{12,13},{13,12},{16,17},{17,16... | collective-permute-start | bytes 196616 | tf_op jit(solution)/shard_map/ppermute | solution.py:344
  96.3 12.0 %collective-permute-start.12 = (f32[128,128]{1,0:T(8,128)S(1)}, f32[128,128]{1,0:T(8,128)S(1)}, u32[]{:S(2)}, u32[]{:S(2)}) collective-permute-start(f32[128,128]{1,0:T(8,128)S(1)} %get-tuple-element.41), channel_id=1, source_target_pairs={{1,2},{2,1},{3,4},{4,3},{5,6},{6,5},{7,8},{8,7},{9,10},{10,9},{11,... | collective-permute-start | bytes 196616 | tf_op jit(solution)/shard_map/ppermute | solution.py:344
  108.3 0.7 collective-permute-start.13
  109.0 0.0 collective-permute-done.10.centre_ref
  109.0 0.0 collective-permute-done.11.early_ref
  109.0 1.6 %collective-permute-done.12.late_ref = f32[128,128]{1,0:T(8,128)S(1)} collective-permute-done((f32[128,128]{1,0:T(8,128)S(1)}, f32[128,128]{1,0:T(8,128)S(1)}, u32[]{:S(2)}, u32[]{:S(2)}) %collective-permute-start.12) | collective-permute-done | bytes 65568 | tf_op jit(solution)/shard_map/ppermute | solution.py:344
  110.7 0.0 collective-permute-done.13.last_ref
  110.7 1.4 %proximal.1 = f32[1,3,1,128,128]{4,3,2,1,0:T(8,128)} custom-call(s32[5]{0:T(128)S(1)} %stack.23.where_ref, s32[1,3,16]{2,1,0:T(4,128)S(1)} %copy.9.refs_0_.slots_ref, f32[3,128,128]{2,1,0:T(8,128)S(1)} %get-tuple-element.38.near_ref, f32[2,128,128]{2,1,0:T(8,128)S(1)} %collective-permute-done.6.outer_ref, f32[128,128]{1,0:T(8,128)S(1)} %collective-permute-done.10.centre_ref, ...), custom_call_target="tpu_custom_call" | custom-call | flops 983040 | bytes 524288 | tf_op jit(solution)/shard_map/proximal/pallas_call | solution.py:301
  (5 shorter events, 0.2 us)
Async XLA Ops:
  0.0 38.2 %collective-permute-start.2 = (f32[256,1024]{1,0:T(8,128)}, f32[256,1024]{1,0:T(8,128)S(1)}, u32[]{:S(2)}, u32[]{:S(2)}) collective-permute-start(f32[256,1024]{1,0:T(8,128)} %refs_1_.1), channel_id=1, source_target_pairs={{0,1},{1,2},{2,3},{3,4},{4,5},{5,6},{6,7},{7,8},{8,9},{9,10},{10,1... | collective-permute-start | bytes 3145736 | tf_op jit(solution)/shard_map/ppermute | solution.py:323
  4.8 37.2 %collective-permute-start.1 = (f32[128,1024]{1,0:T(8,128)S(1)}, f32[128,1024]{1,0:T(8,128)S(1)}, u32[]{:S(2)}, u32[]{:S(2)}) collective-permute-start(f32[128,1024]{1,0:T(8,128)S(1)} %get-tuple-element.43), channel_id=1, source_target_pairs={{0,31},{1,0},{2,1},{3,2},{4,3},{5,4},{6,5},{7,6},{8,7},{9,8},{10,9... | collective-permute-start | bytes 1572872 | tf_op jit(solution)/shard_map/ppermute | solution.py:323
  17.2 35.9 %collective-permute-start = (f32[128,1024]{1,0:T(8,128)S(1)}, f32[128,1024]{1,0:T(8,128)S(1)}, u32[]{:S(2)}, u32[]{:S(2)}) collective-permute-start(f32[128,1024]{1,0:T(8,128)S(1)} %get-tuple-element.44), channel_id=1, source_target_pairs={{0,31},{1,0},{2,1},{3,2},{4,3},{5,4},{6,5},{7,6},{8,7},{9,8},{10,9... | collective-permute-start | bytes 1572872 | tf_op jit(solution)/shard_map/ppermute | solution.py:323
  21.9 1.9 %copy-start = (f32[1,3,16,128,128]{4,3,2,1,0:T(8,128)S(1)}, f32[1,3,16,128,128]{4,3,2,1,0:T(8,128)}, u32[]{:S(2)}) copy-start(f32[1,3,16,128,128]{4,3,2,1,0:T(8,128)} %omega_ref.3) | copy-start | bytes 9437188
  23.8 1.2 %copy-start.2 = (f32[256,1024]{1,0:T(8,128)S(1)}, f32[256,1024]{1,0:T(8,128)}, u32[]{:S(2)}) copy-start(f32[256,1024]{1,0:T(8,128)} %refs_1_.1) | copy-start | bytes 3145732
  25.0 13.2 %copy-start.1 = (f32[1,3,16,128,128]{4,3,2,1,0:T(8,128)S(1)}, f32[1,3,16,128,128]{4,3,2,1,0:T(8,128)}, u32[]{:S(2)}) copy-start(f32[1,3,16,128,128]{4,3,2,1,0:T(8,128)} %omega_ref.3) | copy-start | bytes 9437188
  56.2 5.9 %collective-permute-start.3 = (f32[4,3,128,128]{3,2,1,0:T(8,128)S(1)}, f32[4,3,128,128]{3,2,1,0:T(8,128)S(1)}, u32[]{:S(2)}, u32[]{:S(2)}) collective-permute-start(f32[4,3,128,128]{3,2,1,0:T(8,128)S(1)} %get-tuple-element.31), channel_id=1, source_target_pairs={{0,32},{32,0},{1,33},{33,1},{2,34},{34,2},{3,35},{35,3},{4,36},{36... | collective-permute-start | bytes 2359304 | tf_op jit(solution)/shard_map/ppermute | solution.py:323
  59.7 5.2 %collective-permute-start.7 = (f32[4,3,128,128]{3,2,1,0:T(8,128)S(1)}, f32[4,3,128,128]{3,2,1,0:T(8,128)S(1)}, u32[]{:S(2)}, u32[]{:S(2)}) collective-permute-start(f32[4,3,128,128]{3,2,1,0:T(8,128)S(1)} %get-tuple-element.36), channel_id=1, source_target_pairs={{0,32},{32,0},{1,33},{33,1},{2,34},{34,2},{3,35},{35,3},{4,36},{36... | collective-permute-start | bytes 2359304 | tf_op jit(solution)/shard_map/ppermute | solution.py:323
  62.2 9.7 %collective-permute-start.4 = (f32[2,3,128,128]{3,2,1,0:T(8,128)S(1)}, f32[2,3,128,128]{3,2,1,0:T(8,128)S(1)}, u32[]{:S(2)}, u32[]{:S(2)}) collective-permute-start(f32[2,3,128,128]{3,2,1,0:T(8,128)S(1)} %slice_add_fusion.1), channel_id=1, source_target_pairs={{0,128},{32,416},{128,0},{160,288},{256,384},{288,160},{384,256},{... | collective-permute-start | bytes 1179656 | tf_op jit(solution)/shard_map/ppermute | solution.py:332
  65.0 11.1 %collective-permute-start.8 = (f32[2,3,128,128]{3,2,1,0:T(8,128)S(1)}, f32[2,3,128,128]{3,2,1,0:T(8,128)S(1)}, u32[]{:S(2)}, u32[]{:S(2)}) collective-permute-start(f32[2,3,128,128]{3,2,1,0:T(8,128)S(1)} %slice_add_fusion), channel_id=1, source_target_pairs={{0,128},{32,416},{128,0},{160,288},{256,384},{288,160},{384,256},{... | collective-permute-start | bytes 1179656 | tf_op jit(solution)/shard_map/ppermute | solution.py:332
  71.9 8.8 %collective-permute-start.5 = (f32[3,128,128]{2,1,0:T(8,128)S(1)}, f32[3,128,128]{2,1,0:T(8,128)S(1)}, u32[]{:S(2)}, u32[]{:S(2)}) collective-permute-start(f32[3,128,128]{2,1,0:T(8,128)S(1)} %fusion.1), channel_id=1, source_target_pairs={{0,384},{32,160},{128,256},{160,32},{256,128},{288,416},{384,0},{4... | collective-permute-start | bytes 589832 | tf_op jit(solution)/shard_map/ppermute | solution.py:332
  76.1 14.4 %collective-permute-start.9 = (f32[3,128,128]{2,1,0:T(8,128)S(1)}, f32[3,128,128]{2,1,0:T(8,128)S(1)}, u32[]{:S(2)}, u32[]{:S(2)}) collective-permute-start(f32[3,128,128]{2,1,0:T(8,128)S(1)} %fusion), channel_id=1, source_target_pairs={{0,384},{32,160},{128,256},{160,32},{256,128},{288,416},{384,0},{4... | collective-permute-start | bytes 589832 | tf_op jit(solution)/shard_map/ppermute | solution.py:332
  80.7 12.7 %collective-permute-start.6 = (f32[2,128,128]{2,1,0:T(8,128)S(1)}, f32[2,128,128]{2,1,0:T(8,128)S(1)}, u32[]{:S(2)}, u32[]{:S(2)}) collective-permute-start(f32[2,128,128]{2,1,0:T(8,128)S(1)} %slice_add_fusion.6), channel_id=1, source_target_pairs={{0,64},{64,0},{1,65},{65,1},{2,66},{66,2},{3,67},{67,3},{4,68},{68... | collective-permute-start | bytes 393224 | tf_op jit(solution)/shard_map/ppermute | solution.py:323
  88.3 20.7 %collective-permute-start.10 = (f32[128,128]{1,0:T(8,128)S(1)}, f32[128,128]{1,0:T(8,128)S(1)}, u32[]{:S(2)}, u32[]{:S(2)}) collective-permute-start(f32[128,128]{1,0:T(8,128)S(1)} %fusion.4), channel_id=1, source_target_pairs={{0,64},{64,0},{1,65},{65,1},{2,66},{66,2},{3,67},{67,3},{4,68},{68... | collective-permute-start | bytes 196616 | tf_op jit(solution)/shard_map/ppermute | solution.py:323
  94.1 14.9 %collective-permute-start.11 = (f32[128,128]{1,0:T(8,128)S(1)}, f32[128,128]{1,0:T(8,128)S(1)}, u32[]{:S(2)}, u32[]{:S(2)}) collective-permute-start(f32[128,128]{1,0:T(8,128)S(1)} %get-tuple-element.40), channel_id=1, source_target_pairs={{0,1},{1,0},{4,5},{5,4},{8,9},{9,8},{12,13},{13,12},{16,17},{17,16... | collective-permute-start | bytes 196616 | tf_op jit(solution)/shard_map/ppermute | solution.py:344
  96.3 14.4 %collective-permute-start.12 = (f32[128,128]{1,0:T(8,128)S(1)}, f32[128,128]{1,0:T(8,128)S(1)}, u32[]{:S(2)}, u32[]{:S(2)}) collective-permute-start(f32[128,128]{1,0:T(8,128)S(1)} %get-tuple-element.41), channel_id=1, source_target_pairs={{1,2},{2,1},{3,4},{4,3},{5,6},{6,5},{7,8},{8,7},{9,10},{10,9},{11,... | collective-permute-start | bytes 196616 | tf_op jit(solution)/shard_map/ppermute | solution.py:344
  108.3 2.3 %collective-permute-start.13 = (f32[128,128]{1,0:T(8,128)S(1)}, f32[128,128]{1,0:T(8,128)S(1)}, u32[]{:S(2)}, u32[]{:S(2)}) collective-permute-start(f32[128,128]{1,0:T(8,128)S(1)} %get-tuple-element.42), channel_id=1, source_target_pairs={{2,3},{3,2},{6,7},{7,6},{10,11},{11,10},{14,15},{15,14},{18,19},{1... | collective-permute-start | bytes 196616 | tf_op jit(solution)/shard_map/ppermute | solution.py:344

commit v13 on v12

--- a/solution.py
+++ b/solution.py
@@ -371,7 +371,8 @@
     outer = shifted(outer_out, "y_hi", 1)
     centre_out = sum(x[2] for x in parts[:3]) + after(far_second, outer_out)[2]
     centre_sum = shifted(centre_out, "y_hi", 1)
-    near_second = x_exchange(near_keep[1] + near_got[1] + near_first[1], 1)
+    near_out = after(near_keep[1] + near_got[1] + near_first[1], outer_out)
+    near_second = x_exchange(near_out, 1)
     near_sum, early_out, late_out, last_out = edge_values(
         where, outer, near_keep, near_got, near_first, near_second
     )

time: 113 us -> 113 us (level)
  waiting for transfers between devices: 33.5 us -> 37.5 us
  starting transfers between devices: 59.9 us -> 56.5 us
    ppermute x4, waiting for transfers between devices: 7.17 us -> 14.1 us  [x_exchange(): return lax.ppermute(value, ('x', 'core'), pairs)]
    ppermute x3, starting transfers between devices: 14.9 us -> 11.9 us  [edge_exchange(): return lax.ppermute(value, 'col', pairs)]
    ppermute x7, waiting for transfers between devices: 24.7 us -> 21.8 us  [shifted(): return lax.ppermute(value, axis, pairs)]
  transfers between devices with their start and end apart: 14 -> 14, of which waited for: 8 -> 9; matrix products, arithmetic and copies ran while one was open for 2% -> 2% of each run, Pallas kernels for 8% -> 8%
where the time goes in v13:
time: 113 us
  starting transfers between devices  56.5 us (50%)
  waiting for transfers between devices  37.5 us (33%)
  Pallas kernels  13 us (12%)
  local copies, waits for them, and re-layouts  5.16 us (5%)
    ppermute x7, starting transfers between devices, shifted(): return lax.ppermute(value, axis, pairs)  33.9 us
    ppermute x7, waiting for transfers between devices, shifted(): return lax.ppermute(value, axis, pairs)  21.8 us
    ppermute x4, waiting for transfers between devices, x_exchange(): return lax.ppermute(value, ('x', 'core'), pairs)  14.1 us
    ppermute x3, starting transfers between devices, edge_exchange(): return lax.ppermute(value, 'col', pairs)  11.9 us
    ppermute x4, starting transfers between devices, x_exchange(): return lax.ppermute(value, ('x', 'core'), pairs)  10.6 us
    pallas_call x3, Pallas kernels, partial(): pl.pallas_call(lambda *refs: partial_kernel(offset, first, *refs), name='...  6.29 us
    unnamed x7, local copies, waits for them, and re-layouts  3.8 us
    pallas_call x1, Pallas kernels, far_blocks(): pl.pallas_call(far_kernel, name='far_blocks', grid=(1,), out_shape=GROUP_...  3.12 us
  transfers between devices with their start and end apart: 14, of which 9 were waited for; matrix products, arithmetic and copies ran while one was open for 2% of the time, Pallas kernels for 8%

profile of v13, /device:TPU:6, one launch (start us, length us, event | category | flops | bytes accessed | tf_op | source)
XLA Modules:
  0.0 112.6 jit_solution(8188223268873590233)
XLA Ops:
  0.0 3.5 %collective-permute-start.2 = (f32[256,1024]{1,0:T(8,128)}, f32[256,1024]{1,0:T(8,128)S(1)}, u32[]{:S(2)}, u32[]{:S(2)}) collective-permute-start(f32[256,1024]{1,0:T(8,128)} %refs_1_.1), channel_id=1, source_target_pairs={{0,1},{1,2},{2,3},{3,4},{4,5},{5,6},{6,7},{7,8},{8,9},{9,10},{10,1... | collective-permute-start | bytes 3145736 | tf_op jit(solution)/shard_map/ppermute | solution.py:323
  3.5 1.3 %fusion.5 = (f32[128,1024]{1,0:T(8,128)S(1)}, f32[128,1024]{1,0:T(8,128)S(1)}) fusion(f32[256,1024]{1,0:T(8,128)} %refs_1_.1), kind=kLoop, calls=%fused_computation.16 | loop fusion | bytes 2097152 | tf_op jit(solution)/shard_map/slice | solution.py:353
  4.8 12.4 %collective-permute-start.1 = (f32[128,1024]{1,0:T(8,128)S(1)}, f32[128,1024]{1,0:T(8,128)S(1)}, u32[]{:S(2)}, u32[]{:S(2)}) collective-permute-start(f32[128,1024]{1,0:T(8,128)S(1)} %get-tuple-element.45), channel_id=1, source_target_pairs={{0,31},{1,0},{2,1},{3,2},{4,3},{5,4},{6,5},{7,6},{8,7},{9,8},{10,9... | collective-permute-start | bytes 1572872 | tf_op jit(solution)/shard_map/ppermute | solution.py:323
  17.2 3.9 %collective-permute-start = (f32[128,1024]{1,0:T(8,128)S(1)}, f32[128,1024]{1,0:T(8,128)S(1)}, u32[]{:S(2)}, u32[]{:S(2)}) collective-permute-start(f32[128,1024]{1,0:T(8,128)S(1)} %get-tuple-element.46), channel_id=1, source_target_pairs={{0,31},{1,0},{2,1},{3,2},{4,3},{5,4},{6,5},{7,6},{8,7},{9,8},{10,9... | collective-permute-start | bytes 1572872 | tf_op jit(solution)/shard_map/ppermute | solution.py:323
  21.1 0.7 copy.9.refs_0_.slots_ref
  21.8 0.1 stack.23.where_ref
  21.9 0.0 copy-start
  21.9 1.9 %copy-done = f32[1,3,16,128,128]{4,3,2,1,0:T(8,128)S(1)} copy-done((f32[1,3,16,128,128]{4,3,2,1,0:T(8,128)S(1)}, f32[1,3,16,128,128]{4,3,2,1,0:T(8,128)}, u32[]{:S(2)}) %copy-start) | copy-done | bytes 3145752
  23.8 0.0 copy-start.2
  23.8 1.2 %copy-done.2 = f32[256,1024]{1,0:T(8,128)S(1)} copy-done((f32[256,1024]{1,0:T(8,128)S(1)}, f32[256,1024]{1,0:T(8,128)}, u32[]{:S(2)}) %copy-start.2) | copy-done | bytes 1048600
  25.0 0.0 copy-start.1
  25.0 2.3 %partial_residual.3 = (f32[8,256,128]{2,1,0:T(8,128)S(1)}, bf16[8,256,256]{2,1,0:T(8,128)(2,1)S(1)}) custom-call(s32[1,3,16]{2,1,0:T(4,128)S(1)} %copy.9.refs_0_.slots_ref, f32[256,1024]{1,0:T(8,128)S(1)} %copy-done.2, f32[1,3,16,128,128]{4,3,2,1,0:T(8,128)S(1)} %copy-done), custom_call_target="tpu_custom_call" | custom-call | flops 536870912 | bytes 5242880 | tf_op jit(solution)/shard_map/partial_residual/pallas_call | solution.py:194
  27.3 10.9 %collective-permute-done.2.refs_1_ = f32[256,1024]{1,0:T(8,128)S(1)} collective-permute-done((f32[256,1024]{1,0:T(8,128)}, f32[256,1024]{1,0:T(8,128)S(1)}, u32[]{:S(2)}, u32[]{:S(2)}) %collective-permute-start.2) | collective-permute-done | bytes 1048608 | tf_op jit(solution)/shard_map/ppermute | solution.py:323
  38.2 0.0 copy-done.1
  38.2 2.2 %partial_residual.4 = (f32[8,256,128]{2,1,0:T(8,128)S(1)}, bf16[8,256,256]{2,1,0:T(8,128)(2,1)S(1)}) custom-call(s32[1,3,16]{2,1,0:T(4,128)S(1)} %copy.9.refs_0_.slots_ref, f32[256,1024]{1,0:T(8,128)S(1)} %collective-permute-done.2.refs_1_, f32[1,3,16,128,128]{4,3,2,1,0:T(8,128)S(1)} %copy-done.1, f32[8,256,128]{2,1,0:T(8,128)S(1)} %get-tuple-element.25.refs_3_), custom_call_target="tpu_custom_call" | custom-call | flops 536870912 | bytes 5242880 | tf_op jit(solution)/shard_map/partial_residual/pallas_call | solution.py:194
  40.5 1.5 %collective-permute-done.1.refs_1_ = f32[128,1024]{1,0:T(8,128)S(1)} collective-permute-done((f32[128,1024]{1,0:T(8,128)S(1)}, f32[128,1024]{1,0:T(8,128)S(1)}, u32[]{:S(2)}, u32[]{:S(2)}) %collective-permute-start.1) | collective-permute-done | bytes 524320 | tf_op jit(solution)/shard_map/ppermute | solution.py:323
  41.9 1.8 %partial_residual.5 = (f32[8,256,128]{2,1,0:T(8,128)S(1)}, bf16[8,256,128]{2,1,0:T(8,128)(2,1)S(1)}) custom-call(s32[1,3,16]{2,1,0:T(4,128)S(1)} %copy.9.refs_0_.slots_ref, f32[128,1024]{1,0:T(8,128)S(1)} %collective-permute-done.1.refs_1_, f32[1,3,16,128,128]{4,3,2,1,0:T(8,128)S(1)} %copy-done.1, f32[8,256,128]{2,1,0:T(8,128)S(1)} %get-tuple-element.26.refs_3_), custom_call_target="tpu_custom_call" | custom-call | flops 268435456 | bytes 5242880 | tf_op jit(solution)/shard_map/partial_residual/pallas_call | solution.py:194
  43.7 9.3 %collective-permute-done.x_ref = f32[128,1024]{1,0:T(8,128)S(1)} collective-permute-done((f32[128,1024]{1,0:T(8,128)S(1)}, f32[128,1024]{1,0:T(8,128)S(1)}, u32[]{:S(2)}, u32[]{:S(2)}) %collective-permute-start) | collective-permute-done | bytes 524320 | tf_op jit(solution)/shard_map/ppermute | solution.py:323
  53.1 3.1 %far_blocks.1 = (f32[2,3,128,128]{3,2,1,0:T(8,128)S(1)}, f32[2,3,128,128]{3,2,1,0:T(8,128)S(1)}, f32[4,3,128,128]{3,2,1,0:T(8,128)S(1)}, bf16[8,256,256]{2,1,0:T(8,128)(2,1)S(1)}, bf16[8,256,256]{2,1,0:T(8,128)(2,1)S(1)}) custom-call(s32[1,3,16]{2,1,0:T(4,128)S(1)} %copy.9.refs_0_.slots_ref, s32[5]{0:T(128)S(1)} %stack.23.where_ref, ...), custom_call_target="tpu_custom_call" | custom-call | flops 1342177280 | bytes 8388608 | tf_op jit(solution)/shard_map/far_blocks/pallas_call | solution.py:220
  56.2 1.9 %collective-permute-start.3 = (f32[4,3,128,128]{3,2,1,0:T(8,128)S(1)}, f32[4,3,128,128]{3,2,1,0:T(8,128)S(1)}, u32[]{:S(2)}, u32[]{:S(2)}) collective-permute-start(f32[4,3,128,128]{3,2,1,0:T(8,128)S(1)} %get-tuple-element.32), channel_id=1, source_target_pairs={{0,32},{32,0},{1,33},{33,1},{2,34},{34,2},{3,35},{35,3},{4,36},{36... | collective-permute-start | bytes 2359304 | tf_op jit(solution)/shard_map/ppermute | solution.py:323
  58.1 1.6 %near_blocks.1 = (f32[2,3,128,128]{3,2,1,0:T(8,128)S(1)}, f32[2,3,128,128]{3,2,1,0:T(8,128)S(1)}, f32[4,3,128,128]{3,2,1,0:T(8,128)S(1)}) custom-call(s32[1,3,16]{2,1,0:T(4,128)S(1)} %copy.9.refs_0_.slots_ref, s32[5]{0:T(128)S(1)} %stack.23.where_ref, bf16[8,256,256]{2,1,0:T(8,128)(2,1)S(1)} %get-tuple-element.29.below_ref, ...), custom_call_target="tpu_custom_call" | custom-call | flops 805306368 | bytes 8388608 | tf_op jit(solution)/shard_map/near_blocks/pallas_call | solution.py:249
  59.7 2.4 %collective-permute-start.7 = (f32[4,3,128,128]{3,2,1,0:T(8,128)S(1)}, f32[4,3,128,128]{3,2,1,0:T(8,128)S(1)}, u32[]{:S(2)}, u32[]{:S(2)}) collective-permute-start(f32[4,3,128,128]{3,2,1,0:T(8,128)S(1)} %get-tuple-element.37), channel_id=1, source_target_pairs={{0,32},{32,0},{1,33},{33,1},{2,34},{34,2},{3,35},{35,3},{4,36},{36... | collective-permute-start | bytes 2359304 | tf_op jit(solution)/shard_map/ppermute | solution.py:323
  62.1 0.0 collective-permute-done.3
  62.2 2.7 %collective-permute-start.4 = (f32[2,3,128,128]{3,2,1,0:T(8,128)S(1)}, f32[2,3,128,128]{3,2,1,0:T(8,128)S(1)}, u32[]{:S(2)}, u32[]{:S(2)}) collective-permute-start(f32[2,3,128,128]{3,2,1,0:T(8,128)S(1)} %slice_add_fusion.1), channel_id=1, source_target_pairs={{0,128},{32,416},{128,0},{160,288},{256,384},{288,160},{384,256},{... | collective-permute-start | bytes 1179656 | tf_op jit(solution)/shard_map/ppermute | solution.py:332
  65.0 0.0 collective-permute-done.7.got_ref
  65.0 0.1 slice_add_fusion
  65.0 3.1 %collective-permute-start.8 = (f32[2,3,128,128]{3,2,1,0:T(8,128)S(1)}, f32[2,3,128,128]{3,2,1,0:T(8,128)S(1)}, u32[]{:S(2)}, u32[]{:S(2)}) collective-permute-start(f32[2,3,128,128]{3,2,1,0:T(8,128)S(1)} %slice_add_fusion), channel_id=1, source_target_pairs={{0,128},{32,416},{128,0},{160,288},{256,384},{288,160},{384,256},{... | collective-permute-start | bytes 1179656 | tf_op jit(solution)/shard_map/ppermute | solution.py:332
  68.1 3.7 %collective-permute-done.4 = f32[2,3,128,128]{3,2,1,0:T(8,128)S(1)} collective-permute-done((f32[2,3,128,128]{3,2,1,0:T(8,128)S(1)}, f32[2,3,128,128]{3,2,1,0:T(8,128)S(1)}, u32[]{:S(2)}, u32[]{:S(2)}) %collective-permute-start.4) | collective-permute-done | bytes 393248 | tf_op jit(solution)/shard_map/ppermute | solution.py:332
  71.9 2.4 %collective-permute-start.5 = (f32[3,128,128]{2,1,0:T(8,128)S(1)}, f32[3,128,128]{2,1,0:T(8,128)S(1)}, u32[]{:S(2)}, u32[]{:S(2)}) collective-permute-start(f32[3,128,128]{2,1,0:T(8,128)S(1)} %fusion.1), channel_id=1, source_target_pairs={{0,384},{32,160},{128,256},{160,32},{256,128},{288,416},{384,0},{4... | collective-permute-start | bytes 589832 | tf_op jit(solution)/shard_map/ppermute | solution.py:332
  74.3 1.8 %collective-permute-done.8.first_ref = f32[2,3,128,128]{3,2,1,0:T(8,128)S(1)} collective-permute-done((f32[2,3,128,128]{3,2,1,0:T(8,128)S(1)}, f32[2,3,128,128]{3,2,1,0:T(8,128)S(1)}, u32[]{:S(2)}, u32[]{:S(2)}) %collective-permute-start.8) | collective-permute-done | bytes 393248 | tf_op jit(solution)/shard_map/ppermute | solution.py:332
  76.1 4.6 %collective-permute-done.5 = f32[3,128,128]{2,1,0:T(8,128)S(1)} collective-permute-done((f32[3,128,128]{2,1,0:T(8,128)S(1)}, f32[3,128,128]{2,1,0:T(8,128)S(1)}, u32[]{:S(2)}, u32[]{:S(2)}) %collective-permute-start.5) | collective-permute-done | bytes 196640 | tf_op jit(solution)/shard_map/ppermute | solution.py:332
  80.7 7.5 %collective-permute-start.6 = (f32[2,128,128]{2,1,0:T(8,128)S(1)}, f32[2,128,128]{2,1,0:T(8,128)S(1)}, u32[]{:S(2)}, u32[]{:S(2)}) collective-permute-start(f32[2,128,128]{2,1,0:T(8,128)S(1)} %slice_add_fusion.6), channel_id=1, source_target_pairs={{0,64},{64,0},{1,65},{65,1},{2,66},{66,2},{3,67},{67,3},{4,68},{68... | collective-permute-start | bytes 393224 | tf_op jit(solution)/shard_map/ppermute | solution.py:323
  88.2 2.4 %collective-permute-start.9 = (f32[3,128,128]{2,1,0:T(8,128)S(1)}, f32[3,128,128]{2,1,0:T(8,128)S(1)}, u32[]{:S(2)}, u32[]{:S(2)}) collective-permute-start(f32[3,128,128]{2,1,0:T(8,128)S(1)} %fusion), channel_id=1, source_target_pairs={{0,384},{32,160},{128,256},{160,32},{256,128},{288,416},{384,0},{4... | collective-permute-start | bytes 589832 | tf_op jit(solution)/shard_map/ppermute | solution.py:332
  90.7 2.2 %collective-permute-start.10 = (f32[128,128]{1,0:T(8,128)S(1)}, f32[128,128]{1,0:T(8,128)S(1)}, u32[]{:S(2)}, u32[]{:S(2)}) collective-permute-start(f32[128,128]{1,0:T(8,128)S(1)} %fusion.4), channel_id=1, source_target_pairs={{0,64},{64,0},{1,65},{65,1},{2,66},{66,2},{3,67},{67,3},{4,68},{68... | collective-permute-start | bytes 196616 | tf_op jit(solution)/shard_map/ppermute | solution.py:323
  92.9 0.1 collective-permute-done.6.outer_ref
  93.0 4.0 %collective-permute-done.9.second_ref = f32[3,128,128]{2,1,0:T(8,128)S(1)} collective-permute-done((f32[3,128,128]{2,1,0:T(8,128)S(1)}, f32[3,128,128]{2,1,0:T(8,128)S(1)}, u32[]{:S(2)}, u32[]{:S(2)}) %collective-permute-start.9) | collective-permute-done | bytes 196640 | tf_op jit(solution)/shard_map/ppermute | solution.py:332
  97.0 0.6 edge_values.1
  97.6 2.6 %collective-permute-start.11 = (f32[128,128]{1,0:T(8,128)S(1)}, f32[128,128]{1,0:T(8,128)S(1)}, u32[]{:S(2)}, u32[]{:S(2)}) collective-permute-start(f32[128,128]{1,0:T(8,128)S(1)} %get-tuple-element.42), channel_id=1, source_target_pairs={{0,1},{1,0},{4,5},{5,4},{8,9},{9,8},{12,13},{13,12},{16,17},{17,16... | collective-permute-start | bytes 196616 | tf_op jit(solution)/shard_map/ppermute | solution.py:344
  100.2 8.7 %collective-permute-start.12 = (f32[128,128]{1,0:T(8,128)S(1)}, f32[128,128]{1,0:T(8,128)S(1)}, u32[]{:S(2)}, u32[]{:S(2)}) collective-permute-start(f32[128,128]{1,0:T(8,128)S(1)} %get-tuple-element.43), channel_id=1, source_target_pairs={{1,2},{2,1},{3,4},{4,3},{5,6},{6,5},{7,8},{8,7},{9,10},{10,9},{11,... | collective-permute-start | bytes 196616 | tf_op jit(solution)/shard_map/ppermute | solution.py:344
  108.9 0.7 collective-permute-start.13
  109.6 0.0 collective-permute-done.10.centre_ref
  109.6 0.0 collective-permute-done.11.early_ref
  109.6 1.6 %collective-permute-done.12.late_ref = f32[128,128]{1,0:T(8,128)S(1)} collective-permute-done((f32[128,128]{1,0:T(8,128)S(1)}, f32[128,128]{1,0:T(8,128)S(1)}, u32[]{:S(2)}, u32[]{:S(2)}) %collective-permute-start.12) | collective-permute-done | bytes 65568 | tf_op jit(solution)/shard_map/ppermute | solution.py:344
  111.2 0.0 collective-permute-done.13.last_ref
  111.2 1.4 %proximal.1 = f32[1,3,1,128,128]{4,3,2,1,0:T(8,128)} custom-call(s32[5]{0:T(128)S(1)} %stack.23.where_ref, s32[1,3,16]{2,1,0:T(4,128)S(1)} %copy.9.refs_0_.slots_ref, f32[3,128,128]{2,1,0:T(8,128)S(1)} %get-tuple-element.40.near_ref, f32[2,128,128]{2,1,0:T(8,128)S(1)} %collective-permute-done.6.outer_ref, f32[128,128]{1,0:T(8,128)S(1)} %collective-permute-done.10.centre_ref, ...), custom_call_target="tpu_custom_call" | custom-call | flops 983040 | bytes 524288 | tf_op jit(solution)/shard_map/proximal/pallas_call | solution.py:301
  (5 shorter events, 0.2 us)
Async XLA Ops:
  0.0 38.2 %collective-permute-start.2 = (f32[256,1024]{1,0:T(8,128)}, f32[256,1024]{1,0:T(8,128)S(1)}, u32[]{:S(2)}, u32[]{:S(2)}) collective-permute-start(f32[256,1024]{1,0:T(8,128)} %refs_1_.1), channel_id=1, source_target_pairs={{0,1},{1,2},{2,3},{3,4},{4,5},{5,6},{6,7},{7,8},{8,9},{9,10},{10,1... | collective-permute-start | bytes 3145736 | tf_op jit(solution)/shard_map/ppermute | solution.py:323
  4.8 37.2 %collective-permute-start.1 = (f32[128,1024]{1,0:T(8,128)S(1)}, f32[128,1024]{1,0:T(8,128)S(1)}, u32[]{:S(2)}, u32[]{:S(2)}) collective-permute-start(f32[128,1024]{1,0:T(8,128)S(1)} %get-tuple-element.45), channel_id=1, source_target_pairs={{0,31},{1,0},{2,1},{3,2},{4,3},{5,4},{6,5},{7,6},{8,7},{9,8},{10,9... | collective-permute-start | bytes 1572872 | tf_op jit(solution)/shard_map/ppermute | solution.py:323
  17.2 35.9 %collective-permute-start = (f32[128,1024]{1,0:T(8,128)S(1)}, f32[128,1024]{1,0:T(8,128)S(1)}, u32[]{:S(2)}, u32[]{:S(2)}) collective-permute-start(f32[128,1024]{1,0:T(8,128)S(1)} %get-tuple-element.46), channel_id=1, source_target_pairs={{0,31},{1,0},{2,1},{3,2},{4,3},{5,4},{6,5},{7,6},{8,7},{9,8},{10,9... | collective-permute-start | bytes 1572872 | tf_op jit(solution)/shard_map/ppermute | solution.py:323
  21.9 1.9 %copy-start = (f32[1,3,16,128,128]{4,3,2,1,0:T(8,128)S(1)}, f32[1,3,16,128,128]{4,3,2,1,0:T(8,128)}, u32[]{:S(2)}) copy-start(f32[1,3,16,128,128]{4,3,2,1,0:T(8,128)} %omega_ref.3) | copy-start | bytes 9437188
  23.8 1.2 %copy-start.2 = (f32[256,1024]{1,0:T(8,128)S(1)}, f32[256,1024]{1,0:T(8,128)}, u32[]{:S(2)}) copy-start(f32[256,1024]{1,0:T(8,128)} %refs_1_.1) | copy-start | bytes 3145732
  25.0 13.2 %copy-start.1 = (f32[1,3,16,128,128]{4,3,2,1,0:T(8,128)S(1)}, f32[1,3,16,128,128]{4,3,2,1,0:T(8,128)}, u32[]{:S(2)}) copy-start(f32[1,3,16,128,128]{4,3,2,1,0:T(8,128)} %omega_ref.3) | copy-start | bytes 9437188
  56.2 6.0 %collective-permute-start.3 = (f32[4,3,128,128]{3,2,1,0:T(8,128)S(1)}, f32[4,3,128,128]{3,2,1,0:T(8,128)S(1)}, u32[]{:S(2)}, u32[]{:S(2)}) collective-permute-start(f32[4,3,128,128]{3,2,1,0:T(8,128)S(1)} %get-tuple-element.32), channel_id=1, source_target_pairs={{0,32},{32,0},{1,33},{33,1},{2,34},{34,2},{3,35},{35,3},{4,36},{36... | collective-permute-start | bytes 2359304 | tf_op jit(solution)/shard_map/ppermute | solution.py:323
  59.7 5.2 %collective-permute-start.7 = (f32[4,3,128,128]{3,2,1,0:T(8,128)S(1)}, f32[4,3,128,128]{3,2,1,0:T(8,128)S(1)}, u32[]{:S(2)}, u32[]{:S(2)}) collective-permute-start(f32[4,3,128,128]{3,2,1,0:T(8,128)S(1)} %get-tuple-element.37), channel_id=1, source_target_pairs={{0,32},{32,0},{1,33},{33,1},{2,34},{34,2},{3,35},{35,3},{4,36},{36... | collective-permute-start | bytes 2359304 | tf_op jit(solution)/shard_map/ppermute | solution.py:323
  62.2 9.7 %collective-permute-start.4 = (f32[2,3,128,128]{3,2,1,0:T(8,128)S(1)}, f32[2,3,128,128]{3,2,1,0:T(8,128)S(1)}, u32[]{:S(2)}, u32[]{:S(2)}) collective-permute-start(f32[2,3,128,128]{3,2,1,0:T(8,128)S(1)} %slice_add_fusion.1), channel_id=1, source_target_pairs={{0,128},{32,416},{128,0},{160,288},{256,384},{288,160},{384,256},{... | collective-permute-start | bytes 1179656 | tf_op jit(solution)/shard_map/ppermute | solution.py:332
  65.0 11.1 %collective-permute-start.8 = (f32[2,3,128,128]{3,2,1,0:T(8,128)S(1)}, f32[2,3,128,128]{3,2,1,0:T(8,128)S(1)}, u32[]{:S(2)}, u32[]{:S(2)}) collective-permute-start(f32[2,3,128,128]{3,2,1,0:T(8,128)S(1)} %slice_add_fusion), channel_id=1, source_target_pairs={{0,128},{32,416},{128,0},{160,288},{256,384},{288,160},{384,256},{... | collective-permute-start | bytes 1179656 | tf_op jit(solution)/shard_map/ppermute | solution.py:332
  71.9 8.8 %collective-permute-start.5 = (f32[3,128,128]{2,1,0:T(8,128)S(1)}, f32[3,128,128]{2,1,0:T(8,128)S(1)}, u32[]{:S(2)}, u32[]{:S(2)}) collective-permute-start(f32[3,128,128]{2,1,0:T(8,128)S(1)} %fusion.1), channel_id=1, source_target_pairs={{0,384},{32,160},{128,256},{160,32},{256,128},{288,416},{384,0},{4... | collective-permute-start | bytes 589832 | tf_op jit(solution)/shard_map/ppermute | solution.py:332
  80.7 12.3 %collective-permute-start.6 = (f32[2,128,128]{2,1,0:T(8,128)S(1)}, f32[2,128,128]{2,1,0:T(8,128)S(1)}, u32[]{:S(2)}, u32[]{:S(2)}) collective-permute-start(f32[2,128,128]{2,1,0:T(8,128)S(1)} %slice_add_fusion.6), channel_id=1, source_target_pairs={{0,64},{64,0},{1,65},{65,1},{2,66},{66,2},{3,67},{67,3},{4,68},{68... | collective-permute-start | bytes 393224 | tf_op jit(solution)/shard_map/ppermute | solution.py:323
  88.2 8.8 %collective-permute-start.9 = (f32[3,128,128]{2,1,0:T(8,128)S(1)}, f32[3,128,128]{2,1,0:T(8,128)S(1)}, u32[]{:S(2)}, u32[]{:S(2)}) collective-permute-start(f32[3,128,128]{2,1,0:T(8,128)S(1)} %fusion), channel_id=1, source_target_pairs={{0,384},{32,160},{128,256},{160,32},{256,128},{288,416},{384,0},{4... | collective-permute-start | bytes 589832 | tf_op jit(solution)/shard_map/ppermute | solution.py:332
  90.7 18.9 %collective-permute-start.10 = (f32[128,128]{1,0:T(8,128)S(1)}, f32[128,128]{1,0:T(8,128)S(1)}, u32[]{:S(2)}, u32[]{:S(2)}) collective-permute-start(f32[128,128]{1,0:T(8,128)S(1)} %fusion.4), channel_id=1, source_target_pairs={{0,64},{64,0},{1,65},{65,1},{2,66},{66,2},{3,67},{67,3},{4,68},{68... | collective-permute-start | bytes 196616 | tf_op jit(solution)/shard_map/ppermute | solution.py:323
  97.6 12.0 %collective-permute-start.11 = (f32[128,128]{1,0:T(8,128)S(1)}, f32[128,128]{1,0:T(8,128)S(1)}, u32[]{:S(2)}, u32[]{:S(2)}) collective-permute-start(f32[128,128]{1,0:T(8,128)S(1)} %get-tuple-element.42), channel_id=1, source_target_pairs={{0,1},{1,0},{4,5},{5,4},{8,9},{9,8},{12,13},{13,12},{16,17},{17,16... | collective-permute-start | bytes 196616 | tf_op jit(solution)/shard_map/ppermute | solution.py:344
  100.2 11.0 %collective-permute-start.12 = (f32[128,128]{1,0:T(8,128)S(1)}, f32[128,128]{1,0:T(8,128)S(1)}, u32[]{:S(2)}, u32[]{:S(2)}) collective-permute-start(f32[128,128]{1,0:T(8,128)S(1)} %get-tuple-element.43), channel_id=1, source_target_pairs={{1,2},{2,1},{3,4},{4,3},{5,6},{6,5},{7,8},{8,7},{9,10},{10,9},{11,... | collective-permute-start | bytes 196616 | tf_op jit(solution)/shard_map/ppermute | solution.py:344
  108.9 2.3 %collective-permute-start.13 = (f32[128,128]{1,0:T(8,128)S(1)}, f32[128,128]{1,0:T(8,128)S(1)}, u32[]{:S(2)}, u32[]{:S(2)}) collective-permute-start(f32[128,128]{1,0:T(8,128)S(1)} %get-tuple-element.44), channel_id=1, source_target_pairs={{2,3},{3,2},{6,7},{7,6},{10,11},{11,10},{14,15},{15,14},{18,19},{1... | collective-permute-start | bytes 196616 | tf_op jit(solution)/shard_map/ppermute | solution.py:344

commit v14 on v12

--- a/solution.py
+++ b/solution.py
@@ -54,7 +54,7 @@
         residual_ref[b, start : start + rows] += out[:, :BLK] + out[:, BLK:]
         return carry
 
-    lax.fori_loop(0, KMAX, body, 0, unroll=4)
+    lax.fori_loop(0, KMAX, body, 0, unroll=8)
 
 
 def partial_kernel(offset, first, *refs):

time: 113 us -> 113 us (level)
  the two profiles are of different devices: /device:TPU:6 before, /device:TPU:250 now
where the time goes in v14:
time: 113 us
  starting transfers between devices  50.7 us (45%)
  waiting for transfers between devices  44.9 us (40%)
  Pallas kernels  11.6 us (10%)
  local copies, waits for them, and re-layouts  5.16 us (5%)
    ppermute x7, waiting for transfers between devices, shifted(): return lax.ppermute(value, axis, pairs)  35.8 us
    ppermute x7, starting transfers between devices, shifted(): return lax.ppermute(value, axis, pairs)  25.8 us
    ppermute x3, starting transfers between devices, edge_exchange(): return lax.ppermute(value, 'col', pairs)  12.7 us
    ppermute x4, starting transfers between devices, x_exchange(): return lax.ppermute(value, ('x', 'core'), pairs)  12.2 us
    pallas_call x3, Pallas kernels, partial(): pl.pallas_call(lambda *refs: partial_kernel(offset, first, *refs), name='...  5.23 us
    ppermute x4, waiting for transfers between devices, x_exchange(): return lax.ppermute(value, ('x', 'core'), pairs)  4.98 us
    ppermute x3, waiting for transfers between devices, edge_exchange(): return lax.ppermute(value, 'col', pairs)  4.21 us
    unnamed x7, local copies, waits for them, and re-layouts  3.8 us
  transfers between devices with their start and end apart: 14, of which 8 were waited for; matrix products, arithmetic and copies ran while one was open for 2% of the time, Pallas kernels for 7%

profile of v14, /device:TPU:250, one launch (start us, length us, event | category | flops | bytes accessed | tf_op | source)
XLA Modules:
  0.0 112.9 jit_solution(4582915736519622256)
XLA Ops:
  0.0 7.8 %collective-permute-start.2 = (f32[256,1024]{1,0:T(8,128)}, f32[256,1024]{1,0:T(8,128)S(1)}, u32[]{:S(2)}, u32[]{:S(2)}) collective-permute-start(f32[256,1024]{1,0:T(8,128)} %refs_1_.1), channel_id=1, source_target_pairs={{0,1},{1,2},{2,3},{3,4},{4,5},{5,6},{6,7},{7,8},{8,9},{9,10},{10,1... | collective-permute-start | bytes 3145736 | tf_op jit(solution)/shard_map/ppermute | solution.py:323
  7.8 1.3 %fusion.5 = (f32[128,1024]{1,0:T(8,128)S(1)}, f32[128,1024]{1,0:T(8,128)S(1)}) fusion(f32[256,1024]{1,0:T(8,128)} %refs_1_.1), kind=kLoop, calls=%fused_computation.16 | loop fusion | bytes 2097152 | tf_op jit(solution)/shard_map/slice | solution.py:353
  9.1 1.9 %collective-permute-start.1 = (f32[128,1024]{1,0:T(8,128)S(1)}, f32[128,1024]{1,0:T(8,128)S(1)}, u32[]{:S(2)}, u32[]{:S(2)}) collective-permute-start(f32[128,1024]{1,0:T(8,128)S(1)} %get-tuple-element.43), channel_id=1, source_target_pairs={{0,31},{1,0},{2,1},{3,2},{4,3},{5,4},{6,5},{7,6},{8,7},{9,8},{10,9... | collective-permute-start | bytes 1572872 | tf_op jit(solution)/shard_map/ppermute | solution.py:323
  11.0 1.9 %collective-permute-start = (f32[128,1024]{1,0:T(8,128)S(1)}, f32[128,1024]{1,0:T(8,128)S(1)}, u32[]{:S(2)}, u32[]{:S(2)}) collective-permute-start(f32[128,1024]{1,0:T(8,128)S(1)} %get-tuple-element.44), channel_id=1, source_target_pairs={{0,31},{1,0},{2,1},{3,2},{4,3},{5,4},{6,5},{7,6},{8,7},{9,8},{10,9... | collective-permute-start | bytes 1572872 | tf_op jit(solution)/shard_map/ppermute | solution.py:323
  13.0 0.7 copy.9.refs_0_.slots_ref
  13.7 0.1 stack.23.where_ref
  13.8 0.0 copy-start
  13.8 1.9 %copy-done = f32[1,3,16,128,128]{4,3,2,1,0:T(8,128)S(1)} copy-done((f32[1,3,16,128,128]{4,3,2,1,0:T(8,128)S(1)}, f32[1,3,16,128,128]{4,3,2,1,0:T(8,128)}, u32[]{:S(2)}) %copy-start) | copy-done | bytes 3145752
  15.6 0.0 copy-start.2
  15.6 1.2 %copy-done.2 = f32[256,1024]{1,0:T(8,128)S(1)} copy-done((f32[256,1024]{1,0:T(8,128)S(1)}, f32[256,1024]{1,0:T(8,128)}, u32[]{:S(2)}) %copy-start.2) | copy-done | bytes 1048600
  16.9 0.0 copy-start.1
  16.9 1.9 %partial_residual.3 = (f32[8,256,128]{2,1,0:T(8,128)S(1)}, bf16[8,256,256]{2,1,0:T(8,128)(2,1)S(1)}) custom-call(s32[1,3,16]{2,1,0:T(4,128)S(1)} %copy.9.refs_0_.slots_ref, f32[256,1024]{1,0:T(8,128)S(1)} %copy-done.2, f32[1,3,16,128,128]{4,3,2,1,0:T(8,128)S(1)} %copy-done), custom_call_target="tpu_custom_call" | custom-call | flops 536870912 | bytes 5242880 | tf_op jit(solution)/shard_map/partial_residual/pallas_call | solution.py:194
  18.8 12.9 %collective-permute-done.2.refs_1_ = f32[256,1024]{1,0:T(8,128)S(1)} collective-permute-done((f32[256,1024]{1,0:T(8,128)}, f32[256,1024]{1,0:T(8,128)S(1)}, u32[]{:S(2)}, u32[]{:S(2)}) %collective-permute-start.2) | collective-permute-done | bytes 1048608 | tf_op jit(solution)/shard_map/ppermute | solution.py:323
  31.7 0.0 copy-done.1
  31.7 1.9 %partial_residual.4 = (f32[8,256,128]{2,1,0:T(8,128)S(1)}, bf16[8,256,256]{2,1,0:T(8,128)(2,1)S(1)}) custom-call(s32[1,3,16]{2,1,0:T(4,128)S(1)} %copy.9.refs_0_.slots_ref, f32[256,1024]{1,0:T(8,128)S(1)} %collective-permute-done.2.refs_1_, f32[1,3,16,128,128]{4,3,2,1,0:T(8,128)S(1)} %copy-done.1, f32[8,256,128]{2,1,0:T(8,128)S(1)} %get-tuple-element.24.refs_3_), custom_call_target="tpu_custom_call" | custom-call | flops 536870912 | bytes 5242880 | tf_op jit(solution)/shard_map/partial_residual/pallas_call | solution.py:194
  33.6 10.4 %collective-permute-done.1.refs_1_ = f32[128,1024]{1,0:T(8,128)S(1)} collective-permute-done((f32[128,1024]{1,0:T(8,128)S(1)}, f32[128,1024]{1,0:T(8,128)S(1)}, u32[]{:S(2)}, u32[]{:S(2)}) %collective-permute-start.1) | collective-permute-done | bytes 524320 | tf_op jit(solution)/shard_map/ppermute | solution.py:323
  44.0 1.4 %partial_residual.5 = (f32[8,256,128]{2,1,0:T(8,128)S(1)}, bf16[8,256,128]{2,1,0:T(8,128)(2,1)S(1)}) custom-call(s32[1,3,16]{2,1,0:T(4,128)S(1)} %copy.9.refs_0_.slots_ref, f32[128,1024]{1,0:T(8,128)S(1)} %collective-permute-done.1.refs_1_, f32[1,3,16,128,128]{4,3,2,1,0:T(8,128)S(1)} %copy-done.1, f32[8,256,128]{2,1,0:T(8,128)S(1)} %get-tuple-element.25.refs_3_), custom_call_target="tpu_custom_call" | custom-call | flops 268435456 | bytes 5242880 | tf_op jit(solution)/shard_map/partial_residual/pallas_call | solution.py:194
  45.4 8.6 %collective-permute-done.x_ref = f32[128,1024]{1,0:T(8,128)S(1)} collective-permute-done((f32[128,1024]{1,0:T(8,128)S(1)}, f32[128,1024]{1,0:T(8,128)S(1)}, u32[]{:S(2)}, u32[]{:S(2)}) %collective-permute-start) | collective-permute-done | bytes 524320 | tf_op jit(solution)/shard_map/ppermute | solution.py:323
  54.1 2.8 %far_blocks.1 = (f32[2,3,128,128]{3,2,1,0:T(8,128)S(1)}, f32[2,3,128,128]{3,2,1,0:T(8,128)S(1)}, f32[4,3,128,128]{3,2,1,0:T(8,128)S(1)}, bf16[8,256,256]{2,1,0:T(8,128)(2,1)S(1)}, bf16[8,256,256]{2,1,0:T(8,128)(2,1)S(1)}) custom-call(s32[1,3,16]{2,1,0:T(4,128)S(1)} %copy.9.refs_0_.slots_ref, s32[5]{0:T(128)S(1)} %stack.23.where_ref, ...), custom_call_target="tpu_custom_call" | custom-call | flops 1342177280 | bytes 8388608 | tf_op jit(solution)/shard_map/far_blocks/pallas_call | solution.py:220
  56.8 1.9 %collective-permute-start.3 = (f32[4,3,128,128]{3,2,1,0:T(8,128)S(1)}, f32[4,3,128,128]{3,2,1,0:T(8,128)S(1)}, u32[]{:S(2)}, u32[]{:S(2)}) collective-permute-start(f32[4,3,128,128]{3,2,1,0:T(8,128)S(1)} %get-tuple-element.31), channel_id=1, source_target_pairs={{0,32},{32,0},{1,33},{33,1},{2,34},{34,2},{3,35},{35,3},{4,36},{36... | collective-permute-start | bytes 2359304 | tf_op jit(solution)/shard_map/ppermute | solution.py:323
  58.8 1.6 %near_blocks.1 = (f32[2,3,128,128]{3,2,1,0:T(8,128)S(1)}, f32[2,3,128,128]{3,2,1,0:T(8,128)S(1)}, f32[4,3,128,128]{3,2,1,0:T(8,128)S(1)}) custom-call(s32[1,3,16]{2,1,0:T(4,128)S(1)} %copy.9.refs_0_.slots_ref, s32[5]{0:T(128)S(1)} %stack.23.where_ref, bf16[8,256,256]{2,1,0:T(8,128)(2,1)S(1)} %get-tuple-element.28.below_ref, ...), custom_call_target="tpu_custom_call" | custom-call | flops 805306368 | bytes 8388608 | tf_op jit(solution)/shard_map/near_blocks/pallas_call | solution.py:249
  60.4 2.4 %collective-permute-start.7 = (f32[4,3,128,128]{3,2,1,0:T(8,128)S(1)}, f32[4,3,128,128]{3,2,1,0:T(8,128)S(1)}, u32[]{:S(2)}, u32[]{:S(2)}) collective-permute-start(f32[4,3,128,128]{3,2,1,0:T(8,128)S(1)} %get-tuple-element.36), channel_id=1, source_target_pairs={{0,32},{32,0},{1,33},{33,1},{2,34},{34,2},{3,35},{35,3},{4,36},{36... | collective-permute-start | bytes 2359304 | tf_op jit(solution)/shard_map/ppermute | solution.py:323
  62.8 0.0 collective-permute-done.3
  62.9 2.4 %collective-permute-start.4 = (f32[2,3,128,128]{3,2,1,0:T(8,128)S(1)}, f32[2,3,128,128]{3,2,1,0:T(8,128)S(1)}, u32[]{:S(2)}, u32[]{:S(2)}) collective-permute-start(f32[2,3,128,128]{3,2,1,0:T(8,128)S(1)} %slice_add_fusion.1), channel_id=1, source_target_pairs={{0,128},{32,416},{128,0},{160,288},{256,384},{288,160},{384,256},{... | collective-permute-start | bytes 1179656 | tf_op jit(solution)/shard_map/ppermute | solution.py:332
  65.3 0.0 collective-permute-done.7.got_ref
  65.3 0.1 slice_add_fusion
  65.4 3.4 %collective-permute-start.8 = (f32[2,3,128,128]{3,2,1,0:T(8,128)S(1)}, f32[2,3,128,128]{3,2,1,0:T(8,128)S(1)}, u32[]{:S(2)}, u32[]{:S(2)}) collective-permute-start(f32[2,3,128,128]{3,2,1,0:T(8,128)S(1)} %slice_add_fusion), channel_id=1, source_target_pairs={{0,128},{32,416},{128,0},{160,288},{256,384},{288,160},{384,256},{... | collective-permute-start | bytes 1179656 | tf_op jit(solution)/shard_map/ppermute | solution.py:332
  68.8 3.7 %collective-permute-done.4 = f32[2,3,128,128]{3,2,1,0:T(8,128)S(1)} collective-permute-done((f32[2,3,128,128]{3,2,1,0:T(8,128)S(1)}, f32[2,3,128,128]{3,2,1,0:T(8,128)S(1)}, u32[]{:S(2)}, u32[]{:S(2)}) %collective-permute-start.4) | collective-permute-done | bytes 393248 | tf_op jit(solution)/shard_map/ppermute | solution.py:332
  72.6 3.4 %collective-permute-start.5 = (f32[3,128,128]{2,1,0:T(8,128)S(1)}, f32[3,128,128]{2,1,0:T(8,128)S(1)}, u32[]{:S(2)}, u32[]{:S(2)}) collective-permute-start(f32[3,128,128]{2,1,0:T(8,128)S(1)} %fusion.1), channel_id=1, source_target_pairs={{0,384},{32,160},{128,256},{160,32},{256,128},{288,416},{384,0},{4... | collective-permute-start | bytes 589832 | tf_op jit(solution)/shard_map/ppermute | solution.py:332
  76.0 1.2 %collective-permute-done.8.first_ref = f32[2,3,128,128]{3,2,1,0:T(8,128)S(1)} collective-permute-done((f32[2,3,128,128]{3,2,1,0:T(8,128)S(1)}, f32[2,3,128,128]{3,2,1,0:T(8,128)S(1)}, u32[]{:S(2)}, u32[]{:S(2)}) %collective-permute-start.8) | collective-permute-done | bytes 393248 | tf_op jit(solution)/shard_map/ppermute | solution.py:332
  77.2 3.0 %collective-permute-start.9 = (f32[3,128,128]{2,1,0:T(8,128)S(1)}, f32[3,128,128]{2,1,0:T(8,128)S(1)}, u32[]{:S(2)}, u32[]{:S(2)}) collective-permute-start(f32[3,128,128]{2,1,0:T(8,128)S(1)} %fusion), channel_id=1, source_target_pairs={{0,384},{32,160},{128,256},{160,32},{256,128},{288,416},{384,0},{4... | collective-permute-start | bytes 589832 | tf_op jit(solution)/shard_map/ppermute | solution.py:332
  80.2 0.0 collective-permute-done.5
  80.3 3.5 %collective-permute-start.6 = (f32[2,128,128]{2,1,0:T(8,128)S(1)}, f32[2,128,128]{2,1,0:T(8,128)S(1)}, u32[]{:S(2)}, u32[]{:S(2)}) collective-permute-start(f32[2,128,128]{2,1,0:T(8,128)S(1)} %slice_add_fusion.6), channel_id=1, source_target_pairs={{0,64},{64,0},{1,65},{65,1},{2,66},{66,2},{3,67},{67,3},{4,68},{68... | collective-permute-start | bytes 393224 | tf_op jit(solution)/shard_map/ppermute | solution.py:323
  83.9 6.2 %collective-permute-start.10 = (f32[128,128]{1,0:T(8,128)S(1)}, f32[128,128]{1,0:T(8,128)S(1)}, u32[]{:S(2)}, u32[]{:S(2)}) collective-permute-start(f32[128,128]{1,0:T(8,128)S(1)} %fusion.4), channel_id=1, source_target_pairs={{0,64},{64,0},{1,65},{65,1},{2,66},{66,2},{3,67},{67,3},{4,68},{68... | collective-permute-start | bytes 196616 | tf_op jit(solution)/shard_map/ppermute | solution.py:323
  90.1 0.0 collective-permute-done.9.second_ref
  90.1 3.8 %collective-permute-done.6.outer_ref = f32[2,128,128]{2,1,0:T(8,128)S(1)} collective-permute-done((f32[2,128,128]{2,1,0:T(8,128)S(1)}, f32[2,128,128]{2,1,0:T(8,128)S(1)}, u32[]{:S(2)}, u32[]{:S(2)}) %collective-permute-start.6) | collective-permute-done | bytes 131104 | tf_op jit(solution)/shard_map/ppermute | solution.py:323
  93.9 0.6 edge_values.1
  94.5 0.7 collective-permute-start.11
  95.2 10.2 %collective-permute-start.12 = (f32[128,128]{1,0:T(8,128)S(1)}, f32[128,128]{1,0:T(8,128)S(1)}, u32[]{:S(2)}, u32[]{:S(2)}) collective-permute-start(f32[128,128]{1,0:T(8,128)S(1)} %get-tuple-element.41), channel_id=1, source_target_pairs={{1,2},{2,1},{3,4},{4,3},{5,6},{6,5},{7,8},{8,7},{9,10},{10,9},{11,... | collective-permute-start | bytes 196616 | tf_op jit(solution)/shard_map/ppermute | solution.py:344
  105.4 1.9 %collective-permute-start.13 = (f32[128,128]{1,0:T(8,128)S(1)}, f32[128,128]{1,0:T(8,128)S(1)}, u32[]{:S(2)}, u32[]{:S(2)}) collective-permute-start(f32[128,128]{1,0:T(8,128)S(1)} %get-tuple-element.42), channel_id=1, source_target_pairs={{2,3},{3,2},{6,7},{7,6},{10,11},{11,10},{14,15},{15,14},{18,19},{1... | collective-permute-start | bytes 196616 | tf_op jit(solution)/shard_map/ppermute | solution.py:344
  107.3 0.0 collective-permute-done.10.centre_ref
  107.3 0.0 collective-permute-done.11.early_ref
  107.3 0.4 collective-permute-done.12.late_ref
  107.7 3.9 %collective-permute-done.13.last_ref = f32[128,128]{1,0:T(8,128)S(1)} collective-permute-done((f32[128,128]{1,0:T(8,128)S(1)}, f32[128,128]{1,0:T(8,128)S(1)}, u32[]{:S(2)}, u32[]{:S(2)}) %collective-permute-start.13) | collective-permute-done | bytes 65568 | tf_op jit(solution)/shard_map/ppermute | solution.py:344
  111.5 1.4 %proximal.1 = f32[1,3,1,128,128]{4,3,2,1,0:T(8,128)} custom-call(s32[5]{0:T(128)S(1)} %stack.23.where_ref, s32[1,3,16]{2,1,0:T(4,128)S(1)} %copy.9.refs_0_.slots_ref, f32[3,128,128]{2,1,0:T(8,128)S(1)} %get-tuple-element.38.near_ref, f32[2,128,128]{2,1,0:T(8,128)S(1)} %collective-permute-done.6.outer_ref, f32[128,128]{1,0:T(8,128)S(1)} %collective-permute-done.10.centre_ref, ...), custom_call_target="tpu_custom_call" | custom-call | flops 983040 | bytes 524288 | tf_op jit(solution)/shard_map/proximal/pallas_call | solution.py:301
  (5 shorter events, 0.2 us)
Async XLA Ops:
  0.0 31.7 %collective-permute-start.2 = (f32[256,1024]{1,0:T(8,128)}, f32[256,1024]{1,0:T(8,128)S(1)}, u32[]{:S(2)}, u32[]{:S(2)}) collective-permute-start(f32[256,1024]{1,0:T(8,128)} %refs_1_.1), channel_id=1, source_target_pairs={{0,1},{1,2},{2,3},{3,4},{4,5},{5,6},{6,7},{7,8},{8,9},{9,10},{10,1... | collective-permute-start | bytes 3145736 | tf_op jit(solution)/shard_map/ppermute | solution.py:323
  9.1 34.8 %collective-permute-start.1 = (f32[128,1024]{1,0:T(8,128)S(1)}, f32[128,1024]{1,0:T(8,128)S(1)}, u32[]{:S(2)}, u32[]{:S(2)}) collective-permute-start(f32[128,1024]{1,0:T(8,128)S(1)} %get-tuple-element.43), channel_id=1, source_target_pairs={{0,31},{1,0},{2,1},{3,2},{4,3},{5,4},{6,5},{7,6},{8,7},{9,8},{10,9... | collective-permute-start | bytes 1572872 | tf_op jit(solution)/shard_map/ppermute | solution.py:323
  11.0 43.0 %collective-permute-start = (f32[128,1024]{1,0:T(8,128)S(1)}, f32[128,1024]{1,0:T(8,128)S(1)}, u32[]{:S(2)}, u32[]{:S(2)}) collective-permute-start(f32[128,1024]{1,0:T(8,128)S(1)} %get-tuple-element.44), channel_id=1, source_target_pairs={{0,31},{1,0},{2,1},{3,2},{4,3},{5,4},{6,5},{7,6},{8,7},{9,8},{10,9... | collective-permute-start | bytes 1572872 | tf_op jit(solution)/shard_map/ppermute | solution.py:323
  13.8 1.9 %copy-start = (f32[1,3,16,128,128]{4,3,2,1,0:T(8,128)S(1)}, f32[1,3,16,128,128]{4,3,2,1,0:T(8,128)}, u32[]{:S(2)}) copy-start(f32[1,3,16,128,128]{4,3,2,1,0:T(8,128)} %omega_ref.3) | copy-start | bytes 9437188
  15.6 1.2 %copy-start.2 = (f32[256,1024]{1,0:T(8,128)S(1)}, f32[256,1024]{1,0:T(8,128)}, u32[]{:S(2)}) copy-start(f32[256,1024]{1,0:T(8,128)} %refs_1_.1) | copy-start | bytes 3145732
  16.9 14.8 %copy-start.1 = (f32[1,3,16,128,128]{4,3,2,1,0:T(8,128)S(1)}, f32[1,3,16,128,128]{4,3,2,1,0:T(8,128)}, u32[]{:S(2)}) copy-start(f32[1,3,16,128,128]{4,3,2,1,0:T(8,128)} %omega_ref.3) | copy-start | bytes 9437188
  56.8 6.0 %collective-permute-start.3 = (f32[4,3,128,128]{3,2,1,0:T(8,128)S(1)}, f32[4,3,128,128]{3,2,1,0:T(8,128)S(1)}, u32[]{:S(2)}, u32[]{:S(2)}) collective-permute-start(f32[4,3,128,128]{3,2,1,0:T(8,128)S(1)} %get-tuple-element.31), channel_id=1, source_target_pairs={{0,32},{32,0},{1,33},{33,1},{2,34},{34,2},{3,35},{35,3},{4,36},{36... | collective-permute-start | bytes 2359304 | tf_op jit(solution)/shard_map/ppermute | solution.py:323
  60.4 4.9 %collective-permute-start.7 = (f32[4,3,128,128]{3,2,1,0:T(8,128)S(1)}, f32[4,3,128,128]{3,2,1,0:T(8,128)S(1)}, u32[]{:S(2)}, u32[]{:S(2)}) collective-permute-start(f32[4,3,128,128]{3,2,1,0:T(8,128)S(1)} %get-tuple-element.36), channel_id=1, source_target_pairs={{0,32},{32,0},{1,33},{33,1},{2,34},{34,2},{3,35},{35,3},{4,36},{36... | collective-permute-start | bytes 2359304 | tf_op jit(solution)/shard_map/ppermute | solution.py:323
  62.9 9.7 %collective-permute-start.4 = (f32[2,3,128,128]{3,2,1,0:T(8,128)S(1)}, f32[2,3,128,128]{3,2,1,0:T(8,128)S(1)}, u32[]{:S(2)}, u32[]{:S(2)}) collective-permute-start(f32[2,3,128,128]{3,2,1,0:T(8,128)S(1)} %slice_add_fusion.1), channel_id=1, source_target_pairs={{0,128},{32,416},{128,0},{160,288},{256,384},{288,160},{384,256},{... | collective-permute-start | bytes 1179656 | tf_op jit(solution)/shard_map/ppermute | solution.py:332
  65.4 11.8 %collective-permute-start.8 = (f32[2,3,128,128]{3,2,1,0:T(8,128)S(1)}, f32[2,3,128,128]{3,2,1,0:T(8,128)S(1)}, u32[]{:S(2)}, u32[]{:S(2)}) collective-permute-start(f32[2,3,128,128]{3,2,1,0:T(8,128)S(1)} %slice_add_fusion), channel_id=1, source_target_pairs={{0,128},{32,416},{128,0},{160,288},{256,384},{288,160},{384,256},{... | collective-permute-start | bytes 1179656 | tf_op jit(solution)/shard_map/ppermute | solution.py:332
  72.6 7.7 %collective-permute-start.5 = (f32[3,128,128]{2,1,0:T(8,128)S(1)}, f32[3,128,128]{2,1,0:T(8,128)S(1)}, u32[]{:S(2)}, u32[]{:S(2)}) collective-permute-start(f32[3,128,128]{2,1,0:T(8,128)S(1)} %fusion.1), channel_id=1, source_target_pairs={{0,384},{32,160},{128,256},{160,32},{256,128},{288,416},{384,0},{4... | collective-permute-start | bytes 589832 | tf_op jit(solution)/shard_map/ppermute | solution.py:332
  77.2 12.8 %collective-permute-start.9 = (f32[3,128,128]{2,1,0:T(8,128)S(1)}, f32[3,128,128]{2,1,0:T(8,128)S(1)}, u32[]{:S(2)}, u32[]{:S(2)}) collective-permute-start(f32[3,128,128]{2,1,0:T(8,128)S(1)} %fusion), channel_id=1, source_target_pairs={{0,384},{32,160},{128,256},{160,32},{256,128},{288,416},{384,0},{4... | collective-permute-start | bytes 589832 | tf_op jit(solution)/shard_map/ppermute | solution.py:332
  80.3 13.6 %collective-permute-start.6 = (f32[2,128,128]{2,1,0:T(8,128)S(1)}, f32[2,128,128]{2,1,0:T(8,128)S(1)}, u32[]{:S(2)}, u32[]{:S(2)}) collective-permute-start(f32[2,128,128]{2,1,0:T(8,128)S(1)} %slice_add_fusion.6), channel_id=1, source_target_pairs={{0,64},{64,0},{1,65},{65,1},{2,66},{66,2},{3,67},{67,3},{4,68},{68... | collective-permute-start | bytes 393224 | tf_op jit(solution)/shard_map/ppermute | solution.py:323
  83.9 23.4 %collective-permute-start.10 = (f32[128,128]{1,0:T(8,128)S(1)}, f32[128,128]{1,0:T(8,128)S(1)}, u32[]{:S(2)}, u32[]{:S(2)}) collective-permute-start(f32[128,128]{1,0:T(8,128)S(1)} %fusion.4), channel_id=1, source_target_pairs={{0,64},{64,0},{1,65},{65,1},{2,66},{66,2},{3,67},{67,3},{4,68},{68... | collective-permute-start | bytes 196616 | tf_op jit(solution)/shard_map/ppermute | solution.py:323
  94.5 12.8 %collective-permute-start.11 = (f32[128,128]{1,0:T(8,128)S(1)}, f32[128,128]{1,0:T(8,128)S(1)}, u32[]{:S(2)}, u32[]{:S(2)}) collective-permute-start(f32[128,128]{1,0:T(8,128)S(1)} %get-tuple-element.40), channel_id=1, source_target_pairs={{0,1},{1,0},{4,5},{5,4},{8,9},{9,8},{12,13},{13,12},{16,17},{17,16... | collective-permute-start | bytes 196616 | tf_op jit(solution)/shard_map/ppermute | solution.py:344
  95.2 12.5 %collective-permute-start.12 = (f32[128,128]{1,0:T(8,128)S(1)}, f32[128,128]{1,0:T(8,128)S(1)}, u32[]{:S(2)}, u32[]{:S(2)}) collective-permute-start(f32[128,128]{1,0:T(8,128)S(1)} %get-tuple-element.41), channel_id=1, source_target_pairs={{1,2},{2,1},{3,4},{4,3},{5,6},{6,5},{7,8},{8,7},{9,10},{10,9},{11,... | collective-permute-start | bytes 196616 | tf_op jit(solution)/shard_map/ppermute | solution.py:344
  105.4 6.2 %collective-permute-start.13 = (f32[128,128]{1,0:T(8,128)S(1)}, f32[128,128]{1,0:T(8,128)S(1)}, u32[]{:S(2)}, u32[]{:S(2)}) collective-permute-start(f32[128,128]{1,0:T(8,128)S(1)} %get-tuple-element.42), channel_id=1, source_target_pairs={{2,3},{3,2},{6,7},{7,6},{10,11},{11,10},{14,15},{15,14},{18,19},{1... | collective-permute-start | bytes 196616 | tf_op jit(solution)/shard_map/ppermute | solution.py:344
